TPU v7x, 32 devices: a whole 2x2x4 slice. The times are simulated.
32 devices in a mesh: fsdp: 32 (over z, y, x, core).
Axes of the slice: x: 2, y: 2, z: 4, core: 2. Of those that a mesh axis runs over, the one named last changes fastest.
Arguments:
- frames_in: bfloat16 [4096, 1024], P('fsdp'), may hold values from -6 to 6
- segment_ids: int32 [4096], P('fsdp'), may hold values from 0 to 1, as said below
- gain_attn: bfloat16 [8192], P('fsdp'), may hold values from 0.099609375 to 1.8984375
- w_qkv: bfloat16 [8192, 3072], P('fsdp'), may hold values from -0.1875 to 0.1875
- w_out: bfloat16 [8192, 1024], P('fsdp'), may hold values from -0.375 to 0.375
- gain_ffn: bfloat16 [8192], P('fsdp'), may hold values from 0.099609375 to 1.8984375
- w_gate_up: bfloat16 [8192, 5632], P('fsdp'), may hold values from -0.1875 to 0.1875
- w_down: bfloat16 [22528, 1024], P('fsdp'), may hold values from -0.109375 to 0.109375
- cotangent: bfloat16 [4096, 1024], P('fsdp'), may hold values from -6 to 6
Outputs:
- block_out: bfloat16 [4096, 1024], P('fsdp')
- grad_in: float32 [4096, 1024], P('fsdp')
- grad_gain_attn: float32 [8192], P('fsdp')
- grad_w_qkv: float32 [8192, 3072], P('fsdp')
- grad_w_out: float32 [8192, 1024], P('fsdp')
- grad_gain_ffn: float32 [8192], P('fsdp')
- grad_w_gate_up: float32 [8192, 5632], P('fsdp')
- grad_w_down: float32 [22528, 1024], P('fsdp')
Inputs may be any that keep to these rules, and one draw needn't show every extreme that they name: `segment_ids`: within each frame of 8 tokens the ids are 1 on a leading run of 1 to 8 tokens and 0 on the rest.
All inputs are finite; a program needn't handle non-finite values.
Results may differ from a plain program's by a relative error of at most 0.01.
Values may be sent and summed in bfloat16 or wider, within the bound.
No kernel may reach another device: no remote copies, remote signals or barrier semaphores. Data moves between devices by JAX's collectives and lax.ppermute only.
A program may use at most 192 MiB of HBM per device.

v0:
```python
import jax
import jax.numpy as jnp
from jax import lax
from jax.sharding import PartitionSpec as P

D = 1024
FF = 2816
HEADS = 16
HEAD_DIM = 64
POS = 8


EPSILON = 1e-05


def for_sending(array):

    def short(part):
        return part.astype(jnp.bfloat16) if part.dtype == jnp.float32 else part

    return jax.tree.map(short, array)


def swapped(block, axis, stride):
    count = lax.axis_size(axis)
    route = []
    for low in range(count):
        high = low | 1 << stride
        if high != low and high < count:
            route += [(low, high), (high, low)]
    return lax.ppermute(block, axis, route)


def positions_layout(frame_rows, groups):
    width = frame_rows.shape[-1]
    per_piece = frame_rows.shape[0] // POS // groups
    shaped = frame_rows.reshape(groups, per_piece, POS, width).transpose(2, 0, 1, 3)
    return shaped.reshape(POS * groups, per_piece, width)


def frames_layout(piece_rows, groups):
    width = piece_rows.shape[-1]
    per_piece = piece_rows.shape[1]
    shaped = piece_rows.reshape(POS, groups, per_piece, width).transpose(1, 2, 0, 3)
    return shaped.reshape(groups * per_piece * POS, width)


def inner_rows(left, right):
    return lax.dot_general(
        left, right, (((0,), (0,)), ((), ())), preferred_element_type=jnp.float32
    )


def times_transposed(left, right):
    return lax.dot_general(
        left, right, (((1,), (1,)), ((), ())), preferred_element_type=jnp.float32
    )


def join_pieces(current, partner, member, bit_level):
    upper_half = member >> bit_level & 1 == 1
    return tuple(
        (
            jnp.where(
                upper_half,
                jnp.concatenate([theirs, own_piece], 0),
                jnp.concatenate([own_piece, theirs], 0),
            )
            for own_piece, theirs in zip(current, partner)
        )
    )


def collect_forward(pieces, member, levels):
    current = pieces
    for bit_level in range(levels):
        partner = jax.tree.map(
            lambda part, own: part.astype(own.dtype),
            swapped(for_sending(current), "fsdp", bit_level),
            current,
        )
        current = join_pieces(current, partner, member, bit_level)
    return current


def collect_again(pieces, member, levels):
    current = pieces
    for bit_level in range(levels):
        partner = jax.tree.map(
            lambda part, own: part.astype(own.dtype),
            swapped(for_sending(current), "fsdp", bit_level),
            current,
        )
        current = join_pieces(current, partner, member, bit_level)
    return current


def halving_sum(terms, member, levels, sender):
    current = terms
    for bit_level in reversed(range(levels)):
        upper_half = member >> bit_level & 1 == 1
        leaving = tuple(
            (
                jnp.where(
                    upper_half,
                    term_part[: term_part.shape[0] // 2],
                    term_part[term_part.shape[0] // 2 :],
                )
                for term_part in current
            )
        )
        staying = tuple(
            (
                jnp.where(
                    upper_half,
                    term_part[term_part.shape[0] // 2 :],
                    term_part[: term_part.shape[0] // 2],
                )
                for term_part in current
            )
        )
        arrived = sender(leaving, bit_level)
        current = tuple((held_part + come_part for held_part, come_part in zip(staying, arrived)))
    return current


def send_whole(parts, bit_level):
    return jax.tree.map(
        lambda part, own: part.astype(own.dtype),
        swapped(for_sending(parts), "fsdp", bit_level),
        parts,
    )


def permitted(validity):
    row_place = lax.broadcasted_iota(jnp.int32, (POS, POS), 0)
    column_place = lax.broadcasted_iota(jnp.int32, (POS, POS), 1)
    causal = column_place <= row_place
    same_segment = validity[:, :, None] == validity[:, None, :]
    return (causal[None] & same_segment)[:, None]


def split_projections(qkv_frames):
    frames = qkv_frames.shape[0] // POS
    shaped = qkv_frames.reshape(frames, POS, 3, HEADS, HEAD_DIM)
    return (shaped[:, :, 0], shaped[:, :, 1], shaped[:, :, 2])


def masked_scores(queries, key_rows, allowed):
    scores = jnp.einsum(
        "fqhd,fkhd->fhqk", queries, key_rows, preferred_element_type=jnp.float32
    ) * HEAD_DIM ** (-0.5)
    return jnp.where(allowed, scores, -jnp.inf)


def attend(qkv_frames, validity):
    queries, key_rows, value_rows = split_projections(qkv_frames)
    scores = masked_scores(queries, key_rows, permitted(validity))
    highest = jnp.max(scores, axis=-1, keepdims=True)
    raised = jnp.exp(scores - highest)
    totals = jnp.sum(raised, axis=-1, keepdims=True)
    attn_probs = (raised / totals).astype(jnp.bfloat16)
    attended = jnp.einsum(
        "fhqk,fkhd->fqhd", attn_probs, value_rows, preferred_element_type=jnp.float32
    )
    mixed_heads = attended.reshape(qkv_frames.shape[0], D).astype(jnp.bfloat16)
    return (mixed_heads, highest + jnp.log(totals))


def attend_back(qkv_frames, validity, log_total, d_mixed):
    queries, key_rows, value_rows = split_projections(qkv_frames)
    frames = queries.shape[0]
    scores = masked_scores(queries, key_rows, permitted(validity))
    weights_full = jnp.exp(scores - log_total)
    attn_probs = weights_full.astype(jnp.bfloat16)
    d_heads = d_mixed.reshape(frames, POS, HEADS, HEAD_DIM)
    d_probs = jnp.einsum("fqhd,fkhd->fhqk", d_heads, value_rows, preferred_element_type=jnp.float32)
    d_values = jnp.einsum(
        "fhqk,fqhd->fkhd", attn_probs, d_heads, preferred_element_type=jnp.float32
    )
    d_scores = weights_full * (d_probs - jnp.sum(d_probs * weights_full, axis=-1, keepdims=True))
    d_scores = d_scores.astype(jnp.bfloat16)
    d_queries = jnp.einsum(
        "fhqk,fkhd->fqhd", d_scores, key_rows, preferred_element_type=jnp.float32
    ) * HEAD_DIM ** (-0.5)
    d_keys = jnp.einsum(
        "fhqk,fqhd->fkhd", d_scores, queries, preferred_element_type=jnp.float32
    ) * HEAD_DIM ** (-0.5)
    stacked = jnp.stack([d_queries, d_keys, d_values], axis=2)
    return stacked.reshape(frames * POS, 3 * D).astype(jnp.bfloat16)


def body(frames_in, segment_ids, gain_attn, w_qkv, w_out, gain_ffn, w_gate_up, w_down, cotangent):
    devices = lax.axis_size("fsdp")
    groups = devices // POS
    levels = groups.bit_length() - 1
    member = lax.axis_index("fsdp") % groups
    per_piece = frames_in.shape[0] // POS // groups
    validity = segment_ids.reshape(-1, POS)
    moved_input, moved_cotangent = (
        lax.all_to_all(
            positions_layout(frames_in, groups), "fsdp", split_axis=0, concat_axis=0, tiled=True
        ),
        lax.all_to_all(
            positions_layout(cotangent, groups), "fsdp", split_axis=0, concat_axis=0, tiled=True
        ),
    )
    inputs = moved_input.reshape(-1, D).astype(jnp.float32)
    upstream = moved_cotangent.reshape(-1, D)
    own_pieces = (w_qkv, w_out, w_gate_up, w_down, gain_attn, gain_ffn)
    collected = collect_forward(own_pieces, member, levels)
    whole_qkv, whole_out, whole_gate_up, whole_down, whole_gain_attn, whole_gain_ffn = collected
    gain_first = whole_gain_attn.astype(jnp.float32)
    gain_second = whole_gain_ffn.astype(jnp.float32)
    scale_first = lax.rsqrt(jnp.mean(inputs * inputs, axis=-1, keepdims=True) + EPSILON)
    normed_first = inputs * scale_first
    lowered_first = (normed_first * gain_first).astype(jnp.bfloat16)
    projected = jnp.dot(lowered_first, whole_qkv, preferred_element_type=jnp.float32).astype(
        jnp.bfloat16
    )
    qkv_frames = frames_layout(
        lax.all_to_all(
            projected.reshape(devices, per_piece, 3 * D),
            "fsdp",
            split_axis=0,
            concat_axis=0,
            tiled=True,
        ),
        groups,
    )
    mixed_frames, log_total = attend(qkv_frames, validity)
    mixed_rows = lax.all_to_all(
        positions_layout(mixed_frames, groups), "fsdp", split_axis=0, concat_axis=0, tiled=True
    ).reshape(-1, D)
    residual = inputs + jnp.dot(mixed_rows, whole_out, preferred_element_type=jnp.float32)
    scale_second = lax.rsqrt(jnp.mean(residual * residual, axis=-1, keepdims=True) + EPSILON)
    normed_second = residual * scale_second
    lowered_second = (normed_second * gain_second).astype(jnp.bfloat16)
    gate_up = jnp.dot(lowered_second, whole_gate_up, preferred_element_type=jnp.float32)
    gate_part = gate_up[:, :FF]
    up_part = gate_up[:, FF:]
    sigmoid_gate = jax.nn.sigmoid(gate_part)
    activated = gate_part * sigmoid_gate
    hidden = (activated * up_part).astype(jnp.bfloat16)
    result_rows = (
        residual + jnp.dot(hidden, whole_down, preferred_element_type=jnp.float32)
    ).astype(jnp.bfloat16)
    block_out = frames_layout(
        lax.all_to_all(
            result_rows.reshape(devices, per_piece, D),
            "fsdp",
            split_axis=0,
            concat_axis=0,
            tiled=True,
        ),
        groups,
    )
    collected = collect_again(own_pieces, member, levels)
    whole_qkv, whole_out, whole_gate_up, whole_down, whole_gain_attn, whole_gain_ffn = collected
    gain_first = whole_gain_attn.astype(jnp.float32)
    gain_second = whole_gain_ffn.astype(jnp.float32)
    grad_down_term = inner_rows(hidden, upstream)
    d_hidden = times_transposed(upstream, whole_down)
    d_gate = d_hidden * up_part * sigmoid_gate * (1.0 + gate_part * (1.0 - sigmoid_gate))
    d_up = d_hidden * activated
    d_gate_up = jnp.concatenate([d_gate, d_up], axis=1).astype(jnp.bfloat16)
    grad_gate_up_term = inner_rows(lowered_second, d_gate_up)
    d_second = times_transposed(d_gate_up, whole_gate_up)
    grad_gain_ffn_term = jnp.sum(d_second * normed_second, axis=0)
    scaled_second = d_second * gain_second
    d_residual = upstream.astype(jnp.float32) + scale_second * (
        scaled_second
        - normed_second * jnp.mean(scaled_second * normed_second, axis=-1, keepdims=True)
    )
    d_branch = d_residual.astype(jnp.bfloat16)
    grad_out_term = inner_rows(mixed_rows, d_branch)
    d_mixed = times_transposed(d_branch, whole_out).astype(jnp.bfloat16)
    d_mixed_frames = frames_layout(
        lax.all_to_all(
            d_mixed.reshape(devices, per_piece, D), "fsdp", split_axis=0, concat_axis=0, tiled=True
        ),
        groups,
    )
    d_qkv_frames = attend_back(qkv_frames, validity, log_total, d_mixed_frames)
    d_projected = lax.all_to_all(
        positions_layout(d_qkv_frames, groups), "fsdp", split_axis=0, concat_axis=0, tiled=True
    ).reshape(-1, 3 * D)
    grad_qkv_term = inner_rows(lowered_first, d_projected)
    d_first = times_transposed(d_projected, whole_qkv)
    grad_gain_attn_term = jnp.sum(d_first * normed_first, axis=0)
    scaled_first = d_first * gain_first
    d_inputs = d_residual + scale_first * (
        scaled_first - normed_first * jnp.mean(scaled_first * normed_first, axis=-1, keepdims=True)
    )
    grad_in = frames_layout(
        lax.all_to_all(
            d_inputs.reshape(devices, per_piece, D).astype(jnp.bfloat16),
            "fsdp",
            split_axis=0,
            concat_axis=0,
            tiled=True,
        ).astype(jnp.float32),
        groups,
    )
    shares = halving_sum(
        (
            grad_qkv_term,
            grad_out_term,
            grad_gate_up_term,
            grad_down_term,
            grad_gain_attn_term,
            grad_gain_ffn_term,
        ),
        member,
        levels,
        send_whole,
    )
    return (block_out, grad_in, shares[4], shares[0], shares[1], shares[5], shares[2], shares[3])


def solution(mesh):
    in_specs = (
        P("fsdp", None),
        P("fsdp"),
        P("fsdp"),
        P("fsdp", None),
        P("fsdp", None),
        P("fsdp"),
        P("fsdp", None),
        P("fsdp", None),
        P("fsdp", None),
    )
    out_specs = (
        P("fsdp", None),
        P("fsdp", None),
        P("fsdp"),
        P("fsdp", None),
        P("fsdp", None),
        P("fsdp"),
        P("fsdp", None),
        P("fsdp", None),
    )
    return jax.shard_map(body, mesh=mesh, in_specs=in_specs, out_specs=out_specs, check_vma=False)
```

profile of v0, /device:TPU:0, one launch (start us, length us, event | category | flops | bytes accessed | tf_op | source)
XLA Modules:
  0.0 775.5 jit_solution(7697368398177352639)
XLA Ops:
  1.3 3.3 collective-permute-done.2
  4.6 4.5 maximum_select_fusion.4
  9.1 2.9 collective-permute-start.3
  12.0 7.0 maximum_select_fusion.2
  19.9 6.3 all-to-all-start
  27.5 1.8 collective-permute-start.1
  29.4 177.7 %collective-permute-done.1 = bf16[512]{0:T(512)(128)(2,1)S(1)} collective-permute-done((bf16[512]{0:T(512)(128)(2,1)S(1)}, bf16[512]{0:T(512)(128)(2,1)S(1)}, u32[]{:S(2)}, u32[]{:S(2)}) %collective-permute-start.1) | collective-permute-done | bytes 1056 | tf_op jit(solution)/shard_map/ppermute | solution.py:31
  209.1 6.0 convolution_convert_fusion
  216.3 4.9 all-to-all-start.1
  223.5 1.8 collective-permute-start.7
  225.4 3.1 maximum_select_fusion.11
  228.8 3.9 maximum_select_fusion.5
  232.7 1.8 collective-permute-start.11
  234.4 7.4 all-to-all-done.1
  241.8 3.6 all-to-all-start.4
  247.5 1.6 fusion.41
  251.6 70.3 %all-to-all-done.4 = bf16[32,4,1024]{2,1,0:T(4,128)(2,1)S(1)} async-done(((bf16[32,4,1024]{2,1,0:T(4,128)(2,1)}), bf16[32,4,1024]{2,1,0:T(4,128)(2,1)S(1)}, u32[]{:S(2)}, u32[]{:S(2)}) %all-to-all-start.4) | async-done | bytes 262176 | tf_op jit(solution)/shard_map/all_to_all | solution.py:204
  321.9 3.7 all-to-all-start.2
  326.4 1.6 multiply_convert_fusion.4
  329.0 7.2 all-to-all-done.2
  336.3 3.0 multiply_reduce_fusion.5
  339.3 9.8 %fusion.1 = f32[128,5632]{1,0:T(8,128)S(1)} fusion(bf16[512,5632]{1,0:T(8,128)(2,1)} %maximum_select_fusion.2, bf16[512,5632]{1,0:T(8,128)(2,1)} %collective-permute-done.9, pred[]{:T(512)S(6)} %eq.18, f32[128,1024]{1,0:T(8,128)S(1)} %get-tuple-element.21, f32[1024]{0:T(1024)S(1)} %fusion.30, f32[128]{0:T(128)S(1)} %add_rsqrt_fusion.1), kind=kOutput, calls=%fused_computation.25 | convolution fusion | flops 1528692736 | bytes 14946817 | tf_op jit(solution)/shard_map/dot_general | solution.py:239
  349.1 7.7 multiply_convert_fusion.1
  357.7 5.8 fusion.10
  364.3 10.8 %fusion.12 = f32[1024,5632]{1,0:T(8,128)} fusion(bf16[128,2816]{1,0:T(8,128)(2,1)} %get-tuple-element.13, bf16[128,2816]{1,0:T(8,128)(2,1)} %get-tuple-element.12, f32[128,1024]{1,0:T(8,128)S(1)} %get-tuple-element.21, f32[1024]{0:T(1024)S(1)} %fusion.30, f32[128]{0:T(128)S(1)} %add_rsqrt_fusion.1), kind=kOutput, calls=%fused_computation.58 | convolution fusion | flops 1479671808 | bytes 25039360 | tf_op jit(solution)/shard_map/dot_general | solution.py:49
  375.1 10.2 %multiply_reduce_fusion.1 = (f32[1024]{0:T(1024)S(1)}, f32[128]{0:T(128)S(1)}, f32[128,1024]{1,0:T(8,128)S(1)}) fusion(f32[128,1024]{1,0:T(8,128)S(1)} %get-tuple-element.21, f32[128]{0:T(128)S(1)} %add_rsqrt_fusion.1, f32[1024]{0:T(1024)S(1)} %fusion.30, bf16[512,5632]{1,0:T(8,128)(2,1)} %maximum_select_fusion.2, ...), kind=kOutput, calls=%fused_computation.65 | convolution fusion | flops 1531968384 | bytes 14033921 | tf_op jit(solution)/shard_map/dot_general | solution.py:55
  385.6 2.7 fusion.26
  388.3 3.1 convolution_convert_fusion.3
  392.2 2.6 all-to-all-start.5
  394.8 3.4 select_convert_fusion.6
  398.1 1.6 collective-permute-start.16
  400.7 5.9 fusion.42
  406.7 17.3 %all-to-all-start.3 = ((bf16[32,4,1024]{2,1,0:T(4,128)(2,1)}), bf16[32,4,1024]{2,1,0:T(4,128)(2,1)}, u32[]{:S(2)}, u32[]{:S(2)}) async-start(bf16[32,4,1024]{2,1,0:T(4,128)(2,1)} %reshape.251), calls=%async_computation.3 | async-start | bytes 524288 | tf_op jit(solution)/shard_map/all_to_all | solution.py:249
  427.7 1.5 copy.105
  429.2 3.1 convert_element_type.176
  432.3 2.6 copy.106
  434.9 5.8 all-to-all-start.6
  440.8 11.0 %select_convert_fusion = bf16[512,5632]{1,0:T(8,128)(2,1)} fusion(f32[1024,5632]{1,0:T(8,128)} %fusion.12, pred[]{:T(512)S(6)} %eq.18), kind=kLoop, calls=%fused_computation.2 | loop fusion | flops 2883584 | bytes 17301504 | tf_op jit(solution)/shard_map/convert_element_type | solution.py:19
  451.8 1.7 collective-permute-start.20
  453.6 2.1 select_convert_fusion.2
  457.3 1.8 copy.98
  459.1 2.2 all-to-all-done.6
  461.4 7.5 convolution_bitcast_fusion
  468.9 6.9 select_convert_fusion.1
  475.8 1.5 collective-permute-start.14
  477.3 1.9 convert_add_fusion.6
  480.7 2.4 reshape.260
  483.1 7.6 multiply_reduce_fusion.2
  492.3 149.9 %collective-permute-done.22 = bf16[1408,1024]{1,0:T(8,128)(2,1)} collective-permute-done((bf16[1408,1024]{1,0:T(8,128)(2,1)}, bf16[1408,1024]{1,0:T(8,128)(2,1)}, u32[]{:S(2)}, u32[]{:S(2)}) %collective-permute-start.22) | collective-permute-done | bytes 2883616 | tf_op jit(solution)/shard_map/ppermute | solution.py:31
  642.3 5.9 convert_add_fusion.2
  648.2 4.0 select_convert_fusion.5
  652.2 57.0 %collective-permute-done.14 = bf16[512,3072]{1,0:T(8,128)(2,1)} collective-permute-done((bf16[512,3072]{1,0:T(8,128)(2,1)}, bf16[512,3072]{1,0:T(8,128)(2,1)}, u32[]{:S(2)}, u32[]{:S(2)}) %collective-permute-start.14) | collective-permute-done | bytes 3145760 | tf_op jit(solution)/shard_map/ppermute | solution.py:31
  709.2 7.2 convert_add_fusion.1
  716.5 12.7 %convert_add_fusion = f32[512,5632]{1,0:T(8,128)S(1)} fusion(bf16[512,5632]{1,0:T(8,128)(2,1)} %collective-permute-done.20, f32[1024,5632]{1,0:T(8,128)} %fusion.12, pred[]{:T(512)S(6)} %eq.18), kind=kLoop, calls=%fused_computation.1 | loop fusion | flops 8650752 | bytes 40370176 | tf_op jit(solution)/shard_map/add | solution.py:123
  729.2 4.2 copy-done
  733.4 2.1 select_convert_fusion.3
  738.4 1.7 convert_element_type.178
  740.2 5.3 all-to-all-start.7
  745.8 2.3 convert_add_fusion.7
  748.6 7.4 all-to-all-done.7
  756.1 1.9 copy.107
  758.0 5.5 convert_add_fusion.5
  763.5 6.0 convert_add_fusion.4
  769.6 5.7 convert_add_fusion.3
  (166 shorter events, 30.8 us)
Async XLA Ops:
  0.6 11.4 %copy-start.7 = (bf16[256,5632]{1,0:T(8,128)(2,1)S(1)}, bf16[256,5632]{1,0:T(8,128)(2,1)}, u32[]{:S(2)}) copy-start(bf16[256,5632]{1,0:T(8,128)(2,1)} %param.15) | copy-start | bytes 8650756
  0.6 3.9 collective-permute-start.2
  1.2 10.8 %collective-permute-start.8 = (bf16[256,5632]{1,0:T(8,128)(2,1)}, bf16[256,5632]{1,0:T(8,128)(2,1)}, u32[]{:S(2)}, u32[]{:S(2)}) collective-permute-start(bf16[256,5632]{1,0:T(8,128)(2,1)} %param.15), channel_id=1, source_target_pairs={{0,1},{1,0},{2,3},{3,2},{4,5},{5,4},{6,7},{7,6},{8,9},{9,8},{10,11... | collective-permute-start | bytes 8650760 | tf_op jit(solution)/shard_map/ppermute | solution.py:31
  9.1 9.9 %copy-start.21 = (bf16[128,1024]{1,0:T(8,128)(2,1)S(1)}, bf16[128,1024]{1,0:T(8,128)(2,1)}, u32[]{:S(2)}) copy-start(bf16[128,1024]{1,0:T(8,128)(2,1)} %param.9) | copy-start | bytes 786436
  9.1 17.2 %copy-start.26 = (bf16[256]{0:T(256)(128)(2,1)S(1)}, bf16[256]{0:T(256)(128)(2,1)}, u32[]{:S(2)}) copy-start(bf16[256]{0:T(256)(128)(2,1)} %param.11) | copy-start | bytes 1540
  9.1 199.6 %collective-permute-start.3 = (bf16[512,3072]{1,0:T(8,128)(2,1)}, bf16[512,3072]{1,0:T(8,128)(2,1)}, u32[]{:S(2)}, u32[]{:S(2)}) collective-permute-start(bf16[512,3072]{1,0:T(8,128)(2,1)} %maximum_select_fusion.4), channel_id=1, source_target_pairs={{0,2},{2,0},{1,3},{3,1},{4,6},{6,4},{5,7},{7,5},{8,10},{10,8},{9,1... | collective-permute-start | bytes 9437192 | tf_op jit(solution)/shard_map/ppermute | solution.py:31
  19.0 320.3 %collective-permute-start.9 = (bf16[512,5632]{1,0:T(8,128)(2,1)}, bf16[512,5632]{1,0:T(8,128)(2,1)}, u32[]{:S(2)}, u32[]{:S(2)}) collective-permute-start(bf16[512,5632]{1,0:T(8,128)(2,1)} %maximum_select_fusion.2), channel_id=1, source_target_pairs={{0,2},{2,0},{1,3},{3,1},{4,6},{6,4},{5,7},{7,5},{8,10},{10,8},{9,1... | collective-permute-start | bytes 17301512 | tf_op jit(solution)/shard_map/ppermute | solution.py:31
  19.9 188.3 %all-to-all-start = ((bf16[32,4,1024]{2,1,0:T(4,128)(2,1)}), bf16[32,4,1024]{2,1,0:T(4,128)(2,1)S(1)}, u32[]{:S(2)}, u32[]{:S(2)}) async-start(bf16[32,4,1024]{2,1,0:T(4,128)(2,1)} %bitcast.2), calls=%async_computation | async-start | bytes 524288 | tf_op jit(solution)/shard_map/all_to_all | solution.py:201
  26.3 1.2 collective-permute-start
  27.5 179.5 %collective-permute-start.1 = (bf16[512]{0:T(512)(128)(2,1)S(1)}, bf16[512]{0:T(512)(128)(2,1)S(1)}, u32[]{:S(2)}, u32[]{:S(2)}) collective-permute-start(bf16[512]{0:T(512)(128)(2,1)S(1)} %maximum_select_fusion.18), channel_id=1, source_target_pairs={{0,2},{2,0},{1,3},{3,1},{4,6},{6,4},{5,7},{7,5},{8,10},{10,8},{9,1... | collective-permute-start | bytes 3080 | tf_op jit(solution)/shard_map/ppermute | solution.py:31
  29.4 199.4 %collective-permute-start.10 = (bf16[704,1024]{1,0:T(8,128)(2,1)}, bf16[704,1024]{1,0:T(8,128)(2,1)}, u32[]{:S(2)}, u32[]{:S(2)}) collective-permute-start(bf16[704,1024]{1,0:T(8,128)(2,1)} %param.16), channel_id=1, source_target_pairs={{0,1},{1,0},{2,3},{3,2},{4,5},{5,4},{6,7},{7,6},{8,9},{9,8},{10,11... | collective-permute-start | bytes 4325384 | tf_op jit(solution)/shard_map/ppermute | solution.py:31
  208.6 127.6 %copy-start.8 = (f32[128,1024]{1,0:T(8,128)}, f32[128,1024]{1,0:T(8,128)S(1)}, u32[]{:S(2)}) copy-start(f32[128,1024]{1,0:T(8,128)S(1)} %reshape.264) | copy-start | bytes 1572868
  208.6 12.9 %copy-start.28 = (bf16[256]{0:T(256)(128)(2,1)S(1)}, bf16[256]{0:T(256)(128)(2,1)}, u32[]{:S(2)}) copy-start(bf16[256]{0:T(256)(128)(2,1)} %param.14) | copy-start | bytes 1540
  208.7 13.1 %copy-start.27 = (s32[128]{0:T(128)S(1)}, s32[128]{0:T(128)}, u32[]{:S(2)}) copy-start(s32[128]{0:T(128)} %param.10) | copy-start | bytes 1540
  208.7 13.9 %copy-start.22 = (bf16[128,1024]{1,0:T(8,128)(2,1)S(1)}, bf16[128,1024]{1,0:T(8,128)(2,1)}, u32[]{:S(2)}) copy-start(bf16[128,1024]{1,0:T(8,128)(2,1)} %param.17) | copy-start | bytes 786436
  215.1 13.7 %copy-start.14 = (bf16[704,1024]{1,0:T(8,128)(2,1)S(1)}, bf16[704,1024]{1,0:T(8,128)(2,1)}, u32[]{:S(2)}) copy-start(bf16[704,1024]{1,0:T(8,128)(2,1)} %param.16) | copy-start | bytes 4325380
  216.3 25.5 %all-to-all-start.1 = ((bf16[32,4,3072]{2,1,0:T(4,128)(2,1)}), bf16[32,4,3072]{2,1,0:T(4,128)(2,1)S(1)}, u32[]{:S(2)}, u32[]{:S(2)}) async-start(bf16[32,4,3072]{2,1,0:T(4,128)(2,1)} %reshape.247), calls=%async_computation.1 | async-start | bytes 1572864 | tf_op jit(solution)/shard_map/all_to_all | solution.py:222
  221.2 4.2 collective-permute-start.4
  221.5 2.0 collective-permute-start.6
  223.5 102.1 %collective-permute-start.7 = (bf16[512]{0:T(512)(128)(2,1)S(1)}, bf16[512]{0:T(512)(128)(2,1)}, u32[]{:S(2)}, u32[]{:S(2)}) collective-permute-start(bf16[512]{0:T(512)(128)(2,1)S(1)} %maximum_select_fusion.19), channel_id=1, source_target_pairs={{0,2},{2,0},{1,3},{3,1},{4,6},{6,4},{5,7},{7,5},{8,10},{10,8},{9,1... | collective-permute-start | bytes 3080 | tf_op jit(solution)/shard_map/ppermute | solution.py:31
  228.5 107.7 %collective-permute-start.5 = (bf16[512,1024]{1,0:T(8,128)(2,1)}, bf16[512,1024]{1,0:T(8,128)(2,1)}, u32[]{:S(2)}, u32[]{:S(2)}) collective-permute-start(bf16[512,1024]{1,0:T(8,128)(2,1)} %maximum_select_fusion.11), channel_id=1, source_target_pairs={{0,2},{2,0},{1,3},{3,1},{4,6},{6,4},{5,7},{7,5},{8,10},{10,8},{9,1... | collective-permute-start | bytes 3145736 | tf_op jit(solution)/shard_map/ppermute | solution.py:31
  232.7 116.5 %collective-permute-start.11 = (bf16[1408,1024]{1,0:T(8,128)(2,1)}, bf16[1408,1024]{1,0:T(8,128)(2,1)}, u32[]{:S(2)}, u32[]{:S(2)}) collective-permute-start(bf16[1408,1024]{1,0:T(8,128)(2,1)} %maximum_select_fusion.5), channel_id=1, source_target_pairs={{0,2},{2,0},{1,3},{3,1},{4,6},{6,4},{5,7},{7,5},{8,10},{10,8},{9,1... | collective-permute-start | bytes 8650760 | tf_op jit(solution)/shard_map/ppermute | solution.py:31
  241.8 80.1 %all-to-all-start.4 = ((bf16[32,4,1024]{2,1,0:T(4,128)(2,1)}), bf16[32,4,1024]{2,1,0:T(4,128)(2,1)S(1)}, u32[]{:S(2)}, u32[]{:S(2)}) async-start(bf16[32,4,1024]{2,1,0:T(4,128)(2,1)} %bitcast.16), calls=%async_computation.4 | async-start | bytes 524288 | tf_op jit(solution)/shard_map/all_to_all | solution.py:204
  246.7 3.5 copy-start.12
  321.9 14.3 %all-to-all-start.2 = ((bf16[32,4,1024]{2,1,0:T(4,128)(2,1)}), bf16[32,4,1024]{2,1,0:T(4,128)(2,1)S(1)}, u32[]{:S(2)}, u32[]{:S(2)}) async-start(bf16[32,4,1024]{2,1,0:T(4,128)(2,1)} %bitcast.10), calls=%async_computation.2 | async-start | bytes 524288 | tf_op jit(solution)/shard_map/all_to_all | solution.py:232
  364.3 10.8 %copy-start.17 = (bf16[128,2816]{1,0:T(8,128)(2,1)S(1)}, bf16[128,2816]{1,0:T(8,128)(2,1)}, u32[]{:S(2)}) copy-start(bf16[128,2816]{1,0:T(8,128)(2,1)} %get-tuple-element.12) | copy-start | bytes 2162692
  364.3 10.8 %copy-start.18 = (bf16[128,2816]{1,0:T(8,128)(2,1)S(1)}, bf16[128,2816]{1,0:T(8,128)(2,1)}, u32[]{:S(2)}) copy-start(bf16[128,2816]{1,0:T(8,128)(2,1)} %get-tuple-element.13) | copy-start | bytes 2162692
  385.6 2.7 copy-start.5
  391.4 9.4 %copy-start.16 = (bf16[128,2816]{1,0:T(8,128)(2,1)S(1)}, bf16[128,2816]{1,0:T(8,128)(2,1)}, u32[]{:S(2)}) copy-start(bf16[128,2816]{1,0:T(8,128)(2,1)} %copy-done.15) | copy-start | bytes 2162692
  392.2 14.5 %all-to-all-start.5 = ((bf16[32,4,1024]{2,1,0:T(4,128)(2,1)}), bf16[32,4,1024]{2,1,0:T(4,128)(2,1)S(1)}, u32[]{:S(2)}, u32[]{:S(2)}) async-start(bf16[32,4,1024]{2,1,0:T(4,128)(2,1)} %reshape.257), calls=%async_computation.5 | async-start | bytes 524288 | tf_op jit(solution)/shard_map/all_to_all | solution.py:279
  398.1 79.1 %collective-permute-start.16 = (bf16[512,1024]{1,0:T(8,128)(2,1)}, bf16[512,1024]{1,0:T(8,128)(2,1)}, u32[]{:S(2)}, u32[]{:S(2)}) collective-permute-start(bf16[512,1024]{1,0:T(8,128)(2,1)} %select_convert_fusion.6), channel_id=1, source_target_pairs={{0,2},{2,0},{1,3},{3,1},{4,6},{6,4},{5,7},{7,5},{8,10},{10,8},{9,1... | collective-permute-start | bytes 3145736 | tf_op jit(solution)/shard_map/ppermute | solution.py:31
  400.3 24.0 %copy-start.13 = (bf16[16,8,1,16,64]{4,3,2,0,1:T(8,128)(2,1)S(1)}, bf16[16,8,1,16,64]{4,3,2,0,1:T(8,128)(2,1)}, u32[]{:S(2)}) copy-start(bf16[16,8,1,16,64]{4,3,2,0,1:T(8,128)(2,1)} %copy-done.12) | copy-start | bytes 786436
  400.4 53.1 %collective-permute-start.18 = (bf16[512]{0:T(512)(128)(2,1)}, bf16[512]{0:T(512)(128)(2,1)S(1)}, u32[]{:S(2)}, u32[]{:S(2)}) collective-permute-start(bf16[512]{0:T(512)(128)(2,1)} %select_convert_fusion.8), channel_id=1, source_target_pairs={{0,2},{2,0},{1,3},{3,1},{4,6},{6,4},{5,7},{7,5},{8,10},{10,8},{9,1... | collective-permute-start | bytes 3080 | tf_op jit(solution)/shard_map/ppermute | solution.py:31
  406.7 19.0 %copy-start.11 = (bf16[16,8,1,16,64]{4,3,2,0,1:T(8,128)(2,1)S(1)}, bf16[16,8,1,16,64]{4,3,2,0,1:T(8,128)(2,1)}, u32[]{:S(2)}) copy-start(bf16[16,8,1,16,64]{4,3,2,0,1:T(8,128)(2,1)} %copy-done.10) | copy-start | bytes 786436
  406.7 28.2 %all-to-all-start.3 = ((bf16[32,4,1024]{2,1,0:T(4,128)(2,1)}), bf16[32,4,1024]{2,1,0:T(4,128)(2,1)}, u32[]{:S(2)}, u32[]{:S(2)}) async-start(bf16[32,4,1024]{2,1,0:T(4,128)(2,1)} %reshape.251), calls=%async_computation.3 | async-start | bytes 524288 | tf_op jit(solution)/shard_map/all_to_all | solution.py:249
  429.2 24.4 %slice-start = ((s8[11534336]{0:T(1024)(128)(4,1)}), s8[3145728]{0:T(1024)(128)(4,1)S(1)}, s32[]{:S(2)}) async-start(s8[11534336]{0:T(1024)(128)(4,1)} %bitcast.80), calls=%async_computation.8 | async-start | bytes 6291456
  434.9 26.4 %all-to-all-start.6 = ((bf16[32,4,3072]{2,1,0:T(4,128)(2,1)}), bf16[32,4,3072]{2,1,0:T(4,128)(2,1)}, u32[]{:S(2)}, u32[]{:S(2)}) async-start(bf16[32,4,3072]{2,1,0:T(4,128)(2,1)} %bitcast.86), calls=%async_computation.6 | async-start | bytes 1572864 | tf_op jit(solution)/shard_map/all_to_all | solution.py:285
  440.8 12.8 %slice-start.1 = ((s8[11534336]{0:T(1024)(128)(4,1)}), s8[4194304]{0:T(1024)(128)(4,1)S(1)}, s32[]{:S(2)}) async-start(s8[11534336]{0:T(1024)(128)(4,1)} %bitcast.80), calls=%async_computation.9 | async-start | bytes 8388608
  440.8 12.8 %slice-start.2 = ((s8[11534336]{0:T(1024)(128)(4,1)}), s8[4194304]{0:T(1024)(128)(4,1)S(1)}, s32[]{:S(2)}) async-start(s8[11534336]{0:T(1024)(128)(4,1)} %bitcast.80), calls=%async_computation.10 | async-start | bytes 8388608
  451.8 264.7 %collective-permute-start.20 = (bf16[512,5632]{1,0:T(8,128)(2,1)}, bf16[512,5632]{1,0:T(8,128)(2,1)}, u32[]{:S(2)}, u32[]{:S(2)}) collective-permute-start(bf16[512,5632]{1,0:T(8,128)(2,1)} %select_convert_fusion), channel_id=1, source_target_pairs={{0,2},{2,0},{1,3},{3,1},{4,6},{6,4},{5,7},{7,5},{8,10},{10,8},{9,1... | collective-permute-start | bytes 17301512 | tf_op jit(solution)/shard_map/ppermute | solution.py:31
  453.5 7.8 %copy-start.23 = (bf16[32,4,1024]{2,1,0:T(4,128)(2,1)S(1)}, bf16[32,4,1024]{2,1,0:T(4,128)(2,1)}, u32[]{:S(2)}) copy-start(bf16[32,4,1024]{2,1,0:T(4,128)(2,1)} %multiply_convert_fusion.4) | copy-start | bytes 786436
  453.5 3.2 collective-permute-start.19
  455.7 186.5 %collective-permute-start.22 = (bf16[1408,1024]{1,0:T(8,128)(2,1)}, bf16[1408,1024]{1,0:T(8,128)(2,1)}, u32[]{:S(2)}, u32[]{:S(2)}) collective-permute-start(bf16[1408,1024]{1,0:T(8,128)(2,1)} %select_convert_fusion.2), channel_id=1, source_target_pairs={{0,2},{2,0},{1,3},{3,1},{4,6},{6,4},{5,7},{7,5},{8,10},{10,8},{9,1... | collective-permute-start | bytes 8650760 | tf_op jit(solution)/shard_map/ppermute | solution.py:31
  468.9 8.4 %copy-start.2 = (f32[1024,1024]{1,0:T(8,128)S(1)}, f32[1024,1024]{1,0:T(8,128)}, u32[]{:S(2)}) copy-start(f32[1024,1024]{1,0:T(8,128)} %fusion.26) | copy-start | bytes 12582916
  475.8 233.4 %collective-permute-start.14 = (bf16[512,3072]{1,0:T(8,128)(2,1)}, bf16[512,3072]{1,0:T(8,128)(2,1)}, u32[]{:S(2)}, u32[]{:S(2)}) collective-permute-start(bf16[512,3072]{1,0:T(8,128)(2,1)} %select_convert_fusion.1), channel_id=1, source_target_pairs={{0,2},{2,0},{1,3},{3,1},{4,6},{6,4},{5,7},{7,5},{8,10},{10,8},{9,1... | collective-permute-start | bytes 9437192 | tf_op jit(solution)/shard_map/ppermute | solution.py:31
  480.6 265.1 %collective-permute-start.17 = (bf16[256,1024]{1,0:T(8,128)(2,1)}, bf16[256,1024]{1,0:T(8,128)(2,1)}, u32[]{:S(2)}, u32[]{:S(2)}) collective-permute-start(bf16[256,1024]{1,0:T(8,128)(2,1)} %select_convert_fusion.7), channel_id=1, source_target_pairs={{0,1},{1,0},{2,3},{3,2},{4,5},{5,4},{6,7},{7,6},{8,9},{9,8},{10,11... | collective-permute-start | bytes 1572872 | tf_op jit(solution)/shard_map/ppermute | solution.py:31
  480.6 161.6 %slice-start.3 = ((s8[11534336]{0:T(1024)(128)(4,1)}), s8[3145728]{0:T(1024)(128)(4,1)S(1)}, s32[]{:S(2)}) async-start(s8[11534336]{0:T(1024)(128)(4,1)} %bitcast.82), calls=%async_computation.11 | async-start | bytes 6291456
  483.1 159.2 %slice-start.4 = ((s8[11534336]{0:T(1024)(128)(4,1)}), s8[4194304]{0:T(1024)(128)(4,1)S(1)}, s32[]{:S(2)}) async-start(s8[11534336]{0:T(1024)(128)(4,1)} %bitcast.82), calls=%async_computation.12 | async-start | bytes 8388608
  483.1 159.2 %slice-start.5 = ((s8[11534336]{0:T(1024)(128)(4,1)}), s8[4194304]{0:T(1024)(128)(4,1)S(1)}, s32[]{:S(2)}) async-start(s8[11534336]{0:T(1024)(128)(4,1)} %bitcast.82), calls=%async_computation.13 | async-start | bytes 8388608
  491.3 254.3 %collective-permute-start.12 = (bf16[512]{0:T(512)(128)(2,1)}, bf16[512]{0:T(512)(128)(2,1)S(1)}, u32[]{:S(2)}, u32[]{:S(2)}) collective-permute-start(bf16[512]{0:T(512)(128)(2,1)} %select_convert_fusion.9), channel_id=1, source_target_pairs={{0,2},{2,0},{1,3},{3,1},{4,6},{6,4},{5,7},{7,5},{8,10},{10,8},{9,1... | collective-permute-start | bytes 3080 | tf_op jit(solution)/shard_map/ppermute | solution.py:31
  652.2 105.7 %collective-permute-start.23 = (bf16[704,1024]{1,0:T(8,128)(2,1)}, bf16[704,1024]{1,0:T(8,128)(2,1)S(1)}, u32[]{:S(2)}, u32[]{:S(2)}) collective-permute-start(bf16[704,1024]{1,0:T(8,128)(2,1)} %select_convert_fusion.5), channel_id=1, source_target_pairs={{0,1},{1,0},{2,3},{3,2},{4,5},{5,4},{6,7},{7,6},{8,9},{9,8},{10,11... | collective-permute-start | bytes 4325384 | tf_op jit(solution)/shard_map/ppermute | solution.py:31
  716.5 19.1 %copy-start.1 = (f32[512,3072]{1,0:T(8,128)}, f32[512,3072]{1,0:T(8,128)S(1)}, u32[]{:S(2)}) copy-start(f32[512,3072]{1,0:T(8,128)S(1)} %convert_add_fusion.1) | copy-start | bytes 18874372
  729.2 4.2 copy-start
  735.5 2.0 copy-start.9
  735.5 2.0 copy-start.19
  735.5 2.0 copy-start.25
  735.5 10.3 %copy-start.4 = (f32[512,1024]{1,0:T(8,128)S(1)}, f32[512,1024]{1,0:T(8,128)}, u32[]{:S(2)}) copy-start(f32[512,1024]{1,0:T(8,128)} %copy-done.3) | copy-start | bytes 6291460
  735.5 34.0 %collective-permute-start.21 = (bf16[256,5632]{1,0:T(8,128)(2,1)}, bf16[256,5632]{1,0:T(8,128)(2,1)}, u32[]{:S(2)}, u32[]{:S(2)}) collective-permute-start(bf16[256,5632]{1,0:T(8,128)(2,1)} %select_convert_fusion.3), channel_id=1, source_target_pairs={{0,1},{1,0},{2,3},{3,2},{4,5},{5,4},{6,7},{7,6},{8,9},{9,8},{10,11... | collective-permute-start | bytes 8650760 | tf_op jit(solution)/shard_map/ppermute | solution.py:31
  737.0 26.5 %collective-permute-start.15 = (bf16[256,3072]{1,0:T(8,128)(2,1)}, bf16[256,3072]{1,0:T(8,128)(2,1)}, u32[]{:S(2)}, u32[]{:S(2)}) collective-permute-start(bf16[256,3072]{1,0:T(8,128)(2,1)} %select_convert_fusion.4), channel_id=1, source_target_pairs={{0,1},{1,0},{2,3},{3,2},{4,5},{5,4},{6,7},{7,6},{8,9},{9,8},{10,11... | collective-permute-start | bytes 4718600 | tf_op jit(solution)/shard_map/ppermute | solution.py:31
  740.2 15.9 %all-to-all-start.7 = ((bf16[32,4,1024]{2,1,0:T(4,128)(2,1)}), bf16[32,4,1024]{2,1,0:T(4,128)(2,1)}, u32[]{:S(2)}, u32[]{:S(2)}) async-start(bf16[32,4,1024]{2,1,0:T(4,128)(2,1)} %convert_element_type.178), calls=%async_computation.7 | async-start | bytes 524288 | tf_op jit(solution)/shard_map/all_to_all | solution.py:296
  745.5 2.5 collective-permute-start.13
  758.0 11.6 %slice-start.6 = ((s8[11534336]{0:T(1024)(128)(4,1)}), s8[4194304]{0:T(1024)(128)(4,1)S(1)}, s32[]{:S(2)}) async-start(s8[11534336]{0:T(1024)(128)(4,1)} %bitcast.84), calls=%async_computation.14 | async-start | bytes 8388608
  758.0 11.6 %slice-start.7 = ((s8[11534336]{0:T(1024)(128)(4,1)}), s8[4194304]{0:T(1024)(128)(4,1)S(1)}, s32[]{:S(2)}) async-start(s8[11534336]{0:T(1024)(128)(4,1)} %bitcast.84), calls=%async_computation.15 | async-start | bytes 8388608
  763.5 6.1 slice-start.8
  (6 other events, 6.5 us)
where the time goes:
time: 779 us; the launch traced here: 775 us
  waiting for transfers between devices  485 us (62%)
  other arithmetic  107 us (14%)
  matrix products  85.1 us (11%)
  starting transfers between devices  67.4 us (9%)
  local copies, waits for them, and re-layouts  29.9 us (4%)
    ppermute x24, waiting for transfers between devices, swapped(): return lax.ppermute(block, axis, route)  389 us
    all_to_all x1, waiting for transfers between devices, body(): lax.all_to_all(positions_layout(cotangent, groups), 'fsdp', split_axis=0,...  70.3 us
    add x12, other arithmetic, halving_sum(): held_part + come_part  48.3 us
    convert_element_type x12, other arithmetic, short(): return part.astype(jnp.bfloat16) if part.dtype == jnp.float32 else part  33 us
    dot_general x4, matrix products, times_transposed(): lax.dot_general(left, right, (((1,), (1,)), ((), ())), preferred_element_...  28.7 us
    dot_general x4, matrix products, inner_rows(): lax.dot_general(left, right, (((0,), (0,)), ((), ())), preferred_element_...  27 us
    select_n x6, other arithmetic, join_pieces(): jnp.where(upper_half, jnp.concatenate([theirs, own_piece], 0), jnp.concat...  18.5 us
    ppermute x24, starting transfers between devices, swapped(): return lax.ppermute(block, axis, route)  17.8 us
  transfers between devices with their start and end apart: 32, of which 11 were waited for; matrix products, arithmetic and copies ran while one was open for 22% of the time, Pallas kernels for 0%

commit v1 on v0

--- a/solution.py
+++ b/solution.py
@@ -1,6 +1,11 @@
+import functools
+import math
+
 import jax
 import jax.numpy as jnp
 from jax import lax
+from jax.experimental import pallas as pl
+from jax.experimental.pallas import tpu as pltpu
 from jax.sharding import PartitionSpec as P
 
 D = 1024
@@ -317,6 +322,900 @@
     )
     return (block_out, grad_in, shares[4], shares[0], shares[1], shares[5], shares[2], shares[3])
 
+VMEM = pl.BlockSpec(memory_space=pltpu.VMEM)
+SMEM = pl.BlockSpec(memory_space=pltpu.SMEM)
+HBM = pl.BlockSpec(memory_space=pl.ANY)
+BF16 = jnp.bfloat16
+F32 = jnp.float32
+OWN, FAR, NEAR, ACROSS, SIDE, CORE, POSITION = range(7)
+
+
+def swap(block, mask):
+    count = lax.axis_size("fsdp")
+    return lax.ppermute(block, "fsdp", [(i, i ^ mask) for i in range(count)])
+
+
+def exchange(blocks):
+    stride = lax.axis_size("fsdp") // POS
+    return [blocks[0]] + [swap(blocks[k], stride * k) for k in range(1, POS)]
+
+
+def kernel_call(kernel, name, args, outs, scratch=()):
+    held = sum(
+        math.prod(ref.shape) * jnp.dtype(ref.dtype).itemsize
+        for ref in scratch
+        if ref.memory_space == pltpu.VMEM
+    )
+    return pl.pallas_call(
+        kernel,
+        name=name,
+        in_specs=[spec for spec, _ in args],
+        out_specs=[VMEM] * len(outs),
+        out_shape=[jax.ShapeDtypeStruct(s, d) for s, d in outs],
+        scratch_shapes=list(scratch),
+        cost_estimate=pl.CostEstimate(flops=1, bytes_accessed=1, transcendentals=0),
+        compiler_params=pltpu.CompilerParams(vmem_limit_bytes=held + (8 << 20)),
+    )(*[a for _, a in args])
+
+
+def matmul(left, right):
+    return jnp.dot(left, right, preferred_element_type=F32)
+
+
+def aligned(start, size, step=128):
+    return pl.ds(pl.multiple_of(start, step), size)
+
+
+def rows_of(refs, rel, columns=slice(None)):
+    frames = refs[0].shape[0] // 2
+    return jnp.concatenate([ref[rel * frames : (rel + 1) * frames, columns] for ref in refs], 0)
+
+
+def put_rows(refs, rel, columns, value):
+    frames = refs[0].shape[0] // 2
+    for k, ref in enumerate(refs):
+        ref[rel * frames : (rel + 1) * frames, columns] = value[k * frames : (k + 1) * frames]
+
+
+def block_shapes(rows, width):
+    return [((rows // POS, width), BF16)] * POS
+
+
+def in_vmem(*arrays):
+    return [(VMEM, a) for a in arrays]
+
+
+def place_matrix(size, to_positions, position):
+    frames = size // POS
+    row = lax.broadcasted_iota(jnp.int32, (size, size), 0)
+    column = lax.broadcasted_iota(jnp.int32, (size, size), 1)
+    if not to_positions:
+        row, column = column, row
+    return (column == (row % frames) * POS + ((row // frames) ^ position)).astype(F32).astype(BF16)
+
+
+def to_positions_kernel(place, x_rows, c_rows, *blocks):
+    order = place_matrix(x_rows.shape[0], True, place[POSITION])
+    for rel, rows in enumerate((x_rows, c_rows)):
+        put_rows(blocks, rel, slice(None), matmul(order, rows[...]).astype(BF16))
+
+
+def to_positions(place, x_rows, c_rows):
+    size, width = x_rows.shape
+    return kernel_call(
+        to_positions_kernel,
+        "to_positions",
+        [(SMEM, place)] + in_vmem(x_rows, c_rows),
+        block_shapes(2 * size, width),
+    )
+
+
+def collect_kernel(*refs):
+    blocks, (x_own, c_own) = refs[:POS], refs[POS:]
+    x_own[...] = rows_of(blocks, 0)
+    c_own[...] = rows_of(blocks, 1)
+
+
+def collect(blocks):
+    rows, width = blocks[0].shape
+    return kernel_call(
+        collect_kernel, "collect", in_vmem(*blocks), [((rows * POS // 2, width), BF16)] * 2
+    )
+
+
+def to_frames_kernel(place, *refs):
+    blocks, rows = refs[:POS], refs[POS:]
+    order = place_matrix(rows[0].shape[0], False, place[POSITION])
+    for rel in range(2):
+        rows[rel][...] = matmul(order, rows_of(blocks, rel)).astype(rows[rel].dtype)
+
+
+def to_frames(place, blocks):
+    size = blocks[0].shape[0] * POS // 2
+    return kernel_call(
+        to_frames_kernel,
+        "to_frames",
+        [(SMEM, place)] + in_vmem(*blocks),
+        [((size, D), F32), ((size, D), BF16)],
+    )
+
+
+def first_kernel(
+    place, x_a, x_b, gains_own, gains_far, gains_near, gains_across, w_own, w_far, w_near, w_across,
+    *rest,
+):
+    qkv, (lowered, gains, w, sems) = rest[:POS], rest[POS:]
+    half, width = x_a.shape[0], w_own.shape[0]
+    part = w.shape[1] // 3
+    side = place[SIDE]
+    at_rows = lambda rank: aligned(place[rank] * width, width)
+    copies = [
+        pltpu.make_async_copy(
+            w_own.at[:, aligned((2 * k + side) * part, part)],
+            w.at[at_rows(OWN), pl.ds(k * part, part)],
+            sems.at[k],
+        )
+        for k in range(3)
+    ]
+    copies.append(pltpu.make_async_copy(w_far, w.at[at_rows(FAR)], sems.at[3]))
+    copies.append(pltpu.make_async_copy(w_near, w.at[at_rows(NEAR)], sems.at[4]))
+    copies.append(pltpu.make_async_copy(w_across, w.at[at_rows(ACROSS)], sems.at[5]))
+    for copy in copies:
+        copy.start()
+    gains[:, at_rows(OWN)] = gains_own[...].astype(F32)
+    gains[:, at_rows(FAR)] = gains_far[...].astype(F32)
+    gains[:, at_rows(NEAR)] = gains_near[...].astype(F32)
+    gains[:, at_rows(ACROSS)] = gains_across[...].astype(F32)
+    gain = gains[0:1, :]
+    for rel, ref in enumerate((x_a, x_b)):
+        rows = ref[...].astype(F32)
+        scale = lax.rsqrt(jnp.mean(rows * rows, axis=-1, keepdims=True) + EPSILON)
+        lowered[rel * half : (rel + 1) * half, :] = (rows * scale * gain).astype(BF16)
+    for copy in copies:
+        copy.wait()
+
+    def step(n, carry):
+        columns = aligned(n * 256, 256, 256)
+        value = matmul(lowered[...], w[:, columns]).astype(BF16)
+        put_rows(qkv, 0, columns, value[:half])
+        put_rows(qkv, 1, columns, value[half:])
+        return carry
+
+    lax.fori_loop(0, w.shape[1] // 256, step, 0)
+
+
+def first(
+    place, x_a, x_b, gains_own, gains_far, gains_near, gains_across, w_own, w_far, w_near, w_across
+):
+    half = x_a.shape[0]
+    wide = w_far.shape[1]
+    return kernel_call(
+        first_kernel,
+        "first",
+        [(SMEM, place), (VMEM, x_a), (VMEM, x_b), (VMEM, gains_own), (VMEM, gains_far),
+         (VMEM, gains_near), (VMEM, gains_across), (HBM, w_own), (HBM, w_far), (HBM, w_near),
+         (HBM, w_across)],
+        block_shapes(2 * half, wide) + [((2 * half, D), BF16), ((2, D), F32)],
+        [pltpu.VMEM((D, wide), BF16), pltpu.SemaphoreType.DMA((6,))],
+    )
+
+
+def allowed_pairs(ids, position):
+    size = ids.shape[1]
+    frames = size // POS
+    row = lax.broadcasted_iota(jnp.int32, (size, size), 0)
+    column = lax.broadcasted_iota(jnp.int32, (size, size), 1)
+    across = jnp.broadcast_to(ids.astype(F32), (size, size))
+    same = (across == across.T) & (row % frames == column % frames)
+    mask = same & ((column // frames) ^ position <= (row // frames) ^ position)
+    return jnp.concatenate([mask, mask], 1)
+
+
+def pair_of_heads(rows, low):
+    return jnp.concatenate([rows * low, rows * (1 - low)], 0)
+
+
+def lane_halves(value, reduce):
+    size = value.shape[1] // 2
+    parts = [
+        jnp.broadcast_to(reduce(value[:, k * size : (k + 1) * size]), (value.shape[0], size))
+        for k in range(2)
+    ]
+    return jnp.concatenate(parts, 1)
+
+
+def pair_probs(query, key_pair, mask):
+    scores = times_transposed(query, key_pair) * HEAD_DIM ** (-0.5)
+    scores = jnp.where(mask, scores, -jnp.inf)
+    raised = jnp.exp(scores - lane_halves(scores, lambda a: jnp.max(a, -1, keepdims=True)))
+    return raised / lane_halves(raised, lambda a: jnp.sum(a, -1, keepdims=True))
+
+
+def first_head_lanes():
+    lane = lax.broadcasted_iota(jnp.int32, (1, 2 * HEAD_DIM), 1)
+    return (lane < HEAD_DIM).astype(F32).astype(BF16)
+
+
+def attend_kernel(place, ids_a, ids_b, *refs):
+    qkv, mixed = refs[:POS], refs[POS:]
+    part = mixed[0].shape[1]
+    low = first_head_lanes()
+    for rel, ids in enumerate((ids_a, ids_b)):
+        mask = allowed_pairs(ids[...], place[POSITION])
+        for base in range(0, part, 2 * HEAD_DIM):
+            query, key_rows, value_rows = (
+                rows_of(qkv, rel, slice(k * part + base, k * part + base + 2 * HEAD_DIM))
+                for k in range(3)
+            )
+            probs = pair_probs(query, pair_of_heads(key_rows, low), mask)
+            value = matmul(probs.astype(BF16), pair_of_heads(value_rows, low))
+            put_rows(mixed, rel, slice(base, base + 2 * HEAD_DIM), value.astype(BF16))
+
+
+def attend_local(place, ids_a, ids_b, qkv):
+    rows, wide = qkv[0].shape
+    return kernel_call(
+        attend_kernel,
+        "attend",
+        [(SMEM, place)] + in_vmem(ids_a, ids_b, *qkv),
+        block_shapes(rows * POS, wide // 3),
+    )
+
+
+def attend_back_kernel(place, ids_a, ids_b, *refs):
+    qkv, d_mixed, d_qkv = refs[:POS], refs[POS : 2 * POS], refs[2 * POS :]
+    part = d_mixed[0].shape[1]
+    pair = 2 * HEAD_DIM
+    low = first_head_lanes()
+    size = POS * d_mixed[0].shape[0] // 2
+    low_full = lax.broadcasted_iota(jnp.int32, (size, pair), 1) < HEAD_DIM
+    scale = HEAD_DIM ** (-0.5)
+    for rel, ids in enumerate((ids_a, ids_b)):
+        mask = allowed_pairs(ids[...], place[POSITION])
+        for base in range(0, part, pair):
+            query, key_rows, value_rows = (
+                rows_of(qkv, rel, slice(k * part + base, k * part + base + pair))
+                for k in range(3)
+            )
+            d_rows = rows_of(d_mixed, rel, slice(base, base + pair))
+            keys = pair_of_heads(key_rows, low)
+            probs = pair_probs(query, keys, mask)
+            d_probs = times_transposed(d_rows, pair_of_heads(value_rows, low))
+            inner = lane_halves(d_probs * probs, lambda a: jnp.sum(a, -1, keepdims=True))
+            d_scores = (probs * (d_probs - inner)).astype(BF16)
+            d_query = matmul(d_scores, keys) * scale
+            d_key = inner_rows(d_scores, query) * scale
+            d_value = inner_rows(probs.astype(BF16), d_rows)
+            d_key = jnp.where(low_full, d_key[:size], d_key[size:])
+            d_value = jnp.where(low_full, d_value[:size], d_value[size:])
+            for k, value in enumerate((d_query, d_key, d_value)):
+                columns = slice(k * part + base, k * part + base + pair)
+                put_rows(d_qkv, rel, columns, value.astype(BF16))
+
+
+def attend_back_local(place, ids_a, ids_b, qkv, d_mixed):
+    rows, wide = qkv[0].shape
+    return kernel_call(
+        attend_back_kernel,
+        "attend_back",
+        [(SMEM, place)] + in_vmem(ids_a, ids_b, *qkv, *d_mixed),
+        block_shapes(rows * POS, wide),
+    )
+
+
+def chip_rows(place, own, near, whole, sems):
+    count = own.shape[0]
+    core = place[CORE]
+    return [
+        pltpu.make_async_copy(own, whole.at[aligned(core * count, count, 64)], sems.at[0]),
+        pltpu.make_async_copy(near, whole.at[aligned((1 - core) * count, count, 64)], sems.at[1]),
+    ]
+
+
+def out_kernel(place, w_own, w_near, *refs):
+    mixed, (term, leaving, mixed_rows, w, sems) = refs[:POS], refs[POS:]
+    copies = chip_rows(place, w_own, w_near, w, sems)
+    for copy in copies:
+        copy.start()
+    rows = jnp.concatenate([rows_of(mixed, 0), rows_of(mixed, 1)], 0)
+    mixed_rows[...] = rows
+    half = rows.shape[0] // 2
+    for copy in copies:
+        copy.wait()
+    for base in range(0, D, 512):
+        value = matmul(rows, w[:, base : base + 512])
+        term[:, base : base + 512] = value
+        lowered = value.astype(BF16)
+        leaving[:half, base : base + 512] = lowered[half:]
+        leaving[half:, base : base + 512] = lowered[:half]
+
+
+def out_term(place, mixed, w_own, w_near):
+    rows = POS * mixed[0].shape[0]
+    inner = 2 * w_own.shape[0]
+    return kernel_call(
+        out_kernel,
+        "out_term",
+        [(SMEM, place), (HBM, w_own), (HBM, w_near)] + in_vmem(*mixed),
+        [((rows, D), F32), ((rows, D), BF16), ((rows, inner), BF16)],
+        [pltpu.VMEM((inner, D), BF16), pltpu.SemaphoreType.DMA((2,))],
+    )
+
+
+def ffn_kernel(
+    place, x_a, x_b, term, far, gains, c_a, c_b, *rest
+):
+    pieces, (wd_own, wd_near) = (rest[:4], rest[4:8]), rest[8:10]
+    resid, lowered, hidden, d_gate_up, second, leaving = rest[10:16]
+    w, wd, upstream, sems, down_sems = rest[16:]
+    half, width, steps = x_a.shape[0], pieces[0][0].shape[0], w.shape[0]
+    split = pieces[0][0].shape[1] // 256
+
+    def copies(j, sources, base):
+        return [
+            pltpu.make_async_copy(
+                source.at[:, aligned((j - base) * 256, 256)],
+                w.at[j, aligned(place[rank] * width, width)],
+                sems.at[j, rank],
+            )
+            for rank, source in enumerate(sources)
+        ]
+
+    def begin(sources, base, j, carry):
+        for copy in copies(j, sources, base):
+            copy.start()
+        return carry
+
+    down_copies = chip_rows(place, wd_own, wd_near, wd, down_sems)
+    for copy in down_copies:
+        copy.start()
+    lax.fori_loop(0, split, functools.partial(begin, pieces[0], 0), 0)
+    lax.fori_loop(split, steps, functools.partial(begin, pieces[1], split), 0)
+    gain = gains[1:2, :]
+    for rel, (x_ref, c_ref) in enumerate(((x_a, c_a), (x_b, c_b))):
+        at = pl.ds(rel * half, half)
+        rows = x_ref[...].astype(F32) + (term[at, :] + far[at, :].astype(F32))
+        resid[at, :] = rows
+        scale = lax.rsqrt(jnp.mean(rows * rows, axis=-1, keepdims=True) + EPSILON)
+        lowered[at, :] = (rows * scale * gain).astype(BF16)
+        upstream[at, :] = c_ref[...]
+    for copy in down_copies:
+        copy.wait()
+
+    def step(j, carry):
+        for rank in range(4):
+            rows = w.at[j, pl.ds(rank * width, width)]
+            pltpu.make_async_copy(rows, rows, sems.at[j, rank]).wait()
+        gate_up = matmul(lowered[...], w[j])
+        gate, up = gate_up[:, :128], gate_up[:, 128:]
+        d_hidden = times_transposed(upstream[...], wd[aligned(j * 128, 128), :])
+        sigmoid = jax.nn.sigmoid(gate)
+        activated = gate * sigmoid
+        hidden[:, aligned(j * 128, 128)] = (activated * up).astype(BF16)
+        d_gate = d_hidden * up * sigmoid * (1.0 + gate * (1.0 - sigmoid))
+        d_gate_up[:, aligned(j * 256, 128)] = d_gate.astype(BF16)
+        d_gate_up[:, aligned(j * 256 + 128, 128)] = (d_hidden * activated).astype(BF16)
+        return carry
+
+    lax.fori_loop(0, steps, step, 0)
+
+    def back(n, carry):
+        columns = aligned(n * 256, 256)
+        value = times_transposed(d_gate_up[:, 0:256], w[0, columns, :])
+        for j in range(1, steps):
+            value += times_transposed(d_gate_up[:, j * 256 : (j + 1) * 256], w[j, columns, :])
+        second[:, columns] = value
+        lower = value.astype(BF16)
+        leaving[:half, columns] = lower[half:]
+        leaving[half:, columns] = lower[:half]
+        return carry
+
+    lax.fori_loop(0, D // 256, back, 0)
+
+
+def ffn(place, x_a, x_b, term, far, gains, c_a, c_b, pieces, wd_own, wd_near):
+    rows = term.shape[0]
+    inner = 2 * wd_own.shape[0]
+    wide, steps = 2 * inner, inner // 128
+    return kernel_call(
+        ffn_kernel,
+        "ffn",
+        [(SMEM, place)]
+        + [(VMEM, a) for a in (x_a, x_b, term, far, gains, c_a, c_b)]
+        + [(HBM, a) for a in pieces + (wd_own, wd_near)],
+        [((rows, D), F32), ((rows, D), BF16), ((rows, inner), BF16), ((rows, wide), BF16),
+         ((rows, D), F32), ((rows, D), BF16)],
+        [pltpu.VMEM((steps, D, 256), BF16), pltpu.VMEM((inner, D), BF16),
+         pltpu.VMEM((rows, D), BF16), pltpu.SemaphoreType.DMA((steps, 4)),
+         pltpu.SemaphoreType.DMA((2,))],
+    )
+
+
+def down_kernel(place, hidden, resid, w_own, w_near, kept, leaving, w, sems):
+    copies = chip_rows(place, w_own, w_near, w, sems)
+    for copy in copies:
+        copy.start()
+    half = kept.shape[0]
+    for copy in copies:
+        copy.wait()
+
+    def step(n, carry):
+        columns = aligned(n * 256, 256)
+        value = matmul(hidden[...], w[:, columns])
+        kept[:, columns] = resid[:half, columns] + value[:half]
+        leaving[:, columns] = value[half:].astype(BF16)
+        return carry
+
+    lax.fori_loop(0, D // 256, step, 0)
+
+
+def down_term(place, hidden, resid, w_own, w_near):
+    rows, inner = hidden.shape
+    return kernel_call(
+        down_kernel,
+        "down_term",
+        [(SMEM, place), (VMEM, hidden), (VMEM, resid), (HBM, w_own), (HBM, w_near)],
+        [((rows // 2, D), F32), ((rows // 2, D), BF16)],
+        [pltpu.VMEM((inner, D), BF16), pltpu.SemaphoreType.DMA((2,))],
+    )
+
+
+def mid_kernel(
+    place, second, far, resid, gains, c_a, c_b, w_own, w_near,
+    d_resid, d_branch, gain_terms, *rest,
+):
+    d_mixed, (w, sums, sems) = rest[:POS], rest[POS:]
+    copies = chip_rows(place, w_own, w_near, w, sems)
+    for copy in copies:
+        copy.start()
+    half, width = c_a.shape[0], w_own.shape[0]
+    gain = gains[1:2, :]
+    total = None
+    for rel, c_ref in enumerate((c_a, c_b)):
+        at = pl.ds(rel * half, half)
+        rows = resid[at, :]
+        scale = lax.rsqrt(jnp.mean(rows * rows, axis=-1, keepdims=True) + EPSILON)
+        normed = rows * scale
+        d_rows = second[at, :] + far[at, :].astype(F32)
+        part = jnp.sum(d_rows * normed, axis=0, keepdims=True)
+        total = part if total is None else total + part
+        scaled = d_rows * gain
+        value = c_ref[...].astype(F32) + scale * (
+            scaled - normed * jnp.mean(scaled * normed, axis=-1, keepdims=True)
+        )
+        if rel == 0:
+            d_resid[...] = value
+        d_branch[at, :] = value.astype(BF16)
+    sums[...] = total
+    gain_terms[0] = sums[:, aligned(place[OWN] * width, width)]
+    gain_terms[1] = sums[:, aligned(place[NEAR] * width, width)]
+    for copy in copies:
+        copy.wait()
+    for base in range(0, w.shape[0], 256):
+        value = times_transposed(d_branch[...], w[base : base + 256, :]).astype(BF16)
+        put_rows(d_mixed, 0, slice(base, base + 256), value[:half])
+        put_rows(d_mixed, 1, slice(base, base + 256), value[half:])
+
+
+def mid(place, second, far, resid, gains, c_a, c_b, w_own, w_near):
+    rows = second.shape[0]
+    width = w_own.shape[0]
+    return kernel_call(
+        mid_kernel,
+        "mid",
+        [(SMEM, place), (VMEM, second), (VMEM, far), (VMEM, resid), (VMEM, gains),
+         (VMEM, c_a), (VMEM, c_b), (HBM, w_own), (HBM, w_near)],
+        [((rows // 2, D), F32), ((rows, D), BF16), ((2, 1, width), F32)]
+        + block_shapes(rows, 2 * width),
+        [pltpu.VMEM((2 * width, D), BF16), pltpu.VMEM((1, D), F32),
+         pltpu.SemaphoreType.DMA((2,))],
+    )
+
+
+def back_first_kernel(place, w_own, w_far, w_near, w_across, *refs):
+    d_qkv, (kept, leaving, rows, w, sems) = refs[:POS], refs[POS:]
+    half, width = kept.shape[0], w_own.shape[0]
+    part = w.shape[2] // 3
+    side = place[SIDE]
+    copies = [
+        pltpu.make_async_copy(
+            w_own.at[:, aligned((2 * k + side) * part, part)],
+            w.at[0, :, pl.ds(k * part, part)],
+            sems.at[k],
+        )
+        for k in range(3)
+    ]
+    copies.append(pltpu.make_async_copy(w_far, w.at[1], sems.at[3]))
+    copies.append(pltpu.make_async_copy(w_near, w.at[2], sems.at[4]))
+    copies.append(pltpu.make_async_copy(w_across, w.at[3], sems.at[5]))
+    for copy in copies:
+        copy.start()
+    rows[:half, :] = rows_of(d_qkv, 0)
+    rows[half:, :] = rows_of(d_qkv, 1)
+    for copy in copies:
+        copy.wait()
+
+    def step(rank, carry):
+        columns = aligned(place[rank] * width, width)
+        value = times_transposed(rows[...], w[rank])
+        kept[:, columns] = value[:half]
+        leaving[:, columns] = value[half:].astype(BF16)
+        return carry
+
+    lax.fori_loop(0, 4, step, 0)
+
+
+def back_first(place, d_qkv, w_own, w_far, w_near, w_across):
+    rows, wide = POS * d_qkv[0].shape[0], d_qkv[0].shape[1]
+    return kernel_call(
+        back_first_kernel,
+        "back_first",
+        [(SMEM, place), (HBM, w_own), (HBM, w_far), (HBM, w_near), (HBM, w_across)]
+        + in_vmem(*d_qkv),
+        [((rows // 2, D), F32), ((rows // 2, D), BF16), ((rows, wide), BF16)],
+        [pltpu.VMEM((4, w_own.shape[0], wide), BF16), pltpu.SemaphoreType.DMA((6,))],
+    )
+
+
+def last_kernel(
+    place, kept, far, x_a, gains, d_resid, down_kept, down_far, *rest
+):
+    blocks, (gain_terms, sums) = rest[:POS], rest[POS:]
+    width = gain_terms.shape[2]
+    rows = x_a[...].astype(F32)
+    scale = lax.rsqrt(jnp.mean(rows * rows, axis=-1, keepdims=True) + EPSILON)
+    normed = rows * scale
+    d_rows = kept[...] + far[...].astype(F32)
+    sums[...] = jnp.sum(d_rows * normed, axis=0, keepdims=True)
+    scaled = d_rows * gains[0:1, :]
+    value = d_resid[...] + scale * (
+        scaled - normed * jnp.mean(scaled * normed, axis=-1, keepdims=True)
+    )
+    put_rows(blocks, 0, slice(None), value.astype(BF16))
+    put_rows(blocks, 1, slice(None), (down_kept[...] + down_far[...].astype(F32)).astype(BF16))
+    for slot, rank in enumerate((OWN, NEAR, FAR, ACROSS)):
+        gain_terms[slot] = sums[:, aligned(place[rank] * width, width)]
+
+
+def last(place, kept, far, x_a, gains, d_resid, down_kept, down_far):
+    half = kept.shape[0]
+    arrays = (kept, far, x_a, gains, d_resid, down_kept, down_far)
+    return kernel_call(
+        last_kernel,
+        "last",
+        [(SMEM, place)] + [(VMEM, a) for a in arrays],
+        block_shapes(2 * half, D) + [((4, 1, D // 4), F32)],
+        [pltpu.VMEM((1, D), F32)],
+    )
+
+
+def both_rows(own, near, columns):
+    return jnp.concatenate([own[:, columns], near[:, columns]], 0)
+
+
+def leaving_kernel(first_block, place, left_own, left_near, right_own, right_near, leaving):
+    width = leaving.shape[0]
+    left = both_rows(left_own, left_near, aligned(place[ACROSS] * width, width))
+
+    def step(j, carry):
+        columns = aligned(j * 256, 256)
+        right = both_rows(
+            right_own, right_near, aligned((first_block + j) * 256, 256)
+        )
+        leaving[:, columns] = inner_rows(left, right).astype(BF16)
+        return carry
+
+    lax.fori_loop(0, leaving.shape[1] // 256, step, 0)
+
+
+def leaving_gradient(place, blocks, left_own, left_near, right_own, right_near):
+    width, wide = D // 4, 256 * (blocks[1] - blocks[0])
+    return kernel_call(
+        functools.partial(leaving_kernel, blocks[0]),
+        "leaving_gradient",
+        [(SMEM, place), (VMEM, left_own), (VMEM, left_near), (VMEM, right_own),
+         (VMEM, right_near)],
+        [((width, wide), BF16)],
+    )[0]
+
+
+def staying_kernel(parts, place, left_own, left_near, right_own, right_near, *rest):
+    come, grad = rest[:-1], rest[-1]
+    width = grad.shape[0]
+    part = grad.shape[1] // 2 // parts
+    side = place[SIDE]
+    left = both_rows(left_own, left_near, aligned(place[OWN] * width, width))
+
+    def put(block, who, value):
+        if parts == 2:
+            spots = [(0, block * 128, 0, 128), (1, block * 128, 128, 256)]
+        else:
+            spots = [(block // 2, (block % 2) * 256, 0, 256)]
+        for k, start, low, high in spots:
+            grad[:, aligned((2 * k + who) * part + start, high - low)] = value[:, low:high]
+
+    def step(j, carry):
+        right = both_rows(right_own, right_near, aligned(j * 256, 256))
+        put(j, side, inner_rows(left, right))
+        return carry
+
+    lax.fori_loop(0, right_own.shape[1] // 256, step, 0)
+    base = 0
+    for piece in come:
+        count = piece.shape[1] // 256
+
+        def take(j, carry, piece=piece, base=base):
+            put(base + j, 1 - side, piece[:, aligned(j * 256, 256)].astype(F32))
+            return carry
+
+        lax.fori_loop(0, count, take, 0)
+        base += count
+
+
+def staying_gradient(parts, place, left_own, left_near, right_own, right_near, *come):
+    width = D // 4
+    arrays = (left_own, left_near, right_own, right_near) + come
+    return kernel_call(
+        functools.partial(staying_kernel, parts),
+        "staying_gradient",
+        [(SMEM, place)] + [(VMEM, a) for a in arrays],
+        [((width, 2 * right_own.shape[1]), F32)],
+    )[0]
+
+
+def grad_out_kernel(place, mixed_own, mixed_near, d_own, d_near, grad):
+    left = both_rows(
+        mixed_own, mixed_near, aligned(place[CORE] * grad.shape[0], grad.shape[0])
+    )
+    for base in range(0, D, 512):
+        at = slice(base, base + 512)
+        grad[:, at] = inner_rows(left, jnp.concatenate([d_own[:, at], d_near[:, at]], 0))
+
+
+def grad_out_rows(place, mixed_own, mixed_near, d_own, d_near):
+    width = mixed_own.shape[1] // 2
+    return kernel_call(
+        grad_out_kernel,
+        "grad_out",
+        [(SMEM, place), (VMEM, mixed_own), (VMEM, mixed_near), (VMEM, d_own), (VMEM, d_near)],
+        [((width, D), F32)],
+    )[0]
+
+
+def grad_down_kernel(place, h_own, h_near, ca_own, cb_own, ca_near, cb_near, grad, wide):
+    count, window = grad.shape[0], wide.shape[0]
+    core = place[CORE]
+    skip = h_own.shape[1] - window
+    left = both_rows(h_own, h_near, aligned(core * skip, window))
+
+    def step(n, carry):
+        columns = aligned(n * 256, 256)
+        right = jnp.concatenate(
+            [ref[:, columns] for ref in (ca_own, cb_own, ca_near, cb_near)], 0
+        )
+        wide[:, columns] = inner_rows(left, right)
+        return carry
+
+    lax.fori_loop(0, D // 256, step, 0)
+    grad[...] = wide[aligned(core * (count - skip), count, 64), :]
+
+
+def grad_down_rows(place, h_own, h_near, ca_own, cb_own, ca_near, cb_near):
+    count = h_own.shape[1] // 2
+    window = -(-count // 128) * 128
+    return kernel_call(
+        grad_down_kernel,
+        "grad_down",
+        [(SMEM, place)]
+        + [(VMEM, a) for a in (h_own, h_near, ca_own, cb_own, ca_near, cb_near)],
+        [((count, D), F32)],
+        [pltpu.VMEM((window, D), F32)],
+    )[0]
+
+
+def half_columns_kernel(parts, far, place, weight, half, sems):
+    part = half.shape[1] // parts
+    side = 1 - place[SIDE] if far else place[SIDE]
+    copies = [
+        pltpu.make_async_copy(
+            weight.at[:, aligned((2 * k + side) * part, part)],
+            half.at[:, pl.ds(k * part, part)],
+            sems.at[k],
+        )
+        for k in range(parts)
+    ]
+    for copy in copies:
+        copy.start()
+    for copy in copies:
+        copy.wait()
+
+
+def half_columns(place, weight, parts, far):
+    count, width = weight.shape
+    return kernel_call(
+        functools.partial(half_columns_kernel, parts, far),
+        "far_columns" if far else "kept_columns",
+        [(SMEM, place), (HBM, weight)],
+        [((count, width // 2), BF16)],
+        [pltpu.SemaphoreType.DMA((parts,))],
+    )[0]
+
+
+def spread_kernel(split, place, weight, kept_a, kept_b, leaving_a, leaving_b, sems):
+    part = weight.shape[1] // 4
+    side = place[SIDE]
+    copies = []
+    for k in range(2):
+        for j in range(part // 128):
+            for who, targets in ((side, (kept_a, kept_b)), (1 - side, (leaving_a, leaving_b))):
+                target, at = (targets[0], j) if j < split else (targets[1], j - split)
+                copies.append(
+                    pltpu.make_async_copy(
+                        weight.at[:, aligned((2 * k + who) * part + j * 128, 128)],
+                        target.at[:, pl.ds(at * 256 + k * 128, 128)],
+                        sems.at[len(copies)],
+                    )
+                )
+    for copy in copies:
+        copy.start()
+    for copy in copies:
+        copy.wait()
+
+
+def spread(place, weight, split):
+    count, width = weight.shape
+    sizes = (256 * split, width // 2 - 256 * split) * 2
+    return kernel_call(
+        functools.partial(spread_kernel, split),
+        "spread",
+        [(SMEM, place), (HBM, weight)],
+        [((count, size), BF16) for size in sizes],
+        [pltpu.SemaphoreType.DMA((width // 128,))],
+    )
+
+
+def sync(*values):
+    return lax.optimization_barrier(values)
+
+
+def after(value, *earlier):
+    return lax.optimization_barrier((value,) + earlier)[0]
+
+
+def pair_body(frames_in, segment_ids, gain_attn, w_qkv, w_out, gain_ffn, w_gate_up, w_down, cotangent):
+    member = lax.axis_index("fsdp") % 4
+    side, core = member >> 1, member & 1
+    position = lax.axis_index("fsdp") // 4
+    place = jnp.stack([member, member ^ 2, member ^ 1, member ^ 3, side, core, position])
+    place = place.astype(jnp.int32)
+    frames = frames_in.shape[0] // POS
+    half = POS * frames
+
+    blocks = w_gate_up.shape[1] // 512
+    split = (blocks + 1) // 2
+    near = lambda rows: swap(rows, 1)
+
+    qkv_leaving = half_columns(place, w_qkv, 3, True)
+    qkv_across = swap(qkv_leaving, 3)
+    sent = to_positions(place, after(frames_in, qkv_leaving), cotangent)
+    came = exchange(sent)
+    sent = sent[0]
+    ids_own = segment_ids.reshape(frames, POS).T
+    ids_own = jnp.take(ids_own, jnp.arange(POS) ^ position, axis=0).reshape(1, half)
+    ids_far = swap(after(ids_own, sent), 2)
+    gains_own = jnp.stack([gain_attn, gain_ffn])
+    gains_far = swap(after(gains_own, sent), 2)
+    qkv_kept = half_columns(place, after(w_qkv, sent), 3, False)
+    came, ids_far, gains_far, qkv_kept = sync(came, ids_far, gains_far, qkv_kept)
+
+    x_own, c_own = collect(came)
+    x_far = swap(x_own, 2)
+    gains_near = near(jnp.stack([gains_own, gains_far]))
+    qkv_near = near(qkv_kept)
+    qkv_far = near(qkv_across)
+    kept_a, kept_b, leaving_a, leaving_b = spread(place, after(w_gate_up, x_own), split)
+    x_far, qkv_far, gains_near, qkv_near, leaving_a, c_own = sync(
+        x_far, qkv_far, gains_near, qkv_near, leaving_a, c_own
+    )
+
+    *qkv_sent, lowered_first, gains = first(
+        place, x_own, x_far, gains_own, gains_far, gains_near[0], gains_near[1],
+        w_qkv, qkv_far, qkv_near, qkv_across,
+    )
+    across_a = swap(after(leaving_a, lowered_first), 3)
+    c_far = swap(after(c_own, lowered_first), 2)
+    near_a, near_b, out_near, down_near = (
+        near(after(a, lowered_first)) for a in (kept_a, kept_b, w_out, w_down)
+    )
+    qkv, c_far, near_a, near_b, out_near, down_near = sync(
+        exchange(qkv_sent), c_far, near_a, near_b, out_near, down_near
+    )
+
+    mixed_sent = attend_local(place, ids_own, ids_far, qkv)
+    across_b = swap(after(leaving_b, across_a), 3)
+    far_a = near(across_a)
+    c_own_near, c_far_near, lowered_first_near = (
+        near(after(a, mixed_sent[0])) for a in (c_own, c_far, lowered_first)
+    )
+    mixed, across_b, far_a, c_own_near, c_far_near, lowered_first_near = sync(
+        exchange(mixed_sent), across_b, far_a, c_own_near, c_far_near, lowered_first_near
+    )
+
+    term, leaving, mixed = out_term(place, mixed, w_out, out_near)
+    far = swap(leaving, 2)
+    far, mixed_near, far_b = sync(far, near(mixed), near(after(across_b, leaving)))
+    pieces = (kept_a, far_a, near_a, across_a, kept_b, far_b, near_b, across_b)
+    resid, lowered_second, hidden, d_gate_up, second, leaving = ffn(
+        place, x_own, x_far, term, far, gains, c_own, c_far, pieces, w_down, down_near
+    )
+
+    second_far = swap(leaving, 2)
+    hidden_near, lowered_second_near, d_gate_up_near = (
+        near(after(rows, leaving)) for rows in (hidden, lowered_second, d_gate_up)
+    )
+    down_kept, down_leaving = down_term(place, after(hidden, leaving), resid, w_down, down_near)
+    sides = (lowered_second, lowered_second_near, d_gate_up, d_gate_up_near)
+    cut = blocks // 4
+    gate_up_leaving = leaving_gradient(place, (0, cut), *sides)
+    second_far, down_leaving, gate_up_leaving, hidden_near, lowered_second_near = sync(
+        second_far, down_leaving, gate_up_leaving, hidden_near, lowered_second_near
+    )
+
+    d_resid, d_branch, gain_ffn_terms, *d_mixed = mid(
+        place, second, second_far, resid, gains, c_own, c_far, w_out, out_near
+    )
+    gate_up_come = swap(gate_up_leaving, 3)
+    down_far = swap(after(down_leaving, d_branch), 2)
+    sides = (after(lowered_second, d_branch), lowered_second_near, d_gate_up, d_gate_up_near)
+    gate_up_leaving_rest = leaving_gradient(place, (cut, blocks), *sides)
+    d_branch_near, gain_ffn_near = near(d_branch), near(gain_ffn_terms[1])
+    d_mixed, gate_up_come, down_far, gate_up_leaving_rest, d_branch_near, gain_ffn_near = sync(
+        exchange(d_mixed), gate_up_come, down_far, gate_up_leaving_rest, d_branch_near,
+        gain_ffn_near,
+    )
+
+    d_qkv_sent = attend_back_local(place, ids_own, ids_far, qkv, d_mixed)
+    gate_up_come_rest = swap(gate_up_leaving_rest, 3)
+    grad_down = grad_down_rows(
+        place, after(hidden, d_qkv_sent[0]), hidden_near, c_own, c_far, c_own_near, c_far_near
+    )
+    grad_out = grad_out_rows(place, mixed, mixed_near, after(d_branch, d_qkv_sent[0]), d_branch_near)
+    d_qkv, gate_up_come_rest, grad_down, grad_out = sync(
+        exchange(d_qkv_sent), gate_up_come_rest, grad_down, grad_out
+    )
+
+    kept, leaving, d_projected = back_first(
+        place, d_qkv, w_qkv, qkv_far, qkv_near, qkv_across
+    )
+    first_far = swap(leaving, 2)
+    qkv_sides = (lowered_first, lowered_first_near, d_projected, near(d_projected))
+    qkv_grad_leaving = leaving_gradient(place, (0, qkv_leaving.shape[1] // 256), *qkv_sides)
+    first_far, qkv_grad_leaving = sync(first_far, qkv_grad_leaving)
+
+    qkv_come = swap(qkv_grad_leaving, 3)
+    *out_sent, gain_attn_terms = last(
+        place, kept, first_far, x_own, gains, d_resid, down_kept, down_far
+    )
+    grad_gate_up = staying_gradient(
+        2, place, after(sides[0], gain_attn_terms), *sides[1:], gate_up_come, gate_up_come_rest
+    )
+    gain_sums = gain_attn_terms[:2] + swap(gain_attn_terms[2:], 2)
+    gain_attn_grad = gain_sums[0] + near(gain_sums[1])
+    out_come, grad_gate_up = sync(exchange(out_sent), grad_gate_up)
+    grad_qkv = staying_gradient(3, place, *qkv_sides, qkv_come)
+    grad_in, block_out = to_frames(place, out_come)
+    gain_ffn_grad = (gain_ffn_terms[0] + gain_ffn_near).reshape(-1)
+    return (
+        block_out,
+        grad_in,
+        gain_attn_grad.reshape(-1),
+        grad_qkv,
+        grad_out,
+        gain_ffn_grad,
+        grad_gate_up,
+        grad_down,
+    )
+
 
 def solution(mesh):
     in_specs = (
@@ -340,4 +1239,5 @@
         P("fsdp", None),
         P("fsdp", None),
     )
-    return jax.shard_map(body, mesh=mesh, in_specs=in_specs, out_specs=out_specs, check_vma=False)
+    chosen = pair_body if mesh.shape["fsdp"] == 4 * POS else body
+    return jax.shard_map(chosen, mesh=mesh, in_specs=in_specs, out_specs=out_specs, check_vma=False)

time: 779 us -> 281 us (0.36)
  waiting for transfers between devices: 485 us -> 128 us
  other arithmetic: 107 us -> 1.26 us
  matrix products: 85.1 us -> 0 us
  Pallas kernels: 0 us -> 56.9 us
  local copies, waits for them, and re-layouts: 29.9 us -> 4.89 us
  starting transfers between devices: 67.4 us -> 88 us
    ppermute x24 -> x77, waiting for transfers between devices: 389 us -> 128 us  [swap(): return lax.ppermute(block, 'fsdp', [(i, i ^ mask) for i in range(count)])]
    all_to_all x8 -> x0, waiting for transfers between devices: 95.7 us -> none  [the longest x1 70.3 us: body(): lax.all_to_all(positions_layout(cotangent, groups), 'fsdp', split_axis=0,...]
    dot_general x18 -> x0, matrix products: 85.1 us -> none  [the longest x4 28.7 us: times_transposed(): lax.dot_general(left, right, (((1,), (1,)), ((), ())), preferred_element_...]
    ppermute x24 -> x77, starting transfers between devices: 17.8 us -> 88 us  [swap(): return lax.ppermute(block, 'fsdp', [(i, i ^ mask) for i in range(count)])]
    pallas_call x0 -> x22, Pallas kernels: none -> 56.9 us  [kernel_call(): pl.pallas_call(kernel, name=name, in_specs=[spec for spec, _ in args], ou...]
    all_to_all x8 -> x0, starting transfers between devices: 49.6 us -> none  [the longest x1 17.3 us: body(): lax.all_to_all(result_rows.reshape(devices, per_piece, D), 'fsdp', split_...]
    add x14 -> x3, other arithmetic: 49.5 us -> 1.13 us  [the longest x1 0.56 us: pair_body(): gain_ffn_grad = (gain_ffn_terms[0] + gain_ffn_near).reshape(-1)]
    convert_element_type x17 -> x0, other arithmetic: 36.7 us -> none  [the longest x12 33 us: short(): return part.astype(jnp.bfloat16) if part.dtype == jnp.float32 else part]
  transfers between devices with their start and end apart: 32 -> 77, of which waited for: 11 -> 36; matrix products, arithmetic and copies ran while one was open for 22% -> 1% of each run, Pallas kernels for 0% -> 12%
where the time goes in v1:
time: 281 us; the launch traced here: 280 us
  waiting for transfers between devices  128 us (46%)
  starting transfers between devices  88 us (31%)
  Pallas kernels  56.9 us (20%)
  local copies, waits for them, and re-layouts  4.89 us (2%)
    ppermute x77, waiting for transfers between devices, swap(): return lax.ppermute(block, 'fsdp', [(i, i ^ mask) for i in range(count)])  128 us
    ppermute x77, starting transfers between devices, swap(): return lax.ppermute(block, 'fsdp', [(i, i ^ mask) for i in range(count)])  88 us
    pallas_call x22, Pallas kernels, kernel_call(): pl.pallas_call(kernel, name=name, in_specs=[spec for spec, _ in args], ou...  56.9 us
  transfers between devices with their start and end apart: 77, of which 36 were waited for; matrix products, arithmetic and copies ran while one was open for 1% of the time, Pallas kernels for 12%

profile of v1, /device:TPU:0, one launch (start us, length us, event | category | flops | bytes accessed | tf_op | source)
XLA Modules:
  0.0 280.2 jit_solution(4323163658743104832)
XLA Ops:
  2.8 2.5 collective-permute-start.10
  10.7 1.6 collective-permute-start.1
  14.0 9.4 %collective-permute-done.7.ids_b = s32[1,128]{1,0:T(1,128)S(1)} collective-permute-done((s32[1,128]{1,0:T(1,128)S(1)}, s32[1,128]{1,0:T(1,128)S(1)}, u32[]{:S(2)}, u32[]{:S(2)}) %collective-permute-start.7) | collective-permute-done | bytes 544 | tf_op jit(solution)/shard_map/ppermute | solution.py:335
  23.4 2.3 collective-permute-start.8
  27.2 3.1 %collective-permute-start.3 = (bf16[32,1024]{1,0:T(8,128)(2,1)S(1)}, bf16[32,1024]{1,0:T(8,128)(2,1)S(1)}, u32[]{:S(2)}, u32[]{:S(2)}) collective-permute-start(bf16[32,1024]{1,0:T(8,128)(2,1)S(1)} %get-tuple-element.199), channel_id=1, source_target_pairs={{0,16},{1,17},{2,18},{3,19},{4,20},{5,21},{6,22},{7,23},{8,24},{9,... | collective-permute-start | bytes 196616 | tf_op jit(solution)/shard_map/ppermute | solution.py:335
  31.7 3.6 %collective-permute-start.5 = (bf16[32,1024]{1,0:T(8,128)(2,1)S(1)}, bf16[32,1024]{1,0:T(8,128)(2,1)S(1)}, u32[]{:S(2)}, u32[]{:S(2)}) collective-permute-start(bf16[32,1024]{1,0:T(8,128)(2,1)S(1)} %get-tuple-element.201), channel_id=1, source_target_pairs={{0,24},{1,25},{2,26},{3,27},{4,28},{5,29},{6,30},{7,31},{8,16},{9,... | collective-permute-start | bytes 196616 | tf_op jit(solution)/shard_map/ppermute | solution.py:335
  36.0 4.1 %collective-permute-done.4.refs_5_ = bf16[32,1024]{1,0:T(8,128)(2,1)S(1)} collective-permute-done((bf16[32,1024]{1,0:T(8,128)(2,1)S(1)}, bf16[32,1024]{1,0:T(8,128)(2,1)S(1)}, u32[]{:S(2)}, u32[]{:S(2)}) %collective-permute-start.4) | collective-permute-done | bytes 65568 | tf_op jit(solution)/shard_map/ppermute | solution.py:335
  40.0 2.3 collective-permute-done.6.refs_7_
  44.6 1.6 spread.1
  46.2 5.0 %collective-permute-done.9.x_b = bf16[128,1024]{1,0:T(8,128)(2,1)S(1)} collective-permute-done((bf16[128,1024]{1,0:T(8,128)(2,1)S(1)}, bf16[128,1024]{1,0:T(8,128)(2,1)S(1)}, u32[]{:S(2)}, u32[]{:S(2)}) %collective-permute-start.9) | collective-permute-done | bytes 262176 | tf_op jit(solution)/shard_map/ppermute | solution.py:335
  51.2 2.9 %first.1 = (bf16[32,1536]{1,0:T(8,128)(2,1)S(1)}, bf16[32,1536]{1,0:T(8,128)(2,1)S(1)}, bf16[32,1536]{1,0:T(8,128)(2,1)S(1)}, bf16[32,1536]{1,0:T(8,128)(2,1)S(1...) custom-call(s32[7]{0:T(128)S(1)} %stack.49.place, ...), custom_call_target="tpu_custom_call" | custom-call | flops 1 | bytes 1 | tf_op jit(solution)/shard_map/first/pallas_call | solution.py:349
  54.2 1.6 collective-permute-start.33
  60.6 2.6 collective-permute-start.17
  63.2 2.3 collective-permute-start.18
  65.6 2.3 collective-permute-start.19
  67.9 4.8 %collective-permute-done.17.refs_4_ = bf16[32,1536]{1,0:T(8,128)(2,1)S(1)} collective-permute-done((bf16[32,1536]{1,0:T(8,128)(2,1)S(1)}, bf16[32,1536]{1,0:T(8,128)(2,1)S(1)}, u32[]{:S(2)}, u32[]{:S(2)}) %collective-permute-start.17) | collective-permute-done | bytes 98336 | tf_op jit(solution)/shard_map/ppermute | solution.py:335
  72.7 2.0 collective-permute-done.18.refs_5_
  74.6 3.2 %collective-permute-start.20 = (bf16[32,1536]{1,0:T(8,128)(2,1)S(1)}, bf16[32,1536]{1,0:T(8,128)(2,1)S(1)}, u32[]{:S(2)}, u32[]{:S(2)}) collective-permute-start(bf16[32,1536]{1,0:T(8,128)(2,1)S(1)} %get-tuple-element.232), channel_id=1, source_target_pairs={{0,28},{1,29},{2,30},{3,31},{4,24},{5,25},{6,26},{7,27},{8,20},{9,... | collective-permute-start | bytes 294920 | tf_op jit(solution)/shard_map/ppermute | solution.py:335
  77.8 4.8 %collective-permute-done.20.refs_7_ = bf16[32,1536]{1,0:T(8,128)(2,1)S(1)} collective-permute-done((bf16[32,1536]{1,0:T(8,128)(2,1)S(1)}, bf16[32,1536]{1,0:T(8,128)(2,1)S(1)}, u32[]{:S(2)}, u32[]{:S(2)}) %collective-permute-start.20) | collective-permute-done | bytes 98336 | tf_op jit(solution)/shard_map/ppermute | solution.py:335
  83.2 8.2 %collective-permute-done.21.c_b.cb_own = bf16[128,1024]{1,0:T(8,128)(2,1)S(1)} collective-permute-done((bf16[128,1024]{1,0:T(8,128)(2,1)S(1)}, bf16[128,1024]{1,0:T(8,128)(2,1)S(1)}, u32[]{:S(2)}, u32[]{:S(2)}) %collective-permute-start.21) | collective-permute-done | bytes 262176 | tf_op jit(solution)/shard_map/ppermute | solution.py:335
  92.0 1.8 attend.1
  94.5 13.8 %collective-permute-done.34.rest_7_ = bf16[256,1280]{1,0:T(8,128)(2,1)S(1)} collective-permute-done((bf16[256,1280]{1,0:T(8,128)(2,1)S(1)}, bf16[256,1280]{1,0:T(8,128)(2,1)S(1)}, u32[]{:S(2)}, u32[]{:S(2)}) %collective-permute-start.34) | collective-permute-done | bytes 655392 | tf_op jit(solution)/shard_map/ppermute | solution.py:335
  108.2 1.6 collective-permute-start.26
  109.8 2.3 collective-permute-done.26.refs_1_
  113.7 2.4 collective-permute-done.27.refs_2_
  116.1 2.0 collective-permute-start.28
  118.1 2.8 collective-permute-done.28.refs_3_
  120.9 1.8 collective-permute-start.29
  122.7 3.0 %collective-permute-done.29.refs_4_ = bf16[32,512]{1,0:T(8,128)(2,1)S(1)} collective-permute-done((bf16[32,512]{1,0:T(8,128)(2,1)S(1)}, bf16[32,512]{1,0:T(8,128)(2,1)S(1)}, u32[]{:S(2)}, u32[]{:S(2)}) %collective-permute-start.29) | collective-permute-done | bytes 32800 | tf_op jit(solution)/shard_map/ppermute | solution.py:335
  127.3 4.2 %collective-permute-done.30.refs_5_ = bf16[32,512]{1,0:T(8,128)(2,1)S(1)} collective-permute-done((bf16[32,512]{1,0:T(8,128)(2,1)S(1)}, bf16[32,512]{1,0:T(8,128)(2,1)S(1)}, u32[]{:S(2)}, u32[]{:S(2)}) %collective-permute-start.30) | collective-permute-done | bytes 32800 | tf_op jit(solution)/shard_map/ppermute | solution.py:335
  131.4 1.8 collective-permute-start.31
  133.2 4.0 %collective-permute-done.31.refs_6_ = bf16[32,512]{1,0:T(8,128)(2,1)S(1)} collective-permute-done((bf16[32,512]{1,0:T(8,128)(2,1)S(1)}, bf16[32,512]{1,0:T(8,128)(2,1)S(1)}, u32[]{:S(2)}, u32[]{:S(2)}) %collective-permute-start.31) | collective-permute-done | bytes 32800 | tf_op jit(solution)/shard_map/ppermute | solution.py:335
  137.1 3.4 %collective-permute-start.32 = (bf16[32,512]{1,0:T(8,128)(2,1)S(1)}, bf16[32,512]{1,0:T(8,128)(2,1)S(1)}, u32[]{:S(2)}, u32[]{:S(2)}) collective-permute-start(bf16[32,512]{1,0:T(8,128)(2,1)S(1)} %get-tuple-element.258), channel_id=1, source_target_pairs={{0,28},{1,29},{2,30},{3,31},{4,24},{5,25},{6,26},{7,27},{8,20},{9,... | collective-permute-start | bytes 98312 | tf_op jit(solution)/shard_map/ppermute | solution.py:335
  140.5 3.2 %collective-permute-done.32.refs_7_ = bf16[32,512]{1,0:T(8,128)(2,1)S(1)} collective-permute-done((bf16[32,512]{1,0:T(8,128)(2,1)S(1)}, bf16[32,512]{1,0:T(8,128)(2,1)S(1)}, u32[]{:S(2)}, u32[]{:S(2)}) %collective-permute-start.32) | collective-permute-done | bytes 32800 | tf_op jit(solution)/shard_map/ppermute | solution.py:335
  147.6 11.7 %collective-permute-done.39.far = bf16[256,1024]{1,0:T(8,128)(2,1)S(1)} collective-permute-done((bf16[256,1024]{1,0:T(8,128)(2,1)S(1)}, bf16[256,1024]{1,0:T(8,128)(2,1)S(1)}, u32[]{:S(2)}, u32[]{:S(2)}) %collective-permute-start.39) | collective-permute-done | bytes 524320 | tf_op jit(solution)/shard_map/ppermute | solution.py:335
  159.3 10.0 %ffn.1 = (f32[256,1024]{1,0:T(8,128)S(1)}, bf16[256,1024]{1,0:T(8,128)(2,1)S(1)}, bf16[256,1408]{1,0:T(8,128)(2,1)S(1)}, bf16[256,2816]{1,0:T(8,128)(2,1)S(1)}, ...) custom-call(s32[7]{0:T(128)S(1)} %stack.49.place, bf16[128,1024]{1,0:T(8,128)(2,1)S(1)} %get-tuple-element.214.x_a, ...), custom_call_target="tpu_custom_call" | custom-call | flops 1 | bytes 1 | tf_op jit(solution)/shard_map/ffn/pallas_call | solution.py:349
  170.9 2.7 down_term.1
  175.5 8.7 %collective-permute-done.42.far = bf16[256,1024]{1,0:T(8,128)(2,1)S(1)} collective-permute-done((bf16[256,1024]{1,0:T(8,128)(2,1)S(1)}, bf16[256,1024]{1,0:T(8,128)(2,1)S(1)}, u32[]{:S(2)}, u32[]{:S(2)}) %collective-permute-start.42) | collective-permute-done | bytes 524320 | tf_op jit(solution)/shard_map/ppermute | solution.py:335
  184.2 1.7 mid.1
  186.0 2.6 collective-permute-start.46
  193.1 2.4 collective-permute-done.47.refs_10_
  198.0 2.9 %collective-permute-done.49.refs_12_ = bf16[32,512]{1,0:T(8,128)(2,1)S(1)} collective-permute-done((bf16[32,512]{1,0:T(8,128)(2,1)S(1)}, bf16[32,512]{1,0:T(8,128)(2,1)S(1)}, u32[]{:S(2)}, u32[]{:S(2)}) %collective-permute-start.49) | collective-permute-done | bytes 32800 | tf_op jit(solution)/shard_map/ppermute | solution.py:335
  202.3 1.8 collective-permute-start.52
  204.1 3.3 %leaving_gradient.4 = bf16[256,2304]{1,0:T(8,128)(2,1)S(1)} custom-call(s32[7]{0:T(128)S(1)} %stack.49.place, bf16[256,1024]{1,0:T(8,128)(2,1)S(1)} %get-tuple-element.362.left_own, bf16[256,1024]{1,0:T(8,128)(2,1)S(1)} %collective-permute-done.43.left_near, bf16[256,2816]{1,0:T(8,128)(2,1)S(1)} %get-tuple-element.296.right_own, ...), custom_call_target="tpu_custom_call" | custom-call | flops 1 | bytes 1 | tf_op jit(solution)/shard_map/leaving_gradient/pallas_call | solution.py:349
  207.3 1.6 collective-permute-done.52.refs_15_
  209.0 4.6 %attend_back.1 = (bf16[32,1536]{1,0:T(8,128)(2,1)S(1)}, bf16[32,1536]{1,0:T(8,128)(2,1)S(1)}, bf16[32,1536]{1,0:T(8,128)(2,1)S(1)}, bf16[32,1536]{1,0:T(8,128)(2...) custom-call(s32[7]{0:T(128)S(1)} %stack.49.place, ...), custom_call_target="tpu_custom_call" | custom-call | flops 1 | bytes 1 | tf_op jit(solution)/shard_map/attend_back/pallas_call | solution.py:349
  214.7 2.4 collective-permute-start.59
  220.4 1.7 collective-permute-start.62
  222.0 2.5 collective-permute-done.59.refs_3_
  225.7 2.0 grad_out.1
  227.6 4.0 %grad_down.1 = f32[704,1024]{1,0:T(8,128)} custom-call(s32[7]{0:T(128)S(1)} %stack.49.place, bf16[256,1408]{1,0:T(8,128)(2,1)S(1)} %get-tuple-element.330.hidden.h_own, bf16[256,1408]{1,0:T(8,128)(2,1)S(1)} %collective-permute-done.45.h_near, bf16[128,1024]{1,0:T(8,128)(2,1)S(1)} %get-tuple-element.263.c_a.ca_own, ...), custom_call_target="tpu_custom_call" | custom-call | flops 1 | bytes 1 | tf_op jit(solution)/shard_map/grad_down/pallas_call | solution.py:349
  231.7 2.0 collective-permute-done.61.refs_5_
  233.7 2.8 collective-permute-done.64.rest_1_
  236.5 2.5 back_first.1
  241.3 2.2 leaving_gradient.5
  243.5 4.2 %collective-permute-done.65.far = bf16[128,1024]{1,0:T(8,128)(2,1)S(1)} collective-permute-done((bf16[128,1024]{1,0:T(8,128)(2,1)S(1)}, bf16[128,1024]{1,0:T(8,128)(2,1)S(1)}, u32[]{:S(2)}, u32[]{:S(2)}) %collective-permute-start.65) | collective-permute-done | bytes 262176 | tf_op jit(solution)/shard_map/ppermute | solution.py:335
  251.0 2.1 collective-permute-start.68
  255.0 6.7 %staying_gradient.2 = f32[256,5632]{1,0:T(8,128)} custom-call(s32[7]{0:T(128)S(1)} %stack.49.place, bf16[256,1024]{1,0:T(8,128)(2,1)S(1)} %get-tuple-element.362.left_own, bf16[256,1024]{1,0:T(8,128)(2,1)S(1)} %collective-permute-done.43.left_near, bf16[256,2816]{1,0:T(8,128)(2,1)S(1)} %get-tuple-element.296.right_own, ...), custom_call_target="tpu_custom_call" | custom-call | flops 1 | bytes 1 | tf_op jit(solution)/shard_map/staying_gradient/pallas_call | solution.py:349
  261.7 2.3 collective-permute-start.70
  265.2 2.3 collective-permute-start.72
  267.5 1.9 collective-permute-start.73
  270.5 3.3 %collective-permute-done.71.refs_5_ = bf16[32,1024]{1,0:T(8,128)(2,1)S(1)} collective-permute-done((bf16[32,1024]{1,0:T(8,128)(2,1)S(1)}, bf16[32,1024]{1,0:T(8,128)(2,1)S(1)}, u32[]{:S(2)}, u32[]{:S(2)}) %collective-permute-start.71) | collective-permute-done | bytes 65568 | tf_op jit(solution)/shard_map/ppermute | solution.py:335
  274.6 1.6 to_frames.1
  276.2 4.1 %staying_gradient.3 = f32[256,3072]{1,0:T(8,128)} custom-call(s32[7]{0:T(128)S(1)} %stack.49.place, bf16[256,1024]{1,0:T(8,128)(2,1)S(1)} %get-tuple-element.266.left_own, bf16[256,1024]{1,0:T(8,128)(2,1)S(1)} %collective-permute-done.38.left_near, bf16[256,1536]{1,0:T(8,128)(2,1)S(1)} %get-tuple-element.348.right_own, ...), custom_call_target="tpu_custom_call" | custom-call | flops 1 | bytes 1 | tf_op jit(solution)/shard_map/staying_gradient/pallas_call | solution.py:349
  (153 shorter events, 56.5 us)
Async XLA Ops:
  2.8 39.5 %collective-permute-start.10 = (bf16[256,1536]{1,0:T(8,128)(2,1)S(1)}, bf16[256,1536]{1,0:T(8,128)(2,1)S(1)}, u32[]{:S(2)}, u32[]{:S(2)}) collective-permute-start(bf16[256,1536]{1,0:T(8,128)(2,1)S(1)} %far_columns.1), channel_id=1, source_target_pairs={{0,3},{1,2},{2,1},{3,0},{4,7},{5,6},{6,5},{7,4},{8,11},{9,10},{10,... | collective-permute-start | bytes 2359304 | tf_op jit(solution)/shard_map/ppermute | solution.py:335
  8.3 15.1 %collective-permute-start.7 = (s32[1,128]{1,0:T(1,128)S(1)}, s32[1,128]{1,0:T(1,128)S(1)}, u32[]{:S(2)}, u32[]{:S(2)}) collective-permute-start(s32[1,128]{1,0:T(1,128)S(1)} %select_n.46.ids_a), channel_id=1, source_target_pairs={{0,2},{1,3},{2,0},{3,1},{4,6},{5,7},{6,4},{7,5},{8,10},{9,11},{10,... | collective-permute-start | bytes 1544 | tf_op jit(solution)/shard_map/ppermute | solution.py:335
  9.1 21.2 %collective-permute-start = (bf16[32,1024]{1,0:T(8,128)(2,1)}, bf16[32,1024]{1,0:T(8,128)(2,1)S(1)}, u32[]{:S(2)}, u32[]{:S(2)}) collective-permute-start(bf16[32,1024]{1,0:T(8,128)(2,1)} %copy-done.8), channel_id=1, source_target_pairs={{0,4},{1,5},{2,6},{3,7},{4,0},{5,1},{6,2},{7,3},{8,12},{9,13},{10,... | collective-permute-start | bytes 196616 | tf_op jit(solution)/shard_map/ppermute | solution.py:335
  10.7 21.0 %collective-permute-start.1 = (bf16[32,1024]{1,0:T(8,128)(2,1)}, bf16[32,1024]{1,0:T(8,128)(2,1)S(1)}, u32[]{:S(2)}, u32[]{:S(2)}) collective-permute-start(bf16[32,1024]{1,0:T(8,128)(2,1)} %copy-done.7), channel_id=1, source_target_pairs={{0,8},{1,9},{2,10},{3,11},{4,12},{5,13},{6,14},{7,15},{8,0},{9,1},... | collective-permute-start | bytes 196616 | tf_op jit(solution)/shard_map/ppermute | solution.py:335
  12.2 23.0 %collective-permute-start.2 = (bf16[32,1024]{1,0:T(8,128)(2,1)S(1)}, bf16[32,1024]{1,0:T(8,128)(2,1)S(1)}, u32[]{:S(2)}, u32[]{:S(2)}) collective-permute-start(bf16[32,1024]{1,0:T(8,128)(2,1)S(1)} %get-tuple-element.198), channel_id=1, source_target_pairs={{0,12},{1,13},{2,14},{3,15},{4,8},{5,9},{6,10},{7,11},{8,4},{9,5},... | collective-permute-start | bytes 196616 | tf_op jit(solution)/shard_map/ppermute | solution.py:335
  27.2 8.7 %collective-permute-start.3 = (bf16[32,1024]{1,0:T(8,128)(2,1)S(1)}, bf16[32,1024]{1,0:T(8,128)(2,1)S(1)}, u32[]{:S(2)}, u32[]{:S(2)}) collective-permute-start(bf16[32,1024]{1,0:T(8,128)(2,1)S(1)} %get-tuple-element.199), channel_id=1, source_target_pairs={{0,16},{1,17},{2,18},{3,19},{4,20},{5,21},{6,22},{7,23},{8,24},{9,... | collective-permute-start | bytes 196616 | tf_op jit(solution)/shard_map/ppermute | solution.py:335
  30.4 9.7 %collective-permute-start.4 = (bf16[32,1024]{1,0:T(8,128)(2,1)S(1)}, bf16[32,1024]{1,0:T(8,128)(2,1)S(1)}, u32[]{:S(2)}, u32[]{:S(2)}) collective-permute-start(bf16[32,1024]{1,0:T(8,128)(2,1)S(1)} %get-tuple-element.200), channel_id=1, source_target_pairs={{0,20},{1,21},{2,22},{3,23},{4,16},{5,17},{6,18},{7,19},{8,28},{9,... | collective-permute-start | bytes 196616 | tf_op jit(solution)/shard_map/ppermute | solution.py:335
  31.7 8.4 %collective-permute-start.5 = (bf16[32,1024]{1,0:T(8,128)(2,1)S(1)}, bf16[32,1024]{1,0:T(8,128)(2,1)S(1)}, u32[]{:S(2)}, u32[]{:S(2)}) collective-permute-start(bf16[32,1024]{1,0:T(8,128)(2,1)S(1)} %get-tuple-element.201), channel_id=1, source_target_pairs={{0,24},{1,25},{2,26},{3,27},{4,28},{5,29},{6,30},{7,31},{8,16},{9,... | collective-permute-start | bytes 196616 | tf_op jit(solution)/shard_map/ppermute | solution.py:335
  35.3 7.1 %collective-permute-start.6 = (bf16[32,1024]{1,0:T(8,128)(2,1)S(1)}, bf16[32,1024]{1,0:T(8,128)(2,1)S(1)}, u32[]{:S(2)}, u32[]{:S(2)}) collective-permute-start(bf16[32,1024]{1,0:T(8,128)(2,1)S(1)} %get-tuple-element.202), channel_id=1, source_target_pairs={{0,28},{1,29},{2,30},{3,31},{4,24},{5,25},{6,26},{7,27},{8,20},{9,... | collective-permute-start | bytes 196616 | tf_op jit(solution)/shard_map/ppermute | solution.py:335
  42.3 8.8 %collective-permute-start.13 = (bf16[256,1536]{1,0:T(8,128)(2,1)S(1)}, bf16[256,1536]{1,0:T(8,128)(2,1)S(1)}, u32[]{:S(2)}, u32[]{:S(2)}) collective-permute-start(bf16[256,1536]{1,0:T(8,128)(2,1)S(1)} %kept_columns.1), channel_id=1, source_target_pairs={{0,1},{1,0},{2,3},{3,2},{4,5},{5,4},{6,7},{7,6},{8,9},{9,8},{10,11... | collective-permute-start | bytes 2359304 | tf_op jit(solution)/shard_map/ppermute | solution.py:335
  42.3 8.8 %collective-permute-start.11 = (bf16[256,1536]{1,0:T(8,128)(2,1)S(1)}, bf16[256,1536]{1,0:T(8,128)(2,1)S(1)}, u32[]{:S(2)}, u32[]{:S(2)}) collective-permute-start(bf16[256,1536]{1,0:T(8,128)(2,1)S(1)} %collective-permute-done.10.w_across), channel_id=1, source_target_pairs={{0,1},{1,0},{2,3},{3,2},{4,5},{5,4},{6,7},{7,6},{8,9},{9,8},{10,11... | collective-permute-start | bytes 2359304 | tf_op jit(solution)/shard_map/ppermute | solution.py:335
  42.9 8.3 %collective-permute-start.9 = (bf16[128,1024]{1,0:T(8,128)(2,1)S(1)}, bf16[128,1024]{1,0:T(8,128)(2,1)S(1)}, u32[]{:S(2)}, u32[]{:S(2)}) collective-permute-start(bf16[128,1024]{1,0:T(8,128)(2,1)S(1)} %get-tuple-element.214.x_a), channel_id=1, source_target_pairs={{0,2},{1,3},{2,0},{3,1},{4,6},{5,7},{6,4},{7,5},{8,10},{9,11},{10,... | collective-permute-start | bytes 786440 | tf_op jit(solution)/shard_map/ppermute | solution.py:335
  54.1 37.9 %collective-permute-start.25 = (bf16[704,1024]{1,0:T(8,128)(2,1)S(1)}, bf16[704,1024]{1,0:T(8,128)(2,1)S(1)}, u32[]{:S(2)}, u32[]{:S(2)}) collective-permute-start(bf16[704,1024]{1,0:T(8,128)(2,1)S(1)} %copy-done.2), channel_id=1, source_target_pairs={{0,1},{1,0},{2,3},{3,2},{4,5},{5,4},{6,7},{7,6},{8,9},{9,8},{10,11... | collective-permute-start | bytes 4325384 | tf_op jit(solution)/shard_map/ppermute | solution.py:335
  54.2 28.4 %collective-permute-start.33 = (bf16[256,1536]{1,0:T(8,128)(2,1)S(1)}, bf16[256,1536]{1,0:T(8,128)(2,1)S(1)}, u32[]{:S(2)}, u32[]{:S(2)}) collective-permute-start(bf16[256,1536]{1,0:T(8,128)(2,1)S(1)} %get-tuple-element.261), channel_id=1, source_target_pairs={{0,3},{1,2},{2,1},{3,0},{4,7},{5,6},{6,5},{7,4},{8,11},{9,10},{10,... | collective-permute-start | bytes 2359304 | tf_op jit(solution)/shard_map/ppermute | solution.py:335
  56.3 6.9 %collective-permute-start.15 = (bf16[32,1536]{1,0:T(8,128)(2,1)S(1)}, bf16[32,1536]{1,0:T(8,128)(2,1)S(1)}, u32[]{:S(2)}, u32[]{:S(2)}) collective-permute-start(bf16[32,1536]{1,0:T(8,128)(2,1)S(1)} %get-tuple-element.227), channel_id=1, source_target_pairs={{0,8},{1,9},{2,10},{3,11},{4,12},{5,13},{6,14},{7,15},{8,0},{9,1},... | collective-permute-start | bytes 294920 | tf_op jit(solution)/shard_map/ppermute | solution.py:335
  57.9 7.7 %collective-permute-start.16 = (bf16[32,1536]{1,0:T(8,128)(2,1)S(1)}, bf16[32,1536]{1,0:T(8,128)(2,1)S(1)}, u32[]{:S(2)}, u32[]{:S(2)}) collective-permute-start(bf16[32,1536]{1,0:T(8,128)(2,1)S(1)} %get-tuple-element.228), channel_id=1, source_target_pairs={{0,12},{1,13},{2,14},{3,15},{4,8},{5,9},{6,10},{7,11},{8,4},{9,5},... | collective-permute-start | bytes 294920 | tf_op jit(solution)/shard_map/ppermute | solution.py:335
  60.6 12.1 %collective-permute-start.17 = (bf16[32,1536]{1,0:T(8,128)(2,1)S(1)}, bf16[32,1536]{1,0:T(8,128)(2,1)S(1)}, u32[]{:S(2)}, u32[]{:S(2)}) collective-permute-start(bf16[32,1536]{1,0:T(8,128)(2,1)S(1)} %get-tuple-element.229), channel_id=1, source_target_pairs={{0,16},{1,17},{2,18},{3,19},{4,20},{5,21},{6,22},{7,23},{8,24},{9,... | collective-permute-start | bytes 294920 | tf_op jit(solution)/shard_map/ppermute | solution.py:335
  63.2 11.4 %collective-permute-start.18 = (bf16[32,1536]{1,0:T(8,128)(2,1)S(1)}, bf16[32,1536]{1,0:T(8,128)(2,1)S(1)}, u32[]{:S(2)}, u32[]{:S(2)}) collective-permute-start(bf16[32,1536]{1,0:T(8,128)(2,1)S(1)} %get-tuple-element.230), channel_id=1, source_target_pairs={{0,20},{1,21},{2,22},{3,23},{4,16},{5,17},{6,18},{7,19},{8,28},{9,... | collective-permute-start | bytes 294920 | tf_op jit(solution)/shard_map/ppermute | solution.py:335
  65.6 9.0 %collective-permute-start.19 = (bf16[32,1536]{1,0:T(8,128)(2,1)S(1)}, bf16[32,1536]{1,0:T(8,128)(2,1)S(1)}, u32[]{:S(2)}, u32[]{:S(2)}) collective-permute-start(bf16[32,1536]{1,0:T(8,128)(2,1)S(1)} %get-tuple-element.231), channel_id=1, source_target_pairs={{0,24},{1,25},{2,26},{3,27},{4,28},{5,29},{6,30},{7,31},{8,16},{9,... | collective-permute-start | bytes 294920 | tf_op jit(solution)/shard_map/ppermute | solution.py:335
  72.7 19.4 %collective-permute-start.22 = (bf16[256,1536]{1,0:T(8,128)(2,1)S(1)}, bf16[256,1536]{1,0:T(8,128)(2,1)S(1)}, u32[]{:S(2)}, u32[]{:S(2)}) collective-permute-start(bf16[256,1536]{1,0:T(8,128)(2,1)S(1)} %get-tuple-element.237.rest_0_), channel_id=1, source_target_pairs={{0,1},{1,0},{2,3},{3,2},{4,5},{5,4},{6,7},{7,6},{8,9},{9,8},{10,11... | collective-permute-start | bytes 2359304 | tf_op jit(solution)/shard_map/ppermute | solution.py:335
  74.6 16.7 %collective-permute-start.24 = (bf16[256,1024]{1,0:T(8,128)(2,1)S(1)}, bf16[256,1024]{1,0:T(8,128)(2,1)S(1)}, u32[]{:S(2)}, u32[]{:S(2)}) collective-permute-start(bf16[256,1024]{1,0:T(8,128)(2,1)S(1)} %copy-done.4), channel_id=1, source_target_pairs={{0,1},{1,0},{2,3},{3,2},{4,5},{5,4},{6,7},{7,6},{8,9},{9,8},{10,11... | collective-permute-start | bytes 1572872 | tf_op jit(solution)/shard_map/ppermute | solution.py:335
  74.6 8.0 %collective-permute-start.20 = (bf16[32,1536]{1,0:T(8,128)(2,1)S(1)}, bf16[32,1536]{1,0:T(8,128)(2,1)S(1)}, u32[]{:S(2)}, u32[]{:S(2)}) collective-permute-start(bf16[32,1536]{1,0:T(8,128)(2,1)S(1)} %get-tuple-element.232), channel_id=1, source_target_pairs={{0,28},{1,29},{2,30},{3,31},{4,24},{5,25},{6,26},{7,27},{8,20},{9,... | collective-permute-start | bytes 294920 | tf_op jit(solution)/shard_map/ppermute | solution.py:335
  82.7 9.4 %collective-permute-start.23 = (bf16[256,1280]{1,0:T(8,128)(2,1)S(1)}, bf16[256,1280]{1,0:T(8,128)(2,1)S(1)}, u32[]{:S(2)}, u32[]{:S(2)}) collective-permute-start(bf16[256,1280]{1,0:T(8,128)(2,1)S(1)} %get-tuple-element.239.rest_4_), channel_id=1, source_target_pairs={{0,1},{1,0},{2,3},{3,2},{4,5},{5,4},{6,7},{7,6},{8,9},{9,8},{10,11... | collective-permute-start | bytes 1966088 | tf_op jit(solution)/shard_map/ppermute | solution.py:335
  82.7 8.7 %collective-permute-start.21 = (bf16[128,1024]{1,0:T(8,128)(2,1)S(1)}, bf16[128,1024]{1,0:T(8,128)(2,1)S(1)}, u32[]{:S(2)}, u32[]{:S(2)}) collective-permute-start(bf16[128,1024]{1,0:T(8,128)(2,1)S(1)} %get-tuple-element.263.c_a.ca_own), channel_id=1, source_target_pairs={{0,2},{1,3},{2,0},{3,1},{4,6},{5,7},{6,4},{7,5},{8,10},{9,11},{10,... | collective-permute-start | bytes 786440 | tf_op jit(solution)/shard_map/ppermute | solution.py:335
  91.4 16.9 %collective-permute-start.34 = (bf16[256,1280]{1,0:T(8,128)(2,1)S(1)}, bf16[256,1280]{1,0:T(8,128)(2,1)S(1)}, u32[]{:S(2)}, u32[]{:S(2)}) collective-permute-start(bf16[256,1280]{1,0:T(8,128)(2,1)S(1)} %get-tuple-element.262), channel_id=1, source_target_pairs={{0,3},{1,2},{2,1},{3,0},{4,7},{5,6},{6,5},{7,4},{8,11},{9,10},{10,... | collective-permute-start | bytes 1966088 | tf_op jit(solution)/shard_map/ppermute | solution.py:335
  91.4 52.4 %collective-permute-start.35 = (bf16[256,1536]{1,0:T(8,128)(2,1)S(1)}, bf16[256,1536]{1,0:T(8,128)(2,1)S(1)}, u32[]{:S(2)}, u32[]{:S(2)}) collective-permute-start(bf16[256,1536]{1,0:T(8,128)(2,1)S(1)} %collective-permute-done.33.rest_3_), channel_id=1, source_target_pairs={{0,1},{1,0},{2,3},{3,2},{4,5},{5,4},{6,7},{7,6},{8,9},{9,8},{10,11... | collective-permute-start | bytes 2359304 | tf_op jit(solution)/shard_map/ppermute | solution.py:335
  93.8 49.9 %collective-permute-start.38 = (bf16[256,1024]{1,0:T(8,128)(2,1)S(1)}, bf16[256,1024]{1,0:T(8,128)(2,1)S(1)}, u32[]{:S(2)}, u32[]{:S(2)}) collective-permute-start(bf16[256,1024]{1,0:T(8,128)(2,1)S(1)} %get-tuple-element.266.left_own), channel_id=1, source_target_pairs={{0,1},{1,0},{2,3},{3,2},{4,5},{5,4},{6,7},{7,6},{8,9},{9,8},{10,11... | collective-permute-start | bytes 1572872 | tf_op jit(solution)/shard_map/ppermute | solution.py:335
  93.9 49.8 %collective-permute-start.36 = (bf16[128,1024]{1,0:T(8,128)(2,1)S(1)}, bf16[128,1024]{1,0:T(8,128)(2,1)S(1)}, u32[]{:S(2)}, u32[]{:S(2)}) collective-permute-start(bf16[128,1024]{1,0:T(8,128)(2,1)S(1)} %get-tuple-element.263.c_a.ca_own), channel_id=1, source_target_pairs={{0,1},{1,0},{2,3},{3,2},{4,5},{5,4},{6,7},{7,6},{8,9},{9,8},{10,11... | collective-permute-start | bytes 786440 | tf_op jit(solution)/shard_map/ppermute | solution.py:335
  94.4 49.4 %collective-permute-start.37 = (bf16[128,1024]{1,0:T(8,128)(2,1)S(1)}, bf16[128,1024]{1,0:T(8,128)(2,1)S(1)}, u32[]{:S(2)}, u32[]{:S(2)}) collective-permute-start(bf16[128,1024]{1,0:T(8,128)(2,1)S(1)} %collective-permute-done.21.c_b.cb_own), channel_id=1, source_target_pairs={{0,1},{1,0},{2,3},{3,2},{4,5},{5,4},{6,7},{7,6},{8,9},{9,8},{10,11... | collective-permute-start | bytes 786440 | tf_op jit(solution)/shard_map/ppermute | solution.py:335
  125.7 5.7 %collective-permute-start.30 = (bf16[32,512]{1,0:T(8,128)(2,1)S(1)}, bf16[32,512]{1,0:T(8,128)(2,1)S(1)}, u32[]{:S(2)}, u32[]{:S(2)}) collective-permute-start(bf16[32,512]{1,0:T(8,128)(2,1)S(1)} %get-tuple-element.256), channel_id=1, source_target_pairs={{0,20},{1,21},{2,22},{3,23},{4,16},{5,17},{6,18},{7,19},{8,28},{9,... | collective-permute-start | bytes 98312 | tf_op jit(solution)/shard_map/ppermute | solution.py:335
  131.4 5.7 %collective-permute-start.31 = (bf16[32,512]{1,0:T(8,128)(2,1)S(1)}, bf16[32,512]{1,0:T(8,128)(2,1)S(1)}, u32[]{:S(2)}, u32[]{:S(2)}) collective-permute-start(bf16[32,512]{1,0:T(8,128)(2,1)S(1)} %get-tuple-element.257), channel_id=1, source_target_pairs={{0,24},{1,25},{2,26},{3,27},{4,28},{5,29},{6,30},{7,31},{8,16},{9,... | collective-permute-start | bytes 98312 | tf_op jit(solution)/shard_map/ppermute | solution.py:335
  137.1 6.6 %collective-permute-start.32 = (bf16[32,512]{1,0:T(8,128)(2,1)S(1)}, bf16[32,512]{1,0:T(8,128)(2,1)S(1)}, u32[]{:S(2)}, u32[]{:S(2)}) collective-permute-start(bf16[32,512]{1,0:T(8,128)(2,1)S(1)} %get-tuple-element.258), channel_id=1, source_target_pairs={{0,28},{1,29},{2,30},{3,31},{4,24},{5,25},{6,26},{7,27},{8,20},{9,... | collective-permute-start | bytes 98312 | tf_op jit(solution)/shard_map/ppermute | solution.py:335
  144.9 14.4 %collective-permute-start.41 = (bf16[256,1280]{1,0:T(8,128)(2,1)S(1)}, bf16[256,1280]{1,0:T(8,128)(2,1)S(1)}, u32[]{:S(2)}, u32[]{:S(2)}) collective-permute-start(bf16[256,1280]{1,0:T(8,128)(2,1)S(1)} %collective-permute-done.34.rest_7_), channel_id=1, source_target_pairs={{0,1},{1,0},{2,3},{3,2},{4,5},{5,4},{6,7},{7,6},{8,9},{9,8},{10,11... | collective-permute-start | bytes 1966088 | tf_op jit(solution)/shard_map/ppermute | solution.py:335
  145.0 14.3 %collective-permute-start.39 = (bf16[256,1024]{1,0:T(8,128)(2,1)S(1)}, bf16[256,1024]{1,0:T(8,128)(2,1)S(1)}, u32[]{:S(2)}, u32[]{:S(2)}) collective-permute-start(bf16[256,1024]{1,0:T(8,128)(2,1)S(1)} %get-tuple-element.276), channel_id=1, source_target_pairs={{0,2},{1,3},{2,0},{3,1},{4,6},{5,7},{6,4},{7,5},{8,10},{9,11},{10,... | collective-permute-start | bytes 1572872 | tf_op jit(solution)/shard_map/ppermute | solution.py:335
  169.3 5.1 %collective-permute-start.44 = (bf16[256,2816]{1,0:T(8,128)(2,1)S(1)}, bf16[256,2816]{1,0:T(8,128)(2,1)S(1)}, u32[]{:S(2)}, u32[]{:S(2)}) collective-permute-start(bf16[256,2816]{1,0:T(8,128)(2,1)S(1)} %get-tuple-element.296.right_own), channel_id=1, source_target_pairs={{0,1},{1,0},{2,3},{3,2},{4,5},{5,4},{6,7},{7,6},{8,9},{9,8},{10,11... | collective-permute-start | bytes 4325384 | tf_op jit(solution)/shard_map/ppermute | solution.py:335
  169.4 14.8 %collective-permute-start.45 = (bf16[256,1408]{1,0:T(8,128)(2,1)S(1)}, bf16[256,1408]{1,0:T(8,128)(2,1)S(1)}, u32[]{:S(2)}, u32[]{:S(2)}) collective-permute-start(bf16[256,1408]{1,0:T(8,128)(2,1)S(1)} %get-tuple-element.330.hidden.h_own), channel_id=1, source_target_pairs={{0,1},{1,0},{2,3},{3,2},{4,5},{5,4},{6,7},{7,6},{8,9},{9,8},{10,11... | collective-permute-start | bytes 2162696 | tf_op jit(solution)/shard_map/ppermute | solution.py:335
  169.9 14.3 %collective-permute-start.42 = (bf16[256,1024]{1,0:T(8,128)(2,1)S(1)}, bf16[256,1024]{1,0:T(8,128)(2,1)S(1)}, u32[]{:S(2)}, u32[]{:S(2)}) collective-permute-start(bf16[256,1024]{1,0:T(8,128)(2,1)S(1)} %get-tuple-element.288), channel_id=1, source_target_pairs={{0,2},{1,3},{2,0},{3,1},{4,6},{5,7},{6,4},{7,5},{8,10},{9,11},{10,... | collective-permute-start | bytes 1572872 | tf_op jit(solution)/shard_map/ppermute | solution.py:335
  185.9 23.0 %collective-permute-start.55 = (bf16[256,1024]{1,0:T(8,128)(2,1)S(1)}, bf16[256,1024]{1,0:T(8,128)(2,1)S(1)}, u32[]{:S(2)}, u32[]{:S(2)}) collective-permute-start(bf16[256,1024]{1,0:T(8,128)(2,1)S(1)} %get-tuple-element.335.d_own), channel_id=1, source_target_pairs={{0,1},{1,0},{2,3},{3,2},{4,5},{5,4},{6,7},{7,6},{8,9},{9,8},{10,11... | collective-permute-start | bytes 1572872 | tf_op jit(solution)/shard_map/ppermute | solution.py:335
  186.0 5.6 %collective-permute-start.46 = (bf16[32,512]{1,0:T(8,128)(2,1)S(1)}, bf16[32,512]{1,0:T(8,128)(2,1)S(1)}, u32[]{:S(2)}, u32[]{:S(2)}) collective-permute-start(bf16[32,512]{1,0:T(8,128)(2,1)S(1)} %get-tuple-element.299), channel_id=1, source_target_pairs={{0,4},{1,5},{2,6},{3,7},{4,0},{5,1},{6,2},{7,3},{8,12},{9,13},{10,... | collective-permute-start | bytes 98312 | tf_op jit(solution)/shard_map/ppermute | solution.py:335
  188.6 20.3 %collective-permute-start.54 = (bf16[128,1024]{1,0:T(8,128)(2,1)S(1)}, bf16[128,1024]{1,0:T(8,128)(2,1)S(1)}, u32[]{:S(2)}, u32[]{:S(2)}) collective-permute-start(bf16[128,1024]{1,0:T(8,128)(2,1)S(1)} %get-tuple-element.309), channel_id=1, source_target_pairs={{0,2},{1,3},{2,0},{3,1},{4,6},{5,7},{6,4},{7,5},{8,10},{9,11},{10,... | collective-permute-start | bytes 786440 | tf_op jit(solution)/shard_map/ppermute | solution.py:335
  189.4 19.6 %collective-permute-start.53 = (bf16[256,512]{1,0:T(8,128)(2,1)S(1)}, bf16[256,512]{1,0:T(8,128)(2,1)S(1)}, u32[]{:S(2)}, u32[]{:S(2)}) collective-permute-start(bf16[256,512]{1,0:T(8,128)(2,1)S(1)} %leaving_gradient.3), channel_id=1, source_target_pairs={{0,3},{1,2},{2,1},{3,0},{4,7},{5,6},{6,5},{7,4},{8,11},{9,10},{10,... | collective-permute-start | bytes 786440 | tf_op jit(solution)/shard_map/ppermute | solution.py:335
  195.6 5.2 %collective-permute-start.49 = (bf16[32,512]{1,0:T(8,128)(2,1)S(1)}, bf16[32,512]{1,0:T(8,128)(2,1)S(1)}, u32[]{:S(2)}, u32[]{:S(2)}) collective-permute-start(bf16[32,512]{1,0:T(8,128)(2,1)S(1)} %get-tuple-element.302), channel_id=1, source_target_pairs={{0,16},{1,17},{2,18},{3,19},{4,20},{5,21},{6,22},{7,23},{8,24},{9,... | collective-permute-start | bytes 98312 | tf_op jit(solution)/shard_map/ppermute | solution.py:335
  196.4 5.9 %collective-permute-start.50 = (bf16[32,512]{1,0:T(8,128)(2,1)S(1)}, bf16[32,512]{1,0:T(8,128)(2,1)S(1)}, u32[]{:S(2)}, u32[]{:S(2)}) collective-permute-start(bf16[32,512]{1,0:T(8,128)(2,1)S(1)} %get-tuple-element.303), channel_id=1, source_target_pairs={{0,20},{1,21},{2,22},{3,23},{4,16},{5,17},{6,18},{7,19},{8,28},{9,... | collective-permute-start | bytes 98312 | tf_op jit(solution)/shard_map/ppermute | solution.py:335
  200.8 6.5 %collective-permute-start.51 = (bf16[32,512]{1,0:T(8,128)(2,1)S(1)}, bf16[32,512]{1,0:T(8,128)(2,1)S(1)}, u32[]{:S(2)}, u32[]{:S(2)}) collective-permute-start(bf16[32,512]{1,0:T(8,128)(2,1)S(1)} %get-tuple-element.304), channel_id=1, source_target_pairs={{0,24},{1,25},{2,26},{3,27},{4,28},{5,29},{6,30},{7,31},{8,16},{9,... | collective-permute-start | bytes 98312 | tf_op jit(solution)/shard_map/ppermute | solution.py:335
  202.3 6.6 %collective-permute-start.52 = (bf16[32,512]{1,0:T(8,128)(2,1)S(1)}, bf16[32,512]{1,0:T(8,128)(2,1)S(1)}, u32[]{:S(2)}, u32[]{:S(2)}) collective-permute-start(bf16[32,512]{1,0:T(8,128)(2,1)S(1)} %get-tuple-element.305), channel_id=1, source_target_pairs={{0,28},{1,29},{2,30},{3,31},{4,24},{5,25},{6,26},{7,27},{8,20},{9,... | collective-permute-start | bytes 98312 | tf_op jit(solution)/shard_map/ppermute | solution.py:335
  208.9 27.5 %collective-permute-start.64 = (bf16[256,2304]{1,0:T(8,128)(2,1)S(1)}, bf16[256,2304]{1,0:T(8,128)(2,1)S(1)}, u32[]{:S(2)}, u32[]{:S(2)}) collective-permute-start(bf16[256,2304]{1,0:T(8,128)(2,1)S(1)} %leaving_gradient.4), channel_id=1, source_target_pairs={{0,3},{1,2},{2,1},{3,0},{4,7},{5,6},{6,5},{7,4},{8,11},{9,10},{10,... | collective-permute-start | bytes 3538952 | tf_op jit(solution)/shard_map/ppermute | solution.py:335
  213.6 5.5 %collective-permute-start.57 = (bf16[32,1536]{1,0:T(8,128)(2,1)S(1)}, bf16[32,1536]{1,0:T(8,128)(2,1)S(1)}, u32[]{:S(2)}, u32[]{:S(2)}) collective-permute-start(bf16[32,1536]{1,0:T(8,128)(2,1)S(1)} %get-tuple-element.322), channel_id=1, source_target_pairs={{0,4},{1,5},{2,6},{3,7},{4,0},{5,1},{6,2},{7,3},{8,12},{9,13},{10,... | collective-permute-start | bytes 294920 | tf_op jit(solution)/shard_map/ppermute | solution.py:335
  214.5 5.9 %collective-permute-start.58 = (bf16[32,1536]{1,0:T(8,128)(2,1)S(1)}, bf16[32,1536]{1,0:T(8,128)(2,1)S(1)}, u32[]{:S(2)}, u32[]{:S(2)}) collective-permute-start(bf16[32,1536]{1,0:T(8,128)(2,1)S(1)} %get-tuple-element.323), channel_id=1, source_target_pairs={{0,8},{1,9},{2,10},{3,11},{4,12},{5,13},{6,14},{7,15},{8,0},{9,1},... | collective-permute-start | bytes 294920 | tf_op jit(solution)/shard_map/ppermute | solution.py:335
  214.7 9.9 %collective-permute-start.59 = (bf16[32,1536]{1,0:T(8,128)(2,1)S(1)}, bf16[32,1536]{1,0:T(8,128)(2,1)S(1)}, u32[]{:S(2)}, u32[]{:S(2)}) collective-permute-start(bf16[32,1536]{1,0:T(8,128)(2,1)S(1)} %get-tuple-element.324), channel_id=1, source_target_pairs={{0,12},{1,13},{2,14},{3,15},{4,8},{5,9},{6,10},{7,11},{8,4},{9,5},... | collective-permute-start | bytes 294920 | tf_op jit(solution)/shard_map/ppermute | solution.py:335
  217.1 14.5 %collective-permute-start.60 = (bf16[32,1536]{1,0:T(8,128)(2,1)S(1)}, bf16[32,1536]{1,0:T(8,128)(2,1)S(1)}, u32[]{:S(2)}, u32[]{:S(2)}) collective-permute-start(bf16[32,1536]{1,0:T(8,128)(2,1)S(1)} %get-tuple-element.325), channel_id=1, source_target_pairs={{0,16},{1,17},{2,18},{3,19},{4,20},{5,21},{6,22},{7,23},{8,24},{9,... | collective-permute-start | bytes 294920 | tf_op jit(solution)/shard_map/ppermute | solution.py:335
  219.1 14.6 %collective-permute-start.61 = (bf16[32,1536]{1,0:T(8,128)(2,1)S(1)}, bf16[32,1536]{1,0:T(8,128)(2,1)S(1)}, u32[]{:S(2)}, u32[]{:S(2)}) collective-permute-start(bf16[32,1536]{1,0:T(8,128)(2,1)S(1)} %get-tuple-element.326), channel_id=1, source_target_pairs={{0,20},{1,21},{2,22},{3,23},{4,16},{5,17},{6,18},{7,19},{8,28},{9,... | collective-permute-start | bytes 294920 | tf_op jit(solution)/shard_map/ppermute | solution.py:335
  220.4 13.3 %collective-permute-start.62 = (bf16[32,1536]{1,0:T(8,128)(2,1)S(1)}, bf16[32,1536]{1,0:T(8,128)(2,1)S(1)}, u32[]{:S(2)}, u32[]{:S(2)}) collective-permute-start(bf16[32,1536]{1,0:T(8,128)(2,1)S(1)} %get-tuple-element.327), channel_id=1, source_target_pairs={{0,24},{1,25},{2,26},{3,27},{4,28},{5,29},{6,30},{7,31},{8,16},{9,... | collective-permute-start | bytes 294920 | tf_op jit(solution)/shard_map/ppermute | solution.py:335
  224.6 9.1 %collective-permute-start.63 = (bf16[32,1536]{1,0:T(8,128)(2,1)S(1)}, bf16[32,1536]{1,0:T(8,128)(2,1)S(1)}, u32[]{:S(2)}, u32[]{:S(2)}) collective-permute-start(bf16[32,1536]{1,0:T(8,128)(2,1)S(1)} %get-tuple-element.328), channel_id=1, source_target_pairs={{0,28},{1,29},{2,30},{3,31},{4,24},{5,25},{6,26},{7,27},{8,20},{9,... | collective-permute-start | bytes 294920 | tf_op jit(solution)/shard_map/ppermute | solution.py:335
  239.0 8.7 %collective-permute-start.65 = (bf16[128,1024]{1,0:T(8,128)(2,1)S(1)}, bf16[128,1024]{1,0:T(8,128)(2,1)S(1)}, u32[]{:S(2)}, u32[]{:S(2)}) collective-permute-start(bf16[128,1024]{1,0:T(8,128)(2,1)S(1)} %get-tuple-element.346), channel_id=1, source_target_pairs={{0,2},{1,3},{2,0},{3,1},{4,6},{5,7},{6,4},{7,5},{8,10},{9,11},{10,... | collective-permute-start | bytes 786440 | tf_op jit(solution)/shard_map/ppermute | solution.py:335
  248.7 5.0 %collective-permute-start.74 = (f32[2,1,256]{2,1,0:T(1,128)S(1)}, f32[2,1,256]{2,1,0:T(1,128)S(1)}, u32[]{:S(2)}, u32[]{:S(2)}) collective-permute-start(f32[2,1,256]{2,1,0:T(1,128)S(1)} %slice.28), channel_id=1, source_target_pairs={{0,2},{1,3},{2,0},{3,1},{4,6},{5,7},{6,4},{7,5},{8,10},{9,11},{10,... | collective-permute-start | bytes 6152 | tf_op jit(solution)/shard_map/ppermute | solution.py:335
  250.2 13.9 %collective-permute-start.67 = (bf16[32,1024]{1,0:T(8,128)(2,1)S(1)}, bf16[32,1024]{1,0:T(8,128)(2,1)S(1)}, u32[]{:S(2)}, u32[]{:S(2)}) collective-permute-start(bf16[32,1024]{1,0:T(8,128)(2,1)S(1)} %get-tuple-element.354), channel_id=1, source_target_pairs={{0,4},{1,5},{2,6},{3,7},{4,0},{5,1},{6,2},{7,3},{8,12},{9,13},{10,... | collective-permute-start | bytes 196616 | tf_op jit(solution)/shard_map/ppermute | solution.py:335
  251.0 14.2 %collective-permute-start.68 = (bf16[32,1024]{1,0:T(8,128)(2,1)S(1)}, bf16[32,1024]{1,0:T(8,128)(2,1)S(1)}, u32[]{:S(2)}, u32[]{:S(2)}) collective-permute-start(bf16[32,1024]{1,0:T(8,128)(2,1)S(1)} %get-tuple-element.355), channel_id=1, source_target_pairs={{0,8},{1,9},{2,10},{3,11},{4,12},{5,13},{6,14},{7,15},{8,0},{9,1},... | collective-permute-start | bytes 196616 | tf_op jit(solution)/shard_map/ppermute | solution.py:335
  253.1 14.3 %collective-permute-start.69 = (bf16[32,1024]{1,0:T(8,128)(2,1)S(1)}, bf16[32,1024]{1,0:T(8,128)(2,1)S(1)}, u32[]{:S(2)}, u32[]{:S(2)}) collective-permute-start(bf16[32,1024]{1,0:T(8,128)(2,1)S(1)} %get-tuple-element.356), channel_id=1, source_target_pairs={{0,12},{1,13},{2,14},{3,15},{4,8},{5,9},{6,10},{7,11},{8,4},{9,5},... | collective-permute-start | bytes 196616 | tf_op jit(solution)/shard_map/ppermute | solution.py:335
  253.6 22.5 %collective-permute-start.76 = (bf16[256,1536]{1,0:T(8,128)(2,1)S(1)}, bf16[256,1536]{1,0:T(8,128)(2,1)S(1)}, u32[]{:S(2)}, u32[]{:S(2)}) collective-permute-start(bf16[256,1536]{1,0:T(8,128)(2,1)S(1)} %leaving_gradient.5), channel_id=1, source_target_pairs={{0,3},{1,2},{2,1},{3,0},{4,7},{5,6},{6,5},{7,4},{8,11},{9,10},{10,... | collective-permute-start | bytes 2359304 | tf_op jit(solution)/shard_map/ppermute | solution.py:335
  253.7 8.1 %collective-permute-start.75 = (f32[1,256]{1,0:T(1,128)S(1)}, f32[1,256]{1,0:T(1,128)S(1)}, u32[]{:S(2)}, u32[]{:S(2)}) collective-permute-start(f32[1,256]{1,0:T(1,128)S(1)} %slice_bitcast_fusion), channel_id=1, source_target_pairs={{0,1},{1,0},{2,3},{3,2},{4,5},{5,4},{6,7},{7,6},{8,9},{9,8},{10,11... | collective-permute-start | bytes 3080 | tf_op jit(solution)/shard_map/ppermute | solution.py:335
  261.7 8.7 %collective-permute-start.70 = (bf16[32,1024]{1,0:T(8,128)(2,1)S(1)}, bf16[32,1024]{1,0:T(8,128)(2,1)S(1)}, u32[]{:S(2)}, u32[]{:S(2)}) collective-permute-start(bf16[32,1024]{1,0:T(8,128)(2,1)S(1)} %get-tuple-element.357), channel_id=1, source_target_pairs={{0,16},{1,17},{2,18},{3,19},{4,20},{5,21},{6,22},{7,23},{8,24},{9,... | collective-permute-start | bytes 196616 | tf_op jit(solution)/shard_map/ppermute | solution.py:335
  264.1 9.6 %collective-permute-start.71 = (bf16[32,1024]{1,0:T(8,128)(2,1)S(1)}, bf16[32,1024]{1,0:T(8,128)(2,1)S(1)}, u32[]{:S(2)}, u32[]{:S(2)}) collective-permute-start(bf16[32,1024]{1,0:T(8,128)(2,1)S(1)} %get-tuple-element.358), channel_id=1, source_target_pairs={{0,20},{1,21},{2,22},{3,23},{4,16},{5,17},{6,18},{7,19},{8,28},{9,... | collective-permute-start | bytes 196616 | tf_op jit(solution)/shard_map/ppermute | solution.py:335
  265.2 8.5 %collective-permute-start.72 = (bf16[32,1024]{1,0:T(8,128)(2,1)S(1)}, bf16[32,1024]{1,0:T(8,128)(2,1)S(1)}, u32[]{:S(2)}, u32[]{:S(2)}) collective-permute-start(bf16[32,1024]{1,0:T(8,128)(2,1)S(1)} %get-tuple-element.359), channel_id=1, source_target_pairs={{0,24},{1,25},{2,26},{3,27},{4,28},{5,29},{6,30},{7,31},{8,16},{9,... | collective-permute-start | bytes 196616 | tf_op jit(solution)/shard_map/ppermute | solution.py:335
  267.5 7.1 %collective-permute-start.73 = (bf16[32,1024]{1,0:T(8,128)(2,1)S(1)}, bf16[32,1024]{1,0:T(8,128)(2,1)S(1)}, u32[]{:S(2)}, u32[]{:S(2)}) collective-permute-start(bf16[32,1024]{1,0:T(8,128)(2,1)S(1)} %get-tuple-element.360), channel_id=1, source_target_pairs={{0,28},{1,29},{2,30},{3,31},{4,24},{5,25},{6,26},{7,27},{8,20},{9,... | collective-permute-start | bytes 196616 | tf_op jit(solution)/shard_map/ppermute | solution.py:335
  (23 other events, 129.4 us)

commit v2 on v1

--- a/solution.py
+++ b/solution.py
@@ -324,7 +324,8 @@
 
 VMEM = pl.BlockSpec(memory_space=pltpu.VMEM)
 SMEM = pl.BlockSpec(memory_space=pltpu.SMEM)
-HBM = pl.BlockSpec(memory_space=pl.ANY)
+HBM = pl.BlockSpec(memory_space=pltpu.HBM)
+STAGED = pl.BlockSpec(memory_space=pltpu.HBM)
 BF16 = jnp.bfloat16
 F32 = jnp.float32
 OWN, FAR, NEAR, ACROSS, SIDE, CORE, POSITION = range(7)
@@ -336,26 +337,75 @@
 
 
 def exchange(blocks):
-    stride = lax.axis_size("fsdp") // POS
-    return [blocks[0]] + [swap(blocks[k], stride * k) for k in range(1, POS)]
+    count = lax.axis_size("fsdp")
+    stride = count // POS
+    if len(blocks) == POS:
+        return [blocks[0]] + [swap(blocks[k], stride * k) for k in range(1, POS)]
+    lanes = [[r + stride * k for k in range(POS)] for r in range(stride)]
+    return [
+        lax.all_to_all(
+            blocks[0], "fsdp", split_axis=0, concat_axis=0, tiled=True, axis_index_groups=lanes
+        )
+    ]
 
 
 def kernel_call(kernel, name, args, outs, scratch=()):
+    flat = lambda items: [p for item in items for p in (item if isinstance(item, list) else [item])]
+    staged = [n for n, (spec, _) in enumerate(flat(args)) if spec is STAGED]
+    arrays = [
+        pltpu.with_memory_space_constraint(a, pltpu.HBM) if spec is STAGED or spec is HBM else a
+        for spec, a in flat(args)
+    ]
+    scratch = list(scratch)
+    own = len(scratch)
+    scratch += [pltpu.VMEM(arrays[n].shape, arrays[n].dtype) for n in staged]
+    scratch += [pltpu.SemaphoreType.DMA((max(len(staged), 1),))]
     held = sum(
         math.prod(ref.shape) * jnp.dtype(ref.dtype).itemsize
         for ref in scratch
         if ref.memory_space == pltpu.VMEM
     )
-    return pl.pallas_call(
-        kernel,
+
+    def grouped(items, values):
+        return [
+            [next(values) for _ in item] if isinstance(item, list) else next(values)
+            for item in items
+        ]
+
+    def body_kernel(*refs):
+        inputs, outputs = list(refs[: len(arrays)]), refs[len(arrays) :]
+        outputs, extra = outputs[: len(flat(outs))], outputs[len(flat(outs)) :]
+        extra, landing, sems = extra[:own], extra[own:-1], extra[-1]
+        copies = []
+        for k, n in enumerate(staged):
+            copies.append(pltpu.make_async_copy(inputs[n], landing[k], sems.at[k]))
+            inputs[n] = landing[k]
+        for copy in copies:
+            copy.start()
+
+        def ready():
+            for copy in copies:
+                copy.wait()
+
+        kernel(ready, *grouped(args, iter(inputs)), *grouped(outs, iter(outputs)), *extra)
+
+    result = pl.pallas_call(
+        body_kernel,
         name=name,
-        in_specs=[spec for spec, _ in args],
-        out_specs=[VMEM] * len(outs),
-        out_shape=[jax.ShapeDtypeStruct(s, d) for s, d in outs],
-        scratch_shapes=list(scratch),
+        in_specs=[spec for spec, _ in flat(args)],
+        out_specs=[VMEM] * len(flat(outs)),
+        out_shape=[jax.ShapeDtypeStruct(s, d) for s, d in flat(outs)],
+        scratch_shapes=scratch,
         cost_estimate=pl.CostEstimate(flops=1, bytes_accessed=1, transcendentals=0),
         compiler_params=pltpu.CompilerParams(vmem_limit_bytes=held + (8 << 20)),
-    )(*[a for _, a in args])
+    )(*arrays)
+    return grouped(outs, iter(result))
+
+
+def views(blocks, place):
+    if len(blocks) == POS:
+        return blocks
+    return [blocks[0].at[place[POSITION] ^ k] for k in range(POS)]
 
 
 def matmul(left, right):
@@ -377,12 +427,18 @@
         ref[rel * frames : (rel + 1) * frames, columns] = value[k * frames : (k + 1) * frames]
 
 
-def block_shapes(rows, width):
+def block_shapes(rows, width, joined):
+    if joined:
+        return [((POS, rows // POS, width), BF16)]
     return [((rows // POS, width), BF16)] * POS
 
 
 def in_vmem(*arrays):
     return [(VMEM, a) for a in arrays]
+
+
+def in_stage(*arrays):
+    return [(STAGED, a) for a in arrays]
 
 
 def place_matrix(size, to_positions, position):
@@ -394,8 +450,10 @@
     return (column == (row % frames) * POS + ((row // frames) ^ position)).astype(F32).astype(BF16)
 
 
-def to_positions_kernel(place, x_rows, c_rows, *blocks):
+def to_positions_kernel(ready, place, x_rows, c_rows, blocks):
+    blocks = views(blocks, place)
     order = place_matrix(x_rows.shape[0], True, place[POSITION])
+    ready()
     for rel, rows in enumerate((x_rows, c_rows)):
         put_rows(blocks, rel, slice(None), matmul(order, rows[...]).astype(BF16))
 
@@ -405,46 +463,51 @@
     return kernel_call(
         to_positions_kernel,
         "to_positions",
-        [(SMEM, place)] + in_vmem(x_rows, c_rows),
-        block_shapes(2 * size, width),
-    )
-
-
-def collect_kernel(*refs):
-    blocks, (x_own, c_own) = refs[:POS], refs[POS:]
+        [(SMEM, place)] + in_stage(x_rows, c_rows),
+        [block_shapes(2 * size, width, True)],
+    )[0]
+
+
+def collect_kernel(ready, place, blocks, x_own, c_own):
+    ready()
+    blocks = views(blocks, place)
     x_own[...] = rows_of(blocks, 0)
     c_own[...] = rows_of(blocks, 1)
 
 
-def collect(blocks):
-    rows, width = blocks[0].shape
-    return kernel_call(
-        collect_kernel, "collect", in_vmem(*blocks), [((rows * POS // 2, width), BF16)] * 2
-    )
-
-
-def to_frames_kernel(place, *refs):
-    blocks, rows = refs[:POS], refs[POS:]
+def collect(place, blocks):
+    rows, width = blocks[0].shape[-2:]
+    return kernel_call(
+        collect_kernel,
+        "collect",
+        [(SMEM, place), in_vmem(*blocks)],
+        [((rows * POS // 2, width), BF16)] * 2,
+    )
+
+
+def to_frames_kernel(ready, place, blocks, *rows):
+    ready()
+    blocks = views(blocks, place)
     order = place_matrix(rows[0].shape[0], False, place[POSITION])
     for rel in range(2):
         rows[rel][...] = matmul(order, rows_of(blocks, rel)).astype(rows[rel].dtype)
 
 
 def to_frames(place, blocks):
-    size = blocks[0].shape[0] * POS // 2
+    size = blocks[0].shape[-2] * POS // 2
     return kernel_call(
         to_frames_kernel,
         "to_frames",
-        [(SMEM, place)] + in_vmem(*blocks),
+        [(SMEM, place), in_vmem(*blocks)],
         [((size, D), F32), ((size, D), BF16)],
     )
 
 
 def first_kernel(
-    place, x_a, x_b, gains_own, gains_far, gains_near, gains_across, w_own, w_far, w_near, w_across,
-    *rest,
+    ready, place, x_a, x_b, gains_own, gains_far, gains_near, gains_across, w_own, w_far, w_near, w_across,
+    qkv, lowered, gains, w, sems,
 ):
-    qkv, (lowered, gains, w, sems) = rest[:POS], rest[POS:]
+    qkv = views(qkv, place)
     half, width = x_a.shape[0], w_own.shape[0]
     part = w.shape[1] // 3
     side = place[SIDE]
@@ -462,6 +525,7 @@
     copies.append(pltpu.make_async_copy(w_across, w.at[at_rows(ACROSS)], sems.at[5]))
     for copy in copies:
         copy.start()
+    ready()
     gains[:, at_rows(OWN)] = gains_own[...].astype(F32)
     gains[:, at_rows(FAR)] = gains_far[...].astype(F32)
     gains[:, at_rows(NEAR)] = gains_near[...].astype(F32)
@@ -492,10 +556,10 @@
     return kernel_call(
         first_kernel,
         "first",
-        [(SMEM, place), (VMEM, x_a), (VMEM, x_b), (VMEM, gains_own), (VMEM, gains_far),
+        [(SMEM, place), (STAGED, x_a), (STAGED, x_b), (VMEM, gains_own), (VMEM, gains_far),
          (VMEM, gains_near), (VMEM, gains_across), (HBM, w_own), (HBM, w_far), (HBM, w_near),
          (HBM, w_across)],
-        block_shapes(2 * half, wide) + [((2 * half, D), BF16), ((2, D), F32)],
+        [block_shapes(2 * half, wide, False), ((2 * half, D), BF16), ((2, D), F32)],
         [pltpu.VMEM((D, wide), BF16), pltpu.SemaphoreType.DMA((6,))],
     )
 
@@ -536,10 +600,11 @@
     return (lane < HEAD_DIM).astype(F32).astype(BF16)
 
 
-def attend_kernel(place, ids_a, ids_b, *refs):
-    qkv, mixed = refs[:POS], refs[POS:]
+def attend_kernel(ready, place, ids_a, ids_b, qkv, mixed):
+    qkv, mixed = views(qkv, place), views(mixed, place)
     part = mixed[0].shape[1]
     low = first_head_lanes()
+    ready()
     for rel, ids in enumerate((ids_a, ids_b)):
         mask = allowed_pairs(ids[...], place[POSITION])
         for base in range(0, part, 2 * HEAD_DIM):
@@ -553,23 +618,24 @@
 
 
 def attend_local(place, ids_a, ids_b, qkv):
-    rows, wide = qkv[0].shape
+    rows, wide = qkv[0].shape[-2:]
     return kernel_call(
         attend_kernel,
         "attend",
-        [(SMEM, place)] + in_vmem(ids_a, ids_b, *qkv),
-        block_shapes(rows * POS, wide // 3),
-    )
-
-
-def attend_back_kernel(place, ids_a, ids_b, *refs):
-    qkv, d_mixed, d_qkv = refs[:POS], refs[POS : 2 * POS], refs[2 * POS :]
+        [(SMEM, place), (STAGED, ids_a), (STAGED, ids_b), in_stage(*qkv)],
+        [block_shapes(rows * POS, wide // 3, True)],
+    )[0]
+
+
+def attend_back_kernel(ready, place, ids_a, ids_b, qkv, d_mixed, d_qkv):
+    qkv, d_mixed, d_qkv = (views(blocks, place) for blocks in (qkv, d_mixed, d_qkv))
     part = d_mixed[0].shape[1]
     pair = 2 * HEAD_DIM
     low = first_head_lanes()
     size = POS * d_mixed[0].shape[0] // 2
     low_full = lax.broadcasted_iota(jnp.int32, (size, pair), 1) < HEAD_DIM
     scale = HEAD_DIM ** (-0.5)
+    ready()
     for rel, ids in enumerate((ids_a, ids_b)):
         mask = allowed_pairs(ids[...], place[POSITION])
         for base in range(0, part, pair):
@@ -594,13 +660,13 @@
 
 
 def attend_back_local(place, ids_a, ids_b, qkv, d_mixed):
-    rows, wide = qkv[0].shape
+    rows, wide = qkv[0].shape[-2:]
     return kernel_call(
         attend_back_kernel,
         "attend_back",
-        [(SMEM, place)] + in_vmem(ids_a, ids_b, *qkv, *d_mixed),
-        block_shapes(rows * POS, wide),
-    )
+        [(SMEM, place), (STAGED, ids_a), (STAGED, ids_b), in_stage(*qkv), in_vmem(*d_mixed)],
+        [block_shapes(rows * POS, wide, False)],
+    )[0]
 
 
 def chip_rows(place, own, near, whole, sems):
@@ -612,11 +678,12 @@
     ]
 
 
-def out_kernel(place, w_own, w_near, *refs):
-    mixed, (term, leaving, mixed_rows, w, sems) = refs[:POS], refs[POS:]
+def out_kernel(ready, place, w_own, w_near, mixed, term, leaving, mixed_rows, w, sems):
+    mixed = views(mixed, place)
     copies = chip_rows(place, w_own, w_near, w, sems)
     for copy in copies:
         copy.start()
+    ready()
     rows = jnp.concatenate([rows_of(mixed, 0), rows_of(mixed, 1)], 0)
     mixed_rows[...] = rows
     half = rows.shape[0] // 2
@@ -631,19 +698,19 @@
 
 
 def out_term(place, mixed, w_own, w_near):
-    rows = POS * mixed[0].shape[0]
+    rows = POS * mixed[0].shape[-2]
     inner = 2 * w_own.shape[0]
     return kernel_call(
         out_kernel,
         "out_term",
-        [(SMEM, place), (HBM, w_own), (HBM, w_near)] + in_vmem(*mixed),
+        [(SMEM, place), (HBM, w_own), (HBM, w_near), in_vmem(*mixed)],
         [((rows, D), F32), ((rows, D), BF16), ((rows, inner), BF16)],
         [pltpu.VMEM((inner, D), BF16), pltpu.SemaphoreType.DMA((2,))],
     )
 
 
 def ffn_kernel(
-    place, x_a, x_b, term, far, gains, c_a, c_b, *rest
+    ready, place, x_a, x_b, term, far, gains, c_a, c_b, *rest
 ):
     pieces, (wd_own, wd_near) = (rest[:4], rest[4:8]), rest[8:10]
     resid, lowered, hidden, d_gate_up, second, leaving = rest[10:16]
@@ -671,6 +738,7 @@
         copy.start()
     lax.fori_loop(0, split, functools.partial(begin, pieces[0], 0), 0)
     lax.fori_loop(split, steps, functools.partial(begin, pieces[1], split), 0)
+    ready()
     gain = gains[1:2, :]
     for rel, (x_ref, c_ref) in enumerate(((x_a, c_a), (x_b, c_b))):
         at = pl.ds(rel * half, half)
@@ -721,7 +789,7 @@
         ffn_kernel,
         "ffn",
         [(SMEM, place)]
-        + [(VMEM, a) for a in (x_a, x_b, term, far, gains, c_a, c_b)]
+        + in_stage(x_a, x_b) + in_vmem(term, far) + in_stage(gains, c_a, c_b)
         + [(HBM, a) for a in pieces + (wd_own, wd_near)],
         [((rows, D), F32), ((rows, D), BF16), ((rows, inner), BF16), ((rows, wide), BF16),
          ((rows, D), F32), ((rows, D), BF16)],
@@ -731,11 +799,12 @@
     )
 
 
-def down_kernel(place, hidden, resid, w_own, w_near, kept, leaving, w, sems):
+def down_kernel(ready, place, hidden, resid, w_own, w_near, kept, leaving, w, sems):
     copies = chip_rows(place, w_own, w_near, w, sems)
     for copy in copies:
         copy.start()
     half = kept.shape[0]
+    ready()
     for copy in copies:
         copy.wait()
 
@@ -754,21 +823,22 @@
     return kernel_call(
         down_kernel,
         "down_term",
-        [(SMEM, place), (VMEM, hidden), (VMEM, resid), (HBM, w_own), (HBM, w_near)],
+        [(SMEM, place), (STAGED, hidden), (VMEM, resid), (HBM, w_own), (HBM, w_near)],
         [((rows // 2, D), F32), ((rows // 2, D), BF16)],
         [pltpu.VMEM((inner, D), BF16), pltpu.SemaphoreType.DMA((2,))],
     )
 
 
 def mid_kernel(
-    place, second, far, resid, gains, c_a, c_b, w_own, w_near,
-    d_resid, d_branch, gain_terms, *rest,
+    ready, place, second, far, resid, gains, c_a, c_b, w_own, w_near,
+    d_resid, d_branch, gain_terms, d_mixed, w, sums, sems,
 ):
-    d_mixed, (w, sums, sems) = rest[:POS], rest[POS:]
+    d_mixed = views(d_mixed, place)
     copies = chip_rows(place, w_own, w_near, w, sems)
     for copy in copies:
         copy.start()
     half, width = c_a.shape[0], w_own.shape[0]
+    ready()
     gain = gains[1:2, :]
     total = None
     for rel, c_ref in enumerate((c_a, c_b)):
@@ -803,17 +873,19 @@
     return kernel_call(
         mid_kernel,
         "mid",
-        [(SMEM, place), (VMEM, second), (VMEM, far), (VMEM, resid), (VMEM, gains),
-         (VMEM, c_a), (VMEM, c_b), (HBM, w_own), (HBM, w_near)],
-        [((rows // 2, D), F32), ((rows, D), BF16), ((2, 1, width), F32)]
-        + block_shapes(rows, 2 * width),
+        [(SMEM, place), (VMEM, second), (VMEM, far), (VMEM, resid), (STAGED, gains),
+         (STAGED, c_a), (STAGED, c_b), (HBM, w_own), (HBM, w_near)],
+        [((rows // 2, D), F32), ((rows, D), BF16), ((2, 1, width), F32),
+         block_shapes(rows, 2 * width, True)],
         [pltpu.VMEM((2 * width, D), BF16), pltpu.VMEM((1, D), F32),
          pltpu.SemaphoreType.DMA((2,))],
     )
 
 
-def back_first_kernel(place, w_own, w_far, w_near, w_across, *refs):
-    d_qkv, (kept, leaving, rows, w, sems) = refs[:POS], refs[POS:]
+def back_first_kernel(
+    ready, place, w_own, w_far, w_near, w_across, d_qkv, kept, leaving, rows, w, sems
+):
+    d_qkv = views(d_qkv, place)
     half, width = kept.shape[0], w_own.shape[0]
     part = w.shape[2] // 3
     side = place[SIDE]
@@ -830,6 +902,7 @@
     copies.append(pltpu.make_async_copy(w_across, w.at[3], sems.at[5]))
     for copy in copies:
         copy.start()
+    ready()
     rows[:half, :] = rows_of(d_qkv, 0)
     rows[half:, :] = rows_of(d_qkv, 1)
     for copy in copies:
@@ -846,21 +919,22 @@
 
 
 def back_first(place, d_qkv, w_own, w_far, w_near, w_across):
-    rows, wide = POS * d_qkv[0].shape[0], d_qkv[0].shape[1]
+    rows, wide = POS * d_qkv[0].shape[-2], d_qkv[0].shape[-1]
     return kernel_call(
         back_first_kernel,
         "back_first",
-        [(SMEM, place), (HBM, w_own), (HBM, w_far), (HBM, w_near), (HBM, w_across)]
-        + in_vmem(*d_qkv),
+        [(SMEM, place), (HBM, w_own), (HBM, w_far), (HBM, w_near), (HBM, w_across),
+         in_vmem(*d_qkv)],
         [((rows // 2, D), F32), ((rows // 2, D), BF16), ((rows, wide), BF16)],
         [pltpu.VMEM((4, w_own.shape[0], wide), BF16), pltpu.SemaphoreType.DMA((6,))],
     )
 
 
 def last_kernel(
-    place, kept, far, x_a, gains, d_resid, down_kept, down_far, *rest
+    ready, place, kept, far, x_a, gains, d_resid, down_kept, down_far, blocks, gain_terms, sums
 ):
-    blocks, (gain_terms, sums) = rest[:POS], rest[POS:]
+    ready()
+    blocks = views(blocks, place)
     width = gain_terms.shape[2]
     rows = x_a[...].astype(F32)
     scale = lax.rsqrt(jnp.mean(rows * rows, axis=-1, keepdims=True) + EPSILON)
@@ -879,12 +953,14 @@
 
 def last(place, kept, far, x_a, gains, d_resid, down_kept, down_far):
     half = kept.shape[0]
-    arrays = (kept, far, x_a, gains, d_resid, down_kept, down_far)
     return kernel_call(
         last_kernel,
         "last",
-        [(SMEM, place)] + [(VMEM, a) for a in arrays],
-        block_shapes(2 * half, D) + [((4, 1, D // 4), F32)],
+        [(SMEM, place)]
+        + in_vmem(kept, far)
+        + in_stage(x_a, gains, d_resid, down_kept)
+        + in_vmem(down_far),
+        [block_shapes(2 * half, D, True), ((4, 1, D // 4), F32)],
         [pltpu.VMEM((1, D), F32)],
     )
 
@@ -893,7 +969,10 @@
     return jnp.concatenate([own[:, columns], near[:, columns]], 0)
 
 
-def leaving_kernel(first_block, place, left_own, left_near, right_own, right_near, leaving):
+def leaving_kernel(
+    first_block, ready, place, left_own, left_near, right_own, right_near, leaving
+):
+    ready()
     width = leaving.shape[0]
     left = both_rows(left_own, left_near, aligned(place[ACROSS] * width, width))
 
@@ -913,13 +992,13 @@
     return kernel_call(
         functools.partial(leaving_kernel, blocks[0]),
         "leaving_gradient",
-        [(SMEM, place), (VMEM, left_own), (VMEM, left_near), (VMEM, right_own),
-         (VMEM, right_near)],
+        [(SMEM, place)] + in_stage(left_own, left_near, right_own, right_near),
         [((width, wide), BF16)],
     )[0]
 
 
-def staying_kernel(parts, place, left_own, left_near, right_own, right_near, *rest):
+def staying_kernel(parts, ready, place, left_own, left_near, right_own, right_near, *rest):
+    ready()
     come, grad = rest[:-1], rest[-1]
     width = grad.shape[0]
     part = grad.shape[1] // 2 // parts
@@ -958,12 +1037,13 @@
     return kernel_call(
         functools.partial(staying_kernel, parts),
         "staying_gradient",
-        [(SMEM, place)] + [(VMEM, a) for a in arrays],
+        [(SMEM, place)] + in_stage(*arrays),
         [((width, 2 * right_own.shape[1]), F32)],
     )[0]
 
 
-def grad_out_kernel(place, mixed_own, mixed_near, d_own, d_near, grad):
+def grad_out_kernel(ready, place, mixed_own, mixed_near, d_own, d_near, grad):
+    ready()
     left = both_rows(
         mixed_own, mixed_near, aligned(place[CORE] * grad.shape[0], grad.shape[0])
     )
@@ -977,12 +1057,13 @@
     return kernel_call(
         grad_out_kernel,
         "grad_out",
-        [(SMEM, place), (VMEM, mixed_own), (VMEM, mixed_near), (VMEM, d_own), (VMEM, d_near)],
+        [(SMEM, place)] + in_stage(mixed_own, mixed_near, d_own, d_near),
         [((width, D), F32)],
     )[0]
 
 
-def grad_down_kernel(place, h_own, h_near, ca_own, cb_own, ca_near, cb_near, grad, wide):
+def grad_down_kernel(ready, place, h_own, h_near, ca_own, cb_own, ca_near, cb_near, grad, wide):
+    ready()
     count, window = grad.shape[0], wide.shape[0]
     core = place[CORE]
     skip = h_own.shape[1] - window
@@ -1006,14 +1087,13 @@
     return kernel_call(
         grad_down_kernel,
         "grad_down",
-        [(SMEM, place)]
-        + [(VMEM, a) for a in (h_own, h_near, ca_own, cb_own, ca_near, cb_near)],
+        [(SMEM, place)] + in_stage(h_own, h_near, ca_own, cb_own, ca_near, cb_near),
         [((count, D), F32)],
         [pltpu.VMEM((window, D), F32)],
     )[0]
 
 
-def half_columns_kernel(parts, far, place, weight, half, sems):
+def half_columns_kernel(parts, far, ready, place, weight, half, sems):
     part = half.shape[1] // parts
     side = 1 - place[SIDE] if far else place[SIDE]
     copies = [
@@ -1041,7 +1121,7 @@
     )[0]
 
 
-def spread_kernel(split, place, weight, kept_a, kept_b, leaving_a, leaving_b, sems):
+def spread_kernel(split, ready, place, weight, kept_a, kept_b, leaving_a, leaving_b, sems):
     part = weight.shape[1] // 4
     side = place[SIDE]
     copies = []
@@ -1092,11 +1172,12 @@
     half = POS * frames
 
     blocks = w_gate_up.shape[1] // 512
-    split = (blocks + 1) // 2
+    split = (blocks * 7) // 11
     near = lambda rows: swap(rows, 1)
 
     qkv_leaving = half_columns(place, w_qkv, 3, True)
     qkv_across = swap(qkv_leaving, 3)
+    qkv_far = near(qkv_across)
     sent = to_positions(place, after(frames_in, qkv_leaving), cotangent)
     came = exchange(sent)
     sent = sent[0]
@@ -1106,29 +1187,27 @@
     gains_own = jnp.stack([gain_attn, gain_ffn])
     gains_far = swap(after(gains_own, sent), 2)
     qkv_kept = half_columns(place, after(w_qkv, sent), 3, False)
-    came, ids_far, gains_far, qkv_kept = sync(came, ids_far, gains_far, qkv_kept)
-
-    x_own, c_own = collect(came)
-    x_far = swap(x_own, 2)
+    came, ids_far, gains_far, qkv_kept, qkv_far = sync(came, ids_far, gains_far, qkv_kept, qkv_far)
+
+    x_own, c_own = collect(place, came)
+    x_far, c_far = swap(x_own, 2), swap(c_own, 2)
     gains_near = near(jnp.stack([gains_own, gains_far]))
     qkv_near = near(qkv_kept)
-    qkv_far = near(qkv_across)
     kept_a, kept_b, leaving_a, leaving_b = spread(place, after(w_gate_up, x_own), split)
-    x_far, qkv_far, gains_near, qkv_near, leaving_a, c_own = sync(
-        x_far, qkv_far, gains_near, qkv_near, leaving_a, c_own
-    )
-
-    *qkv_sent, lowered_first, gains = first(
+    x_far, gains_near, qkv_near, leaving_a, c_own, c_far = sync(
+        x_far, gains_near, qkv_near, leaving_a, c_own, c_far
+    )
+
+    qkv_sent, lowered_first, gains = first(
         place, x_own, x_far, gains_own, gains_far, gains_near[0], gains_near[1],
         w_qkv, qkv_far, qkv_near, qkv_across,
     )
     across_a = swap(after(leaving_a, lowered_first), 3)
-    c_far = swap(after(c_own, lowered_first), 2)
     near_a, near_b, out_near, down_near = (
         near(after(a, lowered_first)) for a in (kept_a, kept_b, w_out, w_down)
     )
-    qkv, c_far, near_a, near_b, out_near, down_near = sync(
-        exchange(qkv_sent), c_far, near_a, near_b, out_near, down_near
+    qkv, across_a, near_a, near_b, out_near, down_near = sync(
+        exchange(qkv_sent), across_a, near_a, near_b, out_near, down_near
     )
 
     mixed_sent = attend_local(place, ids_own, ids_far, qkv)
@@ -1155,23 +1234,21 @@
     )
     down_kept, down_leaving = down_term(place, after(hidden, leaving), resid, w_down, down_near)
     sides = (lowered_second, lowered_second_near, d_gate_up, d_gate_up_near)
-    cut = blocks // 4
+    cut = (blocks * 5) // 11
     gate_up_leaving = leaving_gradient(place, (0, cut), *sides)
     second_far, down_leaving, gate_up_leaving, hidden_near, lowered_second_near = sync(
         second_far, down_leaving, gate_up_leaving, hidden_near, lowered_second_near
     )
 
-    d_resid, d_branch, gain_ffn_terms, *d_mixed = mid(
+    d_resid, d_branch, gain_ffn_terms, d_mixed = mid(
         place, second, second_far, resid, gains, c_own, c_far, w_out, out_near
     )
     gate_up_come = swap(gate_up_leaving, 3)
-    down_far = swap(after(down_leaving, d_branch), 2)
     sides = (after(lowered_second, d_branch), lowered_second_near, d_gate_up, d_gate_up_near)
     gate_up_leaving_rest = leaving_gradient(place, (cut, blocks), *sides)
     d_branch_near, gain_ffn_near = near(d_branch), near(gain_ffn_terms[1])
-    d_mixed, gate_up_come, down_far, gate_up_leaving_rest, d_branch_near, gain_ffn_near = sync(
-        exchange(d_mixed), gate_up_come, down_far, gate_up_leaving_rest, d_branch_near,
-        gain_ffn_near,
+    d_mixed, gate_up_come, gate_up_leaving_rest, d_branch_near, gain_ffn_near = sync(
+        exchange(d_mixed), gate_up_come, gate_up_leaving_rest, d_branch_near, gain_ffn_near,
     )
 
     d_qkv_sent = attend_back_local(place, ids_own, ids_far, qkv, d_mixed)
@@ -1188,12 +1265,13 @@
         place, d_qkv, w_qkv, qkv_far, qkv_near, qkv_across
     )
     first_far = swap(leaving, 2)
+    down_far = swap(after(down_leaving, leaving), 2)
     qkv_sides = (lowered_first, lowered_first_near, d_projected, near(d_projected))
     qkv_grad_leaving = leaving_gradient(place, (0, qkv_leaving.shape[1] // 256), *qkv_sides)
-    first_far, qkv_grad_leaving = sync(first_far, qkv_grad_leaving)
+    first_far, down_far, qkv_grad_leaving = sync(first_far, down_far, qkv_grad_leaving)
 
     qkv_come = swap(qkv_grad_leaving, 3)
-    *out_sent, gain_attn_terms = last(
+    out_sent, gain_attn_terms = last(
         place, kept, first_far, x_own, gains, d_resid, down_kept, down_far
     )
     grad_gate_up = staying_gradient(

time: 281 us -> 249 us (0.89)
  waiting for transfers between devices: 128 us -> 74.3 us
  Pallas kernels: 56.9 us -> 90.4 us
  starting transfers between devices: 88 us -> 70.9 us
  local copies, waits for them, and re-layouts: 4.89 us -> 9.52 us
    ppermute x77 -> x49, waiting for transfers between devices: 128 us -> 62.6 us  [swap(): return lax.ppermute(block, 'fsdp', [(i, i ^ mask) for i in range(count)])]
    ppermute x77 -> x49, starting transfers between devices: 88 us -> 51.7 us  [swap(): return lax.ppermute(block, 'fsdp', [(i, i ^ mask) for i in range(count)])]
    pallas_call x22, Pallas kernels: 56.9 us -> 90.4 us  [kernel_call(): pl.pallas_call(body_kernel, name=name, in_specs=[spec for spec, _ in flat...]
    all_to_all x0 -> x4, starting transfers between devices: none -> 19.2 us  [exchange(): lax.all_to_all(blocks[0], 'fsdp', split_axis=0, concat_axis=0, tiled=True...]
    all_to_all x0 -> x4, waiting for transfers between devices: none -> 11.7 us  [exchange(): lax.all_to_all(blocks[0], 'fsdp', split_axis=0, concat_axis=0, tiled=True...]
    unnamed x20 -> x98, local copies, waits for them, and re-layouts: 2.69 us -> 8.62 us
  transfers between devices with their start and end apart: 77 -> 53, of which waited for: 36 -> 23; matrix products, arithmetic and copies ran while one was open for 1% -> 1% of each run, Pallas kernels for 12% -> 25%
where the time goes in v2:
time: 249 us; the launch traced here: 248 us
  Pallas kernels  90.4 us (36%)
  waiting for transfers between devices  74.3 us (30%)
  starting transfers between devices  70.9 us (28%)
  local copies, waits for them, and re-layouts  9.52 us (4%)
    pallas_call x22, Pallas kernels, kernel_call(): pl.pallas_call(body_kernel, name=name, in_specs=[spec for spec, _ in flat...  90.4 us
    ppermute x49, waiting for transfers between devices, swap(): return lax.ppermute(block, 'fsdp', [(i, i ^ mask) for i in range(count)])  62.6 us
    ppermute x49, starting transfers between devices, swap(): return lax.ppermute(block, 'fsdp', [(i, i ^ mask) for i in range(count)])  51.7 us
    all_to_all x4, starting transfers between devices, exchange(): lax.all_to_all(blocks[0], 'fsdp', split_axis=0, concat_axis=0, tiled=True...  19.2 us
    all_to_all x4, waiting for transfers between devices, exchange(): lax.all_to_all(blocks[0], 'fsdp', split_axis=0, concat_axis=0, tiled=True...  11.7 us
    unnamed x98, local copies, waits for them, and re-layouts  8.62 us
  transfers between devices with their start and end apart: 53, of which 23 were waited for; matrix products, arithmetic and copies ran while one was open for 1% of the time, Pallas kernels for 25%

profile of v2, /device:TPU:0, one launch (start us, length us, event | category | flops | bytes accessed | tf_op | source)
XLA Modules:
  0.0 248.0 jit_solution(40626080225785551)
XLA Ops:
  0.7 1.7 far_columns.1
  2.5 2.5 collective-permute-start.2
  5.0 2.7 %to_positions.1 = bf16[8,32,1024]{2,1,0:T(8,128)(2,1)} custom-call(s32[7]{0:T(128)S(1)} %stack.49.refs_0_, bf16[128,1024]{1,0:T(8,128)(2,1)} %refs_1_.4, bf16[128,1024]{1,0:T(8,128)(2,1)} %refs_2_.1), custom_call_target="tpu_custom_call" | custom-call | flops 1 | bytes 1 | tf_op jit(solution)/shard_map/to_positions/pallas_call | solution.py:392
  7.6 5.8 %all-to-all-start = ((bf16[8,32,1024]{2,1,0:T(8,128)(2,1)}), bf16[8,32,1024]{2,1,0:T(8,128)(2,1)S(1)}, u32[]{:S(2)}, u32[]{:S(2)}) async-start(bf16[8,32,1024]{2,1,0:T(8,128)(2,1)} %to_positions.1), calls=%async_computation | async-start | bytes 1048576 | tf_op jit(solution)/shard_map/all_to_all | solution.py:346
  13.5 9.4 %collective-permute-done.2.refs_10_.refs_4_ = bf16[256,1536]{1,0:T(8,128)(2,1)S(1)} collective-permute-done((bf16[256,1536]{1,0:T(8,128)(2,1)S(1)}, bf16[256,1536]{1,0:T(8,128)(2,1)S(1)}, u32[]{:S(2)}, u32[]{:S(2)}) %collective-permute-start.2) | collective-permute-done | bytes 786464 | tf_op jit(solution)/shard_map/ppermute | solution.py:336
  23.0 2.5 %collective-permute-start.1 = (bf16[2,256]{1,0:T(2,128)(2,1)S(1)}, bf16[2,256]{1,0:T(2,128)(2,1)S(1)}, u32[]{:S(2)}, u32[]{:S(2)}) collective-permute-start(bf16[2,256]{1,0:T(2,128)(2,1)S(1)} %pad_maximum_fusion.1.refs_3_), channel_id=1, source_target_pairs={{0,2},{1,3},{2,0},{3,1},{4,6},{5,7},{6,4},{7,5},{8,10},{9,11},{10,... | collective-permute-start | bytes 3080 | tf_op jit(solution)/shard_map/ppermute | solution.py:336
  26.5 1.7 kept_columns.1
  28.2 1.8 collective-permute-done.refs_2_
  31.1 1.8 collective-permute-start.4
  33.0 3.6 %spread.1 = (bf16[256,1792]{1,0:T(8,128)(2,1)S(1)}, bf16[256,1024]{1,0:T(8,128)(2,1)S(1)}, bf16[256,1792]{1,0:T(8,128)(2,1)S(1)}, bf16[256,1024]{1,0:T(8,128)(2,1)}) custom-call(s32[7]{0:T(128)S(1)} %stack.49.refs_0_, bf16[256,5632]{1,0:T(8,128)(2,1)} %refs_1_.6), custom_call_target="tpu_custom_call" | custom-call | flops 1 | bytes 1 | tf_op jit(solution)/shard_map/spread/pallas_call | solution.py:392
  36.7 3.4 %collective-permute-done.7.refs_7_.refs_6_.refs_4_ = bf16[128,1024]{1,0:T(8,128)(2,1)S(1)} collective-permute-done((bf16[128,1024]{1,0:T(8,128)(2,1)S(1)}, bf16[128,1024]{1,0:T(8,128)(2,1)S(1)}, u32[]{:S(2)}, u32[]{:S(2)}) %collective-permute-start.7) | collective-permute-done | bytes 262176 | tf_op jit(solution)/shard_map/ppermute | solution.py:336
  40.1 5.1 %collective-permute-done.4.refs_2_ = bf16[128,1024]{1,0:T(8,128)(2,1)S(1)} collective-permute-done((bf16[128,1024]{1,0:T(8,128)(2,1)S(1)}, bf16[128,1024]{1,0:T(8,128)(2,1)S(1)}, u32[]{:S(2)}, u32[]{:S(2)}) %collective-permute-start.4) | collective-permute-done | bytes 262176 | tf_op jit(solution)/shard_map/ppermute | solution.py:336
  46.2 4.5 %first.1 = (bf16[32,1536]{1,0:T(8,128)(2,1)S(1)}, bf16[32,1536]{1,0:T(8,128)(2,1)S(1)}, bf16[32,1536]{1,0:T(8,128)(2,1)S(1)}, bf16[32,1536]{1,0:T(8,128)(2,1)S(1...) custom-call(s32[7]{0:T(128)S(1)} %stack.49.refs_0_, ...), custom_call_target="tpu_custom_call" | custom-call | flops 1 | bytes 1 | tf_op jit(solution)/shard_map/first/pallas_call | solution.py:392
  51.4 1.6 collective-permute-start.8
  53.6 1.6 collective-permute-start.9
  55.2 1.4 collective-permute-done.8.refs_4_
  56.6 2.5 %collective-permute-start.10 = (bf16[32,1536]{1,0:T(8,128)(2,1)S(1)}, bf16[32,1536]{1,0:T(8,128)(2,1)S(1)}, u32[]{:S(2)}, u32[]{:S(2)}) collective-permute-start(bf16[32,1536]{1,0:T(8,128)(2,1)S(1)} %get-tuple-element.155), channel_id=1, source_target_pairs={{0,12},{1,13},{2,14},{3,15},{4,8},{5,9},{6,10},{7,11},{8,4},{9,5},... | collective-permute-start | bytes 294920 | tf_op jit(solution)/shard_map/ppermute | solution.py:336
  59.1 2.6 %collective-permute-start.11 = (bf16[32,1536]{1,0:T(8,128)(2,1)S(1)}, bf16[32,1536]{1,0:T(8,128)(2,1)S(1)}, u32[]{:S(2)}, u32[]{:S(2)}) collective-permute-start(bf16[32,1536]{1,0:T(8,128)(2,1)S(1)} %get-tuple-element.156), channel_id=1, source_target_pairs={{0,16},{1,17},{2,18},{3,19},{4,20},{5,21},{6,22},{7,23},{8,24},{9,... | collective-permute-start | bytes 294920 | tf_op jit(solution)/shard_map/ppermute | solution.py:336
  61.7 1.3 collective-permute-done.10.refs_6_
  63.0 3.4 %collective-permute-start.12 = (bf16[32,1536]{1,0:T(8,128)(2,1)S(1)}, bf16[32,1536]{1,0:T(8,128)(2,1)S(1)}, u32[]{:S(2)}, u32[]{:S(2)}) collective-permute-start(bf16[32,1536]{1,0:T(8,128)(2,1)S(1)} %get-tuple-element.157), channel_id=1, source_target_pairs={{0,20},{1,21},{2,22},{3,23},{4,16},{5,17},{6,18},{7,19},{8,28},{9,... | collective-permute-start | bytes 294920 | tf_op jit(solution)/shard_map/ppermute | solution.py:336
  66.4 1.1 collective-permute-done.11.refs_7_
  67.6 3.3 %collective-permute-start.13 = (bf16[32,1536]{1,0:T(8,128)(2,1)S(1)}, bf16[32,1536]{1,0:T(8,128)(2,1)S(1)}, u32[]{:S(2)}, u32[]{:S(2)}) collective-permute-start(bf16[32,1536]{1,0:T(8,128)(2,1)S(1)} %get-tuple-element.158), channel_id=1, source_target_pairs={{0,24},{1,25},{2,26},{3,27},{4,28},{5,29},{6,30},{7,31},{8,16},{9,... | collective-permute-start | bytes 294920 | tf_op jit(solution)/shard_map/ppermute | solution.py:336
  70.9 1.7 collective-permute-done.12.refs_8_
  72.6 4.3 %collective-permute-start.14 = (bf16[32,1536]{1,0:T(8,128)(2,1)S(1)}, bf16[32,1536]{1,0:T(8,128)(2,1)S(1)}, u32[]{:S(2)}, u32[]{:S(2)}) collective-permute-start(bf16[32,1536]{1,0:T(8,128)(2,1)S(1)} %get-tuple-element.159), channel_id=1, source_target_pairs={{0,28},{1,29},{2,30},{3,31},{4,24},{5,25},{6,26},{7,27},{8,20},{9,... | collective-permute-start | bytes 294920 | tf_op jit(solution)/shard_map/ppermute | solution.py:336
  77.0 3.0 %collective-permute-done.14.refs_10_ = bf16[32,1536]{1,0:T(8,128)(2,1)S(1)} collective-permute-done((bf16[32,1536]{1,0:T(8,128)(2,1)S(1)}, bf16[32,1536]{1,0:T(8,128)(2,1)S(1)}, u32[]{:S(2)}, u32[]{:S(2)}) %collective-permute-start.14) | collective-permute-done | bytes 98336 | tf_op jit(solution)/shard_map/ppermute | solution.py:336
  80.0 1.9 collective-permute-done.18.refs_2_.refs_8_
  81.9 1.5 copy-done.17
  83.6 3.8 %attend.1 = bf16[8,32,512]{2,1,0:T(8,128)(2,1)} custom-call(s32[7]{0:T(128)S(1)} %stack.49.refs_0_, s32[1,128]{1,0:T(1,128)} %copy-done.44, s32[1,128]{1,0:T(1,128)} %copy-done.45, bf16[32,1536]{1,0:T(8,128)(2,1)} %copy-done.12, bf16[32,1536]{1,0:T(8,128)(2,1)} %copy-done.35, bf16[32,1536]{1,0:T(8,128)(2,1)} %copy-done.36, bf16[32,1536]{1,0:T(8,128)(2,1)} %copy-done.37, ...), custom_call_target="tpu_custom_call" | custom-call | flops 1 | bytes 1 | tf_op jit(solution)/shard_map/attend/pallas_call | solution.py:392
  87.8 5.5 %all-to-all-start.1 = ((bf16[8,32,512]{2,1,0:T(8,128)(2,1)}), bf16[8,32,512]{2,1,0:T(8,128)(2,1)S(1)}, u32[]{:S(2)}, u32[]{:S(2)}) async-start(bf16[8,32,512]{2,1,0:T(8,128)(2,1)} %attend.1), calls=%async_computation.1 | async-start | bytes 524288 | tf_op jit(solution)/shard_map/all_to_all | solution.py:346
  95.5 7.1 %all-to-all-done.1.refs_3_ = bf16[8,32,512]{2,1,0:T(8,128)(2,1)S(1)} async-done(((bf16[8,32,512]{2,1,0:T(8,128)(2,1)}), bf16[8,32,512]{2,1,0:T(8,128)(2,1)S(1)}, u32[]{:S(2)}, u32[]{:S(2)}) %all-to-all-start.1) | async-done | bytes 262176 | tf_op jit(solution)/shard_map/all_to_all | solution.py:346
  102.7 2.2 out_term.1
  105.0 2.1 collective-permute-start.25
  107.2 1.4 collective-permute-done.26.refs_2_
  108.6 11.0 %collective-permute-done.25.refs_4_ = bf16[256,1024]{1,0:T(8,128)(2,1)S(1)} collective-permute-done((bf16[256,1024]{1,0:T(8,128)(2,1)S(1)}, bf16[256,1024]{1,0:T(8,128)(2,1)S(1)}, u32[]{:S(2)}, u32[]{:S(2)}) %collective-permute-start.25) | collective-permute-done | bytes 524320 | tf_op jit(solution)/shard_map/ppermute | solution.py:336
  119.6 10.7 %ffn.1 = (f32[256,1024]{1,0:T(8,128)S(1)}, bf16[256,1024]{1,0:T(8,128)(2,1)S(1)}, bf16[256,1408]{1,0:T(8,128)(2,1)S(1)}, bf16[256,2816]{1,0:T(8,128)(2,1)S(1)}, ...) custom-call(s32[7]{0:T(128)S(1)} %stack.49.refs_0_, bf16[128,1024]{1,0:T(8,128)(2,1)} %copy-done.5, ...), custom_call_target="tpu_custom_call" | custom-call | flops 1 | bytes 1 | tf_op jit(solution)/shard_map/ffn/pallas_call | solution.py:392
  131.0 1.8 collective-permute-start.28
  132.7 4.2 %down_term.1 = (f32[128,1024]{1,0:T(8,128)S(1)}, bf16[128,1024]{1,0:T(8,128)(2,1)S(1)}) custom-call(s32[7]{0:T(128)S(1)} %stack.49.refs_0_, bf16[256,1408]{1,0:T(8,128)(2,1)} %copy-done.3, f32[256,1024]{1,0:T(8,128)S(1)} %get-tuple-element.203.refs_2_.refs_3_, bf16[704,1024]{1,0:T(8,128)(2,1)} %refs_3_.1, bf16[704,1024]{1,0:T(8,128)(2,1)} %copy-done.17), custom_call_target="tpu_custom_call" | custom-call | flops 1 | bytes 1 | tf_op jit(solution)/shard_map/down_term/pallas_call | solution.py:392
  139.7 4.1 %leaving_gradient.3 = bf16[256,1280]{1,0:T(8,128)(2,1)S(1)} custom-call(s32[7]{0:T(128)S(1)} %stack.49.refs_0_, bf16[256,1024]{1,0:T(8,128)(2,1)} %copy-done.1, bf16[256,1024]{1,0:T(8,128)(2,1)} %copy-done.18, bf16[256,2816]{1,0:T(8,128)(2,1)} %copy-done, bf16[256,2816]{1,0:T(8,128)(2,1)} %copy-done.15), custom_call_target="tpu_custom_call" | custom-call | flops 1 | bytes 1 | tf_op jit(solution)/shard_map/leaving_gradient/pallas_call | solution.py:392
  143.8 1.4 collective-permute-done.28.refs_2_
  146.2 3.4 %mid.1 = (f32[128,1024]{1,0:T(8,128)S(1)}, bf16[256,1024]{1,0:T(8,128)(2,1)S(1)}, f32[2,1,256]{2,1,0:T(1,128)S(1)}, bf16[8,32,512]{2,1,0:T(8,128)(2,1)}) custom-call(s32[7]{0:T(128)S(1)} %stack.49.refs_0_, f32[256,1024]{1,0:T(8,128)S(1)} %get-tuple-element.199.refs_1_, bf16[256,1024]{1,0:T(8,128)(2,1)S(1)} %collective-permute-done.28.refs_2_, ...), custom_call_target="tpu_custom_call" | custom-call | flops 1 | bytes 1 | tf_op jit(solution)/shard_map/mid/pallas_call | solution.py:392
  151.4 3.6 %all-to-all-start.2 = ((bf16[8,32,512]{2,1,0:T(8,128)(2,1)}), bf16[8,32,512]{2,1,0:T(8,128)(2,1)S(1)}, u32[]{:S(2)}, u32[]{:S(2)}) async-start(bf16[8,32,512]{2,1,0:T(8,128)(2,1)} %get-tuple-element.210), calls=%async_computation.2 | async-start | bytes 524288 | tf_op jit(solution)/shard_map/all_to_all | solution.py:346
  155.0 4.4 %leaving_gradient.4 = bf16[256,1536]{1,0:T(8,128)(2,1)S(1)} custom-call(s32[7]{0:T(128)S(1)} %stack.49.refs_0_, bf16[256,1024]{1,0:T(8,128)(2,1)} %copy-done.1, bf16[256,1024]{1,0:T(8,128)(2,1)} %copy-done.18, bf16[256,2816]{1,0:T(8,128)(2,1)} %copy-done, bf16[256,2816]{1,0:T(8,128)(2,1)} %copy-done.15), custom_call_target="tpu_custom_call" | custom-call | flops 1 | bytes 1 | tf_op jit(solution)/shard_map/leaving_gradient/pallas_call | solution.py:392
  159.5 4.6 %all-to-all-done.2.refs_11_ = bf16[8,32,512]{2,1,0:T(8,128)(2,1)S(1)} async-done(((bf16[8,32,512]{2,1,0:T(8,128)(2,1)}), bf16[8,32,512]{2,1,0:T(8,128)(2,1)S(1)}, u32[]{:S(2)}, u32[]{:S(2)}) %all-to-all-start.2) | async-done | bytes 262176 | tf_op jit(solution)/shard_map/all_to_all | solution.py:346
  164.1 5.9 %attend_back.1 = (bf16[32,1536]{1,0:T(8,128)(2,1)S(1)}, bf16[32,1536]{1,0:T(8,128)(2,1)S(1)}, bf16[32,1536]{1,0:T(8,128)(2,1)S(1)}, bf16[32,1536]{1,0:T(8,128)(2...) custom-call(s32[7]{0:T(128)S(1)} %stack.49.refs_0_, ...), custom_call_target="tpu_custom_call" | custom-call | flops 1 | bytes 1 | tf_op jit(solution)/shard_map/attend_back/pallas_call | solution.py:392
  170.0 1.5 collective-permute-start.35
  171.5 2.0 collective-permute-start.37
  173.6 1.1 collective-permute-start.38
  175.4 2.0 collective-permute-start.39
  177.3 3.7 %collective-permute-start.40 = (bf16[32,1536]{1,0:T(8,128)(2,1)S(1)}, bf16[32,1536]{1,0:T(8,128)(2,1)S(1)}, u32[]{:S(2)}, u32[]{:S(2)}) collective-permute-start(bf16[32,1536]{1,0:T(8,128)(2,1)S(1)} %get-tuple-element.223), channel_id=1, source_target_pairs={{0,24},{1,25},{2,26},{3,27},{4,28},{5,29},{6,30},{7,31},{8,16},{9,... | collective-permute-start | bytes 294920 | tf_op jit(solution)/shard_map/ppermute | solution.py:336
  181.0 2.9 %collective-permute-start.41 = (bf16[32,1536]{1,0:T(8,128)(2,1)S(1)}, bf16[32,1536]{1,0:T(8,128)(2,1)S(1)}, u32[]{:S(2)}, u32[]{:S(2)}) collective-permute-start(bf16[32,1536]{1,0:T(8,128)(2,1)S(1)} %get-tuple-element.224), channel_id=1, source_target_pairs={{0,28},{1,29},{2,30},{3,31},{4,24},{5,25},{6,26},{7,27},{8,20},{9,... | collective-permute-start | bytes 294920 | tf_op jit(solution)/shard_map/ppermute | solution.py:336
  183.9 3.4 %grad_out.1 = f32[256,1024]{1,0:T(8,128)} custom-call(s32[7]{0:T(128)S(1)} %stack.49.refs_0_, bf16[256,512]{1,0:T(8,128)(2,1)} %copy-done.13, bf16[256,512]{1,0:T(8,128)(2,1)} %copy-done.43, bf16[256,1024]{1,0:T(8,128)(2,1)} %copy-done.11, bf16[256,1024]{1,0:T(8,128)(2,1)} %collective-permute-done.33.refs_4_), custom_call_target="tpu_custom_call" | custom-call | flops 1 | bytes 1 | tf_op jit(solution)/shard_map/grad_out/pallas_call | solution.py:392
  187.3 5.7 %grad_down.1 = f32[704,1024]{1,0:T(8,128)} custom-call(s32[7]{0:T(128)S(1)} %stack.49.refs_0_, bf16[256,1408]{1,0:T(8,128)(2,1)} %copy-done.3, bf16[256,1408]{1,0:T(8,128)(2,1)} %copy-done.31, bf16[128,1024]{1,0:T(8,128)(2,1)} %copy-done.4, bf16[128,1024]{1,0:T(8,128)(2,1)} %copy-done.23, bf16[128,1024]{1,0:T(8,128)(2,1)} %copy-done.42, ...), custom_call_target="tpu_custom_call" | custom-call | flops 1 | bytes 1 | tf_op jit(solution)/shard_map/grad_down/pallas_call | solution.py:392
  193.0 4.1 %back_first.1 = (f32[128,1024]{1,0:T(8,128)S(1)}, bf16[128,1024]{1,0:T(8,128)(2,1)S(1)}, bf16[256,1536]{1,0:T(8,128)(2,1)S(1)}) custom-call(s32[7]{0:T(128)S(1)} %stack.49.refs_0_, bf16[256,3072]{1,0:T(8,128)(2,1)} %refs_1_.8, bf16[256,1536]{1,0:T(8,128)(2,1)} %copy-done.20, bf16[256,1536]{1,0:T(8,128)(2,1)} %copy-done.21, bf16[256,1536]{1,0:T(8,128)(2,1)} %copy-done.19, ...), custom_call_target="tpu_custom_call" | custom-call | flops 1 | bytes 1 | tf_op jit(solution)/shard_map/back_first/pallas_call | solution.py:392
  198.0 1.3 collective-permute-start.43
  200.4 3.9 %leaving_gradient.5 = bf16[256,1536]{1,0:T(8,128)(2,1)S(1)} custom-call(s32[7]{0:T(128)S(1)} %stack.49.refs_0_, bf16[256,1024]{1,0:T(8,128)(2,1)} %copy-done.6, bf16[256,1024]{1,0:T(8,128)(2,1)} %copy-done.26, bf16[256,1536]{1,0:T(8,128)(2,1)} %copy-done.2, bf16[256,1536]{1,0:T(8,128)(2,1)} %copy-done.22), custom_call_target="tpu_custom_call" | custom-call | flops 1 | bytes 1 | tf_op jit(solution)/shard_map/leaving_gradient/pallas_call | solution.py:392
  204.3 2.1 collective-permute-done.44.refs_7_
  206.5 5.1 %collective-permute-done.43.refs_2_ = bf16[128,1024]{1,0:T(8,128)(2,1)S(1)} collective-permute-done((bf16[128,1024]{1,0:T(8,128)(2,1)S(1)}, bf16[128,1024]{1,0:T(8,128)(2,1)S(1)}, u32[]{:S(2)}, u32[]{:S(2)}) %collective-permute-start.43) | collective-permute-done | bytes 262176 | tf_op jit(solution)/shard_map/ppermute | solution.py:336
  211.5 3.0 %last.1 = (bf16[8,32,1024]{2,1,0:T(8,128)(2,1)}, f32[4,1,256]{2,1,0:T(1,128)S(1)}) custom-call(s32[7]{0:T(128)S(1)} %stack.49.refs_0_, f32[128,1024]{1,0:T(8,128)S(1)} %get-tuple-element.241.refs_1_, bf16[128,1024]{1,0:T(8,128)(2,1)S(1)} %collective-permute-done.43.refs_2_, bf16[128,1024]{1,0:T(8,128)(2,1)} %copy-done.5, f32[2,1024]{1,0:T(2,128)} %copy-done.14, ...), custom_call_target="tpu_custom_call" | custom-call | flops 1 | bytes 1 | tf_op jit(solution)/shard_map/last/pallas_call | solution.py:392
  214.6 4.2 %all-to-all-start.3 = ((bf16[8,32,1024]{2,1,0:T(8,128)(2,1)}), bf16[8,32,1024]{2,1,0:T(8,128)(2,1)S(1)}, u32[]{:S(2)}, u32[]{:S(2)}) async-start(bf16[8,32,1024]{2,1,0:T(8,128)(2,1)} %get-tuple-element.251), calls=%async_computation.3 | async-start | bytes 1048576 | tf_op jit(solution)/shard_map/all_to_all | solution.py:346
  219.9 2.5 %collective-permute-done.46 = f32[2,1,256]{2,1,0:T(1,128)S(1)} collective-permute-done((f32[2,1,256]{2,1,0:T(1,128)S(1)}, f32[2,1,256]{2,1,0:T(1,128)S(1)}, u32[]{:S(2)}, u32[]{:S(2)}) %collective-permute-start.46) | collective-permute-done | bytes 2080 | tf_op jit(solution)/shard_map/ppermute | solution.py:336
  223.0 9.2 %staying_gradient.2 = f32[256,5632]{1,0:T(8,128)} custom-call(s32[7]{0:T(128)S(1)} %stack.49.refs_0_, bf16[256,1024]{1,0:T(8,128)(2,1)} %copy-done.1, bf16[256,1024]{1,0:T(8,128)(2,1)} %copy-done.18, bf16[256,2816]{1,0:T(8,128)(2,1)} %copy-done, bf16[256,2816]{1,0:T(8,128)(2,1)} %copy-done.15, bf16[256,1280]{1,0:T(8,128)(2,1)} %collective-permute-done.32.refs_5_, ...), custom_call_target="tpu_custom_call" | custom-call | flops 1 | bytes 1 | tf_op jit(solution)/shard_map/staying_gradient/pallas_call | solution.py:392
  232.8 6.5 %collective-permute-done.48.refs_5_ = bf16[256,1536]{1,0:T(8,128)(2,1)S(1)} collective-permute-done((bf16[256,1536]{1,0:T(8,128)(2,1)S(1)}, bf16[256,1536]{1,0:T(8,128)(2,1)S(1)}, u32[]{:S(2)}, u32[]{:S(2)}) %collective-permute-start.48) | collective-permute-done | bytes 786464 | tf_op jit(solution)/shard_map/ppermute | solution.py:336
  240.2 6.0 %staying_gradient.3 = f32[256,3072]{1,0:T(8,128)} custom-call(s32[7]{0:T(128)S(1)} %stack.49.refs_0_, bf16[256,1024]{1,0:T(8,128)(2,1)} %copy-done.6, bf16[256,1024]{1,0:T(8,128)(2,1)} %copy-done.26, bf16[256,1536]{1,0:T(8,128)(2,1)} %copy-done.2, bf16[256,1536]{1,0:T(8,128)(2,1)} %copy-done.22, bf16[256,1536]{1,0:T(8,128)(2,1)} %copy-done.30), custom_call_target="tpu_custom_call" | custom-call | flops 1 | bytes 1 | tf_op jit(solution)/shard_map/staying_gradient/pallas_call | solution.py:392
  246.2 1.6 to_frames.1
  (183 shorter events, 19.6 us)
Async XLA Ops:
  2.5 23.1 %copy-start.46 = (s32[128]{0:T(128)S(1)}, s32[128]{0:T(128)}, u32[]{:S(2)}) copy-start(s32[128]{0:T(128)} %param.10) | copy-start | bytes 1540
  2.5 20.4 %collective-permute-start.2 = (bf16[256,1536]{1,0:T(8,128)(2,1)S(1)}, bf16[256,1536]{1,0:T(8,128)(2,1)S(1)}, u32[]{:S(2)}, u32[]{:S(2)}) collective-permute-start(bf16[256,1536]{1,0:T(8,128)(2,1)S(1)} %far_columns.1), channel_id=1, source_target_pairs={{0,3},{1,2},{2,1},{3,0},{4,7},{5,6},{6,5},{7,4},{8,11},{9,10},{10,... | collective-permute-start | bytes 2359304 | tf_op jit(solution)/shard_map/ppermute | solution.py:336
  7.6 22.5 %all-to-all-start = ((bf16[8,32,1024]{2,1,0:T(8,128)(2,1)}), bf16[8,32,1024]{2,1,0:T(8,128)(2,1)S(1)}, u32[]{:S(2)}, u32[]{:S(2)}) async-start(bf16[8,32,1024]{2,1,0:T(8,128)(2,1)} %to_positions.1), calls=%async_computation | async-start | bytes 1048576 | tf_op jit(solution)/shard_map/all_to_all | solution.py:346
  22.9 7.2 %collective-permute-start.3 = (bf16[256,1536]{1,0:T(8,128)(2,1)S(1)}, bf16[256,1536]{1,0:T(8,128)(2,1)S(1)}, u32[]{:S(2)}, u32[]{:S(2)}) collective-permute-start(bf16[256,1536]{1,0:T(8,128)(2,1)S(1)} %collective-permute-done.2.refs_10_.refs_4_), channel_id=1, source_target_pairs={{0,1},{1,0},{2,3},{3,2},{4,5},{5,4},{6,7},{7,6},{8,9},{9,8},{10,11... | collective-permute-start | bytes 2359304 | tf_op jit(solution)/shard_map/ppermute | solution.py:336
  23.0 7.1 %collective-permute-start.1 = (bf16[2,256]{1,0:T(2,128)(2,1)S(1)}, bf16[2,256]{1,0:T(2,128)(2,1)S(1)}, u32[]{:S(2)}, u32[]{:S(2)}) collective-permute-start(bf16[2,256]{1,0:T(2,128)(2,1)S(1)} %pad_maximum_fusion.1.refs_3_), channel_id=1, source_target_pairs={{0,2},{1,3},{2,0},{3,1},{4,6},{5,7},{6,4},{7,5},{8,10},{9,11},{10,... | collective-permute-start | bytes 3080 | tf_op jit(solution)/shard_map/ppermute | solution.py:336
  26.5 3.6 %collective-permute-start = (s32[1,128]{1,0:T(1,128)S(1)}, s32[1,128]{1,0:T(1,128)S(1)}, u32[]{:S(2)}, u32[]{:S(2)}) collective-permute-start(s32[1,128]{1,0:T(1,128)S(1)} %select_n.46.refs_1_), channel_id=1, source_target_pairs={{0,2},{1,3},{2,0},{3,1},{4,6},{5,7},{6,4},{7,5},{8,10},{9,11},{10,... | collective-permute-start | bytes 1544 | tf_op jit(solution)/shard_map/ppermute | solution.py:336
  30.1 15.1 %collective-permute-start.6 = (bf16[256,1536]{1,0:T(8,128)(2,1)S(1)}, bf16[256,1536]{1,0:T(8,128)(2,1)S(1)}, u32[]{:S(2)}, u32[]{:S(2)}) collective-permute-start(bf16[256,1536]{1,0:T(8,128)(2,1)S(1)} %kept_columns.1), channel_id=1, source_target_pairs={{0,1},{1,0},{2,3},{3,2},{4,5},{5,4},{6,7},{7,6},{8,9},{9,8},{10,11... | collective-permute-start | bytes 2359304 | tf_op jit(solution)/shard_map/ppermute | solution.py:336
  30.8 62.6 %copy-start.4 = (bf16[128,1024]{1,0:T(8,128)(2,1)}, bf16[128,1024]{1,0:T(8,128)(2,1)S(1)}, u32[]{:S(2)}) copy-start(bf16[128,1024]{1,0:T(8,128)(2,1)S(1)} %get-tuple-element.182.refs_6_.refs_5_.refs_3_) | copy-start | bytes 786436
  30.8 9.2 %collective-permute-start.7 = (bf16[128,1024]{1,0:T(8,128)(2,1)S(1)}, bf16[128,1024]{1,0:T(8,128)(2,1)S(1)}, u32[]{:S(2)}, u32[]{:S(2)}) collective-permute-start(bf16[128,1024]{1,0:T(8,128)(2,1)S(1)} %get-tuple-element.182.refs_6_.refs_5_.refs_3_), channel_id=1, source_target_pairs={{0,2},{1,3},{2,0},{3,1},{4,6},{5,7},{6,4},{7,5},{8,10},{9,11},{10,... | collective-permute-start | bytes 786440 | tf_op jit(solution)/shard_map/ppermute | solution.py:336
  31.1 14.1 %collective-permute-start.4 = (bf16[128,1024]{1,0:T(8,128)(2,1)S(1)}, bf16[128,1024]{1,0:T(8,128)(2,1)S(1)}, u32[]{:S(2)}, u32[]{:S(2)}) collective-permute-start(bf16[128,1024]{1,0:T(8,128)(2,1)S(1)} %get-tuple-element.142.refs_1_.refs_3_), channel_id=1, source_target_pairs={{0,2},{1,3},{2,0},{3,1},{4,6},{5,7},{6,4},{7,5},{8,10},{9,11},{10,... | collective-permute-start | bytes 786440 | tf_op jit(solution)/shard_map/ppermute | solution.py:336
  32.9 3.8 %collective-permute-start.5 = (bf16[2,2,256]{2,1,0:T(2,128)(2,1)S(1)}, bf16[2,2,256]{2,1,0:T(2,128)(2,1)S(1)}, u32[]{:S(2)}, u32[]{:S(2)}) collective-permute-start(bf16[2,2,256]{2,1,0:T(2,128)(2,1)S(1)} %pad_maximum_fusion), channel_id=1, source_target_pairs={{0,1},{1,0},{2,3},{3,2},{4,5},{5,4},{6,7},{7,6},{8,9},{9,8},{10,11... | collective-permute-start | bytes 6152 | tf_op jit(solution)/shard_map/ppermute | solution.py:336
  36.7 40.2 %copy-start.8 = (bf16[256,1024]{1,0:T(8,128)(2,1)}, bf16[256,1024]{1,0:T(8,128)(2,1)S(1)}, u32[]{:S(2)}) copy-start(bf16[256,1024]{1,0:T(8,128)(2,1)S(1)} %get-tuple-element.166.refs_12_) | copy-start | bytes 1572868
  40.1 79.5 %copy-start.23 = (bf16[128,1024]{1,0:T(8,128)(2,1)}, bf16[128,1024]{1,0:T(8,128)(2,1)S(1)}, u32[]{:S(2)}) copy-start(bf16[128,1024]{1,0:T(8,128)(2,1)S(1)} %collective-permute-done.7.refs_7_.refs_6_.refs_4_) | copy-start | bytes 786436
  46.2 33.7 %copy-start.24 = (bf16[256,1024]{1,0:T(8,128)(2,1)S(1)}, bf16[256,1024]{1,0:T(8,128)(2,1)}, u32[]{:S(2)}) copy-start(bf16[256,1024]{1,0:T(8,128)(2,1)} %refs_7_.3) | copy-start | bytes 1572868
  51.3 68.2 %copy-start.6 = (bf16[256,1024]{1,0:T(8,128)(2,1)}, bf16[256,1024]{1,0:T(8,128)(2,1)S(1)}, u32[]{:S(2)}) copy-start(bf16[256,1024]{1,0:T(8,128)(2,1)S(1)} %get-tuple-element.185.refs_1_) | copy-start | bytes 1572868
  51.3 68.2 %copy-start.14 = (f32[2,1024]{1,0:T(2,128)}, f32[2,1024]{1,0:T(2,128)S(1)}, u32[]{:S(2)}) copy-start(f32[2,1024]{1,0:T(2,128)S(1)} %get-tuple-element.193.refs_5_.refs_4_) | copy-start | bytes 24580
  51.4 30.5 %collective-permute-start.19 = (bf16[704,1024]{1,0:T(8,128)(2,1)S(1)}, bf16[704,1024]{1,0:T(8,128)(2,1)S(1)}, u32[]{:S(2)}, u32[]{:S(2)}) collective-permute-start(bf16[704,1024]{1,0:T(8,128)(2,1)S(1)} %copy-done.16), channel_id=1, source_target_pairs={{0,1},{1,0},{2,3},{3,2},{4,5},{5,4},{6,7},{7,6},{8,9},{9,8},{10,11... | collective-permute-start | bytes 4325384 | tf_op jit(solution)/shard_map/ppermute | solution.py:336
  51.4 5.2 %collective-permute-start.8 = (bf16[32,1536]{1,0:T(8,128)(2,1)S(1)}, bf16[32,1536]{1,0:T(8,128)(2,1)S(1)}, u32[]{:S(2)}, u32[]{:S(2)}) collective-permute-start(bf16[32,1536]{1,0:T(8,128)(2,1)S(1)} %get-tuple-element.153), channel_id=1, source_target_pairs={{0,4},{1,5},{2,6},{3,7},{4,0},{5,1},{6,2},{7,3},{8,12},{9,13},{10,... | collective-permute-start | bytes 294920 | tf_op jit(solution)/shard_map/ppermute | solution.py:336
  53.0 28.9 %collective-permute-start.15 = (bf16[256,1792]{1,0:T(8,128)(2,1)S(1)}, bf16[256,1792]{1,0:T(8,128)(2,1)}, u32[]{:S(2)}, u32[]{:S(2)}) collective-permute-start(bf16[256,1792]{1,0:T(8,128)(2,1)S(1)} %get-tuple-element.162), channel_id=1, source_target_pairs={{0,3},{1,2},{2,1},{3,0},{4,7},{5,6},{6,5},{7,4},{8,11},{9,10},{10,... | collective-permute-start | bytes 2752520 | tf_op jit(solution)/shard_map/ppermute | solution.py:336
  53.3 28.6 %collective-permute-start.16 = (bf16[256,1792]{1,0:T(8,128)(2,1)S(1)}, bf16[256,1792]{1,0:T(8,128)(2,1)S(1)}, u32[]{:S(2)}, u32[]{:S(2)}) collective-permute-start(bf16[256,1792]{1,0:T(8,128)(2,1)S(1)} %get-tuple-element.164.refs_8_), channel_id=1, source_target_pairs={{0,1},{1,0},{2,3},{3,2},{4,5},{5,4},{6,7},{7,6},{8,9},{9,8},{10,11... | collective-permute-start | bytes 2752520 | tf_op jit(solution)/shard_map/ppermute | solution.py:336
  53.6 5.5 %collective-permute-start.9 = (bf16[32,1536]{1,0:T(8,128)(2,1)S(1)}, bf16[32,1536]{1,0:T(8,128)(2,1)S(1)}, u32[]{:S(2)}, u32[]{:S(2)}) collective-permute-start(bf16[32,1536]{1,0:T(8,128)(2,1)S(1)} %get-tuple-element.154), channel_id=1, source_target_pairs={{0,8},{1,9},{2,10},{3,11},{4,12},{5,13},{6,14},{7,15},{8,0},{9,1},... | collective-permute-start | bytes 294920 | tf_op jit(solution)/shard_map/ppermute | solution.py:336
  56.6 27.0 %copy-start.35 = (bf16[32,1536]{1,0:T(8,128)(2,1)}, bf16[32,1536]{1,0:T(8,128)(2,1)S(1)}, u32[]{:S(2)}) copy-start(bf16[32,1536]{1,0:T(8,128)(2,1)S(1)} %collective-permute-done.8.refs_4_) | copy-start | bytes 294916
  56.6 6.5 %collective-permute-start.10 = (bf16[32,1536]{1,0:T(8,128)(2,1)S(1)}, bf16[32,1536]{1,0:T(8,128)(2,1)S(1)}, u32[]{:S(2)}, u32[]{:S(2)}) collective-permute-start(bf16[32,1536]{1,0:T(8,128)(2,1)S(1)} %get-tuple-element.155), channel_id=1, source_target_pairs={{0,12},{1,13},{2,14},{3,15},{4,8},{5,9},{6,10},{7,11},{8,4},{9,5},... | collective-permute-start | bytes 294920 | tf_op jit(solution)/shard_map/ppermute | solution.py:336
  59.1 24.5 %copy-start.36 = (bf16[32,1536]{1,0:T(8,128)(2,1)}, bf16[32,1536]{1,0:T(8,128)(2,1)S(1)}, u32[]{:S(2)}) copy-start(bf16[32,1536]{1,0:T(8,128)(2,1)S(1)} %collective-permute-done.9.refs_5_) | copy-start | bytes 294916
  59.1 8.4 %collective-permute-start.11 = (bf16[32,1536]{1,0:T(8,128)(2,1)S(1)}, bf16[32,1536]{1,0:T(8,128)(2,1)S(1)}, u32[]{:S(2)}, u32[]{:S(2)}) collective-permute-start(bf16[32,1536]{1,0:T(8,128)(2,1)S(1)} %get-tuple-element.156), channel_id=1, source_target_pairs={{0,16},{1,17},{2,18},{3,19},{4,20},{5,21},{6,22},{7,23},{8,24},{9,... | collective-permute-start | bytes 294920 | tf_op jit(solution)/shard_map/ppermute | solution.py:336
  63.0 9.6 %collective-permute-start.12 = (bf16[32,1536]{1,0:T(8,128)(2,1)S(1)}, bf16[32,1536]{1,0:T(8,128)(2,1)S(1)}, u32[]{:S(2)}, u32[]{:S(2)}) collective-permute-start(bf16[32,1536]{1,0:T(8,128)(2,1)S(1)} %get-tuple-element.157), channel_id=1, source_target_pairs={{0,20},{1,21},{2,22},{3,23},{4,16},{5,17},{6,18},{7,19},{8,28},{9,... | collective-permute-start | bytes 294920 | tf_op jit(solution)/shard_map/ppermute | solution.py:336
  67.6 9.3 %collective-permute-start.13 = (bf16[32,1536]{1,0:T(8,128)(2,1)S(1)}, bf16[32,1536]{1,0:T(8,128)(2,1)S(1)}, u32[]{:S(2)}, u32[]{:S(2)}) collective-permute-start(bf16[32,1536]{1,0:T(8,128)(2,1)S(1)} %get-tuple-element.158), channel_id=1, source_target_pairs={{0,24},{1,25},{2,26},{3,27},{4,28},{5,29},{6,30},{7,31},{8,16},{9,... | collective-permute-start | bytes 294920 | tf_op jit(solution)/shard_map/ppermute | solution.py:336
  72.6 7.3 %collective-permute-start.14 = (bf16[32,1536]{1,0:T(8,128)(2,1)S(1)}, bf16[32,1536]{1,0:T(8,128)(2,1)S(1)}, u32[]{:S(2)}, u32[]{:S(2)}) collective-permute-start(bf16[32,1536]{1,0:T(8,128)(2,1)S(1)} %get-tuple-element.159), channel_id=1, source_target_pairs={{0,28},{1,29},{2,30},{3,31},{4,24},{5,25},{6,26},{7,27},{8,20},{9,... | collective-permute-start | bytes 294920 | tf_op jit(solution)/shard_map/ppermute | solution.py:336
  76.9 3.0 %collective-permute-start.17 = (bf16[256,1024]{1,0:T(8,128)(2,1)S(1)}, bf16[256,1024]{1,0:T(8,128)(2,1)S(1)}, u32[]{:S(2)}, u32[]{:S(2)}) collective-permute-start(bf16[256,1024]{1,0:T(8,128)(2,1)S(1)} %get-tuple-element.166.refs_12_), channel_id=1, source_target_pairs={{0,1},{1,0},{2,3},{3,2},{4,5},{5,4},{6,7},{7,6},{8,9},{9,8},{10,11... | collective-permute-start | bytes 1572872 | tf_op jit(solution)/shard_map/ppermute | solution.py:336
  79.9 1.9 collective-permute-start.18
  83.4 19.2 %collective-permute-start.21 = (bf16[256,1792]{1,0:T(8,128)(2,1)}, bf16[256,1792]{1,0:T(8,128)(2,1)}, u32[]{:S(2)}, u32[]{:S(2)}) collective-permute-start(bf16[256,1792]{1,0:T(8,128)(2,1)} %collective-permute-done.15.refs_11_), channel_id=1, source_target_pairs={{0,1},{1,0},{2,3},{3,2},{4,5},{5,4},{6,7},{7,6},{8,9},{9,8},{10,11... | collective-permute-start | bytes 2752520 | tf_op jit(solution)/shard_map/ppermute | solution.py:336
  87.4 15.2 %collective-permute-start.24 = (bf16[256,1024]{1,0:T(8,128)(2,1)S(1)}, bf16[256,1024]{1,0:T(8,128)(2,1)S(1)}, u32[]{:S(2)}, u32[]{:S(2)}) collective-permute-start(bf16[256,1024]{1,0:T(8,128)(2,1)S(1)} %get-tuple-element.185.refs_1_), channel_id=1, source_target_pairs={{0,1},{1,0},{2,3},{3,2},{4,5},{5,4},{6,7},{7,6},{8,9},{9,8},{10,11... | collective-permute-start | bytes 1572872 | tf_op jit(solution)/shard_map/ppermute | solution.py:336
  87.8 14.8 %collective-permute-start.20 = (bf16[256,1024]{1,0:T(8,128)(2,1)}, bf16[256,1024]{1,0:T(8,128)(2,1)S(1)}, u32[]{:S(2)}, u32[]{:S(2)}) collective-permute-start(bf16[256,1024]{1,0:T(8,128)(2,1)} %get-tuple-element.180), channel_id=1, source_target_pairs={{0,3},{1,2},{2,1},{3,0},{4,7},{5,6},{6,5},{7,4},{8,11},{9,10},{10,... | collective-permute-start | bytes 1572872 | tf_op jit(solution)/shard_map/ppermute | solution.py:336
  87.8 14.8 %all-to-all-start.1 = ((bf16[8,32,512]{2,1,0:T(8,128)(2,1)}), bf16[8,32,512]{2,1,0:T(8,128)(2,1)S(1)}, u32[]{:S(2)}, u32[]{:S(2)}) async-start(bf16[8,32,512]{2,1,0:T(8,128)(2,1)} %attend.1), calls=%async_computation.1 | async-start | bytes 524288 | tf_op jit(solution)/shard_map/all_to_all | solution.py:346
  93.4 1.6 collective-permute-start.22
  93.5 2.0 collective-permute-start.23
  95.0 35.3 %copy-start.42 = (bf16[128,1024]{1,0:T(8,128)(2,1)}, bf16[128,1024]{1,0:T(8,128)(2,1)S(1)}, u32[]{:S(2)}) copy-start(bf16[128,1024]{1,0:T(8,128)(2,1)S(1)} %collective-permute-done.22.refs_5_) | copy-start | bytes 786436
  104.9 25.4 %copy-start.13 = (bf16[256,512]{1,0:T(8,128)(2,1)}, bf16[256,512]{1,0:T(8,128)(2,1)S(1)}, u32[]{:S(2)}) copy-start(bf16[256,512]{1,0:T(8,128)(2,1)S(1)} %get-tuple-element.189.refs_1_) | copy-start | bytes 786436
  104.9 3.7 %collective-permute-start.27 = (bf16[256,1024]{1,0:T(8,128)(2,1)S(1)}, bf16[256,1024]{1,0:T(8,128)(2,1)S(1)}, u32[]{:S(2)}, u32[]{:S(2)}) collective-permute-start(bf16[256,1024]{1,0:T(8,128)(2,1)S(1)} %collective-permute-done.20.refs_15_), channel_id=1, source_target_pairs={{0,1},{1,0},{2,3},{3,2},{4,5},{5,4},{6,7},{7,6},{8,9},{9,8},{10,11... | collective-permute-start | bytes 1572872 | tf_op jit(solution)/shard_map/ppermute | solution.py:336
  105.0 14.6 %collective-permute-start.25 = (bf16[256,1024]{1,0:T(8,128)(2,1)S(1)}, bf16[256,1024]{1,0:T(8,128)(2,1)S(1)}, u32[]{:S(2)}, u32[]{:S(2)}) collective-permute-start(bf16[256,1024]{1,0:T(8,128)(2,1)S(1)} %get-tuple-element.188), channel_id=1, source_target_pairs={{0,2},{1,3},{2,0},{3,1},{4,6},{5,7},{6,4},{7,5},{8,10},{9,11},{10,... | collective-permute-start | bytes 1572872 | tf_op jit(solution)/shard_map/ppermute | solution.py:336
  107.0 1.5 collective-permute-start.26
  130.3 7.4 %collective-permute-start.30 = (bf16[256,2816]{1,0:T(8,128)(2,1)S(1)}, bf16[256,2816]{1,0:T(8,128)(2,1)S(1)}, u32[]{:S(2)}, u32[]{:S(2)}) collective-permute-start(bf16[256,2816]{1,0:T(8,128)(2,1)S(1)} %get-tuple-element.208.refs_3_), channel_id=1, source_target_pairs={{0,1},{1,0},{2,3},{3,2},{4,5},{5,4},{6,7},{7,6},{8,9},{9,8},{10,11... | collective-permute-start | bytes 4325384 | tf_op jit(solution)/shard_map/ppermute | solution.py:336
  130.4 14.8 %collective-permute-start.31 = (bf16[256,1408]{1,0:T(8,128)(2,1)S(1)}, bf16[256,1408]{1,0:T(8,128)(2,1)S(1)}, u32[]{:S(2)}, u32[]{:S(2)}) collective-permute-start(bf16[256,1408]{1,0:T(8,128)(2,1)S(1)} %get-tuple-element.226.refs_1_), channel_id=1, source_target_pairs={{0,1},{1,0},{2,3},{3,2},{4,5},{5,4},{6,7},{7,6},{8,9},{9,8},{10,11... | collective-permute-start | bytes 2162696 | tf_op jit(solution)/shard_map/ppermute | solution.py:336
  130.9 6.9 %collective-permute-start.29 = (bf16[256,1024]{1,0:T(8,128)(2,1)S(1)}, bf16[256,1024]{1,0:T(8,128)(2,1)S(1)}, u32[]{:S(2)}, u32[]{:S(2)}) collective-permute-start(bf16[256,1024]{1,0:T(8,128)(2,1)S(1)} %get-tuple-element.253.refs_1_), channel_id=1, source_target_pairs={{0,1},{1,0},{2,3},{3,2},{4,5},{5,4},{6,7},{7,6},{8,9},{9,8},{10,11... | collective-permute-start | bytes 1572872 | tf_op jit(solution)/shard_map/ppermute | solution.py:336
  131.0 14.3 %collective-permute-start.28 = (bf16[256,1024]{1,0:T(8,128)(2,1)S(1)}, bf16[256,1024]{1,0:T(8,128)(2,1)S(1)}, u32[]{:S(2)}, u32[]{:S(2)}) collective-permute-start(bf16[256,1024]{1,0:T(8,128)(2,1)S(1)} %get-tuple-element.200), channel_id=1, source_target_pairs={{0,2},{1,3},{2,0},{3,1},{4,6},{5,7},{6,4},{7,5},{8,10},{9,11},{10,... | collective-permute-start | bytes 1572872 | tf_op jit(solution)/shard_map/ppermute | solution.py:336
  145.3 18.8 %collective-permute-start.32 = (bf16[256,1280]{1,0:T(8,128)(2,1)S(1)}, bf16[256,1280]{1,0:T(8,128)(2,1)}, u32[]{:S(2)}, u32[]{:S(2)}) collective-permute-start(bf16[256,1280]{1,0:T(8,128)(2,1)S(1)} %leaving_gradient.3), channel_id=1, source_target_pairs={{0,3},{1,2},{2,1},{3,0},{4,7},{5,6},{6,5},{7,4},{8,11},{9,10},{10,... | collective-permute-start | bytes 1966088 | tf_op jit(solution)/shard_map/ppermute | solution.py:336
  150.4 13.7 %collective-permute-start.33 = (bf16[256,1024]{1,0:T(8,128)(2,1)S(1)}, bf16[256,1024]{1,0:T(8,128)(2,1)}, u32[]{:S(2)}, u32[]{:S(2)}) collective-permute-start(bf16[256,1024]{1,0:T(8,128)(2,1)S(1)} %get-tuple-element.231.refs_3_), channel_id=1, source_target_pairs={{0,1},{1,0},{2,3},{3,2},{4,5},{5,4},{6,7},{7,6},{8,9},{9,8},{10,11... | collective-permute-start | bytes 1572872 | tf_op jit(solution)/shard_map/ppermute | solution.py:336
  151.4 12.7 %all-to-all-start.2 = ((bf16[8,32,512]{2,1,0:T(8,128)(2,1)}), bf16[8,32,512]{2,1,0:T(8,128)(2,1)S(1)}, u32[]{:S(2)}, u32[]{:S(2)}) async-start(bf16[8,32,512]{2,1,0:T(8,128)(2,1)} %get-tuple-element.210), calls=%async_computation.2 | async-start | bytes 524288 | tf_op jit(solution)/shard_map/all_to_all | solution.py:346
  155.0 4.5 %collective-permute-start.34 = (f32[1,256]{1,0:T(1,128)S(1)}, f32[1,256]{1,0:T(1,128)S(1)}, u32[]{:S(2)}, u32[]{:S(2)}) collective-permute-start(f32[1,256]{1,0:T(1,128)S(1)} %slice_bitcast_fusion.2), channel_id=1, source_target_pairs={{0,1},{1,0},{2,3},{3,2},{4,5},{5,4},{6,7},{7,6},{8,9},{9,8},{10,11... | collective-permute-start | bytes 3080 | tf_op jit(solution)/shard_map/ppermute | solution.py:336
  164.1 28.9 %collective-permute-start.42 = (bf16[256,1536]{1,0:T(8,128)(2,1)S(1)}, bf16[256,1536]{1,0:T(8,128)(2,1)S(1)}, u32[]{:S(2)}, u32[]{:S(2)}) collective-permute-start(bf16[256,1536]{1,0:T(8,128)(2,1)S(1)} %leaving_gradient.4), channel_id=1, source_target_pairs={{0,3},{1,2},{2,1},{3,0},{4,7},{5,6},{6,5},{7,4},{8,11},{9,10},{10,... | collective-permute-start | bytes 2359304 | tf_op jit(solution)/shard_map/ppermute | solution.py:336
  170.0 5.4 %collective-permute-start.35 = (bf16[32,1536]{1,0:T(8,128)(2,1)S(1)}, bf16[32,1536]{1,0:T(8,128)(2,1)S(1)}, u32[]{:S(2)}, u32[]{:S(2)}) collective-permute-start(bf16[32,1536]{1,0:T(8,128)(2,1)S(1)} %get-tuple-element.218), channel_id=1, source_target_pairs={{0,4},{1,5},{2,6},{3,7},{4,0},{5,1},{6,2},{7,3},{8,12},{9,13},{10,... | collective-permute-start | bytes 294920 | tf_op jit(solution)/shard_map/ppermute | solution.py:336
  171.5 5.9 %collective-permute-start.36 = (bf16[32,1536]{1,0:T(8,128)(2,1)S(1)}, bf16[32,1536]{1,0:T(8,128)(2,1)S(1)}, u32[]{:S(2)}, u32[]{:S(2)}) collective-permute-start(bf16[32,1536]{1,0:T(8,128)(2,1)S(1)} %get-tuple-element.219), channel_id=1, source_target_pairs={{0,8},{1,9},{2,10},{3,11},{4,12},{5,13},{6,14},{7,15},{8,0},{9,1},... | collective-permute-start | bytes 294920 | tf_op jit(solution)/shard_map/ppermute | solution.py:336
  171.5 9.5 %collective-permute-start.37 = (bf16[32,1536]{1,0:T(8,128)(2,1)S(1)}, bf16[32,1536]{1,0:T(8,128)(2,1)S(1)}, u32[]{:S(2)}, u32[]{:S(2)}) collective-permute-start(bf16[32,1536]{1,0:T(8,128)(2,1)S(1)} %get-tuple-element.220), channel_id=1, source_target_pairs={{0,12},{1,13},{2,14},{3,15},{4,8},{5,9},{6,10},{7,11},{8,4},{9,5},... | collective-permute-start | bytes 294920 | tf_op jit(solution)/shard_map/ppermute | solution.py:336
  173.6 19.4 %collective-permute-start.38 = (bf16[32,1536]{1,0:T(8,128)(2,1)S(1)}, bf16[32,1536]{1,0:T(8,128)(2,1)S(1)}, u32[]{:S(2)}, u32[]{:S(2)}) collective-permute-start(bf16[32,1536]{1,0:T(8,128)(2,1)S(1)} %get-tuple-element.221), channel_id=1, source_target_pairs={{0,16},{1,17},{2,18},{3,19},{4,20},{5,21},{6,22},{7,23},{8,24},{9,... | collective-permute-start | bytes 294920 | tf_op jit(solution)/shard_map/ppermute | solution.py:336
  175.4 17.6 %collective-permute-start.39 = (bf16[32,1536]{1,0:T(8,128)(2,1)S(1)}, bf16[32,1536]{1,0:T(8,128)(2,1)S(1)}, u32[]{:S(2)}, u32[]{:S(2)}) collective-permute-start(bf16[32,1536]{1,0:T(8,128)(2,1)S(1)} %get-tuple-element.222), channel_id=1, source_target_pairs={{0,20},{1,21},{2,22},{3,23},{4,16},{5,17},{6,18},{7,19},{8,28},{9,... | collective-permute-start | bytes 294920 | tf_op jit(solution)/shard_map/ppermute | solution.py:336
  177.3 15.7 %collective-permute-start.40 = (bf16[32,1536]{1,0:T(8,128)(2,1)S(1)}, bf16[32,1536]{1,0:T(8,128)(2,1)S(1)}, u32[]{:S(2)}, u32[]{:S(2)}) collective-permute-start(bf16[32,1536]{1,0:T(8,128)(2,1)S(1)} %get-tuple-element.223), channel_id=1, source_target_pairs={{0,24},{1,25},{2,26},{3,27},{4,28},{5,29},{6,30},{7,31},{8,16},{9,... | collective-permute-start | bytes 294920 | tf_op jit(solution)/shard_map/ppermute | solution.py:336
  181.0 12.0 %collective-permute-start.41 = (bf16[32,1536]{1,0:T(8,128)(2,1)S(1)}, bf16[32,1536]{1,0:T(8,128)(2,1)S(1)}, u32[]{:S(2)}, u32[]{:S(2)}) collective-permute-start(bf16[32,1536]{1,0:T(8,128)(2,1)S(1)} %get-tuple-element.224), channel_id=1, source_target_pairs={{0,28},{1,29},{2,30},{3,31},{4,24},{5,25},{6,26},{7,27},{8,20},{9,... | collective-permute-start | bytes 294920 | tf_op jit(solution)/shard_map/ppermute | solution.py:336
  197.1 2.4 collective-permute-start.45
  197.2 9.2 %collective-permute-start.44 = (bf16[128,1024]{1,0:T(8,128)(2,1)S(1)}, bf16[128,1024]{1,0:T(8,128)(2,1)S(1)}, u32[]{:S(2)}, u32[]{:S(2)}) collective-permute-start(bf16[128,1024]{1,0:T(8,128)(2,1)S(1)} %get-tuple-element.244), channel_id=1, source_target_pairs={{0,2},{1,3},{2,0},{3,1},{4,6},{5,7},{6,4},{7,5},{8,10},{9,11},{10,... | collective-permute-start | bytes 786440 | tf_op jit(solution)/shard_map/ppermute | solution.py:336
  198.0 13.5 %collective-permute-start.43 = (bf16[128,1024]{1,0:T(8,128)(2,1)S(1)}, bf16[128,1024]{1,0:T(8,128)(2,1)S(1)}, u32[]{:S(2)}, u32[]{:S(2)}) collective-permute-start(bf16[128,1024]{1,0:T(8,128)(2,1)S(1)} %get-tuple-element.242), channel_id=1, source_target_pairs={{0,2},{1,3},{2,0},{3,1},{4,6},{5,7},{6,4},{7,5},{8,10},{9,11},{10,... | collective-permute-start | bytes 786440 | tf_op jit(solution)/shard_map/ppermute | solution.py:336
  214.6 31.6 %all-to-all-start.3 = ((bf16[8,32,1024]{2,1,0:T(8,128)(2,1)}), bf16[8,32,1024]{2,1,0:T(8,128)(2,1)S(1)}, u32[]{:S(2)}, u32[]{:S(2)}) async-start(bf16[8,32,1024]{2,1,0:T(8,128)(2,1)} %get-tuple-element.251), calls=%async_computation.3 | async-start | bytes 1048576 | tf_op jit(solution)/shard_map/all_to_all | solution.py:346
  218.8 3.7 %collective-permute-start.46 = (f32[2,1,256]{2,1,0:T(1,128)S(1)}, f32[2,1,256]{2,1,0:T(1,128)S(1)}, u32[]{:S(2)}, u32[]{:S(2)}) collective-permute-start(f32[2,1,256]{2,1,0:T(1,128)S(1)} %slice.28), channel_id=1, source_target_pairs={{0,2},{1,3},{2,0},{3,1},{4,6},{5,7},{6,4},{7,5},{8,10},{9,11},{10,... | collective-permute-start | bytes 6152 | tf_op jit(solution)/shard_map/ppermute | solution.py:336
  219.9 19.4 %collective-permute-start.48 = (bf16[256,1536]{1,0:T(8,128)(2,1)S(1)}, bf16[256,1536]{1,0:T(8,128)(2,1)S(1)}, u32[]{:S(2)}, u32[]{:S(2)}) collective-permute-start(bf16[256,1536]{1,0:T(8,128)(2,1)S(1)} %leaving_gradient.5), channel_id=1, source_target_pairs={{0,3},{1,2},{2,1},{3,0},{4,7},{5,6},{6,5},{7,4},{8,11},{9,10},{10,... | collective-permute-start | bytes 2359304 | tf_op jit(solution)/shard_map/ppermute | solution.py:336
  222.4 9.8 %collective-permute-start.47 = (f32[1,256]{1,0:T(1,128)S(1)}, f32[1,256]{1,0:T(1,128)S(1)}, u32[]{:S(2)}, u32[]{:S(2)}) collective-permute-start(f32[1,256]{1,0:T(1,128)S(1)} %slice_bitcast_fusion), channel_id=1, source_target_pairs={{0,1},{1,0},{2,3},{3,2},{4,5},{5,4},{6,7},{7,6},{8,9},{9,8},{10,11... | collective-permute-start | bytes 3080 | tf_op jit(solution)/shard_map/ppermute | solution.py:336
  (38 other events, 288.5 us)

commit v3 on v2

--- a/solution.py
+++ b/solution.py
@@ -326,6 +326,7 @@
 SMEM = pl.BlockSpec(memory_space=pltpu.SMEM)
 HBM = pl.BlockSpec(memory_space=pltpu.HBM)
 STAGED = pl.BlockSpec(memory_space=pltpu.HBM)
+MOVED = pl.BlockSpec(memory_space=pl.ANY)
 BF16 = jnp.bfloat16
 F32 = jnp.float32
 OWN, FAR, NEAR, ACROSS, SIDE, CORE, POSITION = range(7)
@@ -349,9 +350,9 @@
     ]
 
 
-def kernel_call(kernel, name, args, outs, scratch=()):
+def kernel_call(kernel, name, args, outs, scratch=(), out_spec=None, aliases=()):
     flat = lambda items: [p for item in items for p in (item if isinstance(item, list) else [item])]
-    staged = [n for n, (spec, _) in enumerate(flat(args)) if spec is STAGED]
+    staged = [n for n, (spec, _) in enumerate(flat(args)) if spec is STAGED or spec is MOVED]
     arrays = [
         pltpu.with_memory_space_constraint(a, pltpu.HBM) if spec is STAGED or spec is HBM else a
         for spec, a in flat(args)
@@ -393,8 +394,12 @@
         body_kernel,
         name=name,
         in_specs=[spec for spec, _ in flat(args)],
-        out_specs=[VMEM] * len(flat(outs)),
-        out_shape=[jax.ShapeDtypeStruct(s, d) for s, d in flat(outs)],
+        out_specs=[out_spec or VMEM] * len(flat(outs)),
+        out_shape=[
+            pltpu.HBM(s, d) if out_spec is HBM else jax.ShapeDtypeStruct(s, d)
+            for s, d in flat(outs)
+        ],
+        input_output_aliases=dict(aliases),
         scratch_shapes=scratch,
         cost_estimate=pl.CostEstimate(flops=1, bytes_accessed=1, transcendentals=0),
         compiler_params=pltpu.CompilerParams(vmem_limit_bytes=held + (8 << 20)),
@@ -439,6 +444,10 @@
 
 def in_stage(*arrays):
     return [(STAGED, a) for a in arrays]
+
+
+def moved(*arrays):
+    return [(MOVED, a) for a in arrays]
 
 
 def place_matrix(size, to_positions, position):
@@ -556,10 +565,10 @@
     return kernel_call(
         first_kernel,
         "first",
-        [(SMEM, place), (STAGED, x_a), (STAGED, x_b), (VMEM, gains_own), (VMEM, gains_far),
+        [(SMEM, place), (MOVED, x_a), (MOVED, x_b), (VMEM, gains_own), (VMEM, gains_far),
          (VMEM, gains_near), (VMEM, gains_across), (HBM, w_own), (HBM, w_far), (HBM, w_near),
          (HBM, w_across)],
-        [block_shapes(2 * half, wide, False), ((2 * half, D), BF16), ((2, D), F32)],
+        [block_shapes(2 * half, wide, True), ((2 * half, D), BF16), ((2, D), F32)],
         [pltpu.VMEM((D, wide), BF16), pltpu.SemaphoreType.DMA((6,))],
     )
 
@@ -622,7 +631,7 @@
     return kernel_call(
         attend_kernel,
         "attend",
-        [(SMEM, place), (STAGED, ids_a), (STAGED, ids_b), in_stage(*qkv)],
+        [(SMEM, place), (MOVED, ids_a), (MOVED, ids_b), moved(*qkv)],
         [block_shapes(rows * POS, wide // 3, True)],
     )[0]
 
@@ -664,8 +673,8 @@
     return kernel_call(
         attend_back_kernel,
         "attend_back",
-        [(SMEM, place), (STAGED, ids_a), (STAGED, ids_b), in_stage(*qkv), in_vmem(*d_mixed)],
-        [block_shapes(rows * POS, wide, False)],
+        [(SMEM, place), (MOVED, ids_a), (MOVED, ids_b), moved(*qkv), in_vmem(*d_mixed)],
+        [block_shapes(rows * POS, wide, True)],
     )[0]
 
 
@@ -712,32 +721,24 @@
 def ffn_kernel(
     ready, place, x_a, x_b, term, far, gains, c_a, c_b, *rest
 ):
-    pieces, (wd_own, wd_near) = (rest[:4], rest[4:8]), rest[8:10]
-    resid, lowered, hidden, d_gate_up, second, leaving = rest[10:16]
-    w, wd, upstream, sems, down_sems = rest[16:]
-    half, width, steps = x_a.shape[0], pieces[0][0].shape[0], w.shape[0]
-    split = pieces[0][0].shape[1] // 256
-
-    def copies(j, sources, base):
-        return [
+    pieces, (wd_own, wd_near) = rest[:4], rest[4:6]
+    resid, lowered, hidden, d_gate_up, second, leaving = rest[6:12]
+    w, wd, upstream, sems, down_sems = rest[12:]
+    half, width, steps = x_a.shape[0], pieces[0].shape[0], w.shape[0]
+
+    def begin(j, carry):
+        for rank, source in enumerate(pieces):
             pltpu.make_async_copy(
-                source.at[:, aligned((j - base) * 256, 256)],
+                source.at[:, aligned(j * 256, 256)],
                 w.at[j, aligned(place[rank] * width, width)],
                 sems.at[j, rank],
-            )
-            for rank, source in enumerate(sources)
-        ]
-
-    def begin(sources, base, j, carry):
-        for copy in copies(j, sources, base):
-            copy.start()
+            ).start()
         return carry
 
     down_copies = chip_rows(place, wd_own, wd_near, wd, down_sems)
     for copy in down_copies:
         copy.start()
-    lax.fori_loop(0, split, functools.partial(begin, pieces[0], 0), 0)
-    lax.fori_loop(split, steps, functools.partial(begin, pieces[1], split), 0)
+    lax.fori_loop(0, steps, begin, 0)
     ready()
     gain = gains[1:2, :]
     for rel, (x_ref, c_ref) in enumerate(((x_a, c_a), (x_b, c_b))):
@@ -838,18 +839,22 @@
     for copy in copies:
         copy.start()
     half, width = c_a.shape[0], w_own.shape[0]
+    total = None
+    for rel in range(2):
+        at = pl.ds(rel * half, half)
+        rows = resid[at, :]
+        scale = lax.rsqrt(jnp.mean(rows * rows, axis=-1, keepdims=True) + EPSILON)
+        d_rows = second[at, :] + far[at, :].astype(F32)
+        part = jnp.sum(d_rows * (rows * scale), axis=0, keepdims=True)
+        total = part if total is None else total + part
     ready()
     gain = gains[1:2, :]
-    total = None
     for rel, c_ref in enumerate((c_a, c_b)):
         at = pl.ds(rel * half, half)
         rows = resid[at, :]
         scale = lax.rsqrt(jnp.mean(rows * rows, axis=-1, keepdims=True) + EPSILON)
         normed = rows * scale
-        d_rows = second[at, :] + far[at, :].astype(F32)
-        part = jnp.sum(d_rows * normed, axis=0, keepdims=True)
-        total = part if total is None else total + part
-        scaled = d_rows * gain
+        scaled = (second[at, :] + far[at, :].astype(F32)) * gain
         value = c_ref[...].astype(F32) + scale * (
             scaled - normed * jnp.mean(scaled * normed, axis=-1, keepdims=True)
         )
@@ -958,7 +963,7 @@
         "last",
         [(SMEM, place)]
         + in_vmem(kept, far)
-        + in_stage(x_a, gains, d_resid, down_kept)
+        + moved(x_a, gains, d_resid, down_kept)
         + in_vmem(down_far),
         [block_shapes(2 * half, D, True), ((4, 1, D // 4), F32)],
         [pltpu.VMEM((1, D), F32)],
@@ -970,75 +975,104 @@
 
 
 def leaving_kernel(
-    first_block, ready, place, left_own, left_near, right_own, right_near, leaving
+    target, ready, place, left_own, left_near, right_own, right_near, leaving
 ):
     ready()
     width = leaving.shape[0]
-    left = both_rows(left_own, left_near, aligned(place[ACROSS] * width, width))
+    left = both_rows(left_own, left_near, aligned(place[target] * width, width))
 
     def step(j, carry):
         columns = aligned(j * 256, 256)
-        right = both_rows(
-            right_own, right_near, aligned((first_block + j) * 256, 256)
-        )
+        right = both_rows(right_own, right_near, columns)
         leaving[:, columns] = inner_rows(left, right).astype(BF16)
         return carry
 
     lax.fori_loop(0, leaving.shape[1] // 256, step, 0)
 
 
-def leaving_gradient(place, blocks, left_own, left_near, right_own, right_near):
-    width, wide = D // 4, 256 * (blocks[1] - blocks[0])
-    return kernel_call(
-        functools.partial(leaving_kernel, blocks[0]),
+def leaving_gradient(place, target, left_own, left_near, right_own, right_near):
+    width, wide = D // 4, right_own.shape[1]
+    return kernel_call(
+        functools.partial(leaving_kernel, target),
         "leaving_gradient",
         [(SMEM, place)] + in_stage(left_own, left_near, right_own, right_near),
         [((width, wide), BF16)],
     )[0]
 
 
-def staying_kernel(parts, ready, place, left_own, left_near, right_own, right_near, *rest):
-    ready()
-    come, grad = rest[:-1], rest[-1]
-    width = grad.shape[0]
-    part = grad.shape[1] // 2 // parts
-    side = place[SIDE]
+def put_stripe(parts, stripes, block, value):
+    if parts == 2:
+        at = aligned(block * 128, 128)
+        stripes[0, :, at] = value[:, :128]
+        stripes[1, :, at] = value[:, 128:]
+    else:
+        stripes[block // 2, :, aligned((block % 2) * 256, 256)] = value
+
+
+def write_stripes(who, stripes, grad, sems):
+    parts, _, part = stripes.shape
+    copies = [
+        pltpu.make_async_copy(
+            stripes.at[k], grad.at[:, aligned((2 * k + who) * part, part)], sems.at[k]
+        )
+        for k in range(parts)
+    ]
+    for copy in copies:
+        copy.start()
+    for copy in copies:
+        copy.wait()
+
+
+def staying_kernel(
+    ready, place, left_own, left_near, right_own, right_near, grad, stripes, sems
+):
+    ready()
+    parts, width, _ = stripes.shape
     left = both_rows(left_own, left_near, aligned(place[OWN] * width, width))
-
-    def put(block, who, value):
-        if parts == 2:
-            spots = [(0, block * 128, 0, 128), (1, block * 128, 128, 256)]
-        else:
-            spots = [(block // 2, (block % 2) * 256, 0, 256)]
-        for k, start, low, high in spots:
-            grad[:, aligned((2 * k + who) * part + start, high - low)] = value[:, low:high]
 
     def step(j, carry):
         right = both_rows(right_own, right_near, aligned(j * 256, 256))
-        put(j, side, inner_rows(left, right))
+        put_stripe(parts, stripes, j, inner_rows(left, right))
         return carry
 
     lax.fori_loop(0, right_own.shape[1] // 256, step, 0)
-    base = 0
-    for piece in come:
-        count = piece.shape[1] // 256
-
-        def take(j, carry, piece=piece, base=base):
-            put(base + j, 1 - side, piece[:, aligned(j * 256, 256)].astype(F32))
-            return carry
-
-        lax.fori_loop(0, count, take, 0)
-        base += count
-
-
-def staying_gradient(parts, place, left_own, left_near, right_own, right_near, *come):
-    width = D // 4
-    arrays = (left_own, left_near, right_own, right_near) + come
-    return kernel_call(
-        functools.partial(staying_kernel, parts),
+    write_stripes(place[SIDE], stripes, grad, sems)
+
+
+def staying_gradient(parts, place, left_own, left_near, right_own, right_near):
+    width, wide = D // 4, right_own.shape[1]
+    return kernel_call(
+        staying_kernel,
         "staying_gradient",
-        [(SMEM, place)] + in_stage(*arrays),
-        [((width, 2 * right_own.shape[1]), F32)],
+        [(SMEM, place)] + in_stage(left_own, left_near, right_own, right_near),
+        [((width, 2 * wide), F32)],
+        [pltpu.VMEM((parts, width, wide // parts), F32), pltpu.SemaphoreType.DMA((parts,))],
+        out_spec=HBM,
+    )[0]
+
+
+def coming_kernel(ready, place, come, before, grad, stripes, sems):
+    ready()
+    parts = stripes.shape[0]
+
+    def step(j, carry):
+        put_stripe(parts, stripes, j, come[:, aligned(j * 256, 256)].astype(F32))
+        return carry
+
+    lax.fori_loop(0, come.shape[1] // 256, step, 0)
+    write_stripes(1 - place[SIDE], stripes, grad, sems)
+
+
+def with_coming(parts, place, come, grad):
+    width, wide = come.shape
+    return kernel_call(
+        coming_kernel,
+        "coming_gradient",
+        [(SMEM, place), (STAGED, come), (HBM, grad)],
+        [(grad.shape, F32)],
+        [pltpu.VMEM((parts, width, wide // parts), F32), pltpu.SemaphoreType.DMA((parts,))],
+        out_spec=HBM,
+        aliases=((2, 0),),
     )[0]
 
 
@@ -1087,7 +1121,7 @@
     return kernel_call(
         grad_down_kernel,
         "grad_down",
-        [(SMEM, place)] + in_stage(h_own, h_near, ca_own, cb_own, ca_near, cb_near),
+        [(SMEM, place)] + moved(h_own, h_near, ca_own, cb_own, ca_near, cb_near),
         [((count, D), F32)],
         [pltpu.VMEM((window, D), F32)],
     )[0]
@@ -1121,18 +1155,17 @@
     )[0]
 
 
-def spread_kernel(split, ready, place, weight, kept_a, kept_b, leaving_a, leaving_b, sems):
+def spread_kernel(ready, place, weight, kept, leaving, sems):
     part = weight.shape[1] // 4
     side = place[SIDE]
     copies = []
     for k in range(2):
         for j in range(part // 128):
-            for who, targets in ((side, (kept_a, kept_b)), (1 - side, (leaving_a, leaving_b))):
-                target, at = (targets[0], j) if j < split else (targets[1], j - split)
+            for who, target in ((side, kept), (1 - side, leaving)):
                 copies.append(
                     pltpu.make_async_copy(
                         weight.at[:, aligned((2 * k + who) * part + j * 128, 128)],
-                        target.at[:, pl.ds(at * 256 + k * 128, 128)],
+                        target.at[:, pl.ds(j * 256 + k * 128, 128)],
                         sems.at[len(copies)],
                     )
                 )
@@ -1142,14 +1175,13 @@
         copy.wait()
 
 
-def spread(place, weight, split):
+def spread(place, weight):
     count, width = weight.shape
-    sizes = (256 * split, width // 2 - 256 * split) * 2
-    return kernel_call(
-        functools.partial(spread_kernel, split),
+    return kernel_call(
+        spread_kernel,
         "spread",
         [(SMEM, place), (HBM, weight)],
-        [((count, size), BF16) for size in sizes],
+        [((count, width // 2), BF16)] * 2,
         [pltpu.SemaphoreType.DMA((width // 128,))],
     )
 
@@ -1171,8 +1203,6 @@
     frames = frames_in.shape[0] // POS
     half = POS * frames
 
-    blocks = w_gate_up.shape[1] // 512
-    split = (blocks * 7) // 11
     near = lambda rows: swap(rows, 1)
 
     qkv_leaving = half_columns(place, w_qkv, 3, True)
@@ -1190,42 +1220,39 @@
     came, ids_far, gains_far, qkv_kept, qkv_far = sync(came, ids_far, gains_far, qkv_kept, qkv_far)
 
     x_own, c_own = collect(place, came)
-    x_far, c_far = swap(x_own, 2), swap(c_own, 2)
+    x_far = swap(x_own, 2)
     gains_near = near(jnp.stack([gains_own, gains_far]))
     qkv_near = near(qkv_kept)
-    kept_a, kept_b, leaving_a, leaving_b = spread(place, after(w_gate_up, x_own), split)
-    x_far, gains_near, qkv_near, leaving_a, c_own, c_far = sync(
-        x_far, gains_near, qkv_near, leaving_a, c_own, c_far
-    )
-
+    w_kept, w_leaving = spread(place, after(w_gate_up, x_own))
+    x_far, gains_near, qkv_near, w_leaving, c_own = sync(
+        x_far, gains_near, qkv_near, w_leaving, c_own
+    )
+
+    w_across = swap(w_leaving, 3)
     qkv_sent, lowered_first, gains = first(
         place, x_own, x_far, gains_own, gains_far, gains_near[0], gains_near[1],
         w_qkv, qkv_far, qkv_near, qkv_across,
     )
-    across_a = swap(after(leaving_a, lowered_first), 3)
-    near_a, near_b, out_near, down_near = (
-        near(after(a, lowered_first)) for a in (kept_a, kept_b, w_out, w_down)
-    )
-    qkv, across_a, near_a, near_b, out_near, down_near = sync(
-        exchange(qkv_sent), across_a, near_a, near_b, out_near, down_near
-    )
+    w_near, out_near, down_near = (near(after(a, lowered_first)) for a in (w_kept, w_out, w_down))
+    qkv, w_near, out_near, down_near = sync(exchange(qkv_sent), w_near, out_near, down_near)
 
     mixed_sent = attend_local(place, ids_own, ids_far, qkv)
-    across_b = swap(after(leaving_b, across_a), 3)
-    far_a = near(across_a)
-    c_own_near, c_far_near, lowered_first_near = (
-        near(after(a, mixed_sent[0])) for a in (c_own, c_far, lowered_first)
-    )
-    mixed, across_b, far_a, c_own_near, c_far_near, lowered_first_near = sync(
-        exchange(mixed_sent), across_b, far_a, c_own_near, c_far_near, lowered_first_near
+    c_far = swap(after(c_own, mixed_sent[0]), 2)
+    c_own_near, lowered_first_near = (
+        near(after(a, mixed_sent[0])) for a in (c_own, lowered_first)
+    )
+    mixed, w_across, c_far, c_own_near, lowered_first_near = sync(
+        exchange(mixed_sent), w_across, c_far, c_own_near, lowered_first_near
     )
 
     term, leaving, mixed = out_term(place, mixed, w_out, out_near)
     far = swap(leaving, 2)
-    far, mixed_near, far_b = sync(far, near(mixed), near(after(across_b, leaving)))
-    pieces = (kept_a, far_a, near_a, across_a, kept_b, far_b, near_b, across_b)
+    far, mixed_near, w_far, c_far_near = sync(
+        far, near(mixed), near(after(w_across, leaving)), near(after(c_far, leaving))
+    )
     resid, lowered_second, hidden, d_gate_up, second, leaving = ffn(
-        place, x_own, x_far, term, far, gains, c_own, c_far, pieces, w_down, down_near
+        place, x_own, x_far, term, far, gains, c_own, c_far, (w_kept, w_far, w_near, w_across),
+        w_down, down_near,
     )
 
     second_far = swap(leaving, 2)
@@ -1234,53 +1261,51 @@
     )
     down_kept, down_leaving = down_term(place, after(hidden, leaving), resid, w_down, down_near)
     sides = (lowered_second, lowered_second_near, d_gate_up, d_gate_up_near)
-    cut = (blocks * 5) // 11
-    gate_up_leaving = leaving_gradient(place, (0, cut), *sides)
+    gate_up_leaving = leaving_gradient(place, ACROSS, *sides)
     second_far, down_leaving, gate_up_leaving, hidden_near, lowered_second_near = sync(
         second_far, down_leaving, gate_up_leaving, hidden_near, lowered_second_near
     )
 
+    gate_up_come = swap(gate_up_leaving, 3)
     d_resid, d_branch, gain_ffn_terms, d_mixed = mid(
         place, second, second_far, resid, gains, c_own, c_far, w_out, out_near
     )
-    gate_up_come = swap(gate_up_leaving, 3)
-    sides = (after(lowered_second, d_branch), lowered_second_near, d_gate_up, d_gate_up_near)
-    gate_up_leaving_rest = leaving_gradient(place, (cut, blocks), *sides)
     d_branch_near, gain_ffn_near = near(d_branch), near(gain_ffn_terms[1])
-    d_mixed, gate_up_come, gate_up_leaving_rest, d_branch_near, gain_ffn_near = sync(
-        exchange(d_mixed), gate_up_come, gate_up_leaving_rest, d_branch_near, gain_ffn_near,
+    grad_gate_up = staying_gradient(2, place, after(lowered_second, d_branch), *sides[1:])
+    d_mixed, d_branch_near, gain_ffn_near, grad_gate_up = sync(
+        exchange(d_mixed), d_branch_near, gain_ffn_near, grad_gate_up
     )
 
     d_qkv_sent = attend_back_local(place, ids_own, ids_far, qkv, d_mixed)
-    gate_up_come_rest = swap(gate_up_leaving_rest, 3)
     grad_down = grad_down_rows(
         place, after(hidden, d_qkv_sent[0]), hidden_near, c_own, c_far, c_own_near, c_far_near
     )
     grad_out = grad_out_rows(place, mixed, mixed_near, after(d_branch, d_qkv_sent[0]), d_branch_near)
-    d_qkv, gate_up_come_rest, grad_down, grad_out = sync(
-        exchange(d_qkv_sent), gate_up_come_rest, grad_down, grad_out
+    down_far = swap(after(down_leaving, d_qkv_sent[0]), 2)
+    d_qkv, gate_up_come, down_far, grad_down, grad_out = sync(
+        exchange(d_qkv_sent), gate_up_come, down_far, grad_down, grad_out
     )
 
     kept, leaving, d_projected = back_first(
         place, d_qkv, w_qkv, qkv_far, qkv_near, qkv_across
     )
     first_far = swap(leaving, 2)
-    down_far = swap(after(down_leaving, leaving), 2)
     qkv_sides = (lowered_first, lowered_first_near, d_projected, near(d_projected))
-    qkv_grad_leaving = leaving_gradient(place, (0, qkv_leaving.shape[1] // 256), *qkv_sides)
-    first_far, down_far, qkv_grad_leaving = sync(first_far, down_far, qkv_grad_leaving)
-
-    qkv_come = swap(qkv_grad_leaving, 3)
+    first_far, qkv_leaving = sync(first_far, leaving_gradient(place, FAR, *qkv_sides))
+    qkv_across_come = swap(qkv_leaving, 3)
+
     out_sent, gain_attn_terms = last(
         place, kept, first_far, x_own, gains, d_resid, down_kept, down_far
     )
-    grad_gate_up = staying_gradient(
-        2, place, after(sides[0], gain_attn_terms), *sides[1:], gate_up_come, gate_up_come_rest
-    )
+    grad_gate_up = with_coming(2, place, after(gate_up_come, gain_attn_terms), grad_gate_up)
+    grad_qkv = staying_gradient(3, place, after(lowered_first, gain_attn_terms), *qkv_sides[1:])
     gain_sums = gain_attn_terms[:2] + swap(gain_attn_terms[2:], 2)
     gain_attn_grad = gain_sums[0] + near(gain_sums[1])
-    out_come, grad_gate_up = sync(exchange(out_sent), grad_gate_up)
-    grad_qkv = staying_gradient(3, place, *qkv_sides, qkv_come)
+    qkv_come = near(after(qkv_across_come, grad_gate_up, grad_qkv))
+    out_come, grad_gate_up, grad_qkv, qkv_come = sync(
+        exchange(out_sent), grad_gate_up, grad_qkv, qkv_come
+    )
+    grad_qkv = with_coming(3, place, qkv_come, grad_qkv)
     grad_in, block_out = to_frames(place, out_come)
     gain_ffn_grad = (gain_ffn_terms[0] + gain_ffn_near).reshape(-1)
     return (

time: 249 us -> 228 us (0.916)
  starting transfers between devices: 70.9 us -> 48.6 us
  waiting for transfers between devices: 74.3 us -> 78.9 us
  Pallas kernels: 90.4 us -> 87.1 us
    ppermute x49 -> x32, starting transfers between devices: 51.7 us -> 16.2 us  [swap(): return lax.ppermute(block, 'fsdp', [(i, i ^ mask) for i in range(count)])]
    all_to_all x4 -> x6, starting transfers between devices: 19.2 us -> 32.4 us  [exchange(): lax.all_to_all(blocks[0], 'fsdp', split_axis=0, concat_axis=0, tiled=True...]
    all_to_all x4 -> x6, waiting for transfers between devices: 11.7 us -> 19.5 us  [exchange(): lax.all_to_all(blocks[0], 'fsdp', split_axis=0, concat_axis=0, tiled=True...]
    pallas_call x22 -> x23, Pallas kernels: 90.4 us -> 87.1 us  [kernel_call(): pl.pallas_call(body_kernel, name=name, in_specs=[spec for spec, _ in flat...]
    ppermute x49 -> x32, waiting for transfers between devices: 62.6 us -> 59.4 us  [swap(): return lax.ppermute(block, 'fsdp', [(i, i ^ mask) for i in range(count)])]
    unnamed x98 -> x82, local copies, waits for them, and re-layouts: 8.62 us -> 8.96 us
  transfers between devices with their start and end apart: 53 -> 38, of which waited for: 23 -> 18; matrix products, arithmetic and copies ran while one was open for 1% -> 1% of each run, Pallas kernels for 25% -> 25%
where the time goes in v3:
time: 228 us; the launch traced here: 227 us
  Pallas kernels  87.1 us (38%)
  waiting for transfers between devices  78.9 us (35%)
  starting transfers between devices  48.6 us (21%)
  local copies, waits for them, and re-layouts  9.85 us (4%)
    pallas_call x23, Pallas kernels, kernel_call(): pl.pallas_call(body_kernel, name=name, in_specs=[spec for spec, _ in flat...  87.1 us
    ppermute x32, waiting for transfers between devices, swap(): return lax.ppermute(block, 'fsdp', [(i, i ^ mask) for i in range(count)])  59.4 us
    all_to_all x6, starting transfers between devices, exchange(): lax.all_to_all(blocks[0], 'fsdp', split_axis=0, concat_axis=0, tiled=True...  32.4 us
    all_to_all x6, waiting for transfers between devices, exchange(): lax.all_to_all(blocks[0], 'fsdp', split_axis=0, concat_axis=0, tiled=True...  19.5 us
    ppermute x32, starting transfers between devices, swap(): return lax.ppermute(block, 'fsdp', [(i, i ^ mask) for i in range(count)])  16.2 us
    unnamed x82, local copies, waits for them, and re-layouts  8.96 us
  transfers between devices with their start and end apart: 38, of which 18 were waited for; matrix products, arithmetic and copies ran while one was open for 1% of the time, Pallas kernels for 25%

profile of v3, /device:TPU:0, one launch (start us, length us, event | category | flops | bytes accessed | tf_op | source)
XLA Modules:
  0.0 227.2 jit_solution(17220098297524309012)
XLA Ops:
  0.7 1.7 far_columns.1
  2.5 2.5 %collective-permute-start.2 = (bf16[256,1536]{1,0:T(8,128)(2,1)S(1)}, bf16[256,1536]{1,0:T(8,128)(2,1)S(1)}, u32[]{:S(2)}, u32[]{:S(2)}) collective-permute-start(bf16[256,1536]{1,0:T(8,128)(2,1)S(1)} %far_columns.1), channel_id=1, source_target_pairs={{0,3},{1,2},{2,1},{3,0},{4,7},{5,6},{6,5},{7,4},{8,11},{9,10},{10,... | collective-permute-start | bytes 2359304 | tf_op jit(solution)/shard_map/ppermute | solution.py:337
  5.0 2.7 %to_positions.1 = bf16[8,32,1024]{2,1,0:T(8,128)(2,1)} custom-call(s32[7]{0:T(128)S(1)} %stack.49.refs_0_, bf16[128,1024]{1,0:T(8,128)(2,1)} %refs_1_.4, bf16[128,1024]{1,0:T(8,128)(2,1)} %refs_2_.1), custom_call_target="tpu_custom_call" | custom-call | flops 1 | bytes 1 | tf_op jit(solution)/shard_map/to_positions/pallas_call | solution.py:393
  7.6 5.8 %all-to-all-start = ((bf16[8,32,1024]{2,1,0:T(8,128)(2,1)}), bf16[8,32,1024]{2,1,0:T(8,128)(2,1)S(1)}, u32[]{:S(2)}, u32[]{:S(2)}) async-start(bf16[8,32,1024]{2,1,0:T(8,128)(2,1)} %to_positions.1), calls=%async_computation | async-start | bytes 1048576 | tf_op jit(solution)/shard_map/all_to_all | solution.py:347
  13.5 9.4 %collective-permute-done.2.refs_10_.refs_4_ = bf16[256,1536]{1,0:T(8,128)(2,1)S(1)} collective-permute-done((bf16[256,1536]{1,0:T(8,128)(2,1)S(1)}, bf16[256,1536]{1,0:T(8,128)(2,1)S(1)}, u32[]{:S(2)}, u32[]{:S(2)}) %collective-permute-start.2) | collective-permute-done | bytes 786464 | tf_op jit(solution)/shard_map/ppermute | solution.py:337
  23.0 2.5 %collective-permute-start.1 = (bf16[2,256]{1,0:T(2,128)(2,1)S(1)}, bf16[2,256]{1,0:T(2,128)(2,1)S(1)}, u32[]{:S(2)}, u32[]{:S(2)}) collective-permute-start(bf16[2,256]{1,0:T(2,128)(2,1)S(1)} %pad_maximum_fusion.1.refs_3_), channel_id=1, source_target_pairs={{0,2},{1,3},{2,0},{3,1},{4,6},{5,7},{6,4},{7,5},{8,10},{9,11},{10,... | collective-permute-start | bytes 3080 | tf_op jit(solution)/shard_map/ppermute | solution.py:337
  26.5 1.7 kept_columns.1
  28.2 1.8 collective-permute-done.refs_2_
  30.1 0.6 collect.1
  31.4 2.8 %spread.1 = (bf16[256,2816]{1,0:T(8,128)(2,1)S(1)}, bf16[256,2816]{1,0:T(8,128)(2,1)S(1)}) custom-call(s32[7]{0:T(128)S(1)} %stack.49.refs_0_, bf16[256,5632]{1,0:T(8,128)(2,1)} %refs_1_.6), custom_call_target="tpu_custom_call" | custom-call | flops 1 | bytes 1 | tf_op jit(solution)/shard_map/spread/pallas_call | solution.py:393
  34.3 5.2 %collective-permute-done.4.refs_2_ = bf16[128,1024]{1,0:T(8,128)(2,1)S(1)} collective-permute-done((bf16[128,1024]{1,0:T(8,128)(2,1)S(1)}, bf16[128,1024]{1,0:T(8,128)(2,1)S(1)}, u32[]{:S(2)}, u32[]{:S(2)}) %collective-permute-start.4) | collective-permute-done | bytes 262176 | tf_op jit(solution)/shard_map/ppermute | solution.py:337
  39.6 0.9 copy-done.32
  40.5 4.3 %first.1 = (bf16[8,32,1536]{2,1,0:T(8,128)(2,1)S(1)}, bf16[256,1024]{1,0:T(8,128)(2,1)S(1)}, f32[2,1024]{1,0:T(2,128)S(1)}) custom-call(s32[7]{0:T(128)S(1)} %stack.49.refs_0_, bf16[128,1024]{1,0:T(8,128)(2,1)S(1)} %get-tuple-element.107.refs_1_.refs_3_, bf16[128,1024]{1,0:T(8,128)(2,1)S(1)} %collective-permute-done.4.refs_2_, ...), custom_call_target="tpu_custom_call" | custom-call | flops 1 | bytes 1 | tf_op jit(solution)/shard_map/first/pallas_call | solution.py:393
  45.7 5.8 %all-to-all-start.1 = ((bf16[8,32,1536]{2,1,0:T(8,128)(2,1)}), bf16[8,32,1536]{2,1,0:T(8,128)(2,1)S(1)}, u32[]{:S(2)}, u32[]{:S(2)}) async-start(bf16[8,32,1536]{2,1,0:T(8,128)(2,1)} %copy-done.14), calls=%async_computation.1 | async-start | bytes 1572864 | tf_op jit(solution)/shard_map/all_to_all | solution.py:347
  51.6 0.6 collective-permute-start.8
  52.2 1.9 collective-permute-done.8.refs_2_.refs_8_
  54.1 17.6 %all-to-all-done.1.refs_3_ = bf16[8,32,1536]{2,1,0:T(8,128)(2,1)S(1)} async-done(((bf16[8,32,1536]{2,1,0:T(8,128)(2,1)}), bf16[8,32,1536]{2,1,0:T(8,128)(2,1)S(1)}, u32[]{:S(2)}, u32[]{:S(2)}) %all-to-all-start.1) | async-done | bytes 786464 | tf_op jit(solution)/shard_map/all_to_all | solution.py:347
  71.8 2.6 %attend.1 = bf16[8,32,512]{2,1,0:T(8,128)(2,1)} custom-call(s32[7]{0:T(128)S(1)} %stack.49.refs_0_, s32[1,128]{1,0:T(1,128)S(1)} %select_n.46.refs_1_, s32[1,128]{1,0:T(1,128)S(1)} %collective-permute-done.refs_2_, bf16[8,32,1536]{2,1,0:T(8,128)(2,1)S(1)} %all-to-all-done.1.refs_3_), custom_call_target="tpu_custom_call" | custom-call | flops 1 | bytes 1 | tf_op jit(solution)/shard_map/attend/pallas_call | solution.py:393
  74.4 3.6 %all-to-all-start.2 = ((bf16[8,32,512]{2,1,0:T(8,128)(2,1)}), bf16[8,32,512]{2,1,0:T(8,128)(2,1)S(1)}, u32[]{:S(2)}, u32[]{:S(2)}) async-start(bf16[8,32,512]{2,1,0:T(8,128)(2,1)} %attend.1), calls=%async_computation.2 | async-start | bytes 524288 | tf_op jit(solution)/shard_map/all_to_all | solution.py:347
  78.9 6.9 %collective-permute-done.10.refs_11_ = bf16[256,2816]{1,0:T(8,128)(2,1)} collective-permute-done((bf16[256,2816]{1,0:T(8,128)(2,1)}, bf16[256,2816]{1,0:T(8,128)(2,1)}, u32[]{:S(2)}, u32[]{:S(2)}) %collective-permute-start.10) | collective-permute-done | bytes 1441824 | tf_op jit(solution)/shard_map/ppermute | solution.py:337
  85.8 4.9 %collective-permute-done.11.refs_7_.refs_6_.refs_4_ = bf16[128,1024]{1,0:T(8,128)(2,1)S(1)} collective-permute-done((bf16[128,1024]{1,0:T(8,128)(2,1)S(1)}, bf16[128,1024]{1,0:T(8,128)(2,1)S(1)}, u32[]{:S(2)}, u32[]{:S(2)}) %collective-permute-start.11) | collective-permute-done | bytes 262176 | tf_op jit(solution)/shard_map/ppermute | solution.py:337
  90.8 2.2 out_term.1
  93.2 1.1 collective-permute-start.14
  94.7 2.1 collective-permute-done.17.refs_6_
  96.9 0.7 copy-done.21
  97.6 9.8 %collective-permute-done.14.refs_4_ = bf16[256,1024]{1,0:T(8,128)(2,1)S(1)} collective-permute-done((bf16[256,1024]{1,0:T(8,128)(2,1)S(1)}, bf16[256,1024]{1,0:T(8,128)(2,1)S(1)}, u32[]{:S(2)}, u32[]{:S(2)}) %collective-permute-start.14) | collective-permute-done | bytes 524320 | tf_op jit(solution)/shard_map/ppermute | solution.py:337
  107.4 1.1 copy-done.35
  108.5 10.7 %ffn.1 = (f32[256,1024]{1,0:T(8,128)S(1)}, bf16[256,1024]{1,0:T(8,128)(2,1)S(1)}, bf16[256,1408]{1,0:T(8,128)(2,1)S(1)}, bf16[256,2816]{1,0:T(8,128)(2,1)S(1)}, ...) custom-call(s32[7]{0:T(128)S(1)} %stack.49.refs_0_, bf16[128,1024]{1,0:T(8,128)(2,1)} %copy-done.8, ...), custom_call_target="tpu_custom_call" | custom-call | flops 1 | bytes 1 | tf_op jit(solution)/shard_map/ffn/pallas_call | solution.py:393
  119.9 1.1 collective-permute-start.18
  121.0 4.2 %down_term.1 = (f32[128,1024]{1,0:T(8,128)S(1)}, bf16[128,1024]{1,0:T(8,128)(2,1)S(1)}) custom-call(s32[7]{0:T(128)S(1)} %stack.49.refs_0_, bf16[256,1408]{1,0:T(8,128)(2,1)} %copy-done.2, f32[256,1024]{1,0:T(8,128)S(1)} %get-tuple-element.146.refs_2_.refs_3_, bf16[704,1024]{1,0:T(8,128)(2,1)} %refs_3_.1, ...), custom_call_target="tpu_custom_call" | custom-call | flops 1 | bytes 1 | tf_op jit(solution)/shard_map/down_term/pallas_call | solution.py:393
  125.2 0.7 copy-done.29
  126.0 0.8 copy-done.34
  126.7 1.1 copy-done.30
  127.8 5.8 %leaving_gradient.2 = bf16[256,2816]{1,0:T(8,128)(2,1)S(1)} custom-call(s32[7]{0:T(128)S(1)} %stack.49.refs_0_, bf16[256,1024]{1,0:T(8,128)(2,1)} %copy-done.11, bf16[256,1024]{1,0:T(8,128)(2,1)} %copy-done.34, bf16[256,2816]{1,0:T(8,128)(2,1)} %copy-done, bf16[256,2816]{1,0:T(8,128)(2,1)} %copy-done.30), custom_call_target="tpu_custom_call" | custom-call | flops 1 | bytes 1 | tf_op jit(solution)/shard_map/leaving_gradient/pallas_call | solution.py:393
  134.2 0.9 copy-done.15
  135.0 3.5 %mid.1 = (f32[128,1024]{1,0:T(8,128)S(1)}, bf16[256,1024]{1,0:T(8,128)(2,1)}, f32[2,1,256]{2,1,0:T(1,128)S(1)}, bf16[8,32,512]{2,1,0:T(8,128)(2,1)}) custom-call(s32[7]{0:T(128)S(1)} %stack.49.refs_0_, f32[256,1024]{1,0:T(8,128)S(1)} %get-tuple-element.142.refs_1_, bf16[256,1024]{1,0:T(8,128)(2,1)S(1)} %collective-permute-done.18.refs_2_, ...), custom_call_target="tpu_custom_call" | custom-call | flops 1 | bytes 1 | tf_op jit(solution)/shard_map/mid/pallas_call | solution.py:393
  138.6 0.8 copy-done.17
  139.4 5.6 %all-to-all-start.3 = ((bf16[8,32,512]{2,1,0:T(8,128)(2,1)}), bf16[8,32,512]{2,1,0:T(8,128)(2,1)S(1)}, u32[]{:S(2)}, u32[]{:S(2)}) async-start(bf16[8,32,512]{2,1,0:T(8,128)(2,1)} %get-tuple-element.153), calls=%async_computation.3 | async-start | bytes 524288 | tf_op jit(solution)/shard_map/all_to_all | solution.py:347
  145.0 1.3 collective-permute-start.24
  146.6 7.3 %staying_gradient.2.refs_2_ = f32[256,5632]{1,0:T(8,128)} custom-call(s32[7]{0:T(128)S(1)} %stack.49.refs_0_, bf16[256,1024]{1,0:T(8,128)(2,1)} %copy-done.11, bf16[256,1024]{1,0:T(8,128)(2,1)} %copy-done.34, bf16[256,2816]{1,0:T(8,128)(2,1)} %copy-done, bf16[256,2816]{1,0:T(8,128)(2,1)} %copy-done.30), custom_call_target="tpu_custom_call" | custom-call | flops 1 | bytes 1 | tf_op jit(solution)/shard_map/staying_gradient/pallas_call | solution.py:393
  154.4 5.5 %attend_back.1 = bf16[8,32,1536]{2,1,0:T(8,128)(2,1)} custom-call(s32[7]{0:T(128)S(1)} %stack.49.refs_0_, s32[1,128]{1,0:T(1,128)S(1)} %select_n.46.refs_1_, s32[1,128]{1,0:T(1,128)S(1)} %collective-permute-done.refs_2_, bf16[8,32,1536]{2,1,0:T(8,128)(2,1)S(1)} %all-to-all-done.1.refs_3_, bf16[8,32,512]{2,1,0:T(8,128)(2,1)S(1)} %all-to-all-done.3.refs_4_), custom_call_target="tpu_custom_call" | custom-call | flops 1 | bytes 1 | tf_op jit(solution)/shard_map/attend_back/pallas_call | solution.py:393
  160.0 5.5 %all-to-all-start.4 = ((bf16[8,32,1536]{2,1,0:T(8,128)(2,1)}), bf16[8,32,1536]{2,1,0:T(8,128)(2,1)S(1)}, u32[]{:S(2)}, u32[]{:S(2)}) async-start(bf16[8,32,1536]{2,1,0:T(8,128)(2,1)} %attend_back.1), calls=%async_computation.4 | async-start | bytes 1572864 | tf_op jit(solution)/shard_map/all_to_all | solution.py:347
  165.6 0.6 collective-permute-start.25
  166.2 3.4 %grad_out.1 = f32[256,1024]{1,0:T(8,128)} custom-call(s32[7]{0:T(128)S(1)} %stack.49.refs_0_, bf16[256,512]{1,0:T(8,128)(2,1)} %copy-done.23, bf16[256,512]{1,0:T(8,128)(2,1)} %copy-done.37, bf16[256,1024]{1,0:T(8,128)(2,1)} %get-tuple-element.166.refs_3_, bf16[256,1024]{1,0:T(8,128)(2,1)} %collective-permute-done.22.refs_4_), custom_call_target="tpu_custom_call" | custom-call | flops 1 | bytes 1 | tf_op jit(solution)/shard_map/grad_out/pallas_call | solution.py:393
  169.6 4.7 %grad_down.1 = f32[704,1024]{1,0:T(8,128)} custom-call(s32[7]{0:T(128)S(1)} %stack.49.refs_0_, bf16[256,1408]{1,0:T(8,128)(2,1)S(1)} %copy-done.3, bf16[256,1408]{1,0:T(8,128)(2,1)S(1)} %copy-done.16, bf16[128,1024]{1,0:T(8,128)(2,1)S(1)} %copy-done.5, bf16[128,1024]{1,0:T(8,128)(2,1)S(1)} %copy-done.7, bf16[128,1024]{1,0:T(8,128)(2,1)S(1)} %copy-done.20, ...), custom_call_target="tpu_custom_call" | custom-call | flops 1 | bytes 1 | tf_op jit(solution)/shard_map/grad_down/pallas_call | solution.py:393
  174.3 10.2 %collective-permute-done.25.refs_7_ = bf16[128,1024]{1,0:T(8,128)(2,1)S(1)} collective-permute-done((bf16[128,1024]{1,0:T(8,128)(2,1)}, bf16[128,1024]{1,0:T(8,128)(2,1)S(1)}, u32[]{:S(2)}, u32[]{:S(2)}) %collective-permute-start.25) | collective-permute-done | bytes 262176 | tf_op jit(solution)/shard_map/ppermute | solution.py:337
  184.5 0.7 copy-done.24
  185.2 0.7 all-to-all-done.4.refs_5_
  185.9 4.1 %back_first.1 = (f32[128,1024]{1,0:T(8,128)S(1)}, bf16[128,1024]{1,0:T(8,128)(2,1)S(1)}, bf16[256,1536]{1,0:T(8,128)(2,1)S(1)}) custom-call(s32[7]{0:T(128)S(1)} %stack.49.refs_0_, bf16[256,3072]{1,0:T(8,128)(2,1)} %refs_1_.8, bf16[256,1536]{1,0:T(8,128)(2,1)} %collective-permute-done.3.refs_8_.refs_2_, bf16[256,1536]{1,0:T(8,128)(2,1)} %copy-done.32, ...), custom_call_target="tpu_custom_call" | custom-call | flops 1 | bytes 1 | tf_op jit(solution)/shard_map/back_first/pallas_call | solution.py:393
  190.1 0.9 collective-permute-start.26
  191.0 1.3 collective-permute-done.27.refs_4_
  192.3 0.9 copy-done.33
  193.2 3.9 %leaving_gradient.3 = bf16[256,1536]{1,0:T(8,128)(2,1)S(1)} custom-call(s32[7]{0:T(128)S(1)} %stack.49.refs_0_, bf16[256,1024]{1,0:T(8,128)(2,1)} %copy-done.10, bf16[256,1024]{1,0:T(8,128)(2,1)} %collective-permute-done.13.refs_2_, bf16[256,1536]{1,0:T(8,128)(2,1)} %copy-done.1, bf16[256,1536]{1,0:T(8,128)(2,1)} %copy-done.33), custom_call_target="tpu_custom_call" | custom-call | flops 1 | bytes 1 | tf_op jit(solution)/shard_map/leaving_gradient/pallas_call | solution.py:393
  197.1 1.7 collective-permute-done.26.refs_2_
  198.9 1.9 last.1
  200.7 6.0 %all-to-all-start.5 = ((bf16[8,32,1024]{2,1,0:T(8,128)(2,1)}), bf16[8,32,1024]{2,1,0:T(8,128)(2,1)S(1)}, u32[]{:S(2)}, u32[]{:S(2)}) async-start(bf16[8,32,1024]{2,1,0:T(8,128)(2,1)} %get-tuple-element.177), calls=%async_computation.5 | async-start | bytes 1048576 | tf_op jit(solution)/shard_map/all_to_all | solution.py:347
  206.7 0.9 collective-permute-start.30
  207.6 3.7 %coming_gradient.2 = f32[256,5632]{1,0:T(8,128)} custom-call(s32[7]{0:T(128)S(1)} %stack.49.refs_0_, bf16[256,2816]{1,0:T(8,128)(2,1)} %collective-permute-done.24.refs_1_, f32[256,5632]{1,0:T(8,128)} %staying_gradient.2.refs_2_), custom_call_target="tpu_custom_call", output_to_operand_aliasing={{}: (2, {})} | custom-call | flops 1 | bytes 1 | tf_op jit(solution)/shard_map/coming_gradient/pallas_call | solution.py:393
  211.3 5.1 %staying_gradient.3.refs_2_ = f32[256,3072]{1,0:T(8,128)} custom-call(s32[7]{0:T(128)S(1)} %stack.49.refs_0_, bf16[256,1024]{1,0:T(8,128)(2,1)} %copy-done.10, bf16[256,1024]{1,0:T(8,128)(2,1)} %collective-permute-done.13.refs_2_, bf16[256,1536]{1,0:T(8,128)(2,1)} %copy-done.1, bf16[256,1536]{1,0:T(8,128)(2,1)} %copy-done.33), custom_call_target="tpu_custom_call" | custom-call | flops 1 | bytes 1 | tf_op jit(solution)/shard_map/staying_gradient/pallas_call | solution.py:393
  216.5 2.1 collective-permute-done.28
  219.7 1.3 collective-permute-done.31
  221.6 0.7 all-to-all-done.5.refs_1_
  222.3 1.7 to_frames.1
  224.0 3.0 %coming_gradient.3 = f32[256,3072]{1,0:T(8,128)} custom-call(s32[7]{0:T(128)S(1)} %stack.49.refs_0_, bf16[256,1536]{1,0:T(8,128)(2,1)} %copy-done.36, f32[256,3072]{1,0:T(8,128)} %staying_gradient.3.refs_2_), custom_call_target="tpu_custom_call", output_to_operand_aliasing={{}: (2, {})} | custom-call | flops 1 | bytes 1 | tf_op jit(solution)/shard_map/coming_gradient/pallas_call | solution.py:393
  (138 shorter events, 8.4 us)
Async XLA Ops:
  2.4 20.5 %copy-start.39 = (bf16[256]{0:T(256)(128)(2,1)S(1)}, bf16[256]{0:T(256)(128)(2,1)}, u32[]{:S(2)}) copy-start(bf16[256]{0:T(256)(128)(2,1)} %param.11) | copy-start | bytes 1540
  2.5 20.5 %copy-start.40 = (bf16[256]{0:T(256)(128)(2,1)S(1)}, bf16[256]{0:T(256)(128)(2,1)}, u32[]{:S(2)}) copy-start(bf16[256]{0:T(256)(128)(2,1)} %param.14) | copy-start | bytes 1540
  2.5 23.1 %copy-start.38 = (s32[128]{0:T(128)S(1)}, s32[128]{0:T(128)}, u32[]{:S(2)}) copy-start(s32[128]{0:T(128)} %param.10) | copy-start | bytes 1540
  2.5 20.4 %collective-permute-start.2 = (bf16[256,1536]{1,0:T(8,128)(2,1)S(1)}, bf16[256,1536]{1,0:T(8,128)(2,1)S(1)}, u32[]{:S(2)}, u32[]{:S(2)}) collective-permute-start(bf16[256,1536]{1,0:T(8,128)(2,1)S(1)} %far_columns.1), channel_id=1, source_target_pairs={{0,3},{1,2},{2,1},{3,0},{4,7},{5,6},{6,5},{7,4},{8,11},{9,10},{10,... | collective-permute-start | bytes 2359304 | tf_op jit(solution)/shard_map/ppermute | solution.py:337
  7.6 22.4 %all-to-all-start = ((bf16[8,32,1024]{2,1,0:T(8,128)(2,1)}), bf16[8,32,1024]{2,1,0:T(8,128)(2,1)S(1)}, u32[]{:S(2)}, u32[]{:S(2)}) async-start(bf16[8,32,1024]{2,1,0:T(8,128)(2,1)} %to_positions.1), calls=%async_computation | async-start | bytes 1048576 | tf_op jit(solution)/shard_map/all_to_all | solution.py:347
  22.9 7.8 %copy-start.31 = (bf16[256,1536]{1,0:T(8,128)(2,1)}, bf16[256,1536]{1,0:T(8,128)(2,1)S(1)}, u32[]{:S(2)}) copy-start(bf16[256,1536]{1,0:T(8,128)(2,1)S(1)} %collective-permute-done.2.refs_10_.refs_4_) | copy-start | bytes 2359300
  22.9 7.2 %collective-permute-start.3 = (bf16[256,1536]{1,0:T(8,128)(2,1)S(1)}, bf16[256,1536]{1,0:T(8,128)(2,1)}, u32[]{:S(2)}, u32[]{:S(2)}) collective-permute-start(bf16[256,1536]{1,0:T(8,128)(2,1)S(1)} %collective-permute-done.2.refs_10_.refs_4_), channel_id=1, source_target_pairs={{0,1},{1,0},{2,3},{3,2},{4,5},{5,4},{6,7},{7,6},{8,9},{9,8},{10,11... | collective-permute-start | bytes 2359304 | tf_op jit(solution)/shard_map/ppermute | solution.py:337
  23.0 7.0 %collective-permute-start.1 = (bf16[2,256]{1,0:T(2,128)(2,1)S(1)}, bf16[2,256]{1,0:T(2,128)(2,1)S(1)}, u32[]{:S(2)}, u32[]{:S(2)}) collective-permute-start(bf16[2,256]{1,0:T(2,128)(2,1)S(1)} %pad_maximum_fusion.1.refs_3_), channel_id=1, source_target_pairs={{0,2},{1,3},{2,0},{3,1},{4,6},{5,7},{6,4},{7,5},{8,10},{9,11},{10,... | collective-permute-start | bytes 3080 | tf_op jit(solution)/shard_map/ppermute | solution.py:337
  26.5 3.6 %collective-permute-start = (s32[1,128]{1,0:T(1,128)S(1)}, s32[1,128]{1,0:T(1,128)S(1)}, u32[]{:S(2)}, u32[]{:S(2)}) collective-permute-start(s32[1,128]{1,0:T(1,128)S(1)} %select_n.46.refs_1_), channel_id=1, source_target_pairs={{0,2},{1,3},{2,0},{3,1},{4,6},{5,7},{6,4},{7,5},{8,10},{9,11},{10,... | collective-permute-start | bytes 1544 | tf_op jit(solution)/shard_map/ppermute | solution.py:337
  30.1 9.5 %collective-permute-start.6 = (bf16[256,1536]{1,0:T(8,128)(2,1)S(1)}, bf16[256,1536]{1,0:T(8,128)(2,1)S(1)}, u32[]{:S(2)}, u32[]{:S(2)}) collective-permute-start(bf16[256,1536]{1,0:T(8,128)(2,1)S(1)} %kept_columns.1), channel_id=1, source_target_pairs={{0,1},{1,0},{2,3},{3,2},{4,5},{5,4},{6,7},{7,6},{8,9},{9,8},{10,11... | collective-permute-start | bytes 2359304 | tf_op jit(solution)/shard_map/ppermute | solution.py:337
  30.7 8.8 %copy-start.8 = (bf16[128,1024]{1,0:T(8,128)(2,1)}, bf16[128,1024]{1,0:T(8,128)(2,1)S(1)}, u32[]{:S(2)}) copy-start(bf16[128,1024]{1,0:T(8,128)(2,1)S(1)} %get-tuple-element.107.refs_1_.refs_3_) | copy-start | bytes 786436
  30.8 47.6 %copy-start.4 = (bf16[128,1024]{1,0:T(8,128)(2,1)}, bf16[128,1024]{1,0:T(8,128)(2,1)S(1)}, u32[]{:S(2)}) copy-start(bf16[128,1024]{1,0:T(8,128)(2,1)S(1)} %get-tuple-element.127.refs_6_.refs_5_.refs_3_) | copy-start | bytes 786436
  30.8 8.8 %collective-permute-start.4 = (bf16[128,1024]{1,0:T(8,128)(2,1)S(1)}, bf16[128,1024]{1,0:T(8,128)(2,1)S(1)}, u32[]{:S(2)}, u32[]{:S(2)}) collective-permute-start(bf16[128,1024]{1,0:T(8,128)(2,1)S(1)} %get-tuple-element.107.refs_1_.refs_3_), channel_id=1, source_target_pairs={{0,2},{1,3},{2,0},{3,1},{4,6},{5,7},{6,4},{7,5},{8,10},{9,11},{10,... | collective-permute-start | bytes 786440 | tf_op jit(solution)/shard_map/ppermute | solution.py:337
  31.0 3.3 %collective-permute-start.5 = (bf16[2,2,256]{2,1,0:T(2,128)(2,1)S(1)}, bf16[2,2,256]{2,1,0:T(2,128)(2,1)S(1)}, u32[]{:S(2)}, u32[]{:S(2)}) collective-permute-start(bf16[2,2,256]{2,1,0:T(2,128)(2,1)S(1)} %pad_maximum_fusion), channel_id=1, source_target_pairs={{0,1},{1,0},{2,3},{3,2},{4,5},{5,4},{6,7},{7,6},{8,9},{9,8},{10,11... | collective-permute-start | bytes 6152 | tf_op jit(solution)/shard_map/ppermute | solution.py:337
  34.3 5.3 %copy-start.28 = (bf16[256,2816]{1,0:T(8,128)(2,1)}, bf16[256,2816]{1,0:T(8,128)(2,1)S(1)}, u32[]{:S(2)}) copy-start(bf16[256,2816]{1,0:T(8,128)(2,1)S(1)} %get-tuple-element.125) | copy-start | bytes 4325380
  34.3 10.6 %copy-start.12 = (bf16[256,2816]{1,0:T(8,128)(2,1)}, bf16[256,2816]{1,0:T(8,128)(2,1)S(1)}, u32[]{:S(2)}) copy-start(bf16[256,2816]{1,0:T(8,128)(2,1)S(1)} %get-tuple-element.120.refs_8_) | copy-start | bytes 4325380
  39.5 5.3 %copy-start.13 = (bf16[128,1024]{1,0:T(8,128)(2,1)}, bf16[128,1024]{1,0:T(8,128)(2,1)S(1)}, u32[]{:S(2)}) copy-start(bf16[128,1024]{1,0:T(8,128)(2,1)S(1)} %collective-permute-done.4.refs_2_) | copy-start | bytes 786436
  44.9 29.5 %copy-start.10 = (bf16[256,1024]{1,0:T(8,128)(2,1)}, bf16[256,1024]{1,0:T(8,128)(2,1)S(1)}, u32[]{:S(2)}) copy-start(bf16[256,1024]{1,0:T(8,128)(2,1)S(1)} %get-tuple-element.182.refs_1_) | copy-start | bytes 1572868
  44.9 29.5 %copy-start.26 = (f32[2,1024]{1,0:T(2,128)}, f32[2,1024]{1,0:T(2,128)S(1)}, u32[]{:S(2)}) copy-start(f32[2,1024]{1,0:T(2,128)S(1)} %get-tuple-element.138.refs_5_.refs_4_) | copy-start | bytes 24580
  44.9 26.9 %collective-permute-start.7 = (bf16[256,2816]{1,0:T(8,128)(2,1)S(1)}, bf16[256,2816]{1,0:T(8,128)(2,1)}, u32[]{:S(2)}, u32[]{:S(2)}) collective-permute-start(bf16[256,2816]{1,0:T(8,128)(2,1)S(1)} %get-tuple-element.120.refs_8_), channel_id=1, source_target_pairs={{0,1},{1,0},{2,3},{3,2},{4,5},{5,4},{6,7},{7,6},{8,9},{9,8},{10,11... | collective-permute-start | bytes 4325384 | tf_op jit(solution)/shard_map/ppermute | solution.py:337
  45.0 26.8 %collective-permute-start.9 = (bf16[704,1024]{1,0:T(8,128)(2,1)}, bf16[704,1024]{1,0:T(8,128)(2,1)}, u32[]{:S(2)}, u32[]{:S(2)}) collective-permute-start(bf16[704,1024]{1,0:T(8,128)(2,1)} %refs_3_.1), channel_id=1, source_target_pairs={{0,1},{1,0},{2,3},{3,2},{4,5},{5,4},{6,7},{7,6},{8,9},{9,8},{10,11... | collective-permute-start | bytes 4325384 | tf_op jit(solution)/shard_map/ppermute | solution.py:337
  45.7 26.0 %all-to-all-start.1 = ((bf16[8,32,1536]{2,1,0:T(8,128)(2,1)}), bf16[8,32,1536]{2,1,0:T(8,128)(2,1)S(1)}, u32[]{:S(2)}, u32[]{:S(2)}) async-start(bf16[8,32,1536]{2,1,0:T(8,128)(2,1)} %copy-done.14), calls=%async_computation.1 | async-start | bytes 1572864 | tf_op jit(solution)/shard_map/all_to_all | solution.py:347
  51.6 34.2 %collective-permute-start.10 = (bf16[256,2816]{1,0:T(8,128)(2,1)}, bf16[256,2816]{1,0:T(8,128)(2,1)}, u32[]{:S(2)}, u32[]{:S(2)}) collective-permute-start(bf16[256,2816]{1,0:T(8,128)(2,1)} %copy-done.28), channel_id=1, source_target_pairs={{0,3},{1,2},{2,1},{3,0},{4,7},{5,6},{6,5},{7,4},{8,11},{9,10},{10,... | collective-permute-start | bytes 4325384 | tf_op jit(solution)/shard_map/ppermute | solution.py:337
  51.6 2.5 %collective-permute-start.8 = (bf16[256,1024]{1,0:T(8,128)(2,1)}, bf16[256,1024]{1,0:T(8,128)(2,1)}, u32[]{:S(2)}, u32[]{:S(2)}) collective-permute-start(bf16[256,1024]{1,0:T(8,128)(2,1)} %refs_7_.3), channel_id=1, source_target_pairs={{0,1},{1,0},{2,3},{3,2},{4,5},{5,4},{6,7},{7,6},{8,9},{9,8},{10,11... | collective-permute-start | bytes 1572872 | tf_op jit(solution)/shard_map/ppermute | solution.py:337
  74.3 16.4 %collective-permute-start.13 = (bf16[256,1024]{1,0:T(8,128)(2,1)S(1)}, bf16[256,1024]{1,0:T(8,128)(2,1)}, u32[]{:S(2)}, u32[]{:S(2)}) collective-permute-start(bf16[256,1024]{1,0:T(8,128)(2,1)S(1)} %get-tuple-element.182.refs_1_), channel_id=1, source_target_pairs={{0,1},{1,0},{2,3},{3,2},{4,5},{5,4},{6,7},{7,6},{8,9},{9,8},{10,11... | collective-permute-start | bytes 1572872 | tf_op jit(solution)/shard_map/ppermute | solution.py:337
  74.4 16.3 %all-to-all-start.2 = ((bf16[8,32,512]{2,1,0:T(8,128)(2,1)}), bf16[8,32,512]{2,1,0:T(8,128)(2,1)S(1)}, u32[]{:S(2)}, u32[]{:S(2)}) async-start(bf16[8,32,512]{2,1,0:T(8,128)(2,1)} %attend.1), calls=%async_computation.2 | async-start | bytes 524288 | tf_op jit(solution)/shard_map/all_to_all | solution.py:347
  78.0 7.8 %collective-permute-start.12 = (bf16[128,1024]{1,0:T(8,128)(2,1)S(1)}, bf16[128,1024]{1,0:T(8,128)(2,1)S(1)}, u32[]{:S(2)}, u32[]{:S(2)}) collective-permute-start(bf16[128,1024]{1,0:T(8,128)(2,1)S(1)} %get-tuple-element.127.refs_6_.refs_5_.refs_3_), channel_id=1, source_target_pairs={{0,1},{1,0},{2,3},{3,2},{4,5},{5,4},{6,7},{7,6},{8,9},{9,8},{10,11... | collective-permute-start | bytes 786440 | tf_op jit(solution)/shard_map/ppermute | solution.py:337
  78.4 12.3 %collective-permute-start.11 = (bf16[128,1024]{1,0:T(8,128)(2,1)S(1)}, bf16[128,1024]{1,0:T(8,128)(2,1)S(1)}, u32[]{:S(2)}, u32[]{:S(2)}) collective-permute-start(bf16[128,1024]{1,0:T(8,128)(2,1)S(1)} %get-tuple-element.127.refs_6_.refs_5_.refs_3_), channel_id=1, source_target_pairs={{0,2},{1,3},{2,0},{3,1},{4,6},{5,7},{6,4},{7,5},{8,10},{9,11},{10,... | collective-permute-start | bytes 786440 | tf_op jit(solution)/shard_map/ppermute | solution.py:337
  85.8 21.6 %copy-start.19 = (bf16[128,1024]{1,0:T(8,128)(2,1)}, bf16[128,1024]{1,0:T(8,128)(2,1)S(1)}, u32[]{:S(2)}) copy-start(bf16[128,1024]{1,0:T(8,128)(2,1)S(1)} %collective-permute-done.12.refs_5_) | copy-start | bytes 786436
  90.7 16.7 %copy-start.6 = (bf16[128,1024]{1,0:T(8,128)(2,1)}, bf16[128,1024]{1,0:T(8,128)(2,1)S(1)}, u32[]{:S(2)}) copy-start(bf16[128,1024]{1,0:T(8,128)(2,1)S(1)} %collective-permute-done.11.refs_7_.refs_6_.refs_4_) | copy-start | bytes 786436
  93.0 14.4 %copy-start.23 = (bf16[256,512]{1,0:T(8,128)(2,1)}, bf16[256,512]{1,0:T(8,128)(2,1)S(1)}, u32[]{:S(2)}) copy-start(bf16[256,512]{1,0:T(8,128)(2,1)S(1)} %get-tuple-element.132.refs_1_) | copy-start | bytes 786436
  93.0 14.4 %collective-permute-start.16 = (bf16[256,2816]{1,0:T(8,128)(2,1)}, bf16[256,2816]{1,0:T(8,128)(2,1)S(1)}, u32[]{:S(2)}, u32[]{:S(2)}) collective-permute-start(bf16[256,2816]{1,0:T(8,128)(2,1)} %collective-permute-done.10.refs_11_), channel_id=1, source_target_pairs={{0,1},{1,0},{2,3},{3,2},{4,5},{5,4},{6,7},{7,6},{8,9},{9,8},{10,11... | collective-permute-start | bytes 4325384 | tf_op jit(solution)/shard_map/ppermute | solution.py:337
  93.2 14.2 %collective-permute-start.14 = (bf16[256,1024]{1,0:T(8,128)(2,1)S(1)}, bf16[256,1024]{1,0:T(8,128)(2,1)S(1)}, u32[]{:S(2)}, u32[]{:S(2)}) collective-permute-start(bf16[256,1024]{1,0:T(8,128)(2,1)S(1)} %get-tuple-element.131), channel_id=1, source_target_pairs={{0,2},{1,3},{2,0},{3,1},{4,6},{5,7},{6,4},{7,5},{8,10},{9,11},{10,... | collective-permute-start | bytes 1572872 | tf_op jit(solution)/shard_map/ppermute | solution.py:337
  94.2 2.6 %collective-permute-start.17 = (bf16[128,1024]{1,0:T(8,128)(2,1)S(1)}, bf16[128,1024]{1,0:T(8,128)(2,1)S(1)}, u32[]{:S(2)}, u32[]{:S(2)}) collective-permute-start(bf16[128,1024]{1,0:T(8,128)(2,1)S(1)} %collective-permute-done.11.refs_7_.refs_6_.refs_4_), channel_id=1, source_target_pairs={{0,1},{1,0},{2,3},{3,2},{4,5},{5,4},{6,7},{7,6},{8,9},{9,8},{10,11... | collective-permute-start | bytes 786440 | tf_op jit(solution)/shard_map/ppermute | solution.py:337
  94.4 3.2 %collective-permute-start.15 = (bf16[256,512]{1,0:T(8,128)(2,1)S(1)}, bf16[256,512]{1,0:T(8,128)(2,1)S(1)}, u32[]{:S(2)}, u32[]{:S(2)}) collective-permute-start(bf16[256,512]{1,0:T(8,128)(2,1)S(1)} %get-tuple-element.132.refs_1_), channel_id=1, source_target_pairs={{0,1},{1,0},{2,3},{3,2},{4,5},{5,4},{6,7},{7,6},{8,9},{9,8},{10,11... | collective-permute-start | bytes 786440 | tf_op jit(solution)/shard_map/ppermute | solution.py:337
  97.6 9.9 %copy-start.37 = (bf16[256,512]{1,0:T(8,128)(2,1)}, bf16[256,512]{1,0:T(8,128)(2,1)S(1)}, u32[]{:S(2)}) copy-start(bf16[256,512]{1,0:T(8,128)(2,1)S(1)} %collective-permute-done.15.refs_2_) | copy-start | bytes 786436
  119.2 6.0 %copy-start = (bf16[256,2816]{1,0:T(8,128)(2,1)}, bf16[256,2816]{1,0:T(8,128)(2,1)S(1)}, u32[]{:S(2)}) copy-start(bf16[256,2816]{1,0:T(8,128)(2,1)S(1)} %get-tuple-element.151.refs_3_) | copy-start | bytes 4325380
  119.2 6.0 %copy-start.11 = (bf16[256,1024]{1,0:T(8,128)(2,1)}, bf16[256,1024]{1,0:T(8,128)(2,1)S(1)}, u32[]{:S(2)}) copy-start(bf16[256,1024]{1,0:T(8,128)(2,1)S(1)} %get-tuple-element.156.refs_1_) | copy-start | bytes 1572868
  119.3 6.7 %collective-permute-start.20 = (bf16[256,2816]{1,0:T(8,128)(2,1)S(1)}, bf16[256,2816]{1,0:T(8,128)(2,1)S(1)}, u32[]{:S(2)}, u32[]{:S(2)}) collective-permute-start(bf16[256,2816]{1,0:T(8,128)(2,1)S(1)} %get-tuple-element.151.refs_3_), channel_id=1, source_target_pairs={{0,1},{1,0},{2,3},{3,2},{4,5},{5,4},{6,7},{7,6},{8,9},{9,8},{10,11... | collective-permute-start | bytes 4325384 | tf_op jit(solution)/shard_map/ppermute | solution.py:337
  119.3 14.8 %collective-permute-start.21 = (bf16[256,1408]{1,0:T(8,128)(2,1)S(1)}, bf16[256,1408]{1,0:T(8,128)(2,1)S(1)}, u32[]{:S(2)}, u32[]{:S(2)}) collective-permute-start(bf16[256,1408]{1,0:T(8,128)(2,1)S(1)} %get-tuple-element.161.refs_1_), channel_id=1, source_target_pairs={{0,1},{1,0},{2,3},{3,2},{4,5},{5,4},{6,7},{7,6},{8,9},{9,8},{10,11... | collective-permute-start | bytes 2162696 | tf_op jit(solution)/shard_map/ppermute | solution.py:337
  119.8 5.4 %collective-permute-start.19 = (bf16[256,1024]{1,0:T(8,128)(2,1)S(1)}, bf16[256,1024]{1,0:T(8,128)(2,1)S(1)}, u32[]{:S(2)}, u32[]{:S(2)}) collective-permute-start(bf16[256,1024]{1,0:T(8,128)(2,1)S(1)} %get-tuple-element.156.refs_1_), channel_id=1, source_target_pairs={{0,1},{1,0},{2,3},{3,2},{4,5},{5,4},{6,7},{7,6},{8,9},{9,8},{10,11... | collective-permute-start | bytes 1572872 | tf_op jit(solution)/shard_map/ppermute | solution.py:337
  119.9 14.3 %collective-permute-start.18 = (bf16[256,1024]{1,0:T(8,128)(2,1)S(1)}, bf16[256,1024]{1,0:T(8,128)(2,1)S(1)}, u32[]{:S(2)}, u32[]{:S(2)}) collective-permute-start(bf16[256,1024]{1,0:T(8,128)(2,1)S(1)} %get-tuple-element.143), channel_id=1, source_target_pairs={{0,2},{1,3},{2,0},{3,1},{4,6},{5,7},{6,4},{7,5},{8,10},{9,11},{10,... | collective-permute-start | bytes 1572872 | tf_op jit(solution)/shard_map/ppermute | solution.py:337
  139.4 15.1 %collective-permute-start.22 = (bf16[256,1024]{1,0:T(8,128)(2,1)}, bf16[256,1024]{1,0:T(8,128)(2,1)}, u32[]{:S(2)}, u32[]{:S(2)}) collective-permute-start(bf16[256,1024]{1,0:T(8,128)(2,1)} %get-tuple-element.166.refs_3_), channel_id=1, source_target_pairs={{0,1},{1,0},{2,3},{3,2},{4,5},{5,4},{6,7},{7,6},{8,9},{9,8},{10,11... | collective-permute-start | bytes 1572872 | tf_op jit(solution)/shard_map/ppermute | solution.py:337
  139.4 15.1 %all-to-all-start.3 = ((bf16[8,32,512]{2,1,0:T(8,128)(2,1)}), bf16[8,32,512]{2,1,0:T(8,128)(2,1)S(1)}, u32[]{:S(2)}, u32[]{:S(2)}) async-start(bf16[8,32,512]{2,1,0:T(8,128)(2,1)} %get-tuple-element.153), calls=%async_computation.3 | async-start | bytes 524288 | tf_op jit(solution)/shard_map/all_to_all | solution.py:347
  145.0 40.2 %collective-permute-start.24 = (bf16[256,2816]{1,0:T(8,128)(2,1)S(1)}, bf16[256,2816]{1,0:T(8,128)(2,1)}, u32[]{:S(2)}, u32[]{:S(2)}) collective-permute-start(bf16[256,2816]{1,0:T(8,128)(2,1)S(1)} %leaving_gradient.2), channel_id=1, source_target_pairs={{0,3},{1,2},{2,1},{3,0},{4,7},{5,6},{6,5},{7,4},{8,11},{9,10},{10,... | collective-permute-start | bytes 4325384 | tf_op jit(solution)/shard_map/ppermute | solution.py:337
  146.3 7.6 %collective-permute-start.23 = (f32[1,256]{1,0:T(1,128)S(1)}, f32[1,256]{1,0:T(1,128)S(1)}, u32[]{:S(2)}, u32[]{:S(2)}) collective-permute-start(f32[1,256]{1,0:T(1,128)S(1)} %slice_bitcast_fusion.2), channel_id=1, source_target_pairs={{0,1},{1,0},{2,3},{3,2},{4,5},{5,4},{6,7},{7,6},{8,9},{9,8},{10,11... | collective-permute-start | bytes 3080 | tf_op jit(solution)/shard_map/ppermute | solution.py:337
  160.0 25.9 %all-to-all-start.4 = ((bf16[8,32,1536]{2,1,0:T(8,128)(2,1)}), bf16[8,32,1536]{2,1,0:T(8,128)(2,1)S(1)}, u32[]{:S(2)}, u32[]{:S(2)}) async-start(bf16[8,32,1536]{2,1,0:T(8,128)(2,1)} %attend_back.1), calls=%async_computation.4 | async-start | bytes 1572864 | tf_op jit(solution)/shard_map/all_to_all | solution.py:347
  165.5 4.0 %copy-start.5 = (bf16[128,1024]{1,0:T(8,128)(2,1)S(1)}, bf16[128,1024]{1,0:T(8,128)(2,1)}, u32[]{:S(2)}) copy-start(bf16[128,1024]{1,0:T(8,128)(2,1)} %copy-done.4) | copy-start | bytes 786436
  165.5 4.0 %copy-start.7 = (bf16[128,1024]{1,0:T(8,128)(2,1)S(1)}, bf16[128,1024]{1,0:T(8,128)(2,1)}, u32[]{:S(2)}) copy-start(bf16[128,1024]{1,0:T(8,128)(2,1)} %copy-done.6) | copy-start | bytes 786436
  165.5 4.0 %copy-start.16 = (bf16[256,1408]{1,0:T(8,128)(2,1)S(1)}, bf16[256,1408]{1,0:T(8,128)(2,1)}, u32[]{:S(2)}) copy-start(bf16[256,1408]{1,0:T(8,128)(2,1)} %copy-done.15) | copy-start | bytes 2162692
  165.5 4.0 %copy-start.20 = (bf16[128,1024]{1,0:T(8,128)(2,1)S(1)}, bf16[128,1024]{1,0:T(8,128)(2,1)}, u32[]{:S(2)}) copy-start(bf16[128,1024]{1,0:T(8,128)(2,1)} %copy-done.19) | copy-start | bytes 786436
  165.6 4.0 %copy-start.22 = (bf16[128,1024]{1,0:T(8,128)(2,1)S(1)}, bf16[128,1024]{1,0:T(8,128)(2,1)}, u32[]{:S(2)}) copy-start(bf16[128,1024]{1,0:T(8,128)(2,1)} %copy-done.21) | copy-start | bytes 786436
  165.6 18.9 %collective-permute-start.25 = (bf16[128,1024]{1,0:T(8,128)(2,1)}, bf16[128,1024]{1,0:T(8,128)(2,1)S(1)}, u32[]{:S(2)}, u32[]{:S(2)}) collective-permute-start(bf16[128,1024]{1,0:T(8,128)(2,1)} %copy-done.29), channel_id=1, source_target_pairs={{0,2},{1,3},{2,0},{3,1},{4,6},{5,7},{6,4},{7,5},{8,10},{9,11},{10,... | collective-permute-start | bytes 786440 | tf_op jit(solution)/shard_map/ppermute | solution.py:337
  190.0 2.4 %collective-permute-start.27 = (bf16[256,1536]{1,0:T(8,128)(2,1)S(1)}, bf16[256,1536]{1,0:T(8,128)(2,1)S(1)}, u32[]{:S(2)}, u32[]{:S(2)}) collective-permute-start(bf16[256,1536]{1,0:T(8,128)(2,1)S(1)} %get-tuple-element.172.refs_3_), channel_id=1, source_target_pairs={{0,1},{1,0},{2,3},{3,2},{4,5},{5,4},{6,7},{7,6},{8,9},{9,8},{10,11... | collective-permute-start | bytes 2359304 | tf_op jit(solution)/shard_map/ppermute | solution.py:337
  190.0 8.8 %copy-start.9 = (bf16[128,1024]{1,0:T(8,128)(2,1)S(1)}, bf16[128,1024]{1,0:T(8,128)(2,1)}, u32[]{:S(2)}) copy-start(bf16[128,1024]{1,0:T(8,128)(2,1)} %copy-done.8) | copy-start | bytes 786436
  190.0 8.8 %copy-start.18 = (f32[128,1024]{1,0:T(8,128)S(1)}, f32[128,1024]{1,0:T(8,128)}, u32[]{:S(2)}) copy-start(f32[128,1024]{1,0:T(8,128)} %copy-done.17) | copy-start | bytes 1572868
  190.1 8.8 %copy-start.25 = (bf16[128,1024]{1,0:T(8,128)(2,1)S(1)}, bf16[128,1024]{1,0:T(8,128)(2,1)}, u32[]{:S(2)}) copy-start(bf16[128,1024]{1,0:T(8,128)(2,1)} %copy-done.24) | copy-start | bytes 786436
  190.1 8.8 %copy-start.27 = (f32[2,1024]{1,0:T(2,128)S(1)}, f32[2,1024]{1,0:T(2,128)}, u32[]{:S(2)}) copy-start(f32[2,1024]{1,0:T(2,128)} %copy-done.26) | copy-start | bytes 24580
  190.1 8.7 %collective-permute-start.26 = (bf16[128,1024]{1,0:T(8,128)(2,1)S(1)}, bf16[128,1024]{1,0:T(8,128)(2,1)S(1)}, u32[]{:S(2)}, u32[]{:S(2)}) collective-permute-start(bf16[128,1024]{1,0:T(8,128)(2,1)S(1)} %get-tuple-element.170), channel_id=1, source_target_pairs={{0,2},{1,3},{2,0},{3,1},{4,6},{5,7},{6,4},{7,5},{8,10},{9,11},{10,... | collective-permute-start | bytes 786440 | tf_op jit(solution)/shard_map/ppermute | solution.py:337
  198.8 19.8 %collective-permute-start.28 = (bf16[256,1536]{1,0:T(8,128)(2,1)S(1)}, bf16[256,1536]{1,0:T(8,128)(2,1)}, u32[]{:S(2)}, u32[]{:S(2)}) collective-permute-start(bf16[256,1536]{1,0:T(8,128)(2,1)S(1)} %leaving_gradient.3), channel_id=1, source_target_pairs={{0,3},{1,2},{2,1},{3,0},{4,7},{5,6},{6,5},{7,4},{8,11},{9,10},{10,... | collective-permute-start | bytes 2359304 | tf_op jit(solution)/shard_map/ppermute | solution.py:337
  200.7 21.6 %all-to-all-start.5 = ((bf16[8,32,1024]{2,1,0:T(8,128)(2,1)}), bf16[8,32,1024]{2,1,0:T(8,128)(2,1)S(1)}, u32[]{:S(2)}, u32[]{:S(2)}) async-start(bf16[8,32,1024]{2,1,0:T(8,128)(2,1)} %get-tuple-element.177), calls=%async_computation.5 | async-start | bytes 1048576 | tf_op jit(solution)/shard_map/all_to_all | solution.py:347
  206.7 11.8 %collective-permute-start.30 = (f32[2,1,256]{2,1,0:T(1,128)S(1)}, f32[2,1,256]{2,1,0:T(1,128)S(1)}, u32[]{:S(2)}, u32[]{:S(2)}) collective-permute-start(f32[2,1,256]{2,1,0:T(1,128)S(1)} %slice.28), channel_id=1, source_target_pairs={{0,2},{1,3},{2,0},{3,1},{4,6},{5,7},{6,4},{7,5},{8,10},{9,11},{10,... | collective-permute-start | bytes 6152 | tf_op jit(solution)/shard_map/ppermute | solution.py:337
  218.6 3.8 %collective-permute-start.29 = (bf16[256,1536]{1,0:T(8,128)(2,1)}, bf16[256,1536]{1,0:T(8,128)(2,1)S(1)}, u32[]{:S(2)}, u32[]{:S(2)}) collective-permute-start(bf16[256,1536]{1,0:T(8,128)(2,1)} %collective-permute-done.28), channel_id=1, source_target_pairs={{0,1},{1,0},{2,3},{3,2},{4,5},{5,4},{6,7},{7,6},{8,9},{9,8},{10,11... | collective-permute-start | bytes 2359304 | tf_op jit(solution)/shard_map/ppermute | solution.py:337
  218.6 2.5 %collective-permute-start.31 = (f32[1,256]{1,0:T(1,128)S(1)}, f32[1,256]{1,0:T(1,128)S(1)}, u32[]{:S(2)}, u32[]{:S(2)}) collective-permute-start(f32[1,256]{1,0:T(1,128)S(1)} %slice_bitcast_fusion), channel_id=1, source_target_pairs={{0,1},{1,0},{2,3},{3,2},{4,5},{5,4},{6,7},{7,6},{8,9},{9,8},{10,11... | collective-permute-start | bytes 3080 | tf_op jit(solution)/shard_map/ppermute | solution.py:337
  (15 other events, 19.4 us)

commit v4 on v3

--- a/solution.py
+++ b/solution.py
@@ -327,9 +327,11 @@
 HBM = pl.BlockSpec(memory_space=pltpu.HBM)
 STAGED = pl.BlockSpec(memory_space=pltpu.HBM)
 MOVED = pl.BlockSpec(memory_space=pl.ANY)
+EITHER = pl.BlockSpec(memory_space=pl.ANY)
 BF16 = jnp.bfloat16
 F32 = jnp.float32
 OWN, FAR, NEAR, ACROSS, SIDE, CORE, POSITION = range(7)
+TAIL = 16
 
 
 def swap(block, mask):
@@ -350,7 +352,7 @@
     ]
 
 
-def kernel_call(kernel, name, args, outs, scratch=(), out_spec=None, aliases=()):
+def kernel_call(kernel, name, args, outs, scratch=(), aliases=()):
     flat = lambda items: [p for item in items for p in (item if isinstance(item, list) else [item])]
     staged = [n for n, (spec, _) in enumerate(flat(args)) if spec is STAGED or spec is MOVED]
     arrays = [
@@ -394,10 +396,9 @@
         body_kernel,
         name=name,
         in_specs=[spec for spec, _ in flat(args)],
-        out_specs=[out_spec or VMEM] * len(flat(outs)),
+        out_specs=[spec[0] if spec else VMEM for _, _, *spec in flat(outs)],
         out_shape=[
-            pltpu.HBM(s, d) if out_spec is HBM else jax.ShapeDtypeStruct(s, d)
-            for s, d in flat(outs)
+            pltpu.HBM(s, d) if spec else jax.ShapeDtypeStruct(s, d) for s, d, *spec in flat(outs)
         ],
         input_output_aliases=dict(aliases),
         scratch_shapes=scratch,
@@ -459,39 +460,75 @@
     return (column == (row % frames) * POS + ((row // frames) ^ position)).astype(F32).astype(BF16)
 
 
-def to_positions_kernel(ready, place, x_rows, c_rows, blocks):
-    blocks = views(blocks, place)
+def to_positions_kernel(ready, place, x_rows, c_rows, weight, x_blocks, c_blocks, half, sems):
+    copies = side_columns(weight, half, 1 - place[SIDE], sems)
+    for copy in copies:
+        copy.start()
     order = place_matrix(x_rows.shape[0], True, place[POSITION])
     ready()
-    for rel, rows in enumerate((x_rows, c_rows)):
-        put_rows(blocks, rel, slice(None), matmul(order, rows[...]).astype(BF16))
-
-
-def to_positions(place, x_rows, c_rows):
+    for rows, blocks in ((x_rows, x_blocks), (c_rows, c_blocks)):
+        moved_rows = matmul(order, rows[...]).astype(BF16)
+        count = rows.shape[0] // POS
+        for k, block in enumerate(views(blocks, place)):
+            block[...] = moved_rows[k * count : (k + 1) * count]
+    for copy in copies:
+        copy.wait()
+
+
+def to_positions(place, x_rows, c_rows, weight):
     size, width = x_rows.shape
     return kernel_call(
         to_positions_kernel,
         "to_positions",
-        [(SMEM, place)] + in_stage(x_rows, c_rows),
-        [block_shapes(2 * size, width, True)],
+        [(SMEM, place)] + in_stage(x_rows, c_rows) + [(HBM, weight)],
+        [block_shapes(size, width, True), block_shapes(size, width, True),
+         ((weight.shape[0], weight.shape[1] // 2), BF16)],
+        [pltpu.SemaphoreType.DMA((3,))],
+    )
+
+
+def joined(blocks, place):
+    return jnp.concatenate([block[...] for block in views(blocks, place)], 0)
+
+
+def collect_rows_kernel(ready, place, blocks, rows):
+    ready()
+    rows[...] = joined(blocks, place)
+
+
+def collect_rows(place, blocks):
+    count, width = blocks[0].shape[-2:]
+    return kernel_call(
+        collect_rows_kernel,
+        "collect_rows",
+        [(SMEM, place), in_vmem(*blocks)],
+        [((count * POS, width), BF16)],
     )[0]
 
 
-def collect_kernel(ready, place, blocks, x_own, c_own):
-    ready()
-    blocks = views(blocks, place)
-    x_own[...] = rows_of(blocks, 0)
-    c_own[...] = rows_of(blocks, 1)
-
-
-def collect(place, blocks):
-    rows, width = blocks[0].shape[-2:]
+def collect_kernel(ready, place, blocks, ids, gains_own, gains_near, x_own):
+    ready()
+    half = x_own.shape[0] - TAIL
+    x_own[:half, :] = joined(blocks, place)
+    padded = lambda *parts: jnp.concatenate(
+        parts + (jnp.zeros((1, D - sum(p.shape[1] for p in parts)), F32),), 1
+    )
+    row = lax.broadcasted_iota(jnp.int32, (TAIL, D), 0)
+    tail = jnp.where(row == 2, padded(ids[...].astype(F32)), 0.0)
+    for k in range(2):
+        gain = padded(gains_own[k : k + 1, :].astype(F32), gains_near[k : k + 1, :].astype(F32))
+        tail = jnp.where(row == k, gain, tail)
+    x_own[half:, :] = tail.astype(BF16)
+
+
+def collect(place, blocks, ids, gains_own, gains_near):
+    count, width = blocks[0].shape[-2:]
     return kernel_call(
         collect_kernel,
         "collect",
-        [(SMEM, place), in_vmem(*blocks)],
-        [((rows * POS // 2, width), BF16)] * 2,
-    )
+        [(SMEM, place), in_vmem(*blocks)] + in_vmem(ids, gains_own, gains_near),
+        [((count * POS + TAIL, width), BF16)],
+    )[0]
 
 
 def to_frames_kernel(ready, place, blocks, *rows):
@@ -513,11 +550,11 @@
 
 
 def first_kernel(
-    ready, place, x_a, x_b, gains_own, gains_far, gains_near, gains_across, w_own, w_far, w_near, w_across,
-    qkv, lowered, gains, w, sems,
+    ready, place, x_a, x_b, w_own, w_far, w_near, w_across, qkv, lowered_out, table_out,
+    lowered, table, w, sems,
 ):
     qkv = views(qkv, place)
-    half, width = x_a.shape[0], w_own.shape[0]
+    half, width = lowered.shape[0] // 2, w_own.shape[0]
     part = w.shape[1] // 3
     side = place[SIDE]
     at_rows = lambda rank: aligned(place[rank] * width, width)
@@ -535,15 +572,23 @@
     for copy in copies:
         copy.start()
     ready()
-    gains[:, at_rows(OWN)] = gains_own[...].astype(F32)
-    gains[:, at_rows(FAR)] = gains_far[...].astype(F32)
-    gains[:, at_rows(NEAR)] = gains_near[...].astype(F32)
-    gains[:, at_rows(ACROSS)] = gains_across[...].astype(F32)
-    gain = gains[0:1, :]
+    table[...] = jnp.zeros_like(table)
+    for k, (ref, ranks) in enumerate(((x_a, (OWN, NEAR)), (x_b, (FAR, ACROSS)))):
+        tail = ref[half:, :].astype(F32)
+        for n, rank in enumerate(ranks):
+            table[0:2, at_rows(rank)] = tail[0:2, n * width : (n + 1) * width]
+        table[2 + k : 3 + k, 0:half] = tail[2:3, 0:half]
+    gain = table[0:1, :]
     for rel, ref in enumerate((x_a, x_b)):
-        rows = ref[...].astype(F32)
+        rows = ref[:half, :].astype(F32)
         scale = lax.rsqrt(jnp.mean(rows * rows, axis=-1, keepdims=True) + EPSILON)
         lowered[rel * half : (rel + 1) * half, :] = (rows * scale * gain).astype(BF16)
+    leaving = [
+        pltpu.make_async_copy(lowered, lowered_out, sems.at[6]),
+        pltpu.make_async_copy(table, table_out, sems.at[7]),
+    ]
+    for copy in leaving:
+        copy.start()
     for copy in copies:
         copy.wait()
 
@@ -555,21 +600,21 @@
         return carry
 
     lax.fori_loop(0, w.shape[1] // 256, step, 0)
-
-
-def first(
-    place, x_a, x_b, gains_own, gains_far, gains_near, gains_across, w_own, w_far, w_near, w_across
-):
-    half = x_a.shape[0]
+    for copy in leaving:
+        copy.wait()
+
+
+def first(place, x_a, x_b, w_own, w_far, w_near, w_across):
+    half = x_a.shape[0] - TAIL
     wide = w_far.shape[1]
     return kernel_call(
         first_kernel,
         "first",
-        [(SMEM, place), (MOVED, x_a), (MOVED, x_b), (VMEM, gains_own), (VMEM, gains_far),
-         (VMEM, gains_near), (VMEM, gains_across), (HBM, w_own), (HBM, w_far), (HBM, w_near),
-         (HBM, w_across)],
-        [block_shapes(2 * half, wide, True), ((2 * half, D), BF16), ((2, D), F32)],
-        [pltpu.VMEM((D, wide), BF16), pltpu.SemaphoreType.DMA((6,))],
+        [(SMEM, place), (MOVED, x_a), (MOVED, x_b), (HBM, w_own), (EITHER, w_far),
+         (EITHER, w_near), (EITHER, w_across)],
+        [block_shapes(2 * half, wide, True), ((2 * half, D), BF16, HBM), ((8, D), F32, HBM)],
+        [pltpu.VMEM((2 * half, D), BF16), pltpu.VMEM((8, D), F32), pltpu.VMEM((D, wide), BF16),
+         pltpu.SemaphoreType.DMA((8,))],
     )
 
 
@@ -578,7 +623,7 @@
     frames = size // POS
     row = lax.broadcasted_iota(jnp.int32, (size, size), 0)
     column = lax.broadcasted_iota(jnp.int32, (size, size), 1)
-    across = jnp.broadcast_to(ids.astype(F32), (size, size))
+    across = jnp.broadcast_to(ids, (size, size))
     same = (across == across.T) & (row % frames == column % frames)
     mask = same & ((column // frames) ^ position <= (row // frames) ^ position)
     return jnp.concatenate([mask, mask], 1)
@@ -609,13 +654,14 @@
     return (lane < HEAD_DIM).astype(F32).astype(BF16)
 
 
-def attend_kernel(ready, place, ids_a, ids_b, qkv, mixed):
+def attend_kernel(ready, place, table, qkv, mixed):
     qkv, mixed = views(qkv, place), views(mixed, place)
+    size = POS * mixed[0].shape[0] // 2
     part = mixed[0].shape[1]
     low = first_head_lanes()
     ready()
-    for rel, ids in enumerate((ids_a, ids_b)):
-        mask = allowed_pairs(ids[...], place[POSITION])
+    for rel in range(2):
+        mask = allowed_pairs(table[2 + rel : 3 + rel, 0:size], place[POSITION])
         for base in range(0, part, 2 * HEAD_DIM):
             query, key_rows, value_rows = (
                 rows_of(qkv, rel, slice(k * part + base, k * part + base + 2 * HEAD_DIM))
@@ -626,17 +672,17 @@
             put_rows(mixed, rel, slice(base, base + 2 * HEAD_DIM), value.astype(BF16))
 
 
-def attend_local(place, ids_a, ids_b, qkv):
+def attend_local(place, table, qkv):
     rows, wide = qkv[0].shape[-2:]
     return kernel_call(
         attend_kernel,
         "attend",
-        [(SMEM, place), (MOVED, ids_a), (MOVED, ids_b), moved(*qkv)],
+        [(SMEM, place), (MOVED, table), moved(*qkv)],
         [block_shapes(rows * POS, wide // 3, True)],
     )[0]
 
 
-def attend_back_kernel(ready, place, ids_a, ids_b, qkv, d_mixed, d_qkv):
+def attend_back_kernel(ready, place, table, qkv, d_mixed, d_qkv):
     qkv, d_mixed, d_qkv = (views(blocks, place) for blocks in (qkv, d_mixed, d_qkv))
     part = d_mixed[0].shape[1]
     pair = 2 * HEAD_DIM
@@ -645,8 +691,8 @@
     low_full = lax.broadcasted_iota(jnp.int32, (size, pair), 1) < HEAD_DIM
     scale = HEAD_DIM ** (-0.5)
     ready()
-    for rel, ids in enumerate((ids_a, ids_b)):
-        mask = allowed_pairs(ids[...], place[POSITION])
+    for rel in range(2):
+        mask = allowed_pairs(table[2 + rel : 3 + rel, 0:size], place[POSITION])
         for base in range(0, part, pair):
             query, key_rows, value_rows = (
                 rows_of(qkv, rel, slice(k * part + base, k * part + base + pair))
@@ -668,12 +714,12 @@
                 put_rows(d_qkv, rel, columns, value.astype(BF16))
 
 
-def attend_back_local(place, ids_a, ids_b, qkv, d_mixed):
+def attend_back_local(place, table, qkv, d_mixed):
     rows, wide = qkv[0].shape[-2:]
     return kernel_call(
         attend_back_kernel,
         "attend_back",
-        [(SMEM, place), (MOVED, ids_a), (MOVED, ids_b), moved(*qkv), in_vmem(*d_mixed)],
+        [(SMEM, place), (MOVED, table), moved(*qkv), in_vmem(*d_mixed)],
         [block_shapes(rows * POS, wide, True)],
     )[0]
 
@@ -718,13 +764,38 @@
     )
 
 
+def d_hidden_kernel(ready, place, c_a, c_b, w_own, w_near, d_hidden, w, sems):
+    copies = chip_rows(place, w_own, w_near, w, sems)
+    for copy in copies:
+        copy.start()
+    ready()
+    upstream = jnp.concatenate([c_a[...], c_b[...]], 0)
+    for copy in copies:
+        copy.wait()
+    inner = w.shape[0]
+    for base in range(0, inner, 256):
+        end = min(base + 256, inner)
+        d_hidden[:, base:end] = times_transposed(upstream, w[base:end, :])
+
+
+def d_hidden_rows(place, c_a, c_b, w_own, w_near):
+    rows, inner = 2 * c_a.shape[0], 2 * w_own.shape[0]
+    return kernel_call(
+        d_hidden_kernel,
+        "d_hidden",
+        [(SMEM, place), (MOVED, c_a), (MOVED, c_b), (HBM, w_own), (HBM, w_near)],
+        [((rows, inner), F32)],
+        [pltpu.VMEM((inner, D), BF16), pltpu.SemaphoreType.DMA((2,))],
+    )[0]
+
+
 def ffn_kernel(
-    ready, place, x_a, x_b, term, far, gains, c_a, c_b, *rest
+    ready, place, x_a, x_b, term, far, table, d_hidden_all, *rest
 ):
-    pieces, (wd_own, wd_near) = rest[:4], rest[4:6]
-    resid, lowered, hidden, d_gate_up, second, leaving = rest[6:12]
-    w, wd, upstream, sems, down_sems = rest[12:]
-    half, width, steps = x_a.shape[0], pieces[0].shape[0], w.shape[0]
+    pieces = rest[:4]
+    resid, lowered, hidden, d_gate_up, second, leaving = rest[4:10]
+    w, sems = rest[10:]
+    half, width, steps = term.shape[0] // 2, pieces[0].shape[0], w.shape[0]
 
     def begin(j, carry):
         for rank, source in enumerate(pieces):
@@ -735,21 +806,15 @@
             ).start()
         return carry
 
-    down_copies = chip_rows(place, wd_own, wd_near, wd, down_sems)
-    for copy in down_copies:
-        copy.start()
     lax.fori_loop(0, steps, begin, 0)
     ready()
-    gain = gains[1:2, :]
-    for rel, (x_ref, c_ref) in enumerate(((x_a, c_a), (x_b, c_b))):
+    gain = table[1:2, :]
+    for rel, x_ref in enumerate((x_a, x_b)):
         at = pl.ds(rel * half, half)
-        rows = x_ref[...].astype(F32) + (term[at, :] + far[at, :].astype(F32))
+        rows = x_ref[:half, :].astype(F32) + (term[at, :] + far[at, :].astype(F32))
         resid[at, :] = rows
         scale = lax.rsqrt(jnp.mean(rows * rows, axis=-1, keepdims=True) + EPSILON)
         lowered[at, :] = (rows * scale * gain).astype(BF16)
-        upstream[at, :] = c_ref[...]
-    for copy in down_copies:
-        copy.wait()
 
     def step(j, carry):
         for rank in range(4):
@@ -757,7 +822,7 @@
             pltpu.make_async_copy(rows, rows, sems.at[j, rank]).wait()
         gate_up = matmul(lowered[...], w[j])
         gate, up = gate_up[:, :128], gate_up[:, 128:]
-        d_hidden = times_transposed(upstream[...], wd[aligned(j * 128, 128), :])
+        d_hidden = d_hidden_all[:, aligned(j * 128, 128)]
         sigmoid = jax.nn.sigmoid(gate)
         activated = gate * sigmoid
         hidden[:, aligned(j * 128, 128)] = (activated * up).astype(BF16)
@@ -782,21 +847,18 @@
     lax.fori_loop(0, D // 256, back, 0)
 
 
-def ffn(place, x_a, x_b, term, far, gains, c_a, c_b, pieces, wd_own, wd_near):
-    rows = term.shape[0]
-    inner = 2 * wd_own.shape[0]
+def ffn(place, x_a, x_b, term, far, table, d_hidden, pieces):
+    rows, inner = d_hidden.shape
     wide, steps = 2 * inner, inner // 128
     return kernel_call(
         ffn_kernel,
         "ffn",
         [(SMEM, place)]
-        + in_stage(x_a, x_b) + in_vmem(term, far) + in_stage(gains, c_a, c_b)
-        + [(HBM, a) for a in pieces + (wd_own, wd_near)],
+        + in_stage(x_a, x_b) + in_vmem(term, far) + in_stage(table) + in_vmem(d_hidden)
+        + [(EITHER if rank in (FAR, NEAR) else HBM, a) for rank, a in enumerate(pieces)],
         [((rows, D), F32), ((rows, D), BF16), ((rows, inner), BF16), ((rows, wide), BF16),
          ((rows, D), F32), ((rows, D), BF16)],
-        [pltpu.VMEM((steps, D, 256), BF16), pltpu.VMEM((inner, D), BF16),
-         pltpu.VMEM((rows, D), BF16), pltpu.SemaphoreType.DMA((steps, 4)),
-         pltpu.SemaphoreType.DMA((2,))],
+        [pltpu.VMEM((steps, D, 256), BF16), pltpu.SemaphoreType.DMA((steps, 4))],
     )
 
 
@@ -832,7 +894,7 @@
 
 def mid_kernel(
     ready, place, second, far, resid, gains, c_a, c_b, w_own, w_near,
-    d_resid, d_branch, gain_terms, d_mixed, w, sums, sems,
+    d_resid_out, d_branch, gain_terms, d_mixed, d_resid, w, sums, sems,
 ):
     d_mixed = views(d_mixed, place)
     copies = chip_rows(place, w_own, w_near, w, sems)
@@ -860,6 +922,8 @@
         )
         if rel == 0:
             d_resid[...] = value
+            leaving = pltpu.make_async_copy(d_resid, d_resid_out, sems.at[2])
+            leaving.start()
         d_branch[at, :] = value.astype(BF16)
     sums[...] = total
     gain_terms[0] = sums[:, aligned(place[OWN] * width, width)]
@@ -870,6 +934,7 @@
         value = times_transposed(d_branch[...], w[base : base + 256, :]).astype(BF16)
         put_rows(d_mixed, 0, slice(base, base + 256), value[:half])
         put_rows(d_mixed, 1, slice(base, base + 256), value[half:])
+    leaving.wait()
 
 
 def mid(place, second, far, resid, gains, c_a, c_b, w_own, w_near):
@@ -878,12 +943,12 @@
     return kernel_call(
         mid_kernel,
         "mid",
-        [(SMEM, place), (VMEM, second), (VMEM, far), (VMEM, resid), (STAGED, gains),
-         (STAGED, c_a), (STAGED, c_b), (HBM, w_own), (HBM, w_near)],
-        [((rows // 2, D), F32), ((rows, D), BF16), ((2, 1, width), F32),
+        [(SMEM, place), (VMEM, second), (VMEM, far), (VMEM, resid), (MOVED, gains),
+         (MOVED, c_a), (MOVED, c_b), (HBM, w_own), (HBM, w_near)],
+        [((rows // 2, D), F32, HBM), ((rows, D), BF16), ((2, 1, width), F32),
          block_shapes(rows, 2 * width, True)],
-        [pltpu.VMEM((2 * width, D), BF16), pltpu.VMEM((1, D), F32),
-         pltpu.SemaphoreType.DMA((2,))],
+        [pltpu.VMEM((rows // 2, D), F32), pltpu.VMEM((2 * width, D), BF16),
+         pltpu.VMEM((1, D), F32), pltpu.SemaphoreType.DMA((3,))],
     )
 
 
@@ -910,17 +975,13 @@
     ready()
     rows[:half, :] = rows_of(d_qkv, 0)
     rows[half:, :] = rows_of(d_qkv, 1)
-    for copy in copies:
-        copy.wait()
-
-    def step(rank, carry):
+    for rank in range(4):
+        for copy in copies[:3] if rank == 0 else copies[rank + 2 : rank + 3]:
+            copy.wait()
         columns = aligned(place[rank] * width, width)
         value = times_transposed(rows[...], w[rank])
         kept[:, columns] = value[:half]
         leaving[:, columns] = value[half:].astype(BF16)
-        return carry
-
-    lax.fori_loop(0, 4, step, 0)
 
 
 def back_first(place, d_qkv, w_own, w_far, w_near, w_across):
@@ -941,7 +1002,7 @@
     ready()
     blocks = views(blocks, place)
     width = gain_terms.shape[2]
-    rows = x_a[...].astype(F32)
+    rows = x_a[: kept.shape[0], :].astype(F32)
     scale = lax.rsqrt(jnp.mean(rows * rows, axis=-1, keepdims=True) + EPSILON)
     normed = rows * scale
     d_rows = kept[...] + far[...].astype(F32)
@@ -979,12 +1040,12 @@
 ):
     ready()
     width = leaving.shape[0]
-    left = both_rows(left_own, left_near, aligned(place[target] * width, width))
+    left = both_rows(left_own, left_near, aligned(place[target] * width, width)).T
 
     def step(j, carry):
         columns = aligned(j * 256, 256)
         right = both_rows(right_own, right_near, columns)
-        leaving[:, columns] = inner_rows(left, right).astype(BF16)
+        leaving[:, columns] = matmul(left, right).astype(BF16)
         return carry
 
     lax.fori_loop(0, leaving.shape[1] // 256, step, 0)
@@ -995,7 +1056,7 @@
     return kernel_call(
         functools.partial(leaving_kernel, target),
         "leaving_gradient",
-        [(SMEM, place)] + in_stage(left_own, left_near, right_own, right_near),
+        [(SMEM, place)] + moved(left_own, left_near, right_own, right_near),
         [((width, wide), BF16)],
     )[0]
 
@@ -1009,14 +1070,18 @@
         stripes[block // 2, :, aligned((block % 2) * 256, 256)] = value
 
 
-def write_stripes(who, stripes, grad, sems):
+def stripe_copies(who, stripes, grad, sems):
     parts, _, part = stripes.shape
-    copies = [
+    return [
         pltpu.make_async_copy(
             stripes.at[k], grad.at[:, aligned((2 * k + who) * part, part)], sems.at[k]
         )
         for k in range(parts)
     ]
+
+
+def write_stripes(who, stripes, grad, sems):
+    copies = stripe_copies(who, stripes, grad, sems)
     for copy in copies:
         copy.start()
     for copy in copies:
@@ -1028,11 +1093,11 @@
 ):
     ready()
     parts, width, _ = stripes.shape
-    left = both_rows(left_own, left_near, aligned(place[OWN] * width, width))
+    left = both_rows(left_own, left_near, aligned(place[OWN] * width, width)).T
 
     def step(j, carry):
         right = both_rows(right_own, right_near, aligned(j * 256, 256))
-        put_stripe(parts, stripes, j, inner_rows(left, right))
+        put_stripe(parts, stripes, j, matmul(left, right))
         return carry
 
     lax.fori_loop(0, right_own.shape[1] // 256, step, 0)
@@ -1045,22 +1110,26 @@
         staying_kernel,
         "staying_gradient",
         [(SMEM, place)] + in_stage(left_own, left_near, right_own, right_near),
-        [((width, 2 * wide), F32)],
+        [((width, 2 * wide), F32, HBM)],
         [pltpu.VMEM((parts, width, wide // parts), F32), pltpu.SemaphoreType.DMA((parts,))],
-        out_spec=HBM,
     )[0]
 
 
 def coming_kernel(ready, place, come, before, grad, stripes, sems):
     ready()
-    parts = stripes.shape[0]
-
-    def step(j, carry):
-        put_stripe(parts, stripes, j, come[:, aligned(j * 256, 256)].astype(F32))
-        return carry
-
-    lax.fori_loop(0, come.shape[1] // 256, step, 0)
-    write_stripes(1 - place[SIDE], stripes, grad, sems)
+    parts, _, part = stripes.shape
+    copies = stripe_copies(1 - place[SIDE], stripes, grad, sems)
+    for k, copy in enumerate(copies):
+        for j in range(come.shape[1] // 256):
+            if parts == 2:
+                at = j * 256 + k * 128
+                stripes[k, :, j * 128 : (j + 1) * 128] = come[:, at : at + 128].astype(F32)
+            elif j // 2 == k:
+                at = slice((j % 2) * 256, (j % 2) * 256 + 256)
+                stripes[k, :, at] = come[:, j * 256 : (j + 1) * 256].astype(F32)
+        copy.start()
+    for copy in copies:
+        copy.wait()
 
 
 def with_coming(parts, place, come, grad):
@@ -1068,10 +1137,9 @@
     return kernel_call(
         coming_kernel,
         "coming_gradient",
-        [(SMEM, place), (STAGED, come), (HBM, grad)],
-        [(grad.shape, F32)],
+        [(SMEM, place), (MOVED, come), (HBM, grad)],
+        [(grad.shape, F32, HBM)],
         [pltpu.VMEM((parts, width, wide // parts), F32), pltpu.SemaphoreType.DMA((parts,))],
-        out_spec=HBM,
         aliases=((2, 0),),
     )[0]
 
@@ -1127,31 +1195,34 @@
     )[0]
 
 
-def half_columns_kernel(parts, far, ready, place, weight, half, sems):
-    part = half.shape[1] // parts
-    side = 1 - place[SIDE] if far else place[SIDE]
-    copies = [
+def side_columns(weight, half, side, sems):
+    part = half.shape[1] // 3
+    return [
         pltpu.make_async_copy(
             weight.at[:, aligned((2 * k + side) * part, part)],
             half.at[:, pl.ds(k * part, part)],
             sems.at[k],
         )
-        for k in range(parts)
+        for k in range(3)
     ]
+
+
+def kept_columns_kernel(ready, place, weight, half, sems):
+    copies = side_columns(weight, half, place[SIDE], sems)
     for copy in copies:
         copy.start()
     for copy in copies:
         copy.wait()
 
 
-def half_columns(place, weight, parts, far):
+def kept_columns(place, weight):
     count, width = weight.shape
     return kernel_call(
-        functools.partial(half_columns_kernel, parts, far),
-        "far_columns" if far else "kept_columns",
+        kept_columns_kernel,
+        "kept_columns",
         [(SMEM, place), (HBM, weight)],
         [((count, width // 2), BF16)],
-        [pltpu.SemaphoreType.DMA((parts,))],
+        [pltpu.SemaphoreType.DMA((3,))],
     )[0]
 
 
@@ -1205,38 +1276,36 @@
 
     near = lambda rows: swap(rows, 1)
 
-    qkv_leaving = half_columns(place, w_qkv, 3, True)
+    x_sent, c_sent, qkv_leaving = to_positions(place, frames_in, cotangent, w_qkv)
     qkv_across = swap(qkv_leaving, 3)
     qkv_far = near(qkv_across)
-    sent = to_positions(place, after(frames_in, qkv_leaving), cotangent)
-    came = exchange(sent)
-    sent = sent[0]
+    x_came = exchange(x_sent)
     ids_own = segment_ids.reshape(frames, POS).T
     ids_own = jnp.take(ids_own, jnp.arange(POS) ^ position, axis=0).reshape(1, half)
-    ids_far = swap(after(ids_own, sent), 2)
     gains_own = jnp.stack([gain_attn, gain_ffn])
-    gains_far = swap(after(gains_own, sent), 2)
-    qkv_kept = half_columns(place, after(w_qkv, sent), 3, False)
-    came, ids_far, gains_far, qkv_kept, qkv_far = sync(came, ids_far, gains_far, qkv_kept, qkv_far)
-
-    x_own, c_own = collect(place, came)
-    x_far = swap(x_own, 2)
-    gains_near = near(jnp.stack([gains_own, gains_far]))
+    gains_near = near(after(gains_own, qkv_leaving))
+    qkv_kept = kept_columns(place, after(w_qkv, qkv_leaving))
+    w_kept, w_leaving = spread(place, after(w_gate_up, qkv_leaving))
+    x_came, ids_own, gains_near, qkv_kept, w_kept, w_leaving = sync(
+        x_came, ids_own, gains_near, qkv_kept, w_kept, w_leaving
+    )
+
+    x_own = collect(place, x_came, ids_own, gains_own, gains_near)
+    x_far = near(swap(x_own, 3))
     qkv_near = near(qkv_kept)
-    w_kept, w_leaving = spread(place, after(w_gate_up, x_own))
-    x_far, gains_near, qkv_near, w_leaving, c_own = sync(
-        x_far, gains_near, qkv_near, w_leaving, c_own
-    )
+    c_came = exchange([after(c_sent[0], x_own)])
+    x_far, qkv_far, qkv_near, w_leaving = sync(x_far, qkv_far, qkv_near, w_leaving)
 
     w_across = swap(w_leaving, 3)
-    qkv_sent, lowered_first, gains = first(
-        place, x_own, x_far, gains_own, gains_far, gains_near[0], gains_near[1],
-        w_qkv, qkv_far, qkv_near, qkv_across,
-    )
-    w_near, out_near, down_near = (near(after(a, lowered_first)) for a in (w_kept, w_out, w_down))
-    qkv, w_near, out_near, down_near = sync(exchange(qkv_sent), w_near, out_near, down_near)
-
-    mixed_sent = attend_local(place, ids_own, ids_far, qkv)
+    qkv_sent, lowered_first, table = first(
+        place, x_own, x_far, w_qkv, qkv_far, qkv_near, qkv_across
+    )
+    qkv_sent, c_came = sync(qkv_sent, c_came)
+    c_own = collect_rows(place, c_came)
+    out_near, down_near = (near(after(a, lowered_first)) for a in (w_out, w_down))
+    qkv, out_near, down_near, c_own = sync(exchange(qkv_sent), out_near, down_near, c_own)
+
+    mixed_sent = attend_local(place, table, qkv)
     c_far = swap(after(c_own, mixed_sent[0]), 2)
     c_own_near, lowered_first_near = (
         near(after(a, mixed_sent[0])) for a in (c_own, lowered_first)
@@ -1247,12 +1316,14 @@
 
     term, leaving, mixed = out_term(place, mixed, w_out, out_near)
     far = swap(leaving, 2)
-    far, mixed_near, w_far, c_far_near = sync(
-        far, near(mixed), near(after(w_across, leaving)), near(after(c_far, leaving))
+    d_hidden = d_hidden_rows(place, c_own, after(c_far, leaving), w_down, down_near)
+    w_near = near(after(w_kept, leaving))
+    far, mixed_near, w_far, w_near, c_far_near, d_hidden = sync(
+        far, near(mixed), near(after(w_across, leaving)), w_near, near(after(c_far, leaving)),
+        d_hidden,
     )
     resid, lowered_second, hidden, d_gate_up, second, leaving = ffn(
-        place, x_own, x_far, term, far, gains, c_own, c_far, (w_kept, w_far, w_near, w_across),
-        w_down, down_near,
+        place, x_own, x_far, term, far, table, d_hidden, (w_kept, w_far, w_near, w_across)
     )
 
     second_far = swap(leaving, 2)
@@ -1268,7 +1339,7 @@
 
     gate_up_come = swap(gate_up_leaving, 3)
     d_resid, d_branch, gain_ffn_terms, d_mixed = mid(
-        place, second, second_far, resid, gains, c_own, c_far, w_out, out_near
+        place, second, second_far, resid, table, c_own, c_far, w_out, out_near
     )
     d_branch_near, gain_ffn_near = near(d_branch), near(gain_ffn_terms[1])
     grad_gate_up = staying_gradient(2, place, after(lowered_second, d_branch), *sides[1:])
@@ -1276,7 +1347,7 @@
         exchange(d_mixed), d_branch_near, gain_ffn_near, grad_gate_up
     )
 
-    d_qkv_sent = attend_back_local(place, ids_own, ids_far, qkv, d_mixed)
+    d_qkv_sent = attend_back_local(place, table, qkv, d_mixed)
     grad_down = grad_down_rows(
         place, after(hidden, d_qkv_sent[0]), hidden_near, c_own, c_far, c_own_near, c_far_near
     )
@@ -1295,17 +1366,15 @@
     qkv_across_come = swap(qkv_leaving, 3)
 
     out_sent, gain_attn_terms = last(
-        place, kept, first_far, x_own, gains, d_resid, down_kept, down_far
+        place, kept, first_far, x_own, table, d_resid, down_kept, down_far
     )
     grad_gate_up = with_coming(2, place, after(gate_up_come, gain_attn_terms), grad_gate_up)
     grad_qkv = staying_gradient(3, place, after(lowered_first, gain_attn_terms), *qkv_sides[1:])
     gain_sums = gain_attn_terms[:2] + swap(gain_attn_terms[2:], 2)
     gain_attn_grad = gain_sums[0] + near(gain_sums[1])
     qkv_come = near(after(qkv_across_come, grad_gate_up, grad_qkv))
-    out_come, grad_gate_up, grad_qkv, qkv_come = sync(
-        exchange(out_sent), grad_gate_up, grad_qkv, qkv_come
-    )
     grad_qkv = with_coming(3, place, qkv_come, grad_qkv)
+    out_come, grad_gate_up, grad_qkv = sync(exchange(out_sent), grad_gate_up, grad_qkv)
     grad_in, block_out = to_frames(place, out_come)
     gain_ffn_grad = (gain_ffn_terms[0] + gain_ffn_near).reshape(-1)
     return (

time: 228 us -> 218 us (0.956)
  waiting for transfers between devices: 78.9 us -> 70.3 us
  starting transfers between devices: 48.6 us -> 56.6 us
  Pallas kernels: 87.1 us -> 80.7 us
  local copies, waits for them, and re-layouts: 9.85 us -> 5.92 us
    ppermute x32 -> x31, waiting for transfers between devices: 59.4 us -> 49.5 us  [swap(): return lax.ppermute(block, 'fsdp', [(i, i ^ mask) for i in range(count)])]
    pallas_call x23 -> x24, Pallas kernels: 87.1 us -> 80.7 us  [kernel_call(): pl.pallas_call(body_kernel, name=name, in_specs=[spec for spec, _ in flat...]
    all_to_all x6 -> x7, starting transfers between devices: 32.4 us -> 37 us  [exchange(): lax.all_to_all(blocks[0], 'fsdp', split_axis=0, concat_axis=0, tiled=True...]
    unnamed x82 -> x88, local copies, waits for them, and re-layouts: 8.96 us -> 5.03 us
    ppermute x32 -> x31, starting transfers between devices: 16.2 us -> 19.6 us  [swap(): return lax.ppermute(block, 'fsdp', [(i, i ^ mask) for i in range(count)])]
    all_to_all x6 -> x7, waiting for transfers between devices: 19.5 us -> 20.8 us  [exchange(): lax.all_to_all(blocks[0], 'fsdp', split_axis=0, concat_axis=0, tiled=True...]
  transfers between devices with their start and end apart: 38 -> 38, of which waited for: 18 -> 18; matrix products, arithmetic and copies ran while one was open for 1% -> 1% of each run, Pallas kernels for 25% -> 27%
where the time goes in v4:
time: 218 us; the launch traced here: 216 us
  Pallas kernels  80.7 us (37%)
  waiting for transfers between devices  70.3 us (32%)
  starting transfers between devices  56.6 us (26%)
  local copies, waits for them, and re-layouts  5.92 us (3%)
    pallas_call x24, Pallas kernels, kernel_call(): pl.pallas_call(body_kernel, name=name, in_specs=[spec for spec, _ in flat...  80.7 us
    ppermute x31, waiting for transfers between devices, swap(): return lax.ppermute(block, 'fsdp', [(i, i ^ mask) for i in range(count)])  49.5 us
    all_to_all x7, starting transfers between devices, exchange(): lax.all_to_all(blocks[0], 'fsdp', split_axis=0, concat_axis=0, tiled=True...  37 us
    all_to_all x7, waiting for transfers between devices, exchange(): lax.all_to_all(blocks[0], 'fsdp', split_axis=0, concat_axis=0, tiled=True...  20.8 us
    ppermute x31, starting transfers between devices, swap(): return lax.ppermute(block, 'fsdp', [(i, i ^ mask) for i in range(count)])  19.6 us
    unnamed x88, local copies, waits for them, and re-layouts  5.03 us
  transfers between devices with their start and end apart: 38, of which 18 were waited for; matrix products, arithmetic and copies ran while one was open for 1% of the time, Pallas kernels for 27%

profile of v4, /device:TPU:0, one launch (start us, length us, event | category | flops | bytes accessed | tf_op | source)
XLA Modules:
  0.0 216.4 jit_solution(17104917682339231418)
XLA Ops:
  0.8 2.9 %to_positions.1 = (bf16[8,16,1024]{2,1,0:T(8,128)(2,1)}, bf16[8,16,1024]{2,1,0:T(8,128)(2,1)}, bf16[256,1536]{1,0:T(8,128)(2,1)S(1)}) custom-call(s32[7]{0:T(128)S(1)} %stack.40.refs_0_, bf16[128,1024]{1,0:T(8,128)(2,1)} %refs_1_.3, bf16[128,1024]{1,0:T(8,128)(2,1)} %refs_2_.1, bf16[256,3072]{1,0:T(8,128)(2,1)} %refs_1_.7), custom_call_target="tpu_custom_call" | custom-call | flops 1 | bytes 1 | tf_op jit(solution)/shard_map/to_positions/pallas_call | solution.py:395
  3.6 2.5 %collective-permute-start.3 = (bf16[256,1536]{1,0:T(8,128)(2,1)S(1)}, bf16[256,1536]{1,0:T(8,128)(2,1)S(1)}, u32[]{:S(2)}, u32[]{:S(2)}) collective-permute-start(bf16[256,1536]{1,0:T(8,128)(2,1)S(1)} %get-tuple-element.105), channel_id=1, source_target_pairs={{0,3},{1,2},{2,1},{3,0},{4,7},{5,6},{6,5},{7,4},{8,11},{9,10},{10,... | collective-permute-start | bytes 2359304 | tf_op jit(solution)/shard_map/ppermute | solution.py:339
  6.1 5.8 %all-to-all-start = ((bf16[8,16,1024]{2,1,0:T(8,128)(2,1)}), bf16[8,16,1024]{2,1,0:T(8,128)(2,1)S(1)}, u32[]{:S(2)}, u32[]{:S(2)}) async-start(bf16[8,16,1024]{2,1,0:T(8,128)(2,1)} %get-tuple-element.104), calls=%async_computation | async-start | bytes 524288 | tf_op jit(solution)/shard_map/all_to_all | solution.py:349
  13.3 2.6 %kept_columns.1 = bf16[256,1536]{1,0:T(8,128)(2,1)} custom-call(s32[7]{0:T(128)S(1)} %stack.40.refs_0_, bf16[256,3072]{1,0:T(8,128)(2,1)} %refs_1_.7), custom_call_target="tpu_custom_call" | custom-call | flops 1 | bytes 1 | tf_op jit(solution)/shard_map/kept_columns/pallas_call | solution.py:395
  15.9 2.8 %spread.1 = (bf16[256,2816]{1,0:T(8,128)(2,1)S(1)}, bf16[256,2816]{1,0:T(8,128)(2,1)S(1)}) custom-call(s32[7]{0:T(128)S(1)} %stack.40.refs_0_, bf16[256,5632]{1,0:T(8,128)(2,1)} %refs_1_.5), custom_call_target="tpu_custom_call" | custom-call | flops 1 | bytes 1 | tf_op jit(solution)/shard_map/spread/pallas_call | solution.py:395
  18.7 1.1 copy-done.17
  19.8 1.1 copy-done.36
  21.0 0.7 all-to-all-done.refs_1_
  21.7 2.3 %collective-permute-done.3.refs_6_.refs_4_ = bf16[256,1536]{1,0:T(8,128)(2,1)S(1)} collective-permute-done((bf16[256,1536]{1,0:T(8,128)(2,1)S(1)}, bf16[256,1536]{1,0:T(8,128)(2,1)S(1)}, u32[]{:S(2)}, u32[]{:S(2)}) %collective-permute-start.3) | collective-permute-done | bytes 786464 | tf_op jit(solution)/shard_map/ppermute | solution.py:339
  24.1 0.6 collect.1.refs_1_.refs_3_
  24.7 2.5 %collective-permute-start.1 = (bf16[144,1024]{1,0:T(8,128)(2,1)S(1)}, bf16[144,1024]{1,0:T(8,128)(2,1)S(1)}, u32[]{:S(2)}, u32[]{:S(2)}) collective-permute-start(bf16[144,1024]{1,0:T(8,128)(2,1)S(1)} %collect.1.refs_1_.refs_3_), channel_id=1, source_target_pairs={{0,3},{1,2},{2,1},{3,0},{4,7},{5,6},{6,5},{7,4},{8,11},{9,10},{10,... | collective-permute-start | bytes 884744 | tf_op jit(solution)/shard_map/ppermute | solution.py:339
  27.3 5.8 %all-to-all-start.1 = ((bf16[8,16,1024]{2,1,0:T(8,128)(2,1)}), bf16[8,16,1024]{2,1,0:T(8,128)(2,1)S(1)}, u32[]{:S(2)}, u32[]{:S(2)}) async-start(bf16[8,16,1024]{2,1,0:T(8,128)(2,1)} %get-tuple-element.122), calls=%async_computation.1 | async-start | bytes 524288 | tf_op jit(solution)/shard_map/all_to_all | solution.py:349
  33.1 1.4 collective-permute-done.1
  34.7 1.5 collective-permute-done.2.refs_2_
  36.1 3.7 %first.1 = (bf16[8,32,1536]{2,1,0:T(8,128)(2,1)S(1)}, bf16[256,1024]{1,0:T(8,128)(2,1)}, f32[8,1024]{1,0:T(8,128)}) custom-call(s32[7]{0:T(128)S(1)} %stack.40.refs_0_, bf16[144,1024]{1,0:T(8,128)(2,1)S(1)} %collect.1.refs_1_.refs_3_, bf16[144,1024]{1,0:T(8,128)(2,1)S(1)} %collective-permute-done.2.refs_2_, bf16[256,3072]{1,0:T(8,128)(2,1)} %refs_1_.7, ...), custom_call_target="tpu_custom_call" | custom-call | flops 1 | bytes 1 | tf_op jit(solution)/shard_map/first/pallas_call | solution.py:395
  39.9 0.9 copy-done.23
  41.0 1.4 all-to-all-done.1.refs_1_
  42.3 5.1 %all-to-all-start.2 = ((bf16[8,32,1536]{2,1,0:T(8,128)(2,1)}), bf16[8,32,1536]{2,1,0:T(8,128)(2,1)S(1)}, u32[]{:S(2)}, u32[]{:S(2)}) async-start(bf16[8,32,1536]{2,1,0:T(8,128)(2,1)} %copy-done.23), calls=%async_computation.2 | async-start | bytes 1572864 | tf_op jit(solution)/shard_map/all_to_all | solution.py:349
  47.4 1.0 collective-permute-start.8
  48.4 0.7 collective-permute-start.6
  49.1 0.6 collect_rows.1.refs_1_.refs_5_.refs_3_
  49.6 1.0 collective-permute-done.6.refs_2_.refs_8_
  50.6 17.3 %all-to-all-done.2.refs_2_ = bf16[8,32,1536]{2,1,0:T(8,128)(2,1)S(1)} async-done(((bf16[8,32,1536]{2,1,0:T(8,128)(2,1)}), bf16[8,32,1536]{2,1,0:T(8,128)(2,1)S(1)}, u32[]{:S(2)}, u32[]{:S(2)}) %all-to-all-start.2) | async-done | bytes 786464 | tf_op jit(solution)/shard_map/all_to_all | solution.py:349
  67.9 2.6 %attend.1 = bf16[8,32,512]{2,1,0:T(8,128)(2,1)} custom-call(s32[7]{0:T(128)S(1)} %stack.40.refs_0_, f32[8,1024]{1,0:T(8,128)S(1)} %copy-done.20, bf16[8,32,1536]{2,1,0:T(8,128)(2,1)S(1)} %all-to-all-done.2.refs_2_), custom_call_target="tpu_custom_call" | custom-call | flops 1 | bytes 1 | tf_op jit(solution)/shard_map/attend/pallas_call | solution.py:395
  70.6 3.6 %all-to-all-start.3 = ((bf16[8,32,512]{2,1,0:T(8,128)(2,1)}), bf16[8,32,512]{2,1,0:T(8,128)(2,1)S(1)}, u32[]{:S(2)}, u32[]{:S(2)}) async-start(bf16[8,32,512]{2,1,0:T(8,128)(2,1)} %attend.1), calls=%async_computation.3 | async-start | bytes 524288 | tf_op jit(solution)/shard_map/all_to_all | solution.py:349
  74.5 1.5 collective-permute-start.9
  76.1 5.5 %collective-permute-done.8.refs_10_ = bf16[256,2816]{1,0:T(8,128)(2,1)} collective-permute-done((bf16[256,2816]{1,0:T(8,128)(2,1)}, bf16[256,2816]{1,0:T(8,128)(2,1)}, u32[]{:S(2)}, u32[]{:S(2)}) %collective-permute-start.8) | collective-permute-done | bytes 1441824 | tf_op jit(solution)/shard_map/ppermute | solution.py:339
  81.5 5.6 %collective-permute-done.9.refs_2_.refs_6_.refs_4_ = bf16[128,1024]{1,0:T(8,128)(2,1)S(1)} collective-permute-done((bf16[128,1024]{1,0:T(8,128)(2,1)S(1)}, bf16[128,1024]{1,0:T(8,128)(2,1)S(1)}, u32[]{:S(2)}, u32[]{:S(2)}) %collective-permute-start.9) | collective-permute-done | bytes 262176 | tf_op jit(solution)/shard_map/ppermute | solution.py:339
  87.1 2.2 %out_term.1 = (f32[256,1024]{1,0:T(8,128)S(1)}, bf16[256,1024]{1,0:T(8,128)(2,1)S(1)}, bf16[256,512]{1,0:T(8,128)(2,1)S(1)}) custom-call(s32[7]{0:T(128)S(1)} %stack.40.refs_0_, bf16[256,1024]{1,0:T(8,128)(2,1)} %refs_7_.1, bf16[256,1024]{1,0:T(8,128)(2,1)} %copy-done.39, bf16[8,32,512]{2,1,0:T(8,128)(2,1)S(1)} %all-to-all-done.3.refs_3_), custom_call_target="tpu_custom_call" | custom-call | flops 1 | bytes 1 | tf_op jit(solution)/shard_map/out_term/pallas_call | solution.py:395
  89.9 1.5 collective-permute-start.12
  92.0 3.4 %d_hidden.1.refs_6_ = f32[256,1408]{1,0:T(8,128)S(1)} custom-call(s32[7]{0:T(128)S(1)} %stack.40.refs_0_, bf16[128,1024]{1,0:T(8,128)(2,1)S(1)} %collect_rows.1.refs_1_.refs_5_.refs_3_, bf16[128,1024]{1,0:T(8,128)(2,1)S(1)} %collective-permute-done.9.refs_2_.refs_6_.refs_4_, bf16[704,1024]{1,0:T(8,128)(2,1)} %refs_3_.7, ...), custom_call_target="tpu_custom_call" | custom-call | flops 1 | bytes 1 | tf_op jit(solution)/shard_map/d_hidden/pallas_call | solution.py:395
  95.7 8.2 %collective-permute-done.12.refs_4_ = bf16[256,1024]{1,0:T(8,128)(2,1)S(1)} collective-permute-done((bf16[256,1024]{1,0:T(8,128)(2,1)S(1)}, bf16[256,1024]{1,0:T(8,128)(2,1)S(1)}, u32[]{:S(2)}, u32[]{:S(2)}) %collective-permute-start.12) | collective-permute-done | bytes 524320 | tf_op jit(solution)/shard_map/ppermute | solution.py:339
  103.9 8.3 %ffn.1 = (f32[256,1024]{1,0:T(8,128)S(1)}, bf16[256,1024]{1,0:T(8,128)(2,1)S(1)}, bf16[256,1408]{1,0:T(8,128)(2,1)S(1)}, bf16[256,2816]{1,0:T(8,128)(2,1)S(1)}, ...) custom-call(s32[7]{0:T(128)S(1)} %stack.40.refs_0_, bf16[144,1024]{1,0:T(8,128)(2,1)} %copy-done.2, ...), custom_call_target="tpu_custom_call" | custom-call | flops 1 | bytes 1 | tf_op jit(solution)/shard_map/ffn/pallas_call | solution.py:395
  112.9 1.5 collective-permute-start.17
  114.4 4.2 %down_term.1 = (f32[128,1024]{1,0:T(8,128)S(1)}, bf16[128,1024]{1,0:T(8,128)(2,1)S(1)}) custom-call(s32[7]{0:T(128)S(1)} %stack.40.refs_0_, bf16[256,1408]{1,0:T(8,128)(2,1)} %copy-done.9, f32[256,1024]{1,0:T(8,128)S(1)} %get-tuple-element.153.refs_2_.refs_3_, bf16[704,1024]{1,0:T(8,128)(2,1)} %refs_3_.7, bf16[704,1024]{1,0:T(8,128)(2,1)} %collective-permute-done.7.refs_4_), custom_call_target="tpu_custom_call" | custom-call | flops 1 | bytes 1 | tf_op jit(solution)/shard_map/down_term/pallas_call | solution.py:395
  118.7 3.9 %leaving_gradient.2 = bf16[256,2816]{1,0:T(8,128)(2,1)S(1)} custom-call(s32[7]{0:T(128)S(1)} %stack.40.refs_0_, bf16[256,1024]{1,0:T(8,128)(2,1)S(1)} %get-tuple-element.163.refs_1_, bf16[256,1024]{1,0:T(8,128)(2,1)S(1)} %collective-permute-done.18.refs_2_, bf16[256,2816]{1,0:T(8,128)(2,1)S(1)} %get-tuple-element.158.refs_3_, ...), custom_call_target="tpu_custom_call" | custom-call | flops 1 | bytes 1 | tf_op jit(solution)/shard_map/leaving_gradient/pallas_call | solution.py:395
  122.6 1.1 copy-done.18
  123.7 3.4 %collective-permute-done.17.refs_2_ = bf16[256,1024]{1,0:T(8,128)(2,1)S(1)} collective-permute-done((bf16[256,1024]{1,0:T(8,128)(2,1)S(1)}, bf16[256,1024]{1,0:T(8,128)(2,1)S(1)}, u32[]{:S(2)}, u32[]{:S(2)}) %collective-permute-start.17) | collective-permute-done | bytes 524320 | tf_op jit(solution)/shard_map/ppermute | solution.py:339
  127.2 3.3 %mid.1 = (f32[128,1024]{1,0:T(8,128)}, bf16[256,1024]{1,0:T(8,128)(2,1)}, f32[2,1,256]{2,1,0:T(1,128)S(1)}, bf16[8,32,512]{2,1,0:T(8,128)(2,1)}) custom-call(s32[7]{0:T(128)S(1)} %stack.40.refs_0_, f32[256,1024]{1,0:T(8,128)S(1)} %get-tuple-element.149.refs_1_, bf16[256,1024]{1,0:T(8,128)(2,1)S(1)} %collective-permute-done.17.refs_2_, ...), custom_call_target="tpu_custom_call" | custom-call | flops 1 | bytes 1 | tf_op jit(solution)/shard_map/mid/pallas_call | solution.py:395
  130.6 6.0 %all-to-all-start.4 = ((bf16[8,32,512]{2,1,0:T(8,128)(2,1)}), bf16[8,32,512]{2,1,0:T(8,128)(2,1)S(1)}, u32[]{:S(2)}, u32[]{:S(2)}) async-start(bf16[8,32,512]{2,1,0:T(8,128)(2,1)} %get-tuple-element.160), calls=%async_computation.4 | async-start | bytes 524288 | tf_op jit(solution)/shard_map/all_to_all | solution.py:349
  136.6 0.9 collective-permute-start.23
  137.8 6.9 %staying_gradient.2.refs_2_ = f32[256,5632]{1,0:T(8,128)} custom-call(s32[7]{0:T(128)S(1)} %stack.40.refs_0_, bf16[256,1024]{1,0:T(8,128)(2,1)} %copy-done.15, bf16[256,1024]{1,0:T(8,128)(2,1)} %copy-done.16, bf16[256,2816]{1,0:T(8,128)(2,1)} %copy-done, bf16[256,2816]{1,0:T(8,128)(2,1)} %copy-done.1), custom_call_target="tpu_custom_call" | custom-call | flops 1 | bytes 1 | tf_op jit(solution)/shard_map/staying_gradient/pallas_call | solution.py:395
  144.7 1.4 all-to-all-done.4.refs_3_
  146.1 5.6 %attend_back.1 = bf16[8,32,1536]{2,1,0:T(8,128)(2,1)} custom-call(s32[7]{0:T(128)S(1)} %stack.40.refs_0_, f32[8,1024]{1,0:T(8,128)S(1)} %copy-done.21, bf16[8,32,1536]{2,1,0:T(8,128)(2,1)S(1)} %all-to-all-done.2.refs_2_, bf16[8,32,512]{2,1,0:T(8,128)(2,1)S(1)} %all-to-all-done.4.refs_3_), custom_call_target="tpu_custom_call" | custom-call | flops 1 | bytes 1 | tf_op jit(solution)/shard_map/attend_back/pallas_call | solution.py:395
  151.7 4.6 %all-to-all-start.5 = ((bf16[8,32,1536]{2,1,0:T(8,128)(2,1)}), bf16[8,32,1536]{2,1,0:T(8,128)(2,1)S(1)}, u32[]{:S(2)}, u32[]{:S(2)}) async-start(bf16[8,32,1536]{2,1,0:T(8,128)(2,1)} %attend_back.1), calls=%async_computation.5 | async-start | bytes 1572864 | tf_op jit(solution)/shard_map/all_to_all | solution.py:349
  156.4 1.0 collective-permute-start.24
  157.4 3.4 %grad_out.1 = f32[256,1024]{1,0:T(8,128)} custom-call(s32[7]{0:T(128)S(1)} %stack.40.refs_0_, bf16[256,512]{1,0:T(8,128)(2,1)} %copy-done.33, bf16[256,512]{1,0:T(8,128)(2,1)} %copy-done.40, bf16[256,1024]{1,0:T(8,128)(2,1)} %get-tuple-element.173.refs_3_, bf16[256,1024]{1,0:T(8,128)(2,1)} %collective-permute-done.21.refs_4_), custom_call_target="tpu_custom_call" | custom-call | flops 1 | bytes 1 | tf_op jit(solution)/shard_map/grad_out/pallas_call | solution.py:395
  160.8 4.7 %grad_down.1 = f32[704,1024]{1,0:T(8,128)} custom-call(s32[7]{0:T(128)S(1)} %stack.40.refs_0_, bf16[256,1408]{1,0:T(8,128)(2,1)S(1)} %copy-done.10, bf16[256,1408]{1,0:T(8,128)(2,1)S(1)} %copy-done.25, bf16[128,1024]{1,0:T(8,128)(2,1)S(1)} %collect_rows.1.refs_1_.refs_5_.refs_3_, bf16[128,1024]{1,0:T(8,128)(2,1)S(1)} %collective-permute-done.9.refs_2_.refs_6_.refs_4_, ...), custom_call_target="tpu_custom_call" | custom-call | flops 1 | bytes 1 | tf_op jit(solution)/shard_map/grad_down/pallas_call | solution.py:395
  165.6 10.7 %collective-permute-done.24.refs_7_ = bf16[128,1024]{1,0:T(8,128)(2,1)S(1)} collective-permute-done((bf16[128,1024]{1,0:T(8,128)(2,1)}, bf16[128,1024]{1,0:T(8,128)(2,1)S(1)}, u32[]{:S(2)}, u32[]{:S(2)}) %collective-permute-start.24) | collective-permute-done | bytes 262176 | tf_op jit(solution)/shard_map/ppermute | solution.py:339
  176.3 0.7 copy-done.34
  177.0 4.1 %back_first.1 = (f32[128,1024]{1,0:T(8,128)S(1)}, bf16[128,1024]{1,0:T(8,128)(2,1)S(1)}, bf16[256,1536]{1,0:T(8,128)(2,1)S(1)}) custom-call(s32[7]{0:T(128)S(1)} %stack.40.refs_0_, bf16[256,3072]{1,0:T(8,128)(2,1)} %refs_1_.7, bf16[256,1536]{1,0:T(8,128)(2,1)} %copy-done.6, bf16[256,1536]{1,0:T(8,128)(2,1)} %copy-done.5, bf16[256,1536]{1,0:T(8,128)(2,1)} %copy-done.4, ...), custom_call_target="tpu_custom_call" | custom-call | flops 1 | bytes 1 | tf_op jit(solution)/shard_map/back_first/pallas_call | solution.py:395
  181.2 1.1 collective-permute-start.25
  182.4 1.1 collective-permute-done.26.refs_4_
  183.4 2.3 %leaving_gradient.3 = bf16[256,1536]{1,0:T(8,128)(2,1)S(1)} custom-call(s32[7]{0:T(128)S(1)} %stack.40.refs_0_, bf16[256,1024]{1,0:T(8,128)(2,1)S(1)} %copy-done.12, bf16[256,1024]{1,0:T(8,128)(2,1)S(1)} %copy-done.14, bf16[256,1536]{1,0:T(8,128)(2,1)S(1)} %get-tuple-element.179.refs_3_, bf16[256,1536]{1,0:T(8,128)(2,1)S(1)} %collective-permute-done.26.refs_4_), custom_call_target="tpu_custom_call" | custom-call | flops 1 | bytes 1 | tf_op jit(solution)/shard_map/leaving_gradient/pallas_call | solution.py:395
  185.7 4.2 %collective-permute-done.25.refs_2_ = bf16[128,1024]{1,0:T(8,128)(2,1)S(1)} collective-permute-done((bf16[128,1024]{1,0:T(8,128)(2,1)S(1)}, bf16[128,1024]{1,0:T(8,128)(2,1)S(1)}, u32[]{:S(2)}, u32[]{:S(2)}) %collective-permute-start.25) | collective-permute-done | bytes 262176 | tf_op jit(solution)/shard_map/ppermute | solution.py:339
  190.3 1.9 last.1
  192.2 6.0 %all-to-all-start.6 = ((bf16[8,32,1024]{2,1,0:T(8,128)(2,1)}), bf16[8,32,1024]{2,1,0:T(8,128)(2,1)S(1)}, u32[]{:S(2)}, u32[]{:S(2)}) async-start(bf16[8,32,1024]{2,1,0:T(8,128)(2,1)} %get-tuple-element.184), calls=%async_computation.6 | async-start | bytes 1048576 | tf_op jit(solution)/shard_map/all_to_all | solution.py:349
  198.2 1.0 collective-permute-start.29
  199.2 2.5 %coming_gradient.2 = f32[256,5632]{1,0:T(8,128)} custom-call(s32[7]{0:T(128)S(1)} %stack.40.refs_0_, bf16[256,2816]{1,0:T(8,128)(2,1)S(1)} %collective-permute-done.23.refs_1_, f32[256,5632]{1,0:T(8,128)} %staying_gradient.2.refs_2_), custom_call_target="tpu_custom_call", output_to_operand_aliasing={{}: (2, {})} | custom-call | flops 1 | bytes 1 | tf_op jit(solution)/shard_map/coming_gradient/pallas_call | solution.py:395
  201.7 4.9 %staying_gradient.3.refs_2_ = f32[256,3072]{1,0:T(8,128)} custom-call(s32[7]{0:T(128)S(1)} %stack.40.refs_0_, bf16[256,1024]{1,0:T(8,128)(2,1)} %get-tuple-element.190.refs_1_, bf16[256,1024]{1,0:T(8,128)(2,1)} %copy-done.13, bf16[256,1536]{1,0:T(8,128)(2,1)} %copy-done.7, bf16[256,1536]{1,0:T(8,128)(2,1)} %copy-done.8), custom_call_target="tpu_custom_call" | custom-call | flops 1 | bytes 1 | tf_op jit(solution)/shard_map/staying_gradient/pallas_call | solution.py:395
  206.7 3.0 %collective-permute-done.27 = bf16[256,1536]{1,0:T(8,128)(2,1)} collective-permute-done((bf16[256,1536]{1,0:T(8,128)(2,1)S(1)}, bf16[256,1536]{1,0:T(8,128)(2,1)}, u32[]{:S(2)}, u32[]{:S(2)}) %collective-permute-start.27) | collective-permute-done | bytes 786464 | tf_op jit(solution)/shard_map/ppermute | solution.py:339
  210.9 1.3 collective-permute-done.30
  212.8 1.8 coming_gradient.3
  214.6 1.6 to_frames.1
  (142 shorter events, 6.9 us)
Async XLA Ops:
  0.6 11.3 %copy-start.42 = (bf16[256]{0:T(256)(128)(2,1)S(1)}, bf16[256]{0:T(256)(128)(2,1)}, u32[]{:S(2)}) copy-start(bf16[256]{0:T(256)(128)(2,1)} %param.11) | copy-start | bytes 1540
  0.6 11.3 %copy-start.43 = (bf16[256]{0:T(256)(128)(2,1)S(1)}, bf16[256]{0:T(256)(128)(2,1)}, u32[]{:S(2)}) copy-start(bf16[256]{0:T(256)(128)(2,1)} %param.14) | copy-start | bytes 1540
  0.7 11.8 %copy-start.41 = (s32[128]{0:T(128)S(1)}, s32[128]{0:T(128)}, u32[]{:S(2)}) copy-start(s32[128]{0:T(128)} %param.10) | copy-start | bytes 1540
  3.6 20.4 %collective-permute-start.3 = (bf16[256,1536]{1,0:T(8,128)(2,1)S(1)}, bf16[256,1536]{1,0:T(8,128)(2,1)S(1)}, u32[]{:S(2)}, u32[]{:S(2)}) collective-permute-start(bf16[256,1536]{1,0:T(8,128)(2,1)S(1)} %get-tuple-element.105), channel_id=1, source_target_pairs={{0,3},{1,2},{2,1},{3,0},{4,7},{5,6},{6,5},{7,4},{8,11},{9,10},{10,... | collective-permute-start | bytes 2359304 | tf_op jit(solution)/shard_map/ppermute | solution.py:339
  6.1 15.6 %all-to-all-start = ((bf16[8,16,1024]{2,1,0:T(8,128)(2,1)}), bf16[8,16,1024]{2,1,0:T(8,128)(2,1)S(1)}, u32[]{:S(2)}, u32[]{:S(2)}) async-start(bf16[8,16,1024]{2,1,0:T(8,128)(2,1)} %get-tuple-element.104), calls=%async_computation | async-start | bytes 524288 | tf_op jit(solution)/shard_map/all_to_all | solution.py:349
  12.0 9.0 %collective-permute-start = (bf16[2,256]{1,0:T(2,128)(2,1)S(1)}, bf16[2,256]{1,0:T(2,128)(2,1)S(1)}, u32[]{:S(2)}, u32[]{:S(2)}) collective-permute-start(bf16[2,256]{1,0:T(2,128)(2,1)S(1)} %pad_maximum_fusion.refs_3_), channel_id=1, source_target_pairs={{0,1},{1,0},{2,3},{3,2},{4,5},{5,4},{6,7},{7,6},{8,9},{9,8},{10,11... | collective-permute-start | bytes 3080 | tf_op jit(solution)/shard_map/ppermute | solution.py:339
  21.7 14.4 %collective-permute-start.5 = (bf16[256,1536]{1,0:T(8,128)(2,1)}, bf16[256,1536]{1,0:T(8,128)(2,1)S(1)}, u32[]{:S(2)}, u32[]{:S(2)}) collective-permute-start(bf16[256,1536]{1,0:T(8,128)(2,1)} %kept_columns.1), channel_id=1, source_target_pairs={{0,1},{1,0},{2,3},{3,2},{4,5},{5,4},{6,7},{7,6},{8,9},{9,8},{10,11... | collective-permute-start | bytes 2359304 | tf_op jit(solution)/shard_map/ppermute | solution.py:339
  24.0 15.8 %copy-start.4 = (bf16[256,1536]{1,0:T(8,128)(2,1)}, bf16[256,1536]{1,0:T(8,128)(2,1)S(1)}, u32[]{:S(2)}) copy-start(bf16[256,1536]{1,0:T(8,128)(2,1)S(1)} %collective-permute-done.3.refs_6_.refs_4_) | copy-start | bytes 2359300
  24.0 12.1 %collective-permute-start.4 = (bf16[256,1536]{1,0:T(8,128)(2,1)S(1)}, bf16[256,1536]{1,0:T(8,128)(2,1)S(1)}, u32[]{:S(2)}, u32[]{:S(2)}) collective-permute-start(bf16[256,1536]{1,0:T(8,128)(2,1)S(1)} %collective-permute-done.3.refs_6_.refs_4_), channel_id=1, source_target_pairs={{0,1},{1,0},{2,3},{3,2},{4,5},{5,4},{6,7},{7,6},{8,9},{9,8},{10,11... | collective-permute-start | bytes 2359304 | tf_op jit(solution)/shard_map/ppermute | solution.py:339
  24.7 15.2 %copy-start.2 = (bf16[144,1024]{1,0:T(8,128)(2,1)}, bf16[144,1024]{1,0:T(8,128)(2,1)S(1)}, u32[]{:S(2)}) copy-start(bf16[144,1024]{1,0:T(8,128)(2,1)S(1)} %collect.1.refs_1_.refs_3_) | copy-start | bytes 884740
  24.7 9.8 %collective-permute-start.1 = (bf16[144,1024]{1,0:T(8,128)(2,1)S(1)}, bf16[144,1024]{1,0:T(8,128)(2,1)S(1)}, u32[]{:S(2)}, u32[]{:S(2)}) collective-permute-start(bf16[144,1024]{1,0:T(8,128)(2,1)S(1)} %collect.1.refs_1_.refs_3_), channel_id=1, source_target_pairs={{0,3},{1,2},{2,1},{3,0},{4,7},{5,6},{6,5},{7,4},{8,11},{9,10},{10,... | collective-permute-start | bytes 884744 | tf_op jit(solution)/shard_map/ppermute | solution.py:339
  27.3 15.0 %all-to-all-start.1 = ((bf16[8,16,1024]{2,1,0:T(8,128)(2,1)}), bf16[8,16,1024]{2,1,0:T(8,128)(2,1)S(1)}, u32[]{:S(2)}, u32[]{:S(2)}) async-start(bf16[8,16,1024]{2,1,0:T(8,128)(2,1)} %get-tuple-element.122), calls=%async_computation.1 | async-start | bytes 524288 | tf_op jit(solution)/shard_map/all_to_all | solution.py:349
  34.5 1.6 collective-permute-start.2
  40.8 27.1 %copy-start.20 = (f32[8,1024]{1,0:T(8,128)S(1)}, f32[8,1024]{1,0:T(8,128)}, u32[]{:S(2)}) copy-start(f32[8,1024]{1,0:T(8,128)} %get-tuple-element.119.refs_1_.refs_5_.refs_4_) | copy-start | bytes 98308
  40.8 7.6 %copy-start.38 = (bf16[256,1024]{1,0:T(8,128)(2,1)S(1)}, bf16[256,1024]{1,0:T(8,128)(2,1)}, u32[]{:S(2)}) copy-start(bf16[256,1024]{1,0:T(8,128)(2,1)} %refs_7_.1) | copy-start | bytes 1572868
  40.8 27.1 %collective-permute-start.7 = (bf16[704,1024]{1,0:T(8,128)(2,1)}, bf16[704,1024]{1,0:T(8,128)(2,1)}, u32[]{:S(2)}, u32[]{:S(2)}) collective-permute-start(bf16[704,1024]{1,0:T(8,128)(2,1)} %refs_3_.7), channel_id=1, source_target_pairs={{0,1},{1,0},{2,3},{3,2},{4,5},{5,4},{6,7},{7,6},{8,9},{9,8},{10,11... | collective-permute-start | bytes 4325384 | tf_op jit(solution)/shard_map/ppermute | solution.py:339
  42.3 28.2 %copy-start.11 = (bf16[256,1024]{1,0:T(8,128)(2,1)S(1)}, bf16[256,1024]{1,0:T(8,128)(2,1)}, u32[]{:S(2)}) copy-start(bf16[256,1024]{1,0:T(8,128)(2,1)} %get-tuple-element.190.refs_1_) | copy-start | bytes 1572868
  42.3 25.6 %all-to-all-start.2 = ((bf16[8,32,1536]{2,1,0:T(8,128)(2,1)}), bf16[8,32,1536]{2,1,0:T(8,128)(2,1)S(1)}, u32[]{:S(2)}, u32[]{:S(2)}) async-start(bf16[8,32,1536]{2,1,0:T(8,128)(2,1)} %copy-done.23), calls=%async_computation.2 | async-start | bytes 1572864 | tf_op jit(solution)/shard_map/all_to_all | solution.py:349
  47.4 34.1 %collective-permute-start.8 = (bf16[256,2816]{1,0:T(8,128)(2,1)}, bf16[256,2816]{1,0:T(8,128)(2,1)}, u32[]{:S(2)}, u32[]{:S(2)}) collective-permute-start(bf16[256,2816]{1,0:T(8,128)(2,1)} %copy-done.36), channel_id=1, source_target_pairs={{0,3},{1,2},{2,1},{3,0},{4,7},{5,6},{6,5},{7,4},{8,11},{9,10},{10,... | collective-permute-start | bytes 4325384 | tf_op jit(solution)/shard_map/ppermute | solution.py:339
  48.4 2.2 %collective-permute-start.6 = (bf16[256,1024]{1,0:T(8,128)(2,1)S(1)}, bf16[256,1024]{1,0:T(8,128)(2,1)S(1)}, u32[]{:S(2)}, u32[]{:S(2)}) collective-permute-start(bf16[256,1024]{1,0:T(8,128)(2,1)S(1)} %copy-done.38), channel_id=1, source_target_pairs={{0,1},{1,0},{2,3},{3,2},{4,5},{5,4},{6,7},{7,6},{8,9},{9,8},{10,11... | collective-permute-start | bytes 1572872 | tf_op jit(solution)/shard_map/ppermute | solution.py:339
  50.6 17.3 %copy-start.39 = (bf16[256,1024]{1,0:T(8,128)(2,1)}, bf16[256,1024]{1,0:T(8,128)(2,1)S(1)}, u32[]{:S(2)}) copy-start(bf16[256,1024]{1,0:T(8,128)(2,1)S(1)} %collective-permute-done.6.refs_2_.refs_8_) | copy-start | bytes 1572868
  70.5 16.7 %collective-permute-start.11 = (bf16[256,1024]{1,0:T(8,128)(2,1)S(1)}, bf16[256,1024]{1,0:T(8,128)(2,1)S(1)}, u32[]{:S(2)}, u32[]{:S(2)}) collective-permute-start(bf16[256,1024]{1,0:T(8,128)(2,1)S(1)} %copy-done.11), channel_id=1, source_target_pairs={{0,1},{1,0},{2,3},{3,2},{4,5},{5,4},{6,7},{7,6},{8,9},{9,8},{10,11... | collective-permute-start | bytes 1572872 | tf_op jit(solution)/shard_map/ppermute | solution.py:339
  70.6 16.6 %all-to-all-start.3 = ((bf16[8,32,512]{2,1,0:T(8,128)(2,1)}), bf16[8,32,512]{2,1,0:T(8,128)(2,1)S(1)}, u32[]{:S(2)}, u32[]{:S(2)}) async-start(bf16[8,32,512]{2,1,0:T(8,128)(2,1)} %attend.1), calls=%async_computation.3 | async-start | bytes 524288 | tf_op jit(solution)/shard_map/all_to_all | solution.py:349
  74.2 7.4 %collective-permute-start.10 = (bf16[128,1024]{1,0:T(8,128)(2,1)S(1)}, bf16[128,1024]{1,0:T(8,128)(2,1)S(1)}, u32[]{:S(2)}, u32[]{:S(2)}) collective-permute-start(bf16[128,1024]{1,0:T(8,128)(2,1)S(1)} %collect_rows.1.refs_1_.refs_5_.refs_3_), channel_id=1, source_target_pairs={{0,1},{1,0},{2,3},{3,2},{4,5},{5,4},{6,7},{7,6},{8,9},{9,8},{10,11... | collective-permute-start | bytes 786440 | tf_op jit(solution)/shard_map/ppermute | solution.py:339
  74.5 12.6 %collective-permute-start.9 = (bf16[128,1024]{1,0:T(8,128)(2,1)S(1)}, bf16[128,1024]{1,0:T(8,128)(2,1)S(1)}, u32[]{:S(2)}, u32[]{:S(2)}) collective-permute-start(bf16[128,1024]{1,0:T(8,128)(2,1)S(1)} %collect_rows.1.refs_1_.refs_5_.refs_3_), channel_id=1, source_target_pairs={{0,2},{1,3},{2,0},{3,1},{4,6},{5,7},{6,4},{7,5},{8,10},{9,11},{10,... | collective-permute-start | bytes 786440 | tf_op jit(solution)/shard_map/ppermute | solution.py:339
  81.5 13.9 %copy-start.29 = (bf16[128,1024]{1,0:T(8,128)(2,1)}, bf16[128,1024]{1,0:T(8,128)(2,1)S(1)}, u32[]{:S(2)}) copy-start(bf16[128,1024]{1,0:T(8,128)(2,1)S(1)} %collective-permute-done.10.refs_5_) | copy-start | bytes 786436
  87.1 8.3 %copy-start.13 = (bf16[256,1024]{1,0:T(8,128)(2,1)}, bf16[256,1024]{1,0:T(8,128)(2,1)S(1)}, u32[]{:S(2)}) copy-start(bf16[256,1024]{1,0:T(8,128)(2,1)S(1)} %collective-permute-done.11.refs_2_) | copy-start | bytes 1572868
  89.4 6.1 %copy-start.33 = (bf16[256,512]{1,0:T(8,128)(2,1)}, bf16[256,512]{1,0:T(8,128)(2,1)S(1)}, u32[]{:S(2)}) copy-start(bf16[256,512]{1,0:T(8,128)(2,1)S(1)} %get-tuple-element.137.refs_1_) | copy-start | bytes 786436
  89.4 14.5 %collective-permute-start.14 = (bf16[256,2816]{1,0:T(8,128)(2,1)}, bf16[256,2816]{1,0:T(8,128)(2,1)S(1)}, u32[]{:S(2)}, u32[]{:S(2)}) collective-permute-start(bf16[256,2816]{1,0:T(8,128)(2,1)} %collective-permute-done.8.refs_10_), channel_id=1, source_target_pairs={{0,1},{1,0},{2,3},{3,2},{4,5},{5,4},{6,7},{7,6},{8,9},{9,8},{10,11... | collective-permute-start | bytes 4325384 | tf_op jit(solution)/shard_map/ppermute | solution.py:339
  89.5 14.4 %collective-permute-start.15 = (bf16[256,2816]{1,0:T(8,128)(2,1)}, bf16[256,2816]{1,0:T(8,128)(2,1)S(1)}, u32[]{:S(2)}, u32[]{:S(2)}) collective-permute-start(bf16[256,2816]{1,0:T(8,128)(2,1)} %copy-done.17), channel_id=1, source_target_pairs={{0,1},{1,0},{2,3},{3,2},{4,5},{5,4},{6,7},{7,6},{8,9},{9,8},{10,11... | collective-permute-start | bytes 4325384 | tf_op jit(solution)/shard_map/ppermute | solution.py:339
  89.9 13.9 %collective-permute-start.12 = (bf16[256,1024]{1,0:T(8,128)(2,1)S(1)}, bf16[256,1024]{1,0:T(8,128)(2,1)S(1)}, u32[]{:S(2)}, u32[]{:S(2)}) collective-permute-start(bf16[256,1024]{1,0:T(8,128)(2,1)S(1)} %get-tuple-element.136), channel_id=1, source_target_pairs={{0,2},{1,3},{2,0},{3,1},{4,6},{5,7},{6,4},{7,5},{8,10},{9,11},{10,... | collective-permute-start | bytes 1572872 | tf_op jit(solution)/shard_map/ppermute | solution.py:339
  91.5 4.0 %collective-permute-start.16 = (bf16[128,1024]{1,0:T(8,128)(2,1)S(1)}, bf16[128,1024]{1,0:T(8,128)(2,1)S(1)}, u32[]{:S(2)}, u32[]{:S(2)}) collective-permute-start(bf16[128,1024]{1,0:T(8,128)(2,1)S(1)} %collective-permute-done.9.refs_2_.refs_6_.refs_4_), channel_id=1, source_target_pairs={{0,1},{1,0},{2,3},{3,2},{4,5},{5,4},{6,7},{7,6},{8,9},{9,8},{10,11... | collective-permute-start | bytes 786440 | tf_op jit(solution)/shard_map/ppermute | solution.py:339
  91.5 4.2 %collective-permute-start.13 = (bf16[256,512]{1,0:T(8,128)(2,1)S(1)}, bf16[256,512]{1,0:T(8,128)(2,1)S(1)}, u32[]{:S(2)}, u32[]{:S(2)}) collective-permute-start(bf16[256,512]{1,0:T(8,128)(2,1)S(1)} %get-tuple-element.137.refs_1_), channel_id=1, source_target_pairs={{0,1},{1,0},{2,3},{3,2},{4,5},{5,4},{6,7},{7,6},{8,9},{9,8},{10,11... | collective-permute-start | bytes 786440 | tf_op jit(solution)/shard_map/ppermute | solution.py:339
  95.5 16.7 %copy-start.31 = (bf16[128,1024]{1,0:T(8,128)(2,1)}, bf16[128,1024]{1,0:T(8,128)(2,1)S(1)}, u32[]{:S(2)}) copy-start(bf16[128,1024]{1,0:T(8,128)(2,1)S(1)} %collective-permute-done.16.refs_6_) | copy-start | bytes 786436
  95.7 8.2 %copy-start.40 = (bf16[256,512]{1,0:T(8,128)(2,1)}, bf16[256,512]{1,0:T(8,128)(2,1)S(1)}, u32[]{:S(2)}) copy-start(bf16[256,512]{1,0:T(8,128)(2,1)S(1)} %collective-permute-done.13.refs_2_) | copy-start | bytes 786436
  112.2 6.5 %copy-start = (bf16[256,2816]{1,0:T(8,128)(2,1)}, bf16[256,2816]{1,0:T(8,128)(2,1)S(1)}, u32[]{:S(2)}) copy-start(bf16[256,2816]{1,0:T(8,128)(2,1)S(1)} %get-tuple-element.158.refs_3_) | copy-start | bytes 4325380
  112.2 6.5 %copy-start.15 = (bf16[256,1024]{1,0:T(8,128)(2,1)}, bf16[256,1024]{1,0:T(8,128)(2,1)S(1)}, u32[]{:S(2)}) copy-start(bf16[256,1024]{1,0:T(8,128)(2,1)S(1)} %get-tuple-element.163.refs_1_) | copy-start | bytes 1572868
  112.2 6.4 %collective-permute-start.19 = (bf16[256,2816]{1,0:T(8,128)(2,1)S(1)}, bf16[256,2816]{1,0:T(8,128)(2,1)S(1)}, u32[]{:S(2)}, u32[]{:S(2)}) collective-permute-start(bf16[256,2816]{1,0:T(8,128)(2,1)S(1)} %get-tuple-element.158.refs_3_), channel_id=1, source_target_pairs={{0,1},{1,0},{2,3},{3,2},{4,5},{5,4},{6,7},{7,6},{8,9},{9,8},{10,11... | collective-permute-start | bytes 4325384 | tf_op jit(solution)/shard_map/ppermute | solution.py:339
  112.3 14.8 %collective-permute-start.20 = (bf16[256,1408]{1,0:T(8,128)(2,1)S(1)}, bf16[256,1408]{1,0:T(8,128)(2,1)S(1)}, u32[]{:S(2)}, u32[]{:S(2)}) collective-permute-start(bf16[256,1408]{1,0:T(8,128)(2,1)S(1)} %get-tuple-element.168.refs_1_), channel_id=1, source_target_pairs={{0,1},{1,0},{2,3},{3,2},{4,5},{5,4},{6,7},{7,6},{8,9},{9,8},{10,11... | collective-permute-start | bytes 2162696 | tf_op jit(solution)/shard_map/ppermute | solution.py:339
  112.8 5.8 %collective-permute-start.18 = (bf16[256,1024]{1,0:T(8,128)(2,1)S(1)}, bf16[256,1024]{1,0:T(8,128)(2,1)S(1)}, u32[]{:S(2)}, u32[]{:S(2)}) collective-permute-start(bf16[256,1024]{1,0:T(8,128)(2,1)S(1)} %get-tuple-element.163.refs_1_), channel_id=1, source_target_pairs={{0,1},{1,0},{2,3},{3,2},{4,5},{5,4},{6,7},{7,6},{8,9},{9,8},{10,11... | collective-permute-start | bytes 1572872 | tf_op jit(solution)/shard_map/ppermute | solution.py:339
  112.9 14.3 %collective-permute-start.17 = (bf16[256,1024]{1,0:T(8,128)(2,1)S(1)}, bf16[256,1024]{1,0:T(8,128)(2,1)S(1)}, u32[]{:S(2)}, u32[]{:S(2)}) collective-permute-start(bf16[256,1024]{1,0:T(8,128)(2,1)S(1)} %get-tuple-element.150), channel_id=1, source_target_pairs={{0,2},{1,3},{2,0},{3,1},{4,6},{5,7},{6,4},{7,5},{8,10},{9,11},{10,... | collective-permute-start | bytes 1572872 | tf_op jit(solution)/shard_map/ppermute | solution.py:339
  118.6 8.5 %copy-start.21 = (f32[8,1024]{1,0:T(8,128)S(1)}, f32[8,1024]{1,0:T(8,128)}, u32[]{:S(2)}) copy-start(f32[8,1024]{1,0:T(8,128)} %get-tuple-element.119.refs_1_.refs_5_.refs_4_) | copy-start | bytes 98308
  130.5 15.7 %collective-permute-start.21 = (bf16[256,1024]{1,0:T(8,128)(2,1)}, bf16[256,1024]{1,0:T(8,128)(2,1)}, u32[]{:S(2)}, u32[]{:S(2)}) collective-permute-start(bf16[256,1024]{1,0:T(8,128)(2,1)} %get-tuple-element.173.refs_3_), channel_id=1, source_target_pairs={{0,1},{1,0},{2,3},{3,2},{4,5},{5,4},{6,7},{7,6},{8,9},{9,8},{10,11... | collective-permute-start | bytes 1572872 | tf_op jit(solution)/shard_map/ppermute | solution.py:339
  130.6 15.6 %all-to-all-start.4 = ((bf16[8,32,512]{2,1,0:T(8,128)(2,1)}), bf16[8,32,512]{2,1,0:T(8,128)(2,1)S(1)}, u32[]{:S(2)}, u32[]{:S(2)}) async-start(bf16[8,32,512]{2,1,0:T(8,128)(2,1)} %get-tuple-element.160), calls=%async_computation.4 | async-start | bytes 524288 | tf_op jit(solution)/shard_map/all_to_all | solution.py:349
  136.6 40.4 %collective-permute-start.23 = (bf16[256,2816]{1,0:T(8,128)(2,1)}, bf16[256,2816]{1,0:T(8,128)(2,1)S(1)}, u32[]{:S(2)}, u32[]{:S(2)}) collective-permute-start(bf16[256,2816]{1,0:T(8,128)(2,1)} %copy-done.18), channel_id=1, source_target_pairs={{0,3},{1,2},{2,1},{3,0},{4,7},{5,6},{6,5},{7,4},{8,11},{9,10},{10,... | collective-permute-start | bytes 4325384 | tf_op jit(solution)/shard_map/ppermute | solution.py:339
  137.5 7.3 %collective-permute-start.22 = (f32[1,256]{1,0:T(1,128)S(1)}, f32[1,256]{1,0:T(1,128)S(1)}, u32[]{:S(2)}, u32[]{:S(2)}) collective-permute-start(f32[1,256]{1,0:T(1,128)S(1)} %slice_bitcast_fusion.2), channel_id=1, source_target_pairs={{0,1},{1,0},{2,3},{3,2},{4,5},{5,4},{6,7},{7,6},{8,9},{9,8},{10,11... | collective-permute-start | bytes 3080 | tf_op jit(solution)/shard_map/ppermute | solution.py:339
  151.7 25.3 %all-to-all-start.5 = ((bf16[8,32,1536]{2,1,0:T(8,128)(2,1)}), bf16[8,32,1536]{2,1,0:T(8,128)(2,1)S(1)}, u32[]{:S(2)}, u32[]{:S(2)}) async-start(bf16[8,32,1536]{2,1,0:T(8,128)(2,1)} %attend_back.1), calls=%async_computation.5 | async-start | bytes 1572864 | tf_op jit(solution)/shard_map/all_to_all | solution.py:349
  156.3 4.5 %copy-start.25 = (bf16[256,1408]{1,0:T(8,128)(2,1)S(1)}, bf16[256,1408]{1,0:T(8,128)(2,1)}, u32[]{:S(2)}) copy-start(bf16[256,1408]{1,0:T(8,128)(2,1)} %copy-done.24) | copy-start | bytes 2162692
  156.4 19.9 %collective-permute-start.24 = (bf16[128,1024]{1,0:T(8,128)(2,1)}, bf16[128,1024]{1,0:T(8,128)(2,1)S(1)}, u32[]{:S(2)}, u32[]{:S(2)}) collective-permute-start(bf16[128,1024]{1,0:T(8,128)(2,1)} %copy-done.37), channel_id=1, source_target_pairs={{0,2},{1,3},{2,0},{3,1},{4,6},{5,7},{6,4},{7,5},{8,10},{9,11},{10,... | collective-permute-start | bytes 786440 | tf_op jit(solution)/shard_map/ppermute | solution.py:339
  165.5 17.9 %copy-start.12 = (bf16[256,1024]{1,0:T(8,128)(2,1)S(1)}, bf16[256,1024]{1,0:T(8,128)(2,1)}, u32[]{:S(2)}) copy-start(bf16[256,1024]{1,0:T(8,128)(2,1)} %get-tuple-element.190.refs_1_) | copy-start | bytes 1572868
  165.6 17.9 %copy-start.14 = (bf16[256,1024]{1,0:T(8,128)(2,1)S(1)}, bf16[256,1024]{1,0:T(8,128)(2,1)}, u32[]{:S(2)}) copy-start(bf16[256,1024]{1,0:T(8,128)(2,1)} %copy-done.13) | copy-start | bytes 1572868
  181.1 4.7 %copy-start.7 = (bf16[256,1536]{1,0:T(8,128)(2,1)}, bf16[256,1536]{1,0:T(8,128)(2,1)S(1)}, u32[]{:S(2)}) copy-start(bf16[256,1536]{1,0:T(8,128)(2,1)S(1)} %get-tuple-element.179.refs_3_) | copy-start | bytes 2359300
  181.1 2.4 %collective-permute-start.26 = (bf16[256,1536]{1,0:T(8,128)(2,1)S(1)}, bf16[256,1536]{1,0:T(8,128)(2,1)S(1)}, u32[]{:S(2)}, u32[]{:S(2)}) collective-permute-start(bf16[256,1536]{1,0:T(8,128)(2,1)S(1)} %get-tuple-element.179.refs_3_), channel_id=1, source_target_pairs={{0,1},{1,0},{2,3},{3,2},{4,5},{5,4},{6,7},{7,6},{8,9},{9,8},{10,11... | collective-permute-start | bytes 2359304 | tf_op jit(solution)/shard_map/ppermute | solution.py:339
  181.2 9.1 %copy-start.3 = (bf16[144,1024]{1,0:T(8,128)(2,1)S(1)}, bf16[144,1024]{1,0:T(8,128)(2,1)}, u32[]{:S(2)}) copy-start(bf16[144,1024]{1,0:T(8,128)(2,1)} %copy-done.2) | copy-start | bytes 884740
  181.2 9.1 %copy-start.22 = (f32[8,1024]{1,0:T(8,128)S(1)}, f32[8,1024]{1,0:T(8,128)}, u32[]{:S(2)}) copy-start(f32[8,1024]{1,0:T(8,128)} %get-tuple-element.119.refs_1_.refs_5_.refs_4_) | copy-start | bytes 98308
  181.2 9.1 %copy-start.27 = (f32[128,1024]{1,0:T(8,128)S(1)}, f32[128,1024]{1,0:T(8,128)}, u32[]{:S(2)}) copy-start(f32[128,1024]{1,0:T(8,128)} %copy-done.26) | copy-start | bytes 1572868
  181.2 9.1 %copy-start.28 = (f32[128,1024]{1,0:T(8,128)S(1)}, f32[128,1024]{1,0:T(8,128)}, u32[]{:S(2)}) copy-start(f32[128,1024]{1,0:T(8,128)} %get-tuple-element.181.refs_5_) | copy-start | bytes 1572868
  181.2 9.1 %copy-start.35 = (bf16[128,1024]{1,0:T(8,128)(2,1)S(1)}, bf16[128,1024]{1,0:T(8,128)(2,1)}, u32[]{:S(2)}) copy-start(bf16[128,1024]{1,0:T(8,128)(2,1)} %copy-done.34) | copy-start | bytes 786436
  181.2 8.7 %collective-permute-start.25 = (bf16[128,1024]{1,0:T(8,128)(2,1)S(1)}, bf16[128,1024]{1,0:T(8,128)(2,1)S(1)}, u32[]{:S(2)}, u32[]{:S(2)}) collective-permute-start(bf16[128,1024]{1,0:T(8,128)(2,1)S(1)} %get-tuple-element.177), channel_id=1, source_target_pairs={{0,2},{1,3},{2,0},{3,1},{4,6},{5,7},{6,4},{7,5},{8,10},{9,11},{10,... | collective-permute-start | bytes 786440 | tf_op jit(solution)/shard_map/ppermute | solution.py:339
  190.0 19.8 %collective-permute-start.27 = (bf16[256,1536]{1,0:T(8,128)(2,1)S(1)}, bf16[256,1536]{1,0:T(8,128)(2,1)}, u32[]{:S(2)}, u32[]{:S(2)}) collective-permute-start(bf16[256,1536]{1,0:T(8,128)(2,1)S(1)} %leaving_gradient.3), channel_id=1, source_target_pairs={{0,3},{1,2},{2,1},{3,0},{4,7},{5,6},{6,5},{7,4},{8,11},{9,10},{10,... | collective-permute-start | bytes 2359304 | tf_op jit(solution)/shard_map/ppermute | solution.py:339
  192.2 22.4 %all-to-all-start.6 = ((bf16[8,32,1024]{2,1,0:T(8,128)(2,1)}), bf16[8,32,1024]{2,1,0:T(8,128)(2,1)S(1)}, u32[]{:S(2)}, u32[]{:S(2)}) async-start(bf16[8,32,1024]{2,1,0:T(8,128)(2,1)} %get-tuple-element.184), calls=%async_computation.6 | async-start | bytes 1048576 | tf_op jit(solution)/shard_map/all_to_all | solution.py:349
  198.2 11.5 %collective-permute-start.29 = (f32[2,1,256]{2,1,0:T(1,128)S(1)}, f32[2,1,256]{2,1,0:T(1,128)S(1)}, u32[]{:S(2)}, u32[]{:S(2)}) collective-permute-start(f32[2,1,256]{2,1,0:T(1,128)S(1)} %slice.20), channel_id=1, source_target_pairs={{0,2},{1,3},{2,0},{3,1},{4,6},{5,7},{6,4},{7,5},{8,10},{9,11},{10,... | collective-permute-start | bytes 6152 | tf_op jit(solution)/shard_map/ppermute | solution.py:339
  209.7 3.1 %collective-permute-start.28 = (bf16[256,1536]{1,0:T(8,128)(2,1)}, bf16[256,1536]{1,0:T(8,128)(2,1)S(1)}, u32[]{:S(2)}, u32[]{:S(2)}) collective-permute-start(bf16[256,1536]{1,0:T(8,128)(2,1)} %collective-permute-done.27), channel_id=1, source_target_pairs={{0,1},{1,0},{2,3},{3,2},{4,5},{5,4},{6,7},{7,6},{8,9},{9,8},{10,11... | collective-permute-start | bytes 2359304 | tf_op jit(solution)/shard_map/ppermute | solution.py:339
  209.7 2.5 %collective-permute-start.30 = (f32[1,256]{1,0:T(1,128)S(1)}, f32[1,256]{1,0:T(1,128)S(1)}, u32[]{:S(2)}, u32[]{:S(2)}) collective-permute-start(f32[1,256]{1,0:T(1,128)S(1)} %slice_bitcast_fusion), channel_id=1, source_target_pairs={{0,1},{1,0},{2,3},{3,2},{4,5},{5,4},{6,7},{7,6},{8,9},{9,8},{10,11... | collective-permute-start | bytes 3080 | tf_op jit(solution)/shard_map/ppermute | solution.py:339
  (18 other events, 53.2 us)

commit v5 on v4

--- a/solution.py
+++ b/solution.py
@@ -764,54 +764,65 @@
     )
 
 
-def d_hidden_kernel(ready, place, c_a, c_b, w_own, w_near, d_hidden, w, sems):
+def aside_kernel(ready, place, x_a, x_b, term, c_a, c_b, w_own, w_near, base, d_hidden, w, sems):
     copies = chip_rows(place, w_own, w_near, w, sems)
     for copy in copies:
         copy.start()
     ready()
+    half = c_a.shape[0]
+    for rel, ref in enumerate((x_a, x_b)):
+        at = pl.ds(rel * half, half)
+        base[at, :] = ref[:half, :].astype(F32) + term[at, :]
     upstream = jnp.concatenate([c_a[...], c_b[...]], 0)
     for copy in copies:
         copy.wait()
     inner = w.shape[0]
-    for base in range(0, inner, 256):
-        end = min(base + 256, inner)
-        d_hidden[:, base:end] = times_transposed(upstream, w[base:end, :])
-
-
-def d_hidden_rows(place, c_a, c_b, w_own, w_near):
+    for low in range(0, inner, 256):
+        high = min(low + 256, inner)
+        d_hidden[:, low:high] = times_transposed(upstream, w[low:high, :])
+
+
+def aside(place, x_a, x_b, term, c_a, c_b, w_own, w_near):
     rows, inner = 2 * c_a.shape[0], 2 * w_own.shape[0]
     return kernel_call(
-        d_hidden_kernel,
-        "d_hidden",
-        [(SMEM, place), (MOVED, c_a), (MOVED, c_b), (HBM, w_own), (HBM, w_near)],
-        [((rows, inner), F32)],
+        aside_kernel,
+        "aside",
+        [(SMEM, place), (MOVED, x_a), (MOVED, x_b), (VMEM, term), (MOVED, c_a), (MOVED, c_b),
+         (HBM, w_own), (HBM, w_near)],
+        [((rows, D), F32), ((rows, inner), F32)],
         [pltpu.VMEM((inner, D), BF16), pltpu.SemaphoreType.DMA((2,))],
-    )[0]
+    )
 
 
 def ffn_kernel(
-    ready, place, x_a, x_b, term, far, table, d_hidden_all, *rest
+    ready, place, base, far, table, d_hidden_all, *rest
 ):
-    pieces = rest[:4]
-    resid, lowered, hidden, d_gate_up, second, leaving = rest[4:10]
-    w, sems = rest[10:]
-    half, width, steps = term.shape[0] // 2, pieces[0].shape[0], w.shape[0]
-
-    def begin(j, carry):
-        for rank, source in enumerate(pieces):
+    kept, near, far_a, across_a, far_b, across_b = rest[:6]
+    resid, lowered, hidden, d_gate_up, second, leaving = rest[6:12]
+    w, sems = rest[12:]
+    half, width, steps = base.shape[0] // 2, kept.shape[0], w.shape[0]
+    split = far_a.shape[1] // 256
+
+    def begin(arrived, j, carry):
+        sources = ((kept, OWN, 0), (near, NEAR, 0)) + arrived
+        for source, rank, before in sources:
             pltpu.make_async_copy(
-                source.at[:, aligned(j * 256, 256)],
+                source.at[:, aligned((j - before) * 256, 256)],
                 w.at[j, aligned(place[rank] * width, width)],
                 sems.at[j, rank],
             ).start()
         return carry
 
-    lax.fori_loop(0, steps, begin, 0)
+    for low, high, far_part, across_part in (
+        (0, split, far_a, across_a), (split, steps, far_b, across_b)
+    ):
+        arrived = ((far_part, FAR, low), (across_part, ACROSS, low))
+        lax.fori_loop(low, high, functools.partial(begin, arrived), 0)
     ready()
     gain = table[1:2, :]
-    for rel, x_ref in enumerate((x_a, x_b)):
+    for rel in range(2):
         at = pl.ds(rel * half, half)
-        rows = x_ref[:half, :].astype(F32) + (term[at, :] + far[at, :].astype(F32))
+        rows = base[at, :] + far[at, :].astype(F32)
         resid[at, :] = rows
         scale = lax.rsqrt(jnp.mean(rows * rows, axis=-1, keepdims=True) + EPSILON)
         lowered[at, :] = (rows * scale * gain).astype(BF16)
@@ -847,15 +858,15 @@
     lax.fori_loop(0, D // 256, back, 0)
 
 
-def ffn(place, x_a, x_b, term, far, table, d_hidden, pieces):
+def ffn(place, base, far, table, d_hidden, pieces):
     rows, inner = d_hidden.shape
     wide, steps = 2 * inner, inner // 128
     return kernel_call(
         ffn_kernel,
         "ffn",
         [(SMEM, place)]
-        + in_stage(x_a, x_b) + in_vmem(term, far) + in_stage(table) + in_vmem(d_hidden)
-        + [(EITHER if rank in (FAR, NEAR) else HBM, a) for rank, a in enumerate(pieces)],
+        + in_vmem(base, far) + moved(table) + in_vmem(d_hidden)
+        + [(HBM if n in (0, 3, 5) else EITHER, a) for n, a in enumerate(pieces)],
         [((rows, D), F32), ((rows, D), BF16), ((rows, inner), BF16), ((rows, wide), BF16),
          ((rows, D), F32), ((rows, D), BF16)],
         [pltpu.VMEM((steps, D, 256), BF16), pltpu.SemaphoreType.DMA((steps, 4))],
@@ -1226,17 +1237,18 @@
     )[0]
 
 
-def spread_kernel(ready, place, weight, kept, leaving, sems):
+def spread_kernel(split, ready, place, weight, kept, leaving_a, leaving_b, sems):
     part = weight.shape[1] // 4
     side = place[SIDE]
     copies = []
     for k in range(2):
         for j in range(part // 128):
-            for who, target in ((side, kept), (1 - side, leaving)):
+            leaving, at = (leaving_a, j) if j < split else (leaving_b, j - split)
+            for who, target, spot in ((side, kept, j), (1 - side, leaving, at)):
                 copies.append(
                     pltpu.make_async_copy(
                         weight.at[:, aligned((2 * k + who) * part + j * 128, 128)],
-                        target.at[:, pl.ds(j * 256 + k * 128, 128)],
+                        target.at[:, pl.ds(spot * 256 + k * 128, 128)],
                         sems.at[len(copies)],
                     )
                 )
@@ -1246,13 +1258,13 @@
         copy.wait()
 
 
-def spread(place, weight):
+def spread(place, weight, split):
     count, width = weight.shape
     return kernel_call(
-        spread_kernel,
+        functools.partial(spread_kernel, split),
         "spread",
         [(SMEM, place), (HBM, weight)],
-        [((count, width // 2), BF16)] * 2,
+        [((count, size), BF16) for size in (width // 2, 256 * split, width // 2 - 256 * split)],
         [pltpu.SemaphoreType.DMA((width // 128,))],
     )
 
@@ -1285,22 +1297,23 @@
     gains_own = jnp.stack([gain_attn, gain_ffn])
     gains_near = near(after(gains_own, qkv_leaving))
     qkv_kept = kept_columns(place, after(w_qkv, qkv_leaving))
-    w_kept, w_leaving = spread(place, after(w_gate_up, qkv_leaving))
-    x_came, ids_own, gains_near, qkv_kept, w_kept, w_leaving = sync(
-        x_came, ids_own, gains_near, qkv_kept, w_kept, w_leaving
+    w_kept, leaving_a, leaving_b = spread(place, after(w_gate_up, qkv_leaving), 3)
+    x_came, ids_own, gains_near, qkv_kept, w_kept, leaving_a, leaving_b = sync(
+        x_came, ids_own, gains_near, qkv_kept, w_kept, leaving_a, leaving_b
     )
 
     x_own = collect(place, x_came, ids_own, gains_own, gains_near)
     x_far = near(swap(x_own, 3))
     qkv_near = near(qkv_kept)
     c_came = exchange([after(c_sent[0], x_own)])
-    x_far, qkv_far, qkv_near, w_leaving = sync(x_far, qkv_far, qkv_near, w_leaving)
-
-    w_across = swap(w_leaving, 3)
+    across_a = swap(after(leaving_a, x_own), 3)
+    x_far, qkv_far, qkv_near, leaving_b = sync(x_far, qkv_far, qkv_near, leaving_b)
+
+    across_b = swap(leaving_b, 3)
     qkv_sent, lowered_first, table = first(
         place, x_own, x_far, w_qkv, qkv_far, qkv_near, qkv_across
     )
-    qkv_sent, c_came = sync(qkv_sent, c_came)
+    qkv_sent, c_came, across_a = sync(qkv_sent, c_came, across_a)
     c_own = collect_rows(place, c_came)
     out_near, down_near = (near(after(a, lowered_first)) for a in (w_out, w_down))
     qkv, out_near, down_near, c_own = sync(exchange(qkv_sent), out_near, down_near, c_own)
@@ -1310,20 +1323,23 @@
     c_own_near, lowered_first_near = (
         near(after(a, mixed_sent[0])) for a in (c_own, lowered_first)
     )
-    mixed, w_across, c_far, c_own_near, lowered_first_near = sync(
-        exchange(mixed_sent), w_across, c_far, c_own_near, lowered_first_near
+    mixed, across_b, c_far, c_own_near, lowered_first_near = sync(
+        exchange(mixed_sent), across_b, c_far, c_own_near, lowered_first_near
     )
 
     term, leaving, mixed = out_term(place, mixed, w_out, out_near)
     far = swap(leaving, 2)
-    d_hidden = d_hidden_rows(place, c_own, after(c_far, leaving), w_down, down_near)
-    w_near = near(after(w_kept, leaving))
-    far, mixed_near, w_far, w_near, c_far_near, d_hidden = sync(
-        far, near(mixed), near(after(w_across, leaving)), w_near, near(after(c_far, leaving)),
-        d_hidden,
+    base, d_hidden = aside(
+        place, x_own, x_far, term, c_own, after(c_far, leaving), w_down, down_near
+    )
+    mixed_near, far_a, far_b, w_near, c_far_near = (
+        near(after(a, leaving)) for a in (mixed, across_a, across_b, w_kept, c_far)
+    )
+    far, base, d_hidden, mixed_near, far_a, far_b, w_near, c_far_near = sync(
+        far, base, d_hidden, mixed_near, far_a, far_b, w_near, c_far_near
     )
     resid, lowered_second, hidden, d_gate_up, second, leaving = ffn(
-        place, x_own, x_far, term, far, table, d_hidden, (w_kept, w_far, w_near, w_across)
+        place, base, far, table, d_hidden, (w_kept, w_near, far_a, across_a, far_b, across_b)
     )
 
     second_far = swap(leaving, 2)

time: 218 us -> 215 us (0.986)
  starting transfers between devices: 56.6 us -> 53.8 us
    ppermute x31 -> x33, starting transfers between devices: 19.6 us -> 16.9 us  [swap(): return lax.ppermute(block, 'fsdp', [(i, i ^ mask) for i in range(count)])]
    unnamed x88 -> x78, local copies, waits for them, and re-layouts: 5.03 us -> 4.39 us
    ppermute x31 -> x33, waiting for transfers between devices: 49.5 us -> 49.8 us  [swap(): return lax.ppermute(block, 'fsdp', [(i, i ^ mask) for i in range(count)])]
  transfers between devices with their start and end apart: 38 -> 40, of which waited for: 18 -> 19; matrix products, arithmetic and copies ran while one was open for 1% -> 1% of each run, Pallas kernels for 27% -> 28%
where the time goes in v5:
time: 215 us; the launch traced here: 214 us
  Pallas kernels  81.9 us (38%)
  waiting for transfers between devices  70.6 us (33%)
  starting transfers between devices  53.8 us (25%)
  local copies, waits for them, and re-layouts  5.28 us (2%)
    pallas_call x24, Pallas kernels, kernel_call(): pl.pallas_call(body_kernel, name=name, in_specs=[spec for spec, _ in flat...  81.9 us
    ppermute x33, waiting for transfers between devices, swap(): return lax.ppermute(block, 'fsdp', [(i, i ^ mask) for i in range(count)])  49.8 us
    all_to_all x7, starting transfers between devices, exchange(): lax.all_to_all(blocks[0], 'fsdp', split_axis=0, concat_axis=0, tiled=True...  36.9 us
    all_to_all x7, waiting for transfers between devices, exchange(): lax.all_to_all(blocks[0], 'fsdp', split_axis=0, concat_axis=0, tiled=True...  20.8 us
    ppermute x33, starting transfers between devices, swap(): return lax.ppermute(block, 'fsdp', [(i, i ^ mask) for i in range(count)])  16.9 us
    unnamed x78, local copies, waits for them, and re-layouts  4.39 us
  transfers between devices with their start and end apart: 40, of which 19 were waited for; matrix products, arithmetic and copies ran while one was open for 1% of the time, Pallas kernels for 28%

profile of v5, /device:TPU:0, one launch (start us, length us, event | category | flops | bytes accessed | tf_op | source)
XLA Modules:
  0.0 214.3 jit_solution(10121525889981626033)
XLA Ops:
  0.8 2.9 %to_positions.1 = (bf16[8,16,1024]{2,1,0:T(8,128)(2,1)}, bf16[8,16,1024]{2,1,0:T(8,128)(2,1)}, bf16[256,1536]{1,0:T(8,128)(2,1)S(1)}) custom-call(s32[7]{0:T(128)S(1)} %stack.40.refs_0_, bf16[128,1024]{1,0:T(8,128)(2,1)} %refs_1_.3, bf16[128,1024]{1,0:T(8,128)(2,1)} %refs_2_.1, bf16[256,3072]{1,0:T(8,128)(2,1)} %refs_1_.7), custom_call_target="tpu_custom_call" | custom-call | flops 1 | bytes 1 | tf_op jit(solution)/shard_map/to_positions/pallas_call | solution.py:395
  3.6 2.5 %collective-permute-start.3 = (bf16[256,1536]{1,0:T(8,128)(2,1)S(1)}, bf16[256,1536]{1,0:T(8,128)(2,1)S(1)}, u32[]{:S(2)}, u32[]{:S(2)}) collective-permute-start(bf16[256,1536]{1,0:T(8,128)(2,1)S(1)} %get-tuple-element.115), channel_id=1, source_target_pairs={{0,3},{1,2},{2,1},{3,0},{4,7},{5,6},{6,5},{7,4},{8,11},{9,10},{10,... | collective-permute-start | bytes 2359304 | tf_op jit(solution)/shard_map/ppermute | solution.py:339
  6.1 5.8 %all-to-all-start = ((bf16[8,16,1024]{2,1,0:T(8,128)(2,1)}), bf16[8,16,1024]{2,1,0:T(8,128)(2,1)S(1)}, u32[]{:S(2)}, u32[]{:S(2)}) async-start(bf16[8,16,1024]{2,1,0:T(8,128)(2,1)} %get-tuple-element.114), calls=%async_computation | async-start | bytes 524288 | tf_op jit(solution)/shard_map/all_to_all | solution.py:349
  13.3 2.6 %kept_columns.1 = bf16[256,1536]{1,0:T(8,128)(2,1)} custom-call(s32[7]{0:T(128)S(1)} %stack.40.refs_0_, bf16[256,3072]{1,0:T(8,128)(2,1)} %refs_1_.7), custom_call_target="tpu_custom_call" | custom-call | flops 1 | bytes 1 | tf_op jit(solution)/shard_map/kept_columns/pallas_call | solution.py:395
  15.9 2.8 %spread.1 = (bf16[256,2816]{1,0:T(8,128)(2,1)S(1)}, bf16[256,768]{1,0:T(8,128)(2,1)S(1)}, bf16[256,2048]{1,0:T(8,128)(2,1)S(1)}) custom-call(s32[7]{0:T(128)S(1)} %stack.40.refs_0_, bf16[256,5632]{1,0:T(8,128)(2,1)} %refs_1_.5), custom_call_target="tpu_custom_call" | custom-call | flops 1 | bytes 1 | tf_op jit(solution)/shard_map/spread/pallas_call | solution.py:395
  18.7 1.1 copy-done.18
  19.8 1.0 copy-done.31
  20.9 0.8 all-to-all-done.refs_1_
  21.7 2.3 %collective-permute-done.3.refs_6_.refs_4_ = bf16[256,1536]{1,0:T(8,128)(2,1)S(1)} collective-permute-done((bf16[256,1536]{1,0:T(8,128)(2,1)S(1)}, bf16[256,1536]{1,0:T(8,128)(2,1)S(1)}, u32[]{:S(2)}, u32[]{:S(2)}) %collective-permute-start.3) | collective-permute-done | bytes 786464 | tf_op jit(solution)/shard_map/ppermute | solution.py:339
  24.1 0.6 collect.1.refs_1_.refs_3_
  24.7 2.5 %collective-permute-start.1 = (bf16[144,1024]{1,0:T(8,128)(2,1)S(1)}, bf16[144,1024]{1,0:T(8,128)(2,1)}, u32[]{:S(2)}, u32[]{:S(2)}) collective-permute-start(bf16[144,1024]{1,0:T(8,128)(2,1)S(1)} %collect.1.refs_1_.refs_3_), channel_id=1, source_target_pairs={{0,3},{1,2},{2,1},{3,0},{4,7},{5,6},{6,5},{7,4},{8,11},{9,10},{10,... | collective-permute-start | bytes 884744 | tf_op jit(solution)/shard_map/ppermute | solution.py:339
  27.3 5.8 %all-to-all-start.1 = ((bf16[8,16,1024]{2,1,0:T(8,128)(2,1)}), bf16[8,16,1024]{2,1,0:T(8,128)(2,1)S(1)}, u32[]{:S(2)}, u32[]{:S(2)}) async-start(bf16[8,16,1024]{2,1,0:T(8,128)(2,1)} %get-tuple-element.133), calls=%async_computation.1 | async-start | bytes 524288 | tf_op jit(solution)/shard_map/all_to_all | solution.py:349
  33.1 1.5 collective-permute-done.1
  34.8 1.7 collective-permute-done.2.refs_2_
  36.5 3.7 %first.1 = (bf16[8,32,1536]{2,1,0:T(8,128)(2,1)S(1)}, bf16[256,1024]{1,0:T(8,128)(2,1)}, f32[8,1024]{1,0:T(8,128)}) custom-call(s32[7]{0:T(128)S(1)} %stack.40.refs_0_, bf16[144,1024]{1,0:T(8,128)(2,1)S(1)} %collect.1.refs_1_.refs_3_, bf16[144,1024]{1,0:T(8,128)(2,1)S(1)} %collective-permute-done.2.refs_2_, bf16[256,3072]{1,0:T(8,128)(2,1)} %refs_1_.7, ...), custom_call_target="tpu_custom_call" | custom-call | flops 1 | bytes 1 | tf_op jit(solution)/shard_map/first/pallas_call | solution.py:395
  40.2 0.9 copy-done.20
  41.2 3.6 %collective-permute-done.6.refs_8_ = bf16[256,768]{1,0:T(8,128)(2,1)} collective-permute-done((bf16[256,768]{1,0:T(8,128)(2,1)}, bf16[256,768]{1,0:T(8,128)(2,1)}, u32[]{:S(2)}, u32[]{:S(2)}) %collective-permute-start.6) | collective-permute-done | bytes 393248 | tf_op jit(solution)/shard_map/ppermute | solution.py:339
  44.8 5.9 %all-to-all-start.2 = ((bf16[8,32,1536]{2,1,0:T(8,128)(2,1)}), bf16[8,32,1536]{2,1,0:T(8,128)(2,1)S(1)}, u32[]{:S(2)}, u32[]{:S(2)}) async-start(bf16[8,32,1536]{2,1,0:T(8,128)(2,1)} %copy-done.20), calls=%async_computation.2 | async-start | bytes 1572864 | tf_op jit(solution)/shard_map/all_to_all | solution.py:349
  50.8 0.8 collective-permute-start.9
  51.6 0.6 collect_rows.1.refs_4_.refs_5_.refs_3_
  52.2 0.7 collective-permute-done.7.refs_2_.refs_8_
  52.8 18.1 %all-to-all-done.2.refs_2_ = bf16[8,32,1536]{2,1,0:T(8,128)(2,1)S(1)} async-done(((bf16[8,32,1536]{2,1,0:T(8,128)(2,1)}), bf16[8,32,1536]{2,1,0:T(8,128)(2,1)S(1)}, u32[]{:S(2)}, u32[]{:S(2)}) %all-to-all-start.2) | async-done | bytes 786464 | tf_op jit(solution)/shard_map/all_to_all | solution.py:349
  70.9 2.6 %attend.1 = bf16[8,32,512]{2,1,0:T(8,128)(2,1)} custom-call(s32[7]{0:T(128)S(1)} %stack.40.refs_0_, f32[8,1024]{1,0:T(8,128)S(1)} %copy-done.19, bf16[8,32,1536]{2,1,0:T(8,128)(2,1)S(1)} %all-to-all-done.2.refs_2_), custom_call_target="tpu_custom_call" | custom-call | flops 1 | bytes 1 | tf_op jit(solution)/shard_map/attend/pallas_call | solution.py:395
  73.6 3.6 %all-to-all-start.3 = ((bf16[8,32,512]{2,1,0:T(8,128)(2,1)}), bf16[8,32,512]{2,1,0:T(8,128)(2,1)S(1)}, u32[]{:S(2)}, u32[]{:S(2)}) async-start(bf16[8,32,512]{2,1,0:T(8,128)(2,1)} %attend.1), calls=%async_computation.3 | async-start | bytes 524288 | tf_op jit(solution)/shard_map/all_to_all | solution.py:349
  77.6 1.0 collective-permute-start.10
  78.7 7.2 %collective-permute-done.10.refs_5_.refs_6_.refs_4_ = bf16[128,1024]{1,0:T(8,128)(2,1)S(1)} collective-permute-done((bf16[128,1024]{1,0:T(8,128)(2,1)S(1)}, bf16[128,1024]{1,0:T(8,128)(2,1)S(1)}, u32[]{:S(2)}, u32[]{:S(2)}) %collective-permute-start.10) | collective-permute-done | bytes 262176 | tf_op jit(solution)/shard_map/ppermute | solution.py:339
  85.9 0.9 all-to-all-done.3.refs_3_
  86.8 2.2 %out_term.1 = (f32[256,1024]{1,0:T(8,128)S(1)}, bf16[256,1024]{1,0:T(8,128)(2,1)S(1)}, bf16[256,512]{1,0:T(8,128)(2,1)S(1)}) custom-call(s32[7]{0:T(128)S(1)} %stack.40.refs_0_, bf16[256,1024]{1,0:T(8,128)(2,1)} %refs_7_.1, bf16[256,1024]{1,0:T(8,128)(2,1)} %collective-permute-done.7.refs_2_.refs_8_, bf16[8,32,512]{2,1,0:T(8,128)(2,1)S(1)} %all-to-all-done.3.refs_3_), custom_call_target="tpu_custom_call" | custom-call | flops 1 | bytes 1 | tf_op jit(solution)/shard_map/out_term/pallas_call | solution.py:395
  89.7 1.0 collective-permute-start.13
  90.8 3.6 %collective-permute-done.18.refs_6_ = bf16[128,1024]{1,0:T(8,128)(2,1)S(1)} collective-permute-done((bf16[128,1024]{1,0:T(8,128)(2,1)S(1)}, bf16[128,1024]{1,0:T(8,128)(2,1)S(1)}, u32[]{:S(2)}, u32[]{:S(2)}) %collective-permute-start.18) | collective-permute-done | bytes 262176 | tf_op jit(solution)/shard_map/ppermute | solution.py:339
  94.5 3.6 %aside.1 = (f32[256,1024]{1,0:T(8,128)S(1)}, f32[256,1408]{1,0:T(8,128)S(1)}) custom-call(s32[7]{0:T(128)S(1)} %stack.40.refs_0_, bf16[144,1024]{1,0:T(8,128)(2,1)S(1)} %collect.1.refs_1_.refs_3_, bf16[144,1024]{1,0:T(8,128)(2,1)S(1)} %collective-permute-done.2.refs_2_, f32[256,1024]{1,0:T(8,128)S(1)} %get-tuple-element.149.refs_3_, ...), custom_call_target="tpu_custom_call" | custom-call | flops 1 | bytes 1 | tf_op jit(solution)/shard_map/aside/pallas_call | solution.py:395
  98.2 5.7 %collective-permute-done.13.refs_2_ = bf16[256,1024]{1,0:T(8,128)(2,1)S(1)} collective-permute-done((bf16[256,1024]{1,0:T(8,128)(2,1)S(1)}, bf16[256,1024]{1,0:T(8,128)(2,1)S(1)}, u32[]{:S(2)}, u32[]{:S(2)}) %collective-permute-start.13) | collective-permute-done | bytes 524320 | tf_op jit(solution)/shard_map/ppermute | solution.py:339
  103.9 7.9 %ffn.1 = (f32[256,1024]{1,0:T(8,128)S(1)}, bf16[256,1024]{1,0:T(8,128)(2,1)S(1)}, bf16[256,1408]{1,0:T(8,128)(2,1)S(1)}, bf16[256,2816]{1,0:T(8,128)(2,1)S(1)}, ...) custom-call(s32[7]{0:T(128)S(1)} %stack.40.refs_0_, f32[256,1024]{1,0:T(8,128)S(1)} %get-tuple-element.163.refs_1_, ...), custom_call_target="tpu_custom_call" | custom-call | flops 1 | bytes 1 | tf_op jit(solution)/shard_map/ffn/pallas_call | solution.py:395
  112.6 1.0 collective-permute-start.19
  113.5 4.2 %down_term.1 = (f32[128,1024]{1,0:T(8,128)S(1)}, bf16[128,1024]{1,0:T(8,128)(2,1)S(1)}) custom-call(s32[7]{0:T(128)S(1)} %stack.40.refs_0_, bf16[256,1408]{1,0:T(8,128)(2,1)} %copy-done.7, f32[256,1024]{1,0:T(8,128)S(1)} %get-tuple-element.173.refs_2_.refs_3_, bf16[704,1024]{1,0:T(8,128)(2,1)} %refs_3_.5, ...), custom_call_target="tpu_custom_call" | custom-call | flops 1 | bytes 1 | tf_op jit(solution)/shard_map/down_term/pallas_call | solution.py:395
  117.8 5.0 %leaving_gradient.2 = bf16[256,2816]{1,0:T(8,128)(2,1)} custom-call(s32[7]{0:T(128)S(1)} %stack.40.refs_0_, bf16[256,1024]{1,0:T(8,128)(2,1)S(1)} %get-tuple-element.183.refs_1_, bf16[256,1024]{1,0:T(8,128)(2,1)S(1)} %collective-permute-done.20.refs_2_, bf16[256,2816]{1,0:T(8,128)(2,1)S(1)} %get-tuple-element.178.refs_3_, ...), custom_call_target="tpu_custom_call" | custom-call | flops 1 | bytes 1 | tf_op jit(solution)/shard_map/leaving_gradient/pallas_call | solution.py:395
  122.8 4.0 %collective-permute-done.19.refs_2_ = bf16[256,1024]{1,0:T(8,128)(2,1)S(1)} collective-permute-done((bf16[256,1024]{1,0:T(8,128)(2,1)S(1)}, bf16[256,1024]{1,0:T(8,128)(2,1)S(1)}, u32[]{:S(2)}, u32[]{:S(2)}) %collective-permute-start.19) | collective-permute-done | bytes 524320 | tf_op jit(solution)/shard_map/ppermute | solution.py:339
  126.8 2.4 %mid.1 = (f32[128,1024]{1,0:T(8,128)}, bf16[256,1024]{1,0:T(8,128)(2,1)S(1)}, f32[2,1,256]{2,1,0:T(1,128)S(1)}, bf16[8,32,512]{2,1,0:T(8,128)(2,1)S(1)}) custom-call(s32[7]{0:T(128)S(1)} %stack.40.refs_0_, f32[256,1024]{1,0:T(8,128)S(1)} %get-tuple-element.169.refs_1_, bf16[256,1024]{1,0:T(8,128)(2,1)S(1)} %collective-permute-done.19.refs_2_, ...), custom_call_target="tpu_custom_call" | custom-call | flops 1 | bytes 1 | tf_op jit(solution)/shard_map/mid/pallas_call | solution.py:395
  129.4 0.6 copy-done.27
  130.0 5.1 %all-to-all-start.4 = ((bf16[8,32,512]{2,1,0:T(8,128)(2,1)}), bf16[8,32,512]{2,1,0:T(8,128)(2,1)S(1)}, u32[]{:S(2)}, u32[]{:S(2)}) async-start(bf16[8,32,512]{2,1,0:T(8,128)(2,1)} %copy-done.27), calls=%async_computation.4 | async-start | bytes 524288 | tf_op jit(solution)/shard_map/all_to_all | solution.py:349
  135.3 0.9 collective-permute-start.24
  136.2 6.9 %staying_gradient.2.refs_2_ = f32[256,5632]{1,0:T(8,128)} custom-call(s32[7]{0:T(128)S(1)} %stack.40.refs_0_, bf16[256,1024]{1,0:T(8,128)(2,1)} %copy-done.16, bf16[256,1024]{1,0:T(8,128)(2,1)} %copy-done.17, bf16[256,2816]{1,0:T(8,128)(2,1)} %copy-done, bf16[256,2816]{1,0:T(8,128)(2,1)} %copy-done.1), custom_call_target="tpu_custom_call" | custom-call | flops 1 | bytes 1 | tf_op jit(solution)/shard_map/staying_gradient/pallas_call | solution.py:395
  143.1 0.9 all-to-all-done.4.refs_3_
  144.1 5.6 %attend_back.1 = bf16[8,32,1536]{2,1,0:T(8,128)(2,1)} custom-call(s32[7]{0:T(128)S(1)} %stack.40.refs_0_, f32[8,1024]{1,0:T(8,128)S(1)} %copy-done.19, bf16[8,32,1536]{2,1,0:T(8,128)(2,1)S(1)} %all-to-all-done.2.refs_2_, bf16[8,32,512]{2,1,0:T(8,128)(2,1)S(1)} %all-to-all-done.4.refs_3_), custom_call_target="tpu_custom_call" | custom-call | flops 1 | bytes 1 | tf_op jit(solution)/shard_map/attend_back/pallas_call | solution.py:395
  149.7 5.1 %all-to-all-start.5 = ((bf16[8,32,1536]{2,1,0:T(8,128)(2,1)}), bf16[8,32,1536]{2,1,0:T(8,128)(2,1)S(1)}, u32[]{:S(2)}, u32[]{:S(2)}) async-start(bf16[8,32,1536]{2,1,0:T(8,128)(2,1)} %attend_back.1), calls=%async_computation.5 | async-start | bytes 1572864 | tf_op jit(solution)/shard_map/all_to_all | solution.py:349
  154.8 1.1 collective-permute-start.26
  155.9 3.4 %grad_out.1 = f32[256,1024]{1,0:T(8,128)} custom-call(s32[7]{0:T(128)S(1)} %stack.40.refs_0_, bf16[256,512]{1,0:T(8,128)(2,1)} %copy-done.28, bf16[256,512]{1,0:T(8,128)(2,1)} %copy-done.35, bf16[256,1024]{1,0:T(8,128)(2,1)} %copy-done.22, bf16[256,1024]{1,0:T(8,128)(2,1)} %collective-permute-done.23.refs_4_), custom_call_target="tpu_custom_call" | custom-call | flops 1 | bytes 1 | tf_op jit(solution)/shard_map/grad_out/pallas_call | solution.py:395
  159.4 4.7 %grad_down.1 = f32[704,1024]{1,0:T(8,128)} custom-call(s32[7]{0:T(128)S(1)} %stack.40.refs_0_, bf16[256,1408]{1,0:T(8,128)(2,1)S(1)} %copy-done.8, bf16[256,1408]{1,0:T(8,128)(2,1)S(1)} %collective-permute-done.22.refs_2_, bf16[128,1024]{1,0:T(8,128)(2,1)S(1)} %collect_rows.1.refs_4_.refs_5_.refs_3_, bf16[128,1024]{1,0:T(8,128)(2,1)S(1)} %copy-done.11, ...), custom_call_target="tpu_custom_call" | custom-call | flops 1 | bytes 1 | tf_op jit(solution)/shard_map/grad_down/pallas_call | solution.py:395
  164.1 10.3 %collective-permute-done.26.refs_7_ = bf16[128,1024]{1,0:T(8,128)(2,1)S(1)} collective-permute-done((bf16[128,1024]{1,0:T(8,128)(2,1)}, bf16[128,1024]{1,0:T(8,128)(2,1)S(1)}, u32[]{:S(2)}, u32[]{:S(2)}) %collective-permute-start.26) | collective-permute-done | bytes 262176 | tf_op jit(solution)/shard_map/ppermute | solution.py:339
  174.4 0.7 copy-done.29
  175.1 4.1 %back_first.1 = (f32[128,1024]{1,0:T(8,128)S(1)}, bf16[128,1024]{1,0:T(8,128)(2,1)S(1)}, bf16[256,1536]{1,0:T(8,128)(2,1)S(1)}) custom-call(s32[7]{0:T(128)S(1)} %stack.40.refs_0_, bf16[256,3072]{1,0:T(8,128)(2,1)} %refs_1_.7, bf16[256,1536]{1,0:T(8,128)(2,1)} %copy-done.4, bf16[256,1536]{1,0:T(8,128)(2,1)} %copy-done.3, bf16[256,1536]{1,0:T(8,128)(2,1)} %copy-done.2, ...), custom_call_target="tpu_custom_call" | custom-call | flops 1 | bytes 1 | tf_op jit(solution)/shard_map/back_first/pallas_call | solution.py:395
  179.6 1.0 collective-permute-start.27
  180.5 1.0 collective-permute-done.28.refs_4_
  181.6 2.3 %leaving_gradient.3 = bf16[256,1536]{1,0:T(8,128)(2,1)S(1)} custom-call(s32[7]{0:T(128)S(1)} %stack.40.refs_0_, bf16[256,1024]{1,0:T(8,128)(2,1)S(1)} %copy-done.13, bf16[256,1024]{1,0:T(8,128)(2,1)S(1)} %copy-done.15, bf16[256,1536]{1,0:T(8,128)(2,1)S(1)} %get-tuple-element.199.refs_3_, bf16[256,1536]{1,0:T(8,128)(2,1)S(1)} %collective-permute-done.28.refs_4_), custom_call_target="tpu_custom_call" | custom-call | flops 1 | bytes 1 | tf_op jit(solution)/shard_map/leaving_gradient/pallas_call | solution.py:395
  183.9 4.1 %collective-permute-done.27.refs_2_ = bf16[128,1024]{1,0:T(8,128)(2,1)S(1)} collective-permute-done((bf16[128,1024]{1,0:T(8,128)(2,1)S(1)}, bf16[128,1024]{1,0:T(8,128)(2,1)S(1)}, u32[]{:S(2)}, u32[]{:S(2)}) %collective-permute-start.27) | collective-permute-done | bytes 262176 | tf_op jit(solution)/shard_map/ppermute | solution.py:339
  188.1 1.9 last.1
  190.1 5.5 %all-to-all-start.6 = ((bf16[8,32,1024]{2,1,0:T(8,128)(2,1)}), bf16[8,32,1024]{2,1,0:T(8,128)(2,1)S(1)}, u32[]{:S(2)}, u32[]{:S(2)}) async-start(bf16[8,32,1024]{2,1,0:T(8,128)(2,1)} %get-tuple-element.204), calls=%async_computation.6 | async-start | bytes 1048576 | tf_op jit(solution)/shard_map/all_to_all | solution.py:349
  195.6 1.0 collective-permute-start.31
  196.6 3.6 %coming_gradient.2 = f32[256,5632]{1,0:T(8,128)} custom-call(s32[7]{0:T(128)S(1)} %stack.40.refs_0_, bf16[256,2816]{1,0:T(8,128)(2,1)} %collective-permute-done.25.refs_1_, f32[256,5632]{1,0:T(8,128)} %staying_gradient.2.refs_2_), custom_call_target="tpu_custom_call", output_to_operand_aliasing={{}: (2, {})} | custom-call | flops 1 | bytes 1 | tf_op jit(solution)/shard_map/coming_gradient/pallas_call | solution.py:395
  200.2 4.9 %staying_gradient.3.refs_2_ = f32[256,3072]{1,0:T(8,128)} custom-call(s32[7]{0:T(128)S(1)} %stack.40.refs_0_, bf16[256,1024]{1,0:T(8,128)(2,1)} %get-tuple-element.210.refs_1_, bf16[256,1024]{1,0:T(8,128)(2,1)} %copy-done.14, bf16[256,1536]{1,0:T(8,128)(2,1)} %copy-done.5, bf16[256,1536]{1,0:T(8,128)(2,1)} %copy-done.6), custom_call_target="tpu_custom_call" | custom-call | flops 1 | bytes 1 | tf_op jit(solution)/shard_map/staying_gradient/pallas_call | solution.py:395
  205.2 2.4 %collective-permute-done.29 = bf16[256,1536]{1,0:T(8,128)(2,1)} collective-permute-done((bf16[256,1536]{1,0:T(8,128)(2,1)S(1)}, bf16[256,1536]{1,0:T(8,128)(2,1)}, u32[]{:S(2)}, u32[]{:S(2)}) %collective-permute-start.29) | collective-permute-done | bytes 786464 | tf_op jit(solution)/shard_map/ppermute | solution.py:339
  208.7 1.3 collective-permute-done.32
  210.7 1.8 coming_gradient.3
  212.5 1.6 to_frames.1
  (136 shorter events, 6.8 us)
Async XLA Ops:
  0.6 11.3 %copy-start.37 = (bf16[256]{0:T(256)(128)(2,1)S(1)}, bf16[256]{0:T(256)(128)(2,1)}, u32[]{:S(2)}) copy-start(bf16[256]{0:T(256)(128)(2,1)} %param.11) | copy-start | bytes 1540
  0.6 11.3 %copy-start.38 = (bf16[256]{0:T(256)(128)(2,1)S(1)}, bf16[256]{0:T(256)(128)(2,1)}, u32[]{:S(2)}) copy-start(bf16[256]{0:T(256)(128)(2,1)} %param.14) | copy-start | bytes 1540
  0.7 11.8 %copy-start.36 = (s32[128]{0:T(128)S(1)}, s32[128]{0:T(128)}, u32[]{:S(2)}) copy-start(s32[128]{0:T(128)} %param.10) | copy-start | bytes 1540
  3.6 20.4 %collective-permute-start.3 = (bf16[256,1536]{1,0:T(8,128)(2,1)S(1)}, bf16[256,1536]{1,0:T(8,128)(2,1)S(1)}, u32[]{:S(2)}, u32[]{:S(2)}) collective-permute-start(bf16[256,1536]{1,0:T(8,128)(2,1)S(1)} %get-tuple-element.115), channel_id=1, source_target_pairs={{0,3},{1,2},{2,1},{3,0},{4,7},{5,6},{6,5},{7,4},{8,11},{9,10},{10,... | collective-permute-start | bytes 2359304 | tf_op jit(solution)/shard_map/ppermute | solution.py:339
  6.1 15.6 %all-to-all-start = ((bf16[8,16,1024]{2,1,0:T(8,128)(2,1)}), bf16[8,16,1024]{2,1,0:T(8,128)(2,1)S(1)}, u32[]{:S(2)}, u32[]{:S(2)}) async-start(bf16[8,16,1024]{2,1,0:T(8,128)(2,1)} %get-tuple-element.114), calls=%async_computation | async-start | bytes 524288 | tf_op jit(solution)/shard_map/all_to_all | solution.py:349
  12.0 8.9 %collective-permute-start = (bf16[2,256]{1,0:T(2,128)(2,1)S(1)}, bf16[2,256]{1,0:T(2,128)(2,1)S(1)}, u32[]{:S(2)}, u32[]{:S(2)}) collective-permute-start(bf16[2,256]{1,0:T(2,128)(2,1)S(1)} %pad_maximum_fusion.refs_3_), channel_id=1, source_target_pairs={{0,1},{1,0},{2,3},{3,2},{4,5},{5,4},{6,7},{7,6},{8,9},{9,8},{10,11... | collective-permute-start | bytes 3080 | tf_op jit(solution)/shard_map/ppermute | solution.py:339
  20.8 6.5 %copy-start.32 = (bf16[256,768]{1,0:T(8,128)(2,1)}, bf16[256,768]{1,0:T(8,128)(2,1)S(1)}, u32[]{:S(2)}) copy-start(bf16[256,768]{1,0:T(8,128)(2,1)S(1)} %get-tuple-element.135) | copy-start | bytes 1179652
  21.7 14.7 %collective-permute-start.5 = (bf16[256,1536]{1,0:T(8,128)(2,1)}, bf16[256,1536]{1,0:T(8,128)(2,1)S(1)}, u32[]{:S(2)}, u32[]{:S(2)}) collective-permute-start(bf16[256,1536]{1,0:T(8,128)(2,1)} %kept_columns.1), channel_id=1, source_target_pairs={{0,1},{1,0},{2,3},{3,2},{4,5},{5,4},{6,7},{7,6},{8,9},{9,8},{10,11... | collective-permute-start | bytes 2359304 | tf_op jit(solution)/shard_map/ppermute | solution.py:339
  24.1 16.1 %copy-start.2 = (bf16[256,1536]{1,0:T(8,128)(2,1)}, bf16[256,1536]{1,0:T(8,128)(2,1)S(1)}, u32[]{:S(2)}) copy-start(bf16[256,1536]{1,0:T(8,128)(2,1)S(1)} %collective-permute-done.3.refs_6_.refs_4_) | copy-start | bytes 2359300
  24.1 12.4 %collective-permute-start.4 = (bf16[256,1536]{1,0:T(8,128)(2,1)S(1)}, bf16[256,1536]{1,0:T(8,128)(2,1)S(1)}, u32[]{:S(2)}, u32[]{:S(2)}) collective-permute-start(bf16[256,1536]{1,0:T(8,128)(2,1)S(1)} %collective-permute-done.3.refs_6_.refs_4_), channel_id=1, source_target_pairs={{0,1},{1,0},{2,3},{3,2},{4,5},{5,4},{6,7},{7,6},{8,9},{9,8},{10,11... | collective-permute-start | bytes 2359304 | tf_op jit(solution)/shard_map/ppermute | solution.py:339
  24.7 9.9 %collective-permute-start.1 = (bf16[144,1024]{1,0:T(8,128)(2,1)S(1)}, bf16[144,1024]{1,0:T(8,128)(2,1)}, u32[]{:S(2)}, u32[]{:S(2)}) collective-permute-start(bf16[144,1024]{1,0:T(8,128)(2,1)S(1)} %collect.1.refs_1_.refs_3_), channel_id=1, source_target_pairs={{0,3},{1,2},{2,1},{3,0},{4,7},{5,6},{6,5},{7,4},{8,11},{9,10},{10,... | collective-permute-start | bytes 884744 | tf_op jit(solution)/shard_map/ppermute | solution.py:339
  27.3 17.6 %all-to-all-start.1 = ((bf16[8,16,1024]{2,1,0:T(8,128)(2,1)}), bf16[8,16,1024]{2,1,0:T(8,128)(2,1)S(1)}, u32[]{:S(2)}, u32[]{:S(2)}) async-start(bf16[8,16,1024]{2,1,0:T(8,128)(2,1)} %get-tuple-element.133), calls=%async_computation.1 | async-start | bytes 524288 | tf_op jit(solution)/shard_map/all_to_all | solution.py:349
  33.1 11.7 %collective-permute-start.6 = (bf16[256,768]{1,0:T(8,128)(2,1)}, bf16[256,768]{1,0:T(8,128)(2,1)}, u32[]{:S(2)}, u32[]{:S(2)}) collective-permute-start(bf16[256,768]{1,0:T(8,128)(2,1)} %copy-done.32), channel_id=1, source_target_pairs={{0,3},{1,2},{2,1},{3,0},{4,7},{5,6},{6,5},{7,4},{8,11},{9,10},{10,... | collective-permute-start | bytes 1179656 | tf_op jit(solution)/shard_map/ppermute | solution.py:339
  34.6 1.8 collective-permute-start.2
  41.1 29.8 %copy-start.19 = (f32[8,1024]{1,0:T(8,128)S(1)}, f32[8,1024]{1,0:T(8,128)}, u32[]{:S(2)}) copy-start(f32[8,1024]{1,0:T(8,128)} %get-tuple-element.130.refs_1_.refs_3_.refs_4_) | copy-start | bytes 98308
  41.1 9.6 %copy-start.34 = (bf16[256,1024]{1,0:T(8,128)(2,1)S(1)}, bf16[256,1024]{1,0:T(8,128)(2,1)}, u32[]{:S(2)}) copy-start(bf16[256,1024]{1,0:T(8,128)(2,1)} %refs_7_.1) | copy-start | bytes 1572868
  41.1 29.8 %collective-permute-start.8 = (bf16[704,1024]{1,0:T(8,128)(2,1)}, bf16[704,1024]{1,0:T(8,128)(2,1)}, u32[]{:S(2)}, u32[]{:S(2)}) collective-permute-start(bf16[704,1024]{1,0:T(8,128)(2,1)} %refs_3_.5), channel_id=1, source_target_pairs={{0,1},{1,0},{2,3},{3,2},{4,5},{5,4},{6,7},{7,6},{8,9},{9,8},{10,11... | collective-permute-start | bytes 4325384 | tf_op jit(solution)/shard_map/ppermute | solution.py:339
  44.8 28.7 %copy-start.12 = (bf16[256,1024]{1,0:T(8,128)(2,1)S(1)}, bf16[256,1024]{1,0:T(8,128)(2,1)}, u32[]{:S(2)}) copy-start(bf16[256,1024]{1,0:T(8,128)(2,1)} %get-tuple-element.210.refs_1_) | copy-start | bytes 1572868
  44.8 26.1 %all-to-all-start.2 = ((bf16[8,32,1536]{2,1,0:T(8,128)(2,1)}), bf16[8,32,1536]{2,1,0:T(8,128)(2,1)S(1)}, u32[]{:S(2)}, u32[]{:S(2)}) async-start(bf16[8,32,1536]{2,1,0:T(8,128)(2,1)} %copy-done.20), calls=%async_computation.2 | async-start | bytes 1572864 | tf_op jit(solution)/shard_map/all_to_all | solution.py:349
  50.7 2.1 collective-permute-start.7
  50.8 27.7 %collective-permute-start.9 = (bf16[256,2048]{1,0:T(8,128)(2,1)}, bf16[256,2048]{1,0:T(8,128)(2,1)}, u32[]{:S(2)}, u32[]{:S(2)}) collective-permute-start(bf16[256,2048]{1,0:T(8,128)(2,1)} %copy-done.31), channel_id=1, source_target_pairs={{0,3},{1,2},{2,1},{3,0},{4,7},{5,6},{6,5},{7,4},{8,11},{9,10},{10,... | collective-permute-start | bytes 3145736 | tf_op jit(solution)/shard_map/ppermute | solution.py:339
  73.5 13.3 %collective-permute-start.12 = (bf16[256,1024]{1,0:T(8,128)(2,1)S(1)}, bf16[256,1024]{1,0:T(8,128)(2,1)S(1)}, u32[]{:S(2)}, u32[]{:S(2)}) collective-permute-start(bf16[256,1024]{1,0:T(8,128)(2,1)S(1)} %copy-done.12), channel_id=1, source_target_pairs={{0,1},{1,0},{2,3},{3,2},{4,5},{5,4},{6,7},{7,6},{8,9},{9,8},{10,11... | collective-permute-start | bytes 1572872 | tf_op jit(solution)/shard_map/ppermute | solution.py:339
  73.6 13.2 %all-to-all-start.3 = ((bf16[8,32,512]{2,1,0:T(8,128)(2,1)}), bf16[8,32,512]{2,1,0:T(8,128)(2,1)S(1)}, u32[]{:S(2)}, u32[]{:S(2)}) async-start(bf16[8,32,512]{2,1,0:T(8,128)(2,1)} %attend.1), calls=%async_computation.3 | async-start | bytes 524288 | tf_op jit(solution)/shard_map/all_to_all | solution.py:349
  77.2 1.6 collective-permute-start.11
  77.6 8.3 %collective-permute-start.10 = (bf16[128,1024]{1,0:T(8,128)(2,1)S(1)}, bf16[128,1024]{1,0:T(8,128)(2,1)S(1)}, u32[]{:S(2)}, u32[]{:S(2)}) collective-permute-start(bf16[128,1024]{1,0:T(8,128)(2,1)S(1)} %collect_rows.1.refs_4_.refs_5_.refs_3_), channel_id=1, source_target_pairs={{0,2},{1,3},{2,0},{3,1},{4,6},{5,7},{6,4},{7,5},{8,10},{9,11},{10,... | collective-permute-start | bytes 786440 | tf_op jit(solution)/shard_map/ppermute | solution.py:339
  78.7 19.4 %copy-start.23 = (bf16[128,1024]{1,0:T(8,128)(2,1)}, bf16[128,1024]{1,0:T(8,128)(2,1)S(1)}, u32[]{:S(2)}) copy-start(bf16[128,1024]{1,0:T(8,128)(2,1)S(1)} %collective-permute-done.11.refs_5_) | copy-start | bytes 786436
  85.9 12.2 %copy-start.9 = (bf16[128,1024]{1,0:T(8,128)(2,1)}, bf16[128,1024]{1,0:T(8,128)(2,1)S(1)}, u32[]{:S(2)}) copy-start(bf16[128,1024]{1,0:T(8,128)(2,1)S(1)} %collective-permute-done.10.refs_5_.refs_6_.refs_4_) | copy-start | bytes 786436
  86.8 11.3 %copy-start.14 = (bf16[256,1024]{1,0:T(8,128)(2,1)}, bf16[256,1024]{1,0:T(8,128)(2,1)S(1)}, u32[]{:S(2)}) copy-start(bf16[256,1024]{1,0:T(8,128)(2,1)S(1)} %collective-permute-done.12.refs_2_) | copy-start | bytes 1572868
  89.0 9.1 %copy-start.28 = (bf16[256,512]{1,0:T(8,128)(2,1)}, bf16[256,512]{1,0:T(8,128)(2,1)S(1)}, u32[]{:S(2)}) copy-start(bf16[256,512]{1,0:T(8,128)(2,1)S(1)} %get-tuple-element.156.refs_1_) | copy-start | bytes 786436
  89.0 14.9 %collective-permute-start.17 = (bf16[256,2816]{1,0:T(8,128)(2,1)}, bf16[256,2816]{1,0:T(8,128)(2,1)S(1)}, u32[]{:S(2)}, u32[]{:S(2)}) collective-permute-start(bf16[256,2816]{1,0:T(8,128)(2,1)} %copy-done.18), channel_id=1, source_target_pairs={{0,1},{1,0},{2,3},{3,2},{4,5},{5,4},{6,7},{7,6},{8,9},{9,8},{10,11... | collective-permute-start | bytes 4325384 | tf_op jit(solution)/shard_map/ppermute | solution.py:339
  89.1 14.8 %collective-permute-start.16 = (bf16[256,2048]{1,0:T(8,128)(2,1)}, bf16[256,2048]{1,0:T(8,128)(2,1)S(1)}, u32[]{:S(2)}, u32[]{:S(2)}) collective-permute-start(bf16[256,2048]{1,0:T(8,128)(2,1)} %collective-permute-done.9.refs_10_), channel_id=1, source_target_pairs={{0,1},{1,0},{2,3},{3,2},{4,5},{5,4},{6,7},{7,6},{8,9},{9,8},{10,11... | collective-permute-start | bytes 3145736 | tf_op jit(solution)/shard_map/ppermute | solution.py:339
  89.6 4.8 %collective-permute-start.18 = (bf16[128,1024]{1,0:T(8,128)(2,1)S(1)}, bf16[128,1024]{1,0:T(8,128)(2,1)S(1)}, u32[]{:S(2)}, u32[]{:S(2)}) collective-permute-start(bf16[128,1024]{1,0:T(8,128)(2,1)S(1)} %collective-permute-done.10.refs_5_.refs_6_.refs_4_), channel_id=1, source_target_pairs={{0,1},{1,0},{2,3},{3,2},{4,5},{5,4},{6,7},{7,6},{8,9},{9,8},{10,11... | collective-permute-start | bytes 786440 | tf_op jit(solution)/shard_map/ppermute | solution.py:339
  89.7 14.3 %collective-permute-start.13 = (bf16[256,1024]{1,0:T(8,128)(2,1)S(1)}, bf16[256,1024]{1,0:T(8,128)(2,1)S(1)}, u32[]{:S(2)}, u32[]{:S(2)}) collective-permute-start(bf16[256,1024]{1,0:T(8,128)(2,1)S(1)} %get-tuple-element.148), channel_id=1, source_target_pairs={{0,2},{1,3},{2,0},{3,1},{4,6},{5,7},{6,4},{7,5},{8,10},{9,11},{10,... | collective-permute-start | bytes 1572872 | tf_op jit(solution)/shard_map/ppermute | solution.py:339
  90.6 7.6 %collective-permute-start.15 = (bf16[256,768]{1,0:T(8,128)(2,1)}, bf16[256,768]{1,0:T(8,128)(2,1)S(1)}, u32[]{:S(2)}, u32[]{:S(2)}) collective-permute-start(bf16[256,768]{1,0:T(8,128)(2,1)} %collective-permute-done.6.refs_8_), channel_id=1, source_target_pairs={{0,1},{1,0},{2,3},{3,2},{4,5},{5,4},{6,7},{7,6},{8,9},{9,8},{10,11... | collective-permute-start | bytes 1179656 | tf_op jit(solution)/shard_map/ppermute | solution.py:339
  94.4 3.8 %collective-permute-start.14 = (bf16[256,512]{1,0:T(8,128)(2,1)S(1)}, bf16[256,512]{1,0:T(8,128)(2,1)S(1)}, u32[]{:S(2)}, u32[]{:S(2)}) collective-permute-start(bf16[256,512]{1,0:T(8,128)(2,1)S(1)} %get-tuple-element.156.refs_1_), channel_id=1, source_target_pairs={{0,1},{1,0},{2,3},{3,2},{4,5},{5,4},{6,7},{7,6},{8,9},{9,8},{10,11... | collective-permute-start | bytes 786440 | tf_op jit(solution)/shard_map/ppermute | solution.py:339
  98.2 13.7 %copy-start.35 = (bf16[256,512]{1,0:T(8,128)(2,1)}, bf16[256,512]{1,0:T(8,128)(2,1)S(1)}, u32[]{:S(2)}) copy-start(bf16[256,512]{1,0:T(8,128)(2,1)S(1)} %collective-permute-done.14.refs_2_) | copy-start | bytes 786436
  111.9 5.9 %copy-start = (bf16[256,2816]{1,0:T(8,128)(2,1)}, bf16[256,2816]{1,0:T(8,128)(2,1)S(1)}, u32[]{:S(2)}) copy-start(bf16[256,2816]{1,0:T(8,128)(2,1)S(1)} %get-tuple-element.178.refs_3_) | copy-start | bytes 4325380
  111.9 5.9 %copy-start.16 = (bf16[256,1024]{1,0:T(8,128)(2,1)}, bf16[256,1024]{1,0:T(8,128)(2,1)S(1)}, u32[]{:S(2)}) copy-start(bf16[256,1024]{1,0:T(8,128)(2,1)S(1)} %get-tuple-element.183.refs_1_) | copy-start | bytes 1572868
  111.9 5.9 %collective-permute-start.21 = (bf16[256,2816]{1,0:T(8,128)(2,1)S(1)}, bf16[256,2816]{1,0:T(8,128)(2,1)S(1)}, u32[]{:S(2)}, u32[]{:S(2)}) collective-permute-start(bf16[256,2816]{1,0:T(8,128)(2,1)S(1)} %get-tuple-element.178.refs_3_), channel_id=1, source_target_pairs={{0,1},{1,0},{2,3},{3,2},{4,5},{5,4},{6,7},{7,6},{8,9},{9,8},{10,11... | collective-permute-start | bytes 4325384 | tf_op jit(solution)/shard_map/ppermute | solution.py:339
  112.0 14.8 %collective-permute-start.22 = (bf16[256,1408]{1,0:T(8,128)(2,1)S(1)}, bf16[256,1408]{1,0:T(8,128)(2,1)S(1)}, u32[]{:S(2)}, u32[]{:S(2)}) collective-permute-start(bf16[256,1408]{1,0:T(8,128)(2,1)S(1)} %get-tuple-element.188.refs_1_), channel_id=1, source_target_pairs={{0,1},{1,0},{2,3},{3,2},{4,5},{5,4},{6,7},{7,6},{8,9},{9,8},{10,11... | collective-permute-start | bytes 2162696 | tf_op jit(solution)/shard_map/ppermute | solution.py:339
  112.5 5.3 %collective-permute-start.20 = (bf16[256,1024]{1,0:T(8,128)(2,1)S(1)}, bf16[256,1024]{1,0:T(8,128)(2,1)S(1)}, u32[]{:S(2)}, u32[]{:S(2)}) collective-permute-start(bf16[256,1024]{1,0:T(8,128)(2,1)S(1)} %get-tuple-element.183.refs_1_), channel_id=1, source_target_pairs={{0,1},{1,0},{2,3},{3,2},{4,5},{5,4},{6,7},{7,6},{8,9},{9,8},{10,11... | collective-permute-start | bytes 1572872 | tf_op jit(solution)/shard_map/ppermute | solution.py:339
  112.6 14.3 %collective-permute-start.19 = (bf16[256,1024]{1,0:T(8,128)(2,1)S(1)}, bf16[256,1024]{1,0:T(8,128)(2,1)S(1)}, u32[]{:S(2)}, u32[]{:S(2)}) collective-permute-start(bf16[256,1024]{1,0:T(8,128)(2,1)S(1)} %get-tuple-element.170), channel_id=1, source_target_pairs={{0,2},{1,3},{2,0},{3,1},{4,6},{5,7},{6,4},{7,5},{8,10},{9,11},{10,... | collective-permute-start | bytes 1572872 | tf_op jit(solution)/shard_map/ppermute | solution.py:339
  117.7 5.0 %copy-start.33 = (bf16[128,1024]{1,0:T(8,128)(2,1)}, bf16[128,1024]{1,0:T(8,128)(2,1)S(1)}, u32[]{:S(2)}) copy-start(bf16[128,1024]{1,0:T(8,128)(2,1)S(1)} %get-tuple-element.187) | copy-start | bytes 786436
  117.7 9.1 %copy-start.10 = (bf16[128,1024]{1,0:T(8,128)(2,1)S(1)}, bf16[128,1024]{1,0:T(8,128)(2,1)}, u32[]{:S(2)}) copy-start(bf16[128,1024]{1,0:T(8,128)(2,1)} %copy-done.9) | copy-start | bytes 786436
  117.8 5.0 %copy-start.17 = (bf16[256,1024]{1,0:T(8,128)(2,1)}, bf16[256,1024]{1,0:T(8,128)(2,1)S(1)}, u32[]{:S(2)}) copy-start(bf16[256,1024]{1,0:T(8,128)(2,1)S(1)} %collective-permute-done.20.refs_2_) | copy-start | bytes 1572868
  117.8 5.0 %copy-start.1 = (bf16[256,2816]{1,0:T(8,128)(2,1)}, bf16[256,2816]{1,0:T(8,128)(2,1)S(1)}, u32[]{:S(2)}) copy-start(bf16[256,2816]{1,0:T(8,128)(2,1)S(1)} %collective-permute-done.21.refs_4_) | copy-start | bytes 4325380
  129.3 13.8 %copy-start.22 = (bf16[256,1024]{1,0:T(8,128)(2,1)}, bf16[256,1024]{1,0:T(8,128)(2,1)S(1)}, u32[]{:S(2)}) copy-start(bf16[256,1024]{1,0:T(8,128)(2,1)S(1)} %get-tuple-element.193.refs_3_) | copy-start | bytes 1572868
  129.3 14.8 %collective-permute-start.23 = (bf16[256,1024]{1,0:T(8,128)(2,1)S(1)}, bf16[256,1024]{1,0:T(8,128)(2,1)}, u32[]{:S(2)}, u32[]{:S(2)}) collective-permute-start(bf16[256,1024]{1,0:T(8,128)(2,1)S(1)} %get-tuple-element.193.refs_3_), channel_id=1, source_target_pairs={{0,1},{1,0},{2,3},{3,2},{4,5},{5,4},{6,7},{7,6},{8,9},{9,8},{10,11... | collective-permute-start | bytes 1572872 | tf_op jit(solution)/shard_map/ppermute | solution.py:339
  130.0 14.1 %all-to-all-start.4 = ((bf16[8,32,512]{2,1,0:T(8,128)(2,1)}), bf16[8,32,512]{2,1,0:T(8,128)(2,1)S(1)}, u32[]{:S(2)}, u32[]{:S(2)}) async-start(bf16[8,32,512]{2,1,0:T(8,128)(2,1)} %copy-done.27), calls=%async_computation.4 | async-start | bytes 524288 | tf_op jit(solution)/shard_map/all_to_all | solution.py:349
  135.1 40.0 %collective-permute-start.25 = (bf16[256,2816]{1,0:T(8,128)(2,1)}, bf16[256,2816]{1,0:T(8,128)(2,1)}, u32[]{:S(2)}, u32[]{:S(2)}) collective-permute-start(bf16[256,2816]{1,0:T(8,128)(2,1)} %leaving_gradient.2), channel_id=1, source_target_pairs={{0,3},{1,2},{2,1},{3,0},{4,7},{5,6},{6,5},{7,4},{8,11},{9,10},{10,... | collective-permute-start | bytes 4325384 | tf_op jit(solution)/shard_map/ppermute | solution.py:339
  135.3 7.9 %collective-permute-start.24 = (f32[1,256]{1,0:T(1,128)S(1)}, f32[1,256]{1,0:T(1,128)S(1)}, u32[]{:S(2)}, u32[]{:S(2)}) collective-permute-start(f32[1,256]{1,0:T(1,128)S(1)} %slice_bitcast_fusion.2), channel_id=1, source_target_pairs={{0,1},{1,0},{2,3},{3,2},{4,5},{5,4},{6,7},{7,6},{8,9},{9,8},{10,11... | collective-permute-start | bytes 3080 | tf_op jit(solution)/shard_map/ppermute | solution.py:339
  149.7 25.5 %all-to-all-start.5 = ((bf16[8,32,1536]{2,1,0:T(8,128)(2,1)}), bf16[8,32,1536]{2,1,0:T(8,128)(2,1)S(1)}, u32[]{:S(2)}, u32[]{:S(2)}) async-start(bf16[8,32,1536]{2,1,0:T(8,128)(2,1)} %attend_back.1), calls=%async_computation.5 | async-start | bytes 1572864 | tf_op jit(solution)/shard_map/all_to_all | solution.py:349
  154.8 19.6 %collective-permute-start.26 = (bf16[128,1024]{1,0:T(8,128)(2,1)}, bf16[128,1024]{1,0:T(8,128)(2,1)S(1)}, u32[]{:S(2)}, u32[]{:S(2)}) collective-permute-start(bf16[128,1024]{1,0:T(8,128)(2,1)} %copy-done.33), channel_id=1, source_target_pairs={{0,2},{1,3},{2,0},{3,1},{4,6},{5,7},{6,4},{7,5},{8,10},{9,11},{10,... | collective-permute-start | bytes 786440 | tf_op jit(solution)/shard_map/ppermute | solution.py:339
  164.1 17.5 %copy-start.13 = (bf16[256,1024]{1,0:T(8,128)(2,1)S(1)}, bf16[256,1024]{1,0:T(8,128)(2,1)}, u32[]{:S(2)}) copy-start(bf16[256,1024]{1,0:T(8,128)(2,1)} %get-tuple-element.210.refs_1_) | copy-start | bytes 1572868
  164.1 17.5 %copy-start.15 = (bf16[256,1024]{1,0:T(8,128)(2,1)S(1)}, bf16[256,1024]{1,0:T(8,128)(2,1)}, u32[]{:S(2)}) copy-start(bf16[256,1024]{1,0:T(8,128)(2,1)} %copy-done.14) | copy-start | bytes 1572868
  179.2 2.4 %collective-permute-start.28 = (bf16[256,1536]{1,0:T(8,128)(2,1)S(1)}, bf16[256,1536]{1,0:T(8,128)(2,1)S(1)}, u32[]{:S(2)}, u32[]{:S(2)}) collective-permute-start(bf16[256,1536]{1,0:T(8,128)(2,1)S(1)} %get-tuple-element.199.refs_3_), channel_id=1, source_target_pairs={{0,1},{1,0},{2,3},{3,2},{4,5},{5,4},{6,7},{7,6},{8,9},{9,8},{10,11... | collective-permute-start | bytes 2359304 | tf_op jit(solution)/shard_map/ppermute | solution.py:339
  179.6 8.6 %copy-start.21 = (f32[128,1024]{1,0:T(8,128)S(1)}, f32[128,1024]{1,0:T(8,128)}, u32[]{:S(2)}) copy-start(f32[128,1024]{1,0:T(8,128)} %get-tuple-element.201.refs_5_) | copy-start | bytes 1572868
  179.6 8.6 %copy-start.30 = (bf16[128,1024]{1,0:T(8,128)(2,1)S(1)}, bf16[128,1024]{1,0:T(8,128)(2,1)}, u32[]{:S(2)}) copy-start(bf16[128,1024]{1,0:T(8,128)(2,1)} %copy-done.29) | copy-start | bytes 786436
  179.6 8.4 %collective-permute-start.27 = (bf16[128,1024]{1,0:T(8,128)(2,1)S(1)}, bf16[128,1024]{1,0:T(8,128)(2,1)S(1)}, u32[]{:S(2)}, u32[]{:S(2)}) collective-permute-start(bf16[128,1024]{1,0:T(8,128)(2,1)S(1)} %get-tuple-element.197), channel_id=1, source_target_pairs={{0,2},{1,3},{2,0},{3,1},{4,6},{5,7},{6,4},{7,5},{8,10},{9,11},{10,... | collective-permute-start | bytes 786440 | tf_op jit(solution)/shard_map/ppermute | solution.py:339
  188.0 19.6 %collective-permute-start.29 = (bf16[256,1536]{1,0:T(8,128)(2,1)S(1)}, bf16[256,1536]{1,0:T(8,128)(2,1)}, u32[]{:S(2)}, u32[]{:S(2)}) collective-permute-start(bf16[256,1536]{1,0:T(8,128)(2,1)S(1)} %leaving_gradient.3), channel_id=1, source_target_pairs={{0,3},{1,2},{2,1},{3,0},{4,7},{5,6},{6,5},{7,4},{8,11},{9,10},{10,... | collective-permute-start | bytes 2359304 | tf_op jit(solution)/shard_map/ppermute | solution.py:339
  190.1 22.4 %all-to-all-start.6 = ((bf16[8,32,1024]{2,1,0:T(8,128)(2,1)}), bf16[8,32,1024]{2,1,0:T(8,128)(2,1)S(1)}, u32[]{:S(2)}, u32[]{:S(2)}) async-start(bf16[8,32,1024]{2,1,0:T(8,128)(2,1)} %get-tuple-element.204), calls=%async_computation.6 | async-start | bytes 1048576 | tf_op jit(solution)/shard_map/all_to_all | solution.py:349
  195.6 12.0 %collective-permute-start.31 = (f32[2,1,256]{2,1,0:T(1,128)S(1)}, f32[2,1,256]{2,1,0:T(1,128)S(1)}, u32[]{:S(2)}, u32[]{:S(2)}) collective-permute-start(f32[2,1,256]{2,1,0:T(1,128)S(1)} %slice.20), channel_id=1, source_target_pairs={{0,2},{1,3},{2,0},{3,1},{4,6},{5,7},{6,4},{7,5},{8,10},{9,11},{10,... | collective-permute-start | bytes 6152 | tf_op jit(solution)/shard_map/ppermute | solution.py:339
  207.6 3.1 %collective-permute-start.30 = (bf16[256,1536]{1,0:T(8,128)(2,1)}, bf16[256,1536]{1,0:T(8,128)(2,1)S(1)}, u32[]{:S(2)}, u32[]{:S(2)}) collective-permute-start(bf16[256,1536]{1,0:T(8,128)(2,1)} %collective-permute-done.29), channel_id=1, source_target_pairs={{0,1},{1,0},{2,3},{3,2},{4,5},{5,4},{6,7},{7,6},{8,9},{9,8},{10,11... | collective-permute-start | bytes 2359304 | tf_op jit(solution)/shard_map/ppermute | solution.py:339
  207.6 2.5 %collective-permute-start.32 = (f32[1,256]{1,0:T(1,128)S(1)}, f32[1,256]{1,0:T(1,128)S(1)}, u32[]{:S(2)}, u32[]{:S(2)}) collective-permute-start(f32[1,256]{1,0:T(1,128)S(1)} %slice_bitcast_fusion), channel_id=1, source_target_pairs={{0,1},{1,0},{2,3},{3,2},{4,5},{5,4},{6,7},{7,6},{8,9},{9,8},{10,11... | collective-permute-start | bytes 3080 | tf_op jit(solution)/shard_map/ppermute | solution.py:339
  (15 other events, 42.4 us)

commit v6 on v5

--- a/solution.py
+++ b/solution.py
@@ -758,7 +758,7 @@
     return kernel_call(
         out_kernel,
         "out_term",
-        [(SMEM, place), (HBM, w_own), (HBM, w_near), in_vmem(*mixed)],
+        [(SMEM, place), (EITHER, w_own), (EITHER, w_near), in_vmem(*mixed)],
         [((rows, D), F32), ((rows, D), BF16), ((rows, inner), BF16)],
         [pltpu.VMEM((inner, D), BF16), pltpu.SemaphoreType.DMA((2,))],
     )
@@ -897,7 +897,7 @@
     return kernel_call(
         down_kernel,
         "down_term",
-        [(SMEM, place), (STAGED, hidden), (VMEM, resid), (HBM, w_own), (HBM, w_near)],
+        [(SMEM, place), (MOVED, hidden), (VMEM, resid), (EITHER, w_own), (EITHER, w_near)],
         [((rows // 2, D), F32), ((rows // 2, D), BF16)],
         [pltpu.VMEM((inner, D), BF16), pltpu.SemaphoreType.DMA((2,))],
     )
@@ -955,7 +955,7 @@
         mid_kernel,
         "mid",
         [(SMEM, place), (VMEM, second), (VMEM, far), (VMEM, resid), (MOVED, gains),
-         (MOVED, c_a), (MOVED, c_b), (HBM, w_own), (HBM, w_near)],
+         (MOVED, c_a), (MOVED, c_b), (EITHER, w_own), (EITHER, w_near)],
         [((rows // 2, D), F32, HBM), ((rows, D), BF16), ((2, 1, width), F32),
          block_shapes(rows, 2 * width, True)],
         [pltpu.VMEM((rows // 2, D), F32), pltpu.VMEM((2 * width, D), BF16),

time: 215 us -> 215 us (level)
    unnamed x78 -> x92, local copies, waits for them, and re-layouts: 4.39 us -> 4.38 us
  transfers between devices with their start and end apart: 40 -> 40, of which waited for: 19 -> 20; matrix products, arithmetic and copies ran while one was open for 1% -> 1% of each run, Pallas kernels for 28% -> 28%
where the time goes in v6:
time: 215 us; the launch traced here: 214 us
  Pallas kernels  81.7 us (38%)
  waiting for transfers between devices  70.4 us (33%)
  starting transfers between devices  53.7 us (25%)
  local copies, waits for them, and re-layouts  5.28 us (2%)
    pallas_call x24, Pallas kernels, kernel_call(): pl.pallas_call(body_kernel, name=name, in_specs=[spec for spec, _ in flat...  81.7 us
    ppermute x33, waiting for transfers between devices, swap(): return lax.ppermute(block, 'fsdp', [(i, i ^ mask) for i in range(count)])  49.4 us
    all_to_all x7, starting transfers between devices, exchange(): lax.all_to_all(blocks[0], 'fsdp', split_axis=0, concat_axis=0, tiled=True...  36.4 us
    all_to_all x7, waiting for transfers between devices, exchange(): lax.all_to_all(blocks[0], 'fsdp', split_axis=0, concat_axis=0, tiled=True...  21.1 us
    ppermute x33, starting transfers between devices, swap(): return lax.ppermute(block, 'fsdp', [(i, i ^ mask) for i in range(count)])  17.3 us
    unnamed x92, local copies, waits for them, and re-layouts  4.38 us
  transfers between devices with their start and end apart: 40, of which 20 were waited for; matrix products, arithmetic and copies ran while one was open for 1% of the time, Pallas kernels for 28%

profile of v6, /device:TPU:0, one launch (start us, length us, event | category | flops | bytes accessed | tf_op | source)
XLA Modules:
  0.0 214.0 jit_solution(10203179812750824118)
XLA Ops:
  0.8 2.9 %to_positions.1 = (bf16[8,16,1024]{2,1,0:T(8,128)(2,1)}, bf16[8,16,1024]{2,1,0:T(8,128)(2,1)}, bf16[256,1536]{1,0:T(8,128)(2,1)S(1)}) custom-call(s32[7]{0:T(128)S(1)} %stack.40.refs_0_, bf16[128,1024]{1,0:T(8,128)(2,1)} %refs_1_.3, bf16[128,1024]{1,0:T(8,128)(2,1)} %refs_2_.1, bf16[256,3072]{1,0:T(8,128)(2,1)} %refs_1_.7), custom_call_target="tpu_custom_call" | custom-call | flops 1 | bytes 1 | tf_op jit(solution)/shard_map/to_positions/pallas_call | solution.py:395
  3.7 2.5 %collective-permute-start.3 = (bf16[256,1536]{1,0:T(8,128)(2,1)S(1)}, bf16[256,1536]{1,0:T(8,128)(2,1)S(1)}, u32[]{:S(2)}, u32[]{:S(2)}) collective-permute-start(bf16[256,1536]{1,0:T(8,128)(2,1)S(1)} %get-tuple-element.115), channel_id=1, source_target_pairs={{0,3},{1,2},{2,1},{3,0},{4,7},{5,6},{6,5},{7,4},{8,11},{9,10},{10,... | collective-permute-start | bytes 2359304 | tf_op jit(solution)/shard_map/ppermute | solution.py:339
  6.1 5.8 %all-to-all-start = ((bf16[8,16,1024]{2,1,0:T(8,128)(2,1)}), bf16[8,16,1024]{2,1,0:T(8,128)(2,1)S(1)}, u32[]{:S(2)}, u32[]{:S(2)}) async-start(bf16[8,16,1024]{2,1,0:T(8,128)(2,1)} %get-tuple-element.114), calls=%async_computation | async-start | bytes 524288 | tf_op jit(solution)/shard_map/all_to_all | solution.py:349
  12.6 0.6 gather_fusion
  13.3 2.6 %kept_columns.1 = bf16[256,1536]{1,0:T(8,128)(2,1)} custom-call(s32[7]{0:T(128)S(1)} %stack.40.refs_0_, bf16[256,3072]{1,0:T(8,128)(2,1)} %refs_1_.7), custom_call_target="tpu_custom_call" | custom-call | flops 1 | bytes 1 | tf_op jit(solution)/shard_map/kept_columns/pallas_call | solution.py:395
  15.9 2.8 %spread.1 = (bf16[256,2816]{1,0:T(8,128)(2,1)S(1)}, bf16[256,768]{1,0:T(8,128)(2,1)S(1)}, bf16[256,2048]{1,0:T(8,128)(2,1)S(1)}) custom-call(s32[7]{0:T(128)S(1)} %stack.40.refs_0_, bf16[256,5632]{1,0:T(8,128)(2,1)} %refs_1_.5), custom_call_target="tpu_custom_call" | custom-call | flops 1 | bytes 1 | tf_op jit(solution)/shard_map/spread/pallas_call | solution.py:395
  18.7 1.1 copy-done.20
  19.8 1.0 copy-done.38
  20.9 0.8 all-to-all-done.refs_1_
  21.7 2.3 %collective-permute-done.3.refs_6_.refs_4_ = bf16[256,1536]{1,0:T(8,128)(2,1)S(1)} collective-permute-done((bf16[256,1536]{1,0:T(8,128)(2,1)S(1)}, bf16[256,1536]{1,0:T(8,128)(2,1)S(1)}, u32[]{:S(2)}, u32[]{:S(2)}) %collective-permute-start.3) | collective-permute-done | bytes 786464 | tf_op jit(solution)/shard_map/ppermute | solution.py:339
  24.1 0.6 collect.1.refs_1_.refs_3_
  24.7 2.5 %collective-permute-start.1 = (bf16[144,1024]{1,0:T(8,128)(2,1)S(1)}, bf16[144,1024]{1,0:T(8,128)(2,1)}, u32[]{:S(2)}, u32[]{:S(2)}) collective-permute-start(bf16[144,1024]{1,0:T(8,128)(2,1)S(1)} %collect.1.refs_1_.refs_3_), channel_id=1, source_target_pairs={{0,3},{1,2},{2,1},{3,0},{4,7},{5,6},{6,5},{7,4},{8,11},{9,10},{10,... | collective-permute-start | bytes 884744 | tf_op jit(solution)/shard_map/ppermute | solution.py:339
  27.3 5.8 %all-to-all-start.1 = ((bf16[8,16,1024]{2,1,0:T(8,128)(2,1)}), bf16[8,16,1024]{2,1,0:T(8,128)(2,1)}, u32[]{:S(2)}, u32[]{:S(2)}) async-start(bf16[8,16,1024]{2,1,0:T(8,128)(2,1)} %get-tuple-element.133), calls=%async_computation.1 | async-start | bytes 524288 | tf_op jit(solution)/shard_map/all_to_all | solution.py:349
  33.2 1.5 collective-permute-done.1
  34.8 1.7 collective-permute-done.2.refs_2_
  36.5 4.2 %first.1 = (bf16[8,32,1536]{2,1,0:T(8,128)(2,1)S(1)}, bf16[256,1024]{1,0:T(8,128)(2,1)}, f32[8,1024]{1,0:T(8,128)}) custom-call(s32[7]{0:T(128)S(1)} %stack.40.refs_0_, bf16[144,1024]{1,0:T(8,128)(2,1)S(1)} %collect.1.refs_1_.refs_3_, bf16[144,1024]{1,0:T(8,128)(2,1)S(1)} %collective-permute-done.2.refs_2_, bf16[256,3072]{1,0:T(8,128)(2,1)} %refs_1_.7, ...), custom_call_target="tpu_custom_call" | custom-call | flops 1 | bytes 1 | tf_op jit(solution)/shard_map/first/pallas_call | solution.py:395
  40.9 0.6 copy-done.25
  41.6 3.3 %collective-permute-done.6.refs_8_ = bf16[256,768]{1,0:T(8,128)(2,1)} collective-permute-done((bf16[256,768]{1,0:T(8,128)(2,1)}, bf16[256,768]{1,0:T(8,128)(2,1)}, u32[]{:S(2)}, u32[]{:S(2)}) %collective-permute-start.6) | collective-permute-done | bytes 393248 | tf_op jit(solution)/shard_map/ppermute | solution.py:339
  44.9 5.7 %all-to-all-start.2 = ((bf16[8,32,1536]{2,1,0:T(8,128)(2,1)}), bf16[8,32,1536]{2,1,0:T(8,128)(2,1)S(1)}, u32[]{:S(2)}, u32[]{:S(2)}) async-start(bf16[8,32,1536]{2,1,0:T(8,128)(2,1)} %copy-done.25), calls=%async_computation.2 | async-start | bytes 1572864 | tf_op jit(solution)/shard_map/all_to_all | solution.py:349
  50.7 0.8 collective-permute-start.9
  51.5 1.0 collect_rows.1.refs_4_.refs_5_.refs_3_
  52.6 0.8 copy-done.13
  53.4 17.4 %all-to-all-done.2.refs_2_ = bf16[8,32,1536]{2,1,0:T(8,128)(2,1)S(1)} async-done(((bf16[8,32,1536]{2,1,0:T(8,128)(2,1)}), bf16[8,32,1536]{2,1,0:T(8,128)(2,1)S(1)}, u32[]{:S(2)}, u32[]{:S(2)}) %all-to-all-start.2) | async-done | bytes 786464 | tf_op jit(solution)/shard_map/all_to_all | solution.py:349
  70.8 2.6 %attend.1 = bf16[8,32,512]{2,1,0:T(8,128)(2,1)} custom-call(s32[7]{0:T(128)S(1)} %stack.40.refs_0_, f32[8,1024]{1,0:T(8,128)S(1)} %copy-done.24, bf16[8,32,1536]{2,1,0:T(8,128)(2,1)S(1)} %all-to-all-done.2.refs_2_), custom_call_target="tpu_custom_call" | custom-call | flops 1 | bytes 1 | tf_op jit(solution)/shard_map/attend/pallas_call | solution.py:395
  73.5 4.1 %all-to-all-start.3 = ((bf16[8,32,512]{2,1,0:T(8,128)(2,1)}), bf16[8,32,512]{2,1,0:T(8,128)(2,1)}, u32[]{:S(2)}, u32[]{:S(2)}) async-start(bf16[8,32,512]{2,1,0:T(8,128)(2,1)} %attend.1), calls=%async_computation.3 | async-start | bytes 524288 | tf_op jit(solution)/shard_map/all_to_all | solution.py:349
  78.1 1.0 collective-permute-start.10
  79.2 0.7 copy-done.31
  79.9 6.4 %collective-permute-done.10.refs_5_.refs_6_.refs_4_ = bf16[128,1024]{1,0:T(8,128)(2,1)S(1)} collective-permute-done((bf16[128,1024]{1,0:T(8,128)(2,1)S(1)}, bf16[128,1024]{1,0:T(8,128)(2,1)S(1)}, u32[]{:S(2)}, u32[]{:S(2)}) %collective-permute-start.10) | collective-permute-done | bytes 262176 | tf_op jit(solution)/shard_map/ppermute | solution.py:339
  86.4 1.0 all-to-all-done.3.refs_3_
  87.4 1.7 out_term.1
  89.8 1.0 collective-permute-start.13
  90.9 3.6 %collective-permute-done.18.refs_6_ = bf16[128,1024]{1,0:T(8,128)(2,1)S(1)} collective-permute-done((bf16[128,1024]{1,0:T(8,128)(2,1)S(1)}, bf16[128,1024]{1,0:T(8,128)(2,1)S(1)}, u32[]{:S(2)}, u32[]{:S(2)}) %collective-permute-start.18) | collective-permute-done | bytes 262176 | tf_op jit(solution)/shard_map/ppermute | solution.py:339
  94.6 3.6 %aside.1 = (f32[256,1024]{1,0:T(8,128)S(1)}, f32[256,1408]{1,0:T(8,128)S(1)}) custom-call(s32[7]{0:T(128)S(1)} %stack.40.refs_0_, bf16[144,1024]{1,0:T(8,128)(2,1)S(1)} %collect.1.refs_1_.refs_3_, bf16[144,1024]{1,0:T(8,128)(2,1)S(1)} %copy-done.23, f32[256,1024]{1,0:T(8,128)S(1)} %get-tuple-element.149.refs_3_, ...), custom_call_target="tpu_custom_call" | custom-call | flops 1 | bytes 1 | tf_op jit(solution)/shard_map/aside/pallas_call | solution.py:395
  98.3 5.8 %collective-permute-done.13.refs_2_ = bf16[256,1024]{1,0:T(8,128)(2,1)S(1)} collective-permute-done((bf16[256,1024]{1,0:T(8,128)(2,1)S(1)}, bf16[256,1024]{1,0:T(8,128)(2,1)S(1)}, u32[]{:S(2)}, u32[]{:S(2)}) %collective-permute-start.13) | collective-permute-done | bytes 524320 | tf_op jit(solution)/shard_map/ppermute | solution.py:339
  104.0 7.9 %ffn.1 = (f32[256,1024]{1,0:T(8,128)S(1)}, bf16[256,1024]{1,0:T(8,128)(2,1)S(1)}, bf16[256,1408]{1,0:T(8,128)(2,1)S(1)}, bf16[256,2816]{1,0:T(8,128)(2,1)S(1)}, ...) custom-call(s32[7]{0:T(128)S(1)} %stack.40.refs_0_, f32[256,1024]{1,0:T(8,128)S(1)} %get-tuple-element.163.refs_1_, ...), custom_call_target="tpu_custom_call" | custom-call | flops 1 | bytes 1 | tf_op jit(solution)/shard_map/ffn/pallas_call | solution.py:395
  112.7 1.0 collective-permute-start.19
  113.6 4.1 %down_term.1 = (f32[128,1024]{1,0:T(8,128)S(1)}, bf16[128,1024]{1,0:T(8,128)(2,1)S(1)}) custom-call(s32[7]{0:T(128)S(1)} %stack.40.refs_0_, bf16[256,1408]{1,0:T(8,128)(2,1)S(1)} %get-tuple-element.188.refs_1_, f32[256,1024]{1,0:T(8,128)S(1)} %get-tuple-element.173.refs_2_.refs_3_, bf16[704,1024]{1,0:T(8,128)(2,1)S(1)} %copy-done.3, ...), custom_call_target="tpu_custom_call" | custom-call | flops 1 | bytes 1 | tf_op jit(solution)/shard_map/down_term/pallas_call | solution.py:395
  117.9 3.8 %leaving_gradient.2 = bf16[256,2816]{1,0:T(8,128)(2,1)S(1)} custom-call(s32[7]{0:T(128)S(1)} %stack.40.refs_0_, bf16[256,1024]{1,0:T(8,128)(2,1)S(1)} %get-tuple-element.183.refs_1_, bf16[256,1024]{1,0:T(8,128)(2,1)S(1)} %collective-permute-done.20.refs_2_, bf16[256,2816]{1,0:T(8,128)(2,1)S(1)} %get-tuple-element.178.refs_3_, ...), custom_call_target="tpu_custom_call" | custom-call | flops 1 | bytes 1 | tf_op jit(solution)/shard_map/leaving_gradient/pallas_call | solution.py:395
  121.8 5.2 %collective-permute-done.19.refs_2_ = bf16[256,1024]{1,0:T(8,128)(2,1)S(1)} collective-permute-done((bf16[256,1024]{1,0:T(8,128)(2,1)S(1)}, bf16[256,1024]{1,0:T(8,128)(2,1)S(1)}, u32[]{:S(2)}, u32[]{:S(2)}) %collective-permute-start.19) | collective-permute-done | bytes 524320 | tf_op jit(solution)/shard_map/ppermute | solution.py:339
  127.0 3.1 %mid.1 = (f32[128,1024]{1,0:T(8,128)}, bf16[256,1024]{1,0:T(8,128)(2,1)}, f32[2,1,256]{2,1,0:T(1,128)S(1)}, bf16[8,32,512]{2,1,0:T(8,128)(2,1)}) custom-call(s32[7]{0:T(128)S(1)} %stack.40.refs_0_, f32[256,1024]{1,0:T(8,128)S(1)} %get-tuple-element.169.refs_1_, bf16[256,1024]{1,0:T(8,128)(2,1)S(1)} %collective-permute-done.19.refs_2_, ...), custom_call_target="tpu_custom_call" | custom-call | flops 1 | bytes 1 | tf_op jit(solution)/shard_map/mid/pallas_call | solution.py:395
  130.2 4.8 %all-to-all-start.4 = ((bf16[8,32,512]{2,1,0:T(8,128)(2,1)}), bf16[8,32,512]{2,1,0:T(8,128)(2,1)S(1)}, u32[]{:S(2)}, u32[]{:S(2)}) async-start(bf16[8,32,512]{2,1,0:T(8,128)(2,1)} %get-tuple-element.180), calls=%async_computation.4 | async-start | bytes 524288 | tf_op jit(solution)/shard_map/all_to_all | solution.py:349
  135.0 0.8 collective-permute-start.25
  136.1 6.9 %staying_gradient.2.refs_2_ = f32[256,5632]{1,0:T(8,128)} custom-call(s32[7]{0:T(128)S(1)} %stack.40.refs_0_, bf16[256,1024]{1,0:T(8,128)(2,1)} %copy-done.18, bf16[256,1024]{1,0:T(8,128)(2,1)} %copy-done.19, bf16[256,2816]{1,0:T(8,128)(2,1)} %copy-done, bf16[256,2816]{1,0:T(8,128)(2,1)} %copy-done.1), custom_call_target="tpu_custom_call" | custom-call | flops 1 | bytes 1 | tf_op jit(solution)/shard_map/staying_gradient/pallas_call | solution.py:395
  143.1 1.5 all-to-all-done.4.refs_3_
  144.6 5.6 %attend_back.1 = bf16[8,32,1536]{2,1,0:T(8,128)(2,1)} custom-call(s32[7]{0:T(128)S(1)} %stack.40.refs_0_, f32[8,1024]{1,0:T(8,128)S(1)} %copy-done.24, bf16[8,32,1536]{2,1,0:T(8,128)(2,1)S(1)} %all-to-all-done.2.refs_2_, bf16[8,32,512]{2,1,0:T(8,128)(2,1)S(1)} %all-to-all-done.4.refs_3_), custom_call_target="tpu_custom_call" | custom-call | flops 1 | bytes 1 | tf_op jit(solution)/shard_map/attend_back/pallas_call | solution.py:395
  150.2 4.5 %all-to-all-start.5 = ((bf16[8,32,1536]{2,1,0:T(8,128)(2,1)}), bf16[8,32,1536]{2,1,0:T(8,128)(2,1)S(1)}, u32[]{:S(2)}, u32[]{:S(2)}) async-start(bf16[8,32,1536]{2,1,0:T(8,128)(2,1)} %attend_back.1), calls=%async_computation.5 | async-start | bytes 1572864 | tf_op jit(solution)/shard_map/all_to_all | solution.py:349
  154.7 1.1 collective-permute-start.26
  155.9 3.4 %grad_out.1 = f32[256,1024]{1,0:T(8,128)} custom-call(s32[7]{0:T(128)S(1)} %stack.40.refs_0_, bf16[256,512]{1,0:T(8,128)(2,1)} %copy-done.35, bf16[256,512]{1,0:T(8,128)(2,1)} %copy-done.42, bf16[256,1024]{1,0:T(8,128)(2,1)} %get-tuple-element.193.refs_3_, bf16[256,1024]{1,0:T(8,128)(2,1)} %collective-permute-done.23.refs_4_), custom_call_target="tpu_custom_call" | custom-call | flops 1 | bytes 1 | tf_op jit(solution)/shard_map/grad_out/pallas_call | solution.py:395
  159.3 4.7 %grad_down.1 = f32[704,1024]{1,0:T(8,128)} custom-call(s32[7]{0:T(128)S(1)} %stack.40.refs_0_, bf16[256,1408]{1,0:T(8,128)(2,1)S(1)} %get-tuple-element.188.refs_1_, bf16[256,1408]{1,0:T(8,128)(2,1)S(1)} %copy-done.27, bf16[128,1024]{1,0:T(8,128)(2,1)S(1)} %collect_rows.1.refs_4_.refs_5_.refs_3_, bf16[128,1024]{1,0:T(8,128)(2,1)S(1)} %copy-done.10, ...), custom_call_target="tpu_custom_call" | custom-call | flops 1 | bytes 1 | tf_op jit(solution)/shard_map/grad_down/pallas_call | solution.py:395
  164.0 10.7 %collective-permute-done.26.refs_7_ = bf16[128,1024]{1,0:T(8,128)(2,1)S(1)} collective-permute-done((bf16[128,1024]{1,0:T(8,128)(2,1)S(1)}, bf16[128,1024]{1,0:T(8,128)(2,1)S(1)}, u32[]{:S(2)}, u32[]{:S(2)}) %collective-permute-start.26) | collective-permute-done | bytes 262176 | tf_op jit(solution)/shard_map/ppermute | solution.py:339
  175.0 4.1 %back_first.1 = (f32[128,1024]{1,0:T(8,128)S(1)}, bf16[128,1024]{1,0:T(8,128)(2,1)S(1)}, bf16[256,1536]{1,0:T(8,128)(2,1)S(1)}) custom-call(s32[7]{0:T(128)S(1)} %stack.40.refs_0_, bf16[256,3072]{1,0:T(8,128)(2,1)} %refs_1_.7, bf16[256,1536]{1,0:T(8,128)(2,1)} %collective-permute-done.4.refs_4_.refs_2_, bf16[256,1536]{1,0:T(8,128)(2,1)} %copy-done.5, ...), custom_call_target="tpu_custom_call" | custom-call | flops 1 | bytes 1 | tf_op jit(solution)/shard_map/back_first/pallas_call | solution.py:395
  179.3 1.1 collective-permute-start.27
  180.4 1.1 collective-permute-done.28.refs_4_
  181.5 2.3 %leaving_gradient.3 = bf16[256,1536]{1,0:T(8,128)(2,1)S(1)} custom-call(s32[7]{0:T(128)S(1)} %stack.40.refs_0_, bf16[256,1024]{1,0:T(8,128)(2,1)S(1)} %copy-done.16, bf16[256,1024]{1,0:T(8,128)(2,1)S(1)} %collective-permute-done.12.refs_2_, bf16[256,1536]{1,0:T(8,128)(2,1)S(1)} %get-tuple-element.199.refs_3_, ...), custom_call_target="tpu_custom_call" | custom-call | flops 1 | bytes 1 | tf_op jit(solution)/shard_map/leaving_gradient/pallas_call | solution.py:395
  183.8 4.1 %collective-permute-done.27.refs_2_ = bf16[128,1024]{1,0:T(8,128)(2,1)S(1)} collective-permute-done((bf16[128,1024]{1,0:T(8,128)(2,1)S(1)}, bf16[128,1024]{1,0:T(8,128)(2,1)S(1)}, u32[]{:S(2)}, u32[]{:S(2)}) %collective-permute-start.27) | collective-permute-done | bytes 262176 | tf_op jit(solution)/shard_map/ppermute | solution.py:339
  188.2 1.9 last.1
  190.1 5.6 %all-to-all-start.6 = ((bf16[8,32,1024]{2,1,0:T(8,128)(2,1)}), bf16[8,32,1024]{2,1,0:T(8,128)(2,1)S(1)}, u32[]{:S(2)}, u32[]{:S(2)}) async-start(bf16[8,32,1024]{2,1,0:T(8,128)(2,1)} %get-tuple-element.204), calls=%async_computation.6 | async-start | bytes 1048576 | tf_op jit(solution)/shard_map/all_to_all | solution.py:349
  195.7 1.1 collective-permute-start.31
  196.9 3.6 %coming_gradient.2 = f32[256,5632]{1,0:T(8,128)} custom-call(s32[7]{0:T(128)S(1)} %stack.40.refs_0_, bf16[256,2816]{1,0:T(8,128)(2,1)} %collective-permute-done.25.refs_1_, f32[256,5632]{1,0:T(8,128)} %staying_gradient.2.refs_2_), custom_call_target="tpu_custom_call", output_to_operand_aliasing={{}: (2, {})} | custom-call | flops 1 | bytes 1 | tf_op jit(solution)/shard_map/coming_gradient/pallas_call | solution.py:395
  200.5 4.9 %staying_gradient.3.refs_2_ = f32[256,3072]{1,0:T(8,128)} custom-call(s32[7]{0:T(128)S(1)} %stack.40.refs_0_, bf16[256,1024]{1,0:T(8,128)(2,1)} %get-tuple-element.210.refs_1_, bf16[256,1024]{1,0:T(8,128)(2,1)} %copy-done.17, bf16[256,1536]{1,0:T(8,128)(2,1)} %copy-done.6, bf16[256,1536]{1,0:T(8,128)(2,1)} %copy-done.7), custom_call_target="tpu_custom_call" | custom-call | flops 1 | bytes 1 | tf_op jit(solution)/shard_map/staying_gradient/pallas_call | solution.py:395
  205.4 2.1 collective-permute-done.29
  208.7 1.1 collective-permute-done.32
  210.4 1.8 coming_gradient.3
  212.2 1.7 to_frames.1
  (150 shorter events, 6.9 us)
Async XLA Ops:
  0.6 11.3 %copy-start.44 = (bf16[256]{0:T(256)(128)(2,1)S(1)}, bf16[256]{0:T(256)(128)(2,1)}, u32[]{:S(2)}) copy-start(bf16[256]{0:T(256)(128)(2,1)} %param.11) | copy-start | bytes 1540
  0.6 11.3 %copy-start.45 = (bf16[256]{0:T(256)(128)(2,1)S(1)}, bf16[256]{0:T(256)(128)(2,1)}, u32[]{:S(2)}) copy-start(bf16[256]{0:T(256)(128)(2,1)} %param.14) | copy-start | bytes 1540
  0.7 11.8 %copy-start.43 = (s32[128]{0:T(128)S(1)}, s32[128]{0:T(128)}, u32[]{:S(2)}) copy-start(s32[128]{0:T(128)} %param.10) | copy-start | bytes 1540
  3.7 20.4 %collective-permute-start.3 = (bf16[256,1536]{1,0:T(8,128)(2,1)S(1)}, bf16[256,1536]{1,0:T(8,128)(2,1)S(1)}, u32[]{:S(2)}, u32[]{:S(2)}) collective-permute-start(bf16[256,1536]{1,0:T(8,128)(2,1)S(1)} %get-tuple-element.115), channel_id=1, source_target_pairs={{0,3},{1,2},{2,1},{3,0},{4,7},{5,6},{6,5},{7,4},{8,11},{9,10},{10,... | collective-permute-start | bytes 2359304 | tf_op jit(solution)/shard_map/ppermute | solution.py:339
  6.1 15.6 %all-to-all-start = ((bf16[8,16,1024]{2,1,0:T(8,128)(2,1)}), bf16[8,16,1024]{2,1,0:T(8,128)(2,1)S(1)}, u32[]{:S(2)}, u32[]{:S(2)}) async-start(bf16[8,16,1024]{2,1,0:T(8,128)(2,1)} %get-tuple-element.114), calls=%async_computation | async-start | bytes 524288 | tf_op jit(solution)/shard_map/all_to_all | solution.py:349
  12.0 8.9 %collective-permute-start = (bf16[2,256]{1,0:T(2,128)(2,1)S(1)}, bf16[2,256]{1,0:T(2,128)(2,1)S(1)}, u32[]{:S(2)}, u32[]{:S(2)}) collective-permute-start(bf16[2,256]{1,0:T(2,128)(2,1)S(1)} %pad_maximum_fusion.refs_3_), channel_id=1, source_target_pairs={{0,1},{1,0},{2,3},{3,2},{4,5},{5,4},{6,7},{7,6},{8,9},{9,8},{10,11... | collective-permute-start | bytes 3080 | tf_op jit(solution)/shard_map/ppermute | solution.py:339
  20.8 6.5 %copy-start.39 = (bf16[256,768]{1,0:T(8,128)(2,1)}, bf16[256,768]{1,0:T(8,128)(2,1)S(1)}, u32[]{:S(2)}) copy-start(bf16[256,768]{1,0:T(8,128)(2,1)S(1)} %get-tuple-element.135) | copy-start | bytes 1179652
  21.7 14.7 %collective-permute-start.5 = (bf16[256,1536]{1,0:T(8,128)(2,1)}, bf16[256,1536]{1,0:T(8,128)(2,1)S(1)}, u32[]{:S(2)}, u32[]{:S(2)}) collective-permute-start(bf16[256,1536]{1,0:T(8,128)(2,1)} %kept_columns.1), channel_id=1, source_target_pairs={{0,1},{1,0},{2,3},{3,2},{4,5},{5,4},{6,7},{7,6},{8,9},{9,8},{10,11... | collective-permute-start | bytes 2359304 | tf_op jit(solution)/shard_map/ppermute | solution.py:339
  24.1 16.6 %copy-start.4 = (bf16[256,1536]{1,0:T(8,128)(2,1)}, bf16[256,1536]{1,0:T(8,128)(2,1)S(1)}, u32[]{:S(2)}) copy-start(bf16[256,1536]{1,0:T(8,128)(2,1)S(1)} %collective-permute-done.3.refs_6_.refs_4_) | copy-start | bytes 2359300
  24.1 12.4 %collective-permute-start.4 = (bf16[256,1536]{1,0:T(8,128)(2,1)S(1)}, bf16[256,1536]{1,0:T(8,128)(2,1)}, u32[]{:S(2)}, u32[]{:S(2)}) collective-permute-start(bf16[256,1536]{1,0:T(8,128)(2,1)S(1)} %collective-permute-done.3.refs_6_.refs_4_), channel_id=1, source_target_pairs={{0,1},{1,0},{2,3},{3,2},{4,5},{5,4},{6,7},{7,6},{8,9},{9,8},{10,11... | collective-permute-start | bytes 2359304 | tf_op jit(solution)/shard_map/ppermute | solution.py:339
  24.7 9.9 %collective-permute-start.1 = (bf16[144,1024]{1,0:T(8,128)(2,1)S(1)}, bf16[144,1024]{1,0:T(8,128)(2,1)}, u32[]{:S(2)}, u32[]{:S(2)}) collective-permute-start(bf16[144,1024]{1,0:T(8,128)(2,1)S(1)} %collect.1.refs_1_.refs_3_), channel_id=1, source_target_pairs={{0,3},{1,2},{2,1},{3,0},{4,7},{5,6},{6,5},{7,4},{8,11},{9,10},{10,... | collective-permute-start | bytes 884744 | tf_op jit(solution)/shard_map/ppermute | solution.py:339
  27.3 17.6 %all-to-all-start.1 = ((bf16[8,16,1024]{2,1,0:T(8,128)(2,1)}), bf16[8,16,1024]{2,1,0:T(8,128)(2,1)}, u32[]{:S(2)}, u32[]{:S(2)}) async-start(bf16[8,16,1024]{2,1,0:T(8,128)(2,1)} %get-tuple-element.133), calls=%async_computation.1 | async-start | bytes 524288 | tf_op jit(solution)/shard_map/all_to_all | solution.py:349
  33.1 7.6 %copy-start.2 = (bf16[704,1024]{1,0:T(8,128)(2,1)S(1)}, bf16[704,1024]{1,0:T(8,128)(2,1)}, u32[]{:S(2)}) copy-start(bf16[704,1024]{1,0:T(8,128)(2,1)} %refs_3_.5) | copy-start | bytes 4325380
  33.1 11.8 %collective-permute-start.6 = (bf16[256,768]{1,0:T(8,128)(2,1)}, bf16[256,768]{1,0:T(8,128)(2,1)}, u32[]{:S(2)}, u32[]{:S(2)}) collective-permute-start(bf16[256,768]{1,0:T(8,128)(2,1)} %copy-done.39), channel_id=1, source_target_pairs={{0,3},{1,2},{2,1},{3,0},{4,7},{5,6},{6,5},{7,4},{8,11},{9,10},{10,... | collective-permute-start | bytes 1179656 | tf_op jit(solution)/shard_map/ppermute | solution.py:339
  34.7 1.8 collective-permute-start.2
  40.7 30.1 %copy-start.24 = (f32[8,1024]{1,0:T(8,128)S(1)}, f32[8,1024]{1,0:T(8,128)}, u32[]{:S(2)}) copy-start(f32[8,1024]{1,0:T(8,128)} %get-tuple-element.130.refs_1_.refs_3_.refs_4_) | copy-start | bytes 98308
  40.7 9.9 %copy-start.11 = (bf16[256,1024]{1,0:T(8,128)(2,1)S(1)}, bf16[256,1024]{1,0:T(8,128)(2,1)}, u32[]{:S(2)}) copy-start(bf16[256,1024]{1,0:T(8,128)(2,1)} %refs_7_.1) | copy-start | bytes 1572868
  40.7 30.0 %collective-permute-start.8 = (bf16[704,1024]{1,0:T(8,128)(2,1)S(1)}, bf16[704,1024]{1,0:T(8,128)(2,1)}, u32[]{:S(2)}, u32[]{:S(2)}) collective-permute-start(bf16[704,1024]{1,0:T(8,128)(2,1)S(1)} %copy-done.2), channel_id=1, source_target_pairs={{0,1},{1,0},{2,3},{3,2},{4,5},{5,4},{6,7},{7,6},{8,9},{9,8},{10,11... | collective-permute-start | bytes 4325384 | tf_op jit(solution)/shard_map/ppermute | solution.py:339
  44.9 25.9 %all-to-all-start.2 = ((bf16[8,32,1536]{2,1,0:T(8,128)(2,1)}), bf16[8,32,1536]{2,1,0:T(8,128)(2,1)S(1)}, u32[]{:S(2)}, u32[]{:S(2)}) async-start(bf16[8,32,1536]{2,1,0:T(8,128)(2,1)} %copy-done.25), calls=%async_computation.2 | async-start | bytes 1572864 | tf_op jit(solution)/shard_map/all_to_all | solution.py:349
  50.6 2.0 collective-permute-start.7
  50.7 28.4 %collective-permute-start.9 = (bf16[256,2048]{1,0:T(8,128)(2,1)}, bf16[256,2048]{1,0:T(8,128)(2,1)}, u32[]{:S(2)}, u32[]{:S(2)}) collective-permute-start(bf16[256,2048]{1,0:T(8,128)(2,1)} %copy-done.38), channel_id=1, source_target_pairs={{0,3},{1,2},{2,1},{3,0},{4,7},{5,6},{6,5},{7,4},{8,11},{9,10},{10,... | collective-permute-start | bytes 3145736 | tf_op jit(solution)/shard_map/ppermute | solution.py:339
  70.8 16.6 %copy-start.14 = (bf16[256,1024]{1,0:T(8,128)(2,1)S(1)}, bf16[256,1024]{1,0:T(8,128)(2,1)}, u32[]{:S(2)}) copy-start(bf16[256,1024]{1,0:T(8,128)(2,1)} %copy-done.13) | copy-start | bytes 1572868
  70.8 23.9 %copy-start.23 = (bf16[144,1024]{1,0:T(8,128)(2,1)S(1)}, bf16[144,1024]{1,0:T(8,128)(2,1)}, u32[]{:S(2)}) copy-start(bf16[144,1024]{1,0:T(8,128)(2,1)} %copy-done.22) | copy-start | bytes 884740
  73.4 14.0 %collective-permute-start.12 = (bf16[256,1024]{1,0:T(8,128)(2,1)}, bf16[256,1024]{1,0:T(8,128)(2,1)S(1)}, u32[]{:S(2)}, u32[]{:S(2)}) collective-permute-start(bf16[256,1024]{1,0:T(8,128)(2,1)} %get-tuple-element.210.refs_1_), channel_id=1, source_target_pairs={{0,1},{1,0},{2,3},{3,2},{4,5},{5,4},{6,7},{7,6},{8,9},{9,8},{10,11... | collective-permute-start | bytes 1572872 | tf_op jit(solution)/shard_map/ppermute | solution.py:339
  73.5 13.9 %all-to-all-start.3 = ((bf16[8,32,512]{2,1,0:T(8,128)(2,1)}), bf16[8,32,512]{2,1,0:T(8,128)(2,1)}, u32[]{:S(2)}, u32[]{:S(2)}) async-start(bf16[8,32,512]{2,1,0:T(8,128)(2,1)} %attend.1), calls=%async_computation.3 | async-start | bytes 524288 | tf_op jit(solution)/shard_map/all_to_all | solution.py:349
  77.5 1.7 collective-permute-start.11
  78.1 8.3 %collective-permute-start.10 = (bf16[128,1024]{1,0:T(8,128)(2,1)S(1)}, bf16[128,1024]{1,0:T(8,128)(2,1)S(1)}, u32[]{:S(2)}, u32[]{:S(2)}) collective-permute-start(bf16[128,1024]{1,0:T(8,128)(2,1)S(1)} %collect_rows.1.refs_4_.refs_5_.refs_3_), channel_id=1, source_target_pairs={{0,2},{1,3},{2,0},{3,1},{4,6},{5,7},{6,4},{7,5},{8,10},{9,11},{10,... | collective-permute-start | bytes 786440 | tf_op jit(solution)/shard_map/ppermute | solution.py:339
  86.4 11.8 %copy-start.8 = (bf16[128,1024]{1,0:T(8,128)(2,1)}, bf16[128,1024]{1,0:T(8,128)(2,1)S(1)}, u32[]{:S(2)}) copy-start(bf16[128,1024]{1,0:T(8,128)(2,1)S(1)} %collective-permute-done.10.refs_5_.refs_6_.refs_4_) | copy-start | bytes 786436
  87.4 94.1 %copy-start.17 = (bf16[256,1024]{1,0:T(8,128)(2,1)}, bf16[256,1024]{1,0:T(8,128)(2,1)S(1)}, u32[]{:S(2)}) copy-start(bf16[256,1024]{1,0:T(8,128)(2,1)S(1)} %collective-permute-done.12.refs_2_) | copy-start | bytes 1572868
  89.1 9.1 %copy-start.35 = (bf16[256,512]{1,0:T(8,128)(2,1)}, bf16[256,512]{1,0:T(8,128)(2,1)S(1)}, u32[]{:S(2)}) copy-start(bf16[256,512]{1,0:T(8,128)(2,1)S(1)} %get-tuple-element.156.refs_1_) | copy-start | bytes 786436
  89.1 14.9 %collective-permute-start.17 = (bf16[256,2816]{1,0:T(8,128)(2,1)}, bf16[256,2816]{1,0:T(8,128)(2,1)S(1)}, u32[]{:S(2)}, u32[]{:S(2)}) collective-permute-start(bf16[256,2816]{1,0:T(8,128)(2,1)} %copy-done.20), channel_id=1, source_target_pairs={{0,1},{1,0},{2,3},{3,2},{4,5},{5,4},{6,7},{7,6},{8,9},{9,8},{10,11... | collective-permute-start | bytes 4325384 | tf_op jit(solution)/shard_map/ppermute | solution.py:339
  89.2 14.8 %collective-permute-start.16 = (bf16[256,2048]{1,0:T(8,128)(2,1)}, bf16[256,2048]{1,0:T(8,128)(2,1)S(1)}, u32[]{:S(2)}, u32[]{:S(2)}) collective-permute-start(bf16[256,2048]{1,0:T(8,128)(2,1)} %collective-permute-done.9.refs_10_), channel_id=1, source_target_pairs={{0,1},{1,0},{2,3},{3,2},{4,5},{5,4},{6,7},{7,6},{8,9},{9,8},{10,11... | collective-permute-start | bytes 3145736 | tf_op jit(solution)/shard_map/ppermute | solution.py:339
  89.7 4.8 %collective-permute-start.18 = (bf16[128,1024]{1,0:T(8,128)(2,1)S(1)}, bf16[128,1024]{1,0:T(8,128)(2,1)S(1)}, u32[]{:S(2)}, u32[]{:S(2)}) collective-permute-start(bf16[128,1024]{1,0:T(8,128)(2,1)S(1)} %collective-permute-done.10.refs_5_.refs_6_.refs_4_), channel_id=1, source_target_pairs={{0,1},{1,0},{2,3},{3,2},{4,5},{5,4},{6,7},{7,6},{8,9},{9,8},{10,11... | collective-permute-start | bytes 786440 | tf_op jit(solution)/shard_map/ppermute | solution.py:339
  89.8 14.3 %collective-permute-start.13 = (bf16[256,1024]{1,0:T(8,128)(2,1)S(1)}, bf16[256,1024]{1,0:T(8,128)(2,1)S(1)}, u32[]{:S(2)}, u32[]{:S(2)}) collective-permute-start(bf16[256,1024]{1,0:T(8,128)(2,1)S(1)} %get-tuple-element.148), channel_id=1, source_target_pairs={{0,2},{1,3},{2,0},{3,1},{4,6},{5,7},{6,4},{7,5},{8,10},{9,11},{10,... | collective-permute-start | bytes 1572872 | tf_op jit(solution)/shard_map/ppermute | solution.py:339
  90.7 7.5 %collective-permute-start.15 = (bf16[256,768]{1,0:T(8,128)(2,1)}, bf16[256,768]{1,0:T(8,128)(2,1)S(1)}, u32[]{:S(2)}, u32[]{:S(2)}) collective-permute-start(bf16[256,768]{1,0:T(8,128)(2,1)} %collective-permute-done.6.refs_8_), channel_id=1, source_target_pairs={{0,1},{1,0},{2,3},{3,2},{4,5},{5,4},{6,7},{7,6},{8,9},{9,8},{10,11... | collective-permute-start | bytes 1179656 | tf_op jit(solution)/shard_map/ppermute | solution.py:339
  94.5 3.7 %collective-permute-start.14 = (bf16[256,512]{1,0:T(8,128)(2,1)S(1)}, bf16[256,512]{1,0:T(8,128)(2,1)S(1)}, u32[]{:S(2)}, u32[]{:S(2)}) collective-permute-start(bf16[256,512]{1,0:T(8,128)(2,1)S(1)} %get-tuple-element.156.refs_1_), channel_id=1, source_target_pairs={{0,1},{1,0},{2,3},{3,2},{4,5},{5,4},{6,7},{7,6},{8,9},{9,8},{10,11... | collective-permute-start | bytes 786440 | tf_op jit(solution)/shard_map/ppermute | solution.py:339
  104.0 9.6 %copy-start.3 = (bf16[704,1024]{1,0:T(8,128)(2,1)S(1)}, bf16[704,1024]{1,0:T(8,128)(2,1)}, u32[]{:S(2)}) copy-start(bf16[704,1024]{1,0:T(8,128)(2,1)} %refs_3_.5) | copy-start | bytes 4325380
  112.0 5.8 %copy-start = (bf16[256,2816]{1,0:T(8,128)(2,1)}, bf16[256,2816]{1,0:T(8,128)(2,1)S(1)}, u32[]{:S(2)}) copy-start(bf16[256,2816]{1,0:T(8,128)(2,1)S(1)} %get-tuple-element.178.refs_3_) | copy-start | bytes 4325380
  112.0 5.8 %collective-permute-start.21 = (bf16[256,2816]{1,0:T(8,128)(2,1)S(1)}, bf16[256,2816]{1,0:T(8,128)(2,1)S(1)}, u32[]{:S(2)}, u32[]{:S(2)}) collective-permute-start(bf16[256,2816]{1,0:T(8,128)(2,1)S(1)} %get-tuple-element.178.refs_3_), channel_id=1, source_target_pairs={{0,1},{1,0},{2,3},{3,2},{4,5},{5,4},{6,7},{7,6},{8,9},{9,8},{10,11... | collective-permute-start | bytes 4325384 | tf_op jit(solution)/shard_map/ppermute | solution.py:339
  112.1 14.8 %collective-permute-start.22 = (bf16[256,1408]{1,0:T(8,128)(2,1)S(1)}, bf16[256,1408]{1,0:T(8,128)(2,1)S(1)}, u32[]{:S(2)}, u32[]{:S(2)}) collective-permute-start(bf16[256,1408]{1,0:T(8,128)(2,1)S(1)} %get-tuple-element.188.refs_1_), channel_id=1, source_target_pairs={{0,1},{1,0},{2,3},{3,2},{4,5},{5,4},{6,7},{7,6},{8,9},{9,8},{10,11... | collective-permute-start | bytes 2162696 | tf_op jit(solution)/shard_map/ppermute | solution.py:339
  112.6 5.2 %collective-permute-start.20 = (bf16[256,1024]{1,0:T(8,128)(2,1)S(1)}, bf16[256,1024]{1,0:T(8,128)(2,1)S(1)}, u32[]{:S(2)}, u32[]{:S(2)}) collective-permute-start(bf16[256,1024]{1,0:T(8,128)(2,1)S(1)} %get-tuple-element.183.refs_1_), channel_id=1, source_target_pairs={{0,1},{1,0},{2,3},{3,2},{4,5},{5,4},{6,7},{7,6},{8,9},{9,8},{10,11... | collective-permute-start | bytes 1572872 | tf_op jit(solution)/shard_map/ppermute | solution.py:339
  112.7 14.3 %collective-permute-start.19 = (bf16[256,1024]{1,0:T(8,128)(2,1)S(1)}, bf16[256,1024]{1,0:T(8,128)(2,1)S(1)}, u32[]{:S(2)}, u32[]{:S(2)}) collective-permute-start(bf16[256,1024]{1,0:T(8,128)(2,1)S(1)} %get-tuple-element.170), channel_id=1, source_target_pairs={{0,2},{1,3},{2,0},{3,1},{4,6},{5,7},{6,4},{7,5},{8,10},{9,11},{10,... | collective-permute-start | bytes 1572872 | tf_op jit(solution)/shard_map/ppermute | solution.py:339
  117.8 9.2 %copy-start.9 = (bf16[128,1024]{1,0:T(8,128)(2,1)S(1)}, bf16[128,1024]{1,0:T(8,128)(2,1)}, u32[]{:S(2)}) copy-start(bf16[128,1024]{1,0:T(8,128)(2,1)} %copy-done.8) | copy-start | bytes 786436
  117.8 9.2 %copy-start.12 = (bf16[256,1024]{1,0:T(8,128)(2,1)S(1)}, bf16[256,1024]{1,0:T(8,128)(2,1)}, u32[]{:S(2)}) copy-start(bf16[256,1024]{1,0:T(8,128)(2,1)} %refs_7_.1) | copy-start | bytes 1572868
  117.8 9.2 %copy-start.15 = (bf16[256,1024]{1,0:T(8,128)(2,1)S(1)}, bf16[256,1024]{1,0:T(8,128)(2,1)}, u32[]{:S(2)}) copy-start(bf16[256,1024]{1,0:T(8,128)(2,1)} %copy-done.13) | copy-start | bytes 1572868
  121.7 8.4 %copy-start.21 = (bf16[256,2816]{1,0:T(8,128)(2,1)}, bf16[256,2816]{1,0:T(8,128)(2,1)S(1)}, u32[]{:S(2)}) copy-start(bf16[256,2816]{1,0:T(8,128)(2,1)S(1)} %leaving_gradient.2) | copy-start | bytes 4325380
  130.1 14.5 %collective-permute-start.23 = (bf16[256,1024]{1,0:T(8,128)(2,1)}, bf16[256,1024]{1,0:T(8,128)(2,1)}, u32[]{:S(2)}, u32[]{:S(2)}) collective-permute-start(bf16[256,1024]{1,0:T(8,128)(2,1)} %get-tuple-element.193.refs_3_), channel_id=1, source_target_pairs={{0,1},{1,0},{2,3},{3,2},{4,5},{5,4},{6,7},{7,6},{8,9},{9,8},{10,11... | collective-permute-start | bytes 1572872 | tf_op jit(solution)/shard_map/ppermute | solution.py:339
  130.2 14.4 %all-to-all-start.4 = ((bf16[8,32,512]{2,1,0:T(8,128)(2,1)}), bf16[8,32,512]{2,1,0:T(8,128)(2,1)S(1)}, u32[]{:S(2)}, u32[]{:S(2)}) async-start(bf16[8,32,512]{2,1,0:T(8,128)(2,1)} %get-tuple-element.180), calls=%async_computation.4 | async-start | bytes 524288 | tf_op jit(solution)/shard_map/all_to_all | solution.py:349
  135.0 39.7 %collective-permute-start.25 = (bf16[256,2816]{1,0:T(8,128)(2,1)}, bf16[256,2816]{1,0:T(8,128)(2,1)}, u32[]{:S(2)}, u32[]{:S(2)}) collective-permute-start(bf16[256,2816]{1,0:T(8,128)(2,1)} %copy-done.21), channel_id=1, source_target_pairs={{0,3},{1,2},{2,1},{3,0},{4,7},{5,6},{6,5},{7,4},{8,11},{9,10},{10,... | collective-permute-start | bytes 4325384 | tf_op jit(solution)/shard_map/ppermute | solution.py:339
  135.8 7.3 %collective-permute-start.24 = (f32[1,256]{1,0:T(1,128)S(1)}, f32[1,256]{1,0:T(1,128)S(1)}, u32[]{:S(2)}, u32[]{:S(2)}) collective-permute-start(f32[1,256]{1,0:T(1,128)S(1)} %slice_bitcast_fusion.2), channel_id=1, source_target_pairs={{0,1},{1,0},{2,3},{3,2},{4,5},{5,4},{6,7},{7,6},{8,9},{9,8},{10,11... | collective-permute-start | bytes 3080 | tf_op jit(solution)/shard_map/ppermute | solution.py:339
  143.1 11.6 %copy-start.41 = (bf16[128,1024]{1,0:T(8,128)(2,1)S(1)}, bf16[128,1024]{1,0:T(8,128)(2,1)}, u32[]{:S(2)}) copy-start(bf16[128,1024]{1,0:T(8,128)(2,1)} %copy-done.40) | copy-start | bytes 786436
  150.2 24.9 %all-to-all-start.5 = ((bf16[8,32,1536]{2,1,0:T(8,128)(2,1)}), bf16[8,32,1536]{2,1,0:T(8,128)(2,1)S(1)}, u32[]{:S(2)}, u32[]{:S(2)}) async-start(bf16[8,32,1536]{2,1,0:T(8,128)(2,1)} %attend_back.1), calls=%async_computation.5 | async-start | bytes 1572864 | tf_op jit(solution)/shard_map/all_to_all | solution.py:349
  154.7 20.0 %collective-permute-start.26 = (bf16[128,1024]{1,0:T(8,128)(2,1)S(1)}, bf16[128,1024]{1,0:T(8,128)(2,1)S(1)}, u32[]{:S(2)}, u32[]{:S(2)}) collective-permute-start(bf16[128,1024]{1,0:T(8,128)(2,1)S(1)} %copy-done.41), channel_id=1, source_target_pairs={{0,2},{1,3},{2,0},{3,1},{4,6},{5,7},{6,4},{7,5},{8,10},{9,11},{10,... | collective-permute-start | bytes 786440 | tf_op jit(solution)/shard_map/ppermute | solution.py:339
  164.0 17.5 %copy-start.16 = (bf16[256,1024]{1,0:T(8,128)(2,1)S(1)}, bf16[256,1024]{1,0:T(8,128)(2,1)}, u32[]{:S(2)}) copy-start(bf16[256,1024]{1,0:T(8,128)(2,1)} %get-tuple-element.210.refs_1_) | copy-start | bytes 1572868
  179.1 2.4 %collective-permute-start.28 = (bf16[256,1536]{1,0:T(8,128)(2,1)S(1)}, bf16[256,1536]{1,0:T(8,128)(2,1)S(1)}, u32[]{:S(2)}, u32[]{:S(2)}) collective-permute-start(bf16[256,1536]{1,0:T(8,128)(2,1)S(1)} %get-tuple-element.199.refs_3_), channel_id=1, source_target_pairs={{0,1},{1,0},{2,3},{3,2},{4,5},{5,4},{6,7},{7,6},{8,9},{9,8},{10,11... | collective-permute-start | bytes 2359304 | tf_op jit(solution)/shard_map/ppermute | solution.py:339
  179.2 9.0 %copy-start.29 = (f32[128,1024]{1,0:T(8,128)S(1)}, f32[128,1024]{1,0:T(8,128)}, u32[]{:S(2)}) copy-start(f32[128,1024]{1,0:T(8,128)} %copy-done.28) | copy-start | bytes 1572868
  179.2 8.9 %copy-start.30 = (f32[128,1024]{1,0:T(8,128)S(1)}, f32[128,1024]{1,0:T(8,128)}, u32[]{:S(2)}) copy-start(f32[128,1024]{1,0:T(8,128)} %get-tuple-element.201.refs_5_) | copy-start | bytes 1572868
  179.2 8.9 %copy-start.37 = (bf16[128,1024]{1,0:T(8,128)(2,1)S(1)}, bf16[128,1024]{1,0:T(8,128)(2,1)}, u32[]{:S(2)}) copy-start(bf16[128,1024]{1,0:T(8,128)(2,1)} %copy-done.36) | copy-start | bytes 786436
  179.3 8.7 %collective-permute-start.27 = (bf16[128,1024]{1,0:T(8,128)(2,1)S(1)}, bf16[128,1024]{1,0:T(8,128)(2,1)S(1)}, u32[]{:S(2)}, u32[]{:S(2)}) collective-permute-start(bf16[128,1024]{1,0:T(8,128)(2,1)S(1)} %get-tuple-element.197), channel_id=1, source_target_pairs={{0,2},{1,3},{2,0},{3,1},{4,6},{5,7},{6,4},{7,5},{8,10},{9,11},{10,... | collective-permute-start | bytes 786440 | tf_op jit(solution)/shard_map/ppermute | solution.py:339
  187.9 19.6 %collective-permute-start.29 = (bf16[256,1536]{1,0:T(8,128)(2,1)S(1)}, bf16[256,1536]{1,0:T(8,128)(2,1)S(1)}, u32[]{:S(2)}, u32[]{:S(2)}) collective-permute-start(bf16[256,1536]{1,0:T(8,128)(2,1)S(1)} %leaving_gradient.3), channel_id=1, source_target_pairs={{0,3},{1,2},{2,1},{3,0},{4,7},{5,6},{6,5},{7,4},{8,11},{9,10},{10,... | collective-permute-start | bytes 2359304 | tf_op jit(solution)/shard_map/ppermute | solution.py:339
  190.1 22.1 %all-to-all-start.6 = ((bf16[8,32,1024]{2,1,0:T(8,128)(2,1)}), bf16[8,32,1024]{2,1,0:T(8,128)(2,1)S(1)}, u32[]{:S(2)}, u32[]{:S(2)}) async-start(bf16[8,32,1024]{2,1,0:T(8,128)(2,1)} %get-tuple-element.204), calls=%async_computation.6 | async-start | bytes 1048576 | tf_op jit(solution)/shard_map/all_to_all | solution.py:349
  195.7 11.8 %collective-permute-start.31 = (f32[2,1,256]{2,1,0:T(1,128)S(1)}, f32[2,1,256]{2,1,0:T(1,128)S(1)}, u32[]{:S(2)}, u32[]{:S(2)}) collective-permute-start(f32[2,1,256]{2,1,0:T(1,128)S(1)} %slice.20), channel_id=1, source_target_pairs={{0,2},{1,3},{2,0},{3,1},{4,6},{5,7},{6,4},{7,5},{8,10},{9,11},{10,... | collective-permute-start | bytes 6152 | tf_op jit(solution)/shard_map/ppermute | solution.py:339
  207.5 2.9 %collective-permute-start.30 = (bf16[256,1536]{1,0:T(8,128)(2,1)S(1)}, bf16[256,1536]{1,0:T(8,128)(2,1)S(1)}, u32[]{:S(2)}, u32[]{:S(2)}) collective-permute-start(bf16[256,1536]{1,0:T(8,128)(2,1)S(1)} %collective-permute-done.29), channel_id=1, source_target_pairs={{0,1},{1,0},{2,3},{3,2},{4,5},{5,4},{6,7},{7,6},{8,9},{9,8},{10,11... | collective-permute-start | bytes 2359304 | tf_op jit(solution)/shard_map/ppermute | solution.py:339
  207.6 2.3 %collective-permute-start.32 = (f32[1,256]{1,0:T(1,128)S(1)}, f32[1,256]{1,0:T(1,128)S(1)}, u32[]{:S(2)}, u32[]{:S(2)}) collective-permute-start(f32[1,256]{1,0:T(1,128)S(1)} %slice_bitcast_fusion), channel_id=1, source_target_pairs={{0,1},{1,0},{2,3},{3,2},{4,5},{5,4},{6,7},{7,6},{8,9},{9,8},{10,11... | collective-permute-start | bytes 3080 | tf_op jit(solution)/shard_map/ppermute | solution.py:339
  (22 other events, 76.7 us)
